TPU v7x, 32 devices: a whole 2x2x4 slice. The times are simulated.
32 devices in a mesh: groups: 2 (over x), seq: 16 (over z, y, core).
Axes of the slice: x: 2, y: 2, z: 4, core: 2. Of those that a mesh axis runs over, the one named last changes fastest.
Arguments:
- queries: bfloat16 [16384, 2048], P(('groups', 'seq')), parts along dimension 0, may hold values from -8 to 8
- keys: bfloat16 [16384, 512], P(('groups', 'seq')), parts along dimension 0, may hold values from -8 to 8
- values: bfloat16 [16384, 512], P(('groups', 'seq')), parts along dimension 0, may hold values from -6 to 6
- block_table: int32 [128, 8], P(('groups', 'seq')), parts along dimension 0, may hold values from 0 to 63, as said below
- out_weight: bfloat16 [2048, 4096], P('seq'), may hold values from -0.125 to 0.125
Outputs:
- projected: bfloat16 [16384, 4096], P(('groups', 'seq')), parts along dimension 0
There are 2 independent parts, one for each index of `groups`. A program takes and returns all parts, laid end to end along the dimension named above; an argument that names none is the same for every part. Nothing has to cross between parts.
Inputs may be any that keep to these rules, and one draw needn't show every extreme that they name: `block_table`: entry j of the row of query block b names a key block held by index (b // 4 + j * 2 - ((b mod 4) mod 2)) mod 16 of seq, that is a block number s * 4 + r with that index s and 0 <= r < 4.
All inputs are finite; a program needn't handle non-finite values.
Results may differ from a plain program's by a relative error of at most 0.013.
Values may be sent and summed in bfloat16 or wider, within the bound.
No kernel may reach another device: no remote copies, remote signals or barrier semaphores. Data moves between devices by JAX's collectives and lax.ppermute only.
A program may use at most 320 MiB of HBM per device.

v0:
```python
import functools

import jax
import jax.numpy as jnp
from jax import lax
from jax.experimental import pallas as pl
from jax.experimental.pallas import tpu as pltpu
from jax.sharding import PartitionSpec as P

H = 16
KVH = 4
HD = 128
QB = 128
ENTRIES = 8
GROUP = H // KVH
SCALE_LOG2 = HD ** (-0.5) * 1.4426950408889634


def attention_kernel(
    n_chip, hops, odd, where_ref, table_ref, q_ref, *refs
):
    count = len(hops)
    key_refs = refs[:count]
    value_refs = refs[count : 2 * count]
    o_ref, kbuf, vbuf, sems = refs[2 * count :]
    step = pl.program_id(0)
    head = pl.program_id(1)
    n_outer = n_chip // 2
    per_entry = n_chip // ENTRIES
    outer, side, core = where_ref[0], where_ref[1], where_ref[2]
    chip = outer * 2 + side

    @pl.when((step == 0) & (head == 0))
    def _():
        for at, (shift, flip) in enumerate(hops):
            source_outer = outer + shift
            source = source_outer * 2 + (1 - side if flip else side)
            ahead = source - chip + (core if odd else 0)
            ahead = lax.rem(ahead + 2 * n_chip, n_chip)
            usable = (source_outer >= 0) & (source_outer < n_outer)
            if per_entry > 1:
                usable = usable & (lax.rem(ahead, per_entry) == 0)
            entry = ahead // per_entry

            @pl.when(usable)
            def _():
                for block in range(2):
                    row = table_ref[2 * block + (1 if odd else 0), entry] & 3
                    rows = pl.ds(pl.multiple_of(row * QB, QB), QB)
                    slot = pl.ds(pl.multiple_of(entry * QB, QB), QB)
                    pltpu.make_async_copy(
                        key_refs[at].at[rows, :], kbuf.at[block, slot, :], sems.at[block, 0]
                    ).start()
                    pltpu.make_async_copy(
                        value_refs[at].at[rows, :], vbuf.at[block, slot, :], sems.at[block, 1]
                    ).start()

    @pl.when(head == 0)
    def _():
        pltpu.make_async_copy(kbuf.at[step], kbuf.at[step], sems.at[step, 0]).wait()
        pltpu.make_async_copy(vbuf.at[step], vbuf.at[step], sems.at[step, 1]).wait()

    columns = pl.ds(pl.multiple_of(head * HD, HD), HD)
    keys = kbuf[step, :, columns]
    values = vbuf[step, :, columns]
    for g in range(GROUP):
        query = q_ref[0, :, g * HD : (g + 1) * HD]
        scores = lax.dot_general(
            query, keys, (((1,), (1,)), ((), ())), preferred_element_type=jnp.float32
        )
        highest = jnp.max(scores, axis=-1, keepdims=True)
        weights = jnp.exp2((scores - highest) * SCALE_LOG2)
        total = jnp.sum(weights, axis=-1, keepdims=True)
        mixed = jnp.dot(
            weights.astype(jnp.bfloat16), values, preferred_element_type=jnp.float32
        )
        o_ref[0, :, g * HD : (g + 1) * HD] = (mixed / total).astype(jnp.bfloat16)


def attention(queries, where, table, hops, key_list, value_list, n_chip, odd):
    spread = queries.shape[0] // 2
    width = GROUP * HD
    rows = ENTRIES * QB
    hbm = pl.BlockSpec(memory_space=pl.ANY)
    return pl.pallas_call(
        functools.partial(attention_kernel, n_chip, hops, odd),
        out_shape=jax.ShapeDtypeStruct((2, QB, H * HD), jnp.bfloat16),
        grid_spec=pltpu.PrefetchScalarGridSpec(
            num_scalar_prefetch=2,
            grid=(2, KVH),
            in_specs=[pl.BlockSpec((1, QB, width), lambda b, h, w, t: (b * spread, 0, h))]
            + [hbm] * (2 * len(hops)),
            out_specs=pl.BlockSpec((1, QB, width), lambda b, h, w, t: (b, 0, h)),
            scratch_shapes=[
                pltpu.VMEM((2, rows, KVH * HD), jnp.bfloat16),
                pltpu.VMEM((2, rows, KVH * HD), jnp.bfloat16),
                pltpu.SemaphoreType.DMA((2, 2)),
            ],
        ),
        compiler_params=pltpu.CompilerParams(vmem_limit_bytes=32 * 1024 * 1024),
        cost_estimate=pl.CostEstimate(
            flops=4 * 2 * QB * rows * H * HD,
            bytes_accessed=2 * rows * 2 * KVH * HD * 2 + 4 * QB * H * HD * 2,
            transcendentals=2 * QB * rows * H,
        ),
    )(where, table, queries, *key_list, *value_list)


def project_kernel(even_ref, odd_ref, w_ref, o_ref, rows):
    @pl.when((pl.program_id(0) == 0) & (pl.program_id(1) == 0))
    def _():
        for block in range(2):
            rows[2 * block * QB : (2 * block + 1) * QB, :] = even_ref[block]
            rows[(2 * block + 1) * QB : (2 * block + 2) * QB, :] = odd_ref[block]

    o_ref[...] = jnp.dot(
        rows[...], w_ref[0], preferred_element_type=jnp.float32
    ).astype(jnp.bfloat16)


def project(even, odd, weights, tile=512):
    parts, depth, columns = weights.shape
    tiles = columns // tile
    whole = pl.BlockSpec((2, QB, depth), lambda p, t: (0, 0, 0))
    return pl.pallas_call(
        project_kernel,
        out_shape=jax.ShapeDtypeStruct((4 * QB, parts * columns), jnp.bfloat16),
        grid_spec=pl.GridSpec(
            grid=(parts, tiles),
            in_specs=[whole, whole, pl.BlockSpec((1, depth, tile), lambda p, t: (p, 0, t))],
            out_specs=pl.BlockSpec((4 * QB, tile), lambda p, t: (0, p * tiles + t)),
            scratch_shapes=[pltpu.VMEM((4 * QB, depth), jnp.bfloat16)],
        ),
        compiler_params=pltpu.CompilerParams(vmem_limit_bytes=32 * 1024 * 1024),
        cost_estimate=pl.CostEstimate(
            flops=2 * 4 * QB * depth * parts * columns,
            bytes_accessed=2 * (depth * parts * columns + 4 * QB * (depth + parts * columns)),
            transcendentals=0,
        ),
    )(even, odd, weights)


def body(n_groups, n_seq, queries, keys, values, block_table, out_weight):
    n_chip = n_seq // 2
    n_outer = n_chip // 2

    def index(outer, side, core):
        return (outer * 2 + side) * 2 + core

    places = [(o, s, c) for o in range(n_outer) for s in range(2) for c in range(2)]
    me = lax.axis_index("seq")
    where = jnp.stack([me // 4, (me // 2) % 2, me % 2]).astype(jnp.int32)

    def swap_core(array):
        return lax.ppermute(
            array, "seq", [(index(o, s, c), index(o, s, 1 - c)) for o, s, c in places]
        )

    def swap_side(array, shift):
        return lax.ppermute(
            array,
            "seq",
            [
                (index(o, s, c), index(o, 1 - s, c))
                for o, s, c in places
                if 0 <= o + shift < n_outer
            ],
        )

    def move(array, shift, way):
        return lax.ppermute(
            array,
            "seq",
            [
                (index(o, s, c), index(o + way, s, c))
                for o, s, c in places
                if 0 <= o + way < n_outer and 0 <= o + way + shift < n_outer
            ],
        )

    query_blocks = queries.reshape(4, QB, H * HD)
    far_queries = swap_core(query_blocks.reshape(2, 2, QB, H * HD)[:, 1])
    far_table = swap_core(block_table)

    group = lax.axis_index("groups")
    part = out_weight.shape[1] // n_groups
    mine = lax.dynamic_slice_in_dim(out_weight, group * part, part, 1)
    gathered = lax.all_gather(mine, ("groups", "seq"), axis=0, tiled=True)
    gathered = gathered.reshape(n_groups, n_seq * out_weight.shape[0], part)

    held = {0: (keys, values)}
    hops = [(0, False)]
    pieces = {(0, False): (keys, values)}
    for step in range(n_outer):
        for shift in ([0] if step == 0 else [-step, step]):
            pieces[(shift, True)] = tuple(swap_side(a, shift) for a in pieces[(shift, False)])
            hops.append((shift, True))
        if step + 1 < n_outer:
            for way in (1, -1):
                shift = -way * (step + 1)
                before = pieces[(-way * step, False)]
                pieces[(shift, False)] = tuple(move(a, shift, way) for a in before)
                hops.append((shift, False))

    key_list = [pieces[hop][0] for hop in hops]
    value_list = [pieces[hop][1] for hop in hops]
    far = attention(far_queries, where, far_table, hops, key_list, value_list, n_chip, True)
    odd = swap_core(far)
    even = attention(query_blocks, where, block_table, hops, key_list, value_list, n_chip, False)
    return project(even, odd, gathered)


def solution(mesh):
    in_specs = (
        P(("groups", "seq"), None),
        P(("groups", "seq"), None),
        P(("groups", "seq"), None),
        P(("groups", "seq"), None),
        P("seq", None),
    )
    out_specs = P(("groups", "seq"), None)
    run = functools.partial(body, mesh.shape["groups"], mesh.shape["seq"])
    return jax.shard_map(run, mesh=mesh, in_specs=in_specs, out_specs=out_specs, check_vma=False)
```

profile of v0, /device:TPU:0, one launch (start us, length us, event | category | flops | bytes accessed | tf_op | source)
XLA Modules:
  0.0 276.3 jit_solution(15810988113548217079)
XLA Ops:
  6.5 1.2 copy-done
  7.8 0.8 constant_dynamic-slice_fusion
  8.6 5.0 %collective-permute-start.1 = (bf16[512,512]{1,0:T(8,128)(2,1)}, bf16[512,512]{1,0:T(8,128)(2,1)S(1)}, u32[]{:S(2)}, u32[]{:S(2)}) collective-permute-start(bf16[512,512]{1,0:T(8,128)(2,1)} %refs_0_.3), channel_id=1, source_target_pairs={{0,4},{1,5},{2,6},{3,7},{4,8},{5,9},{6,10},{7,11},{8,12},{9,13},{1... | collective-permute-start | bytes 1572872 | tf_op jit(solution)/shard_map/ppermute | solution.py:171
  13.6 1.3 collective-permute-start.2
  14.9 4.6 %collective-permute-start.14 = (bf16[512,512]{1,0:T(8,128)(2,1)}, bf16[512,512]{1,0:T(8,128)(2,1)S(1)}, u32[]{:S(2)}, u32[]{:S(2)}) collective-permute-start(bf16[512,512]{1,0:T(8,128)(2,1)} %refs_14_.3), channel_id=1, source_target_pairs={{0,4},{1,5},{2,6},{3,7},{4,8},{5,9},{6,10},{7,11},{8,12},{9,13},{1... | collective-permute-start | bytes 1572872 | tf_op jit(solution)/shard_map/ppermute | solution.py:171
  19.6 1.3 collective-permute-start.15
  20.9 1.5 collective-permute-start
  22.5 7.2 %collective-permute-done.1.refs_2_ = bf16[512,512]{1,0:T(8,128)(2,1)S(1)} collective-permute-done((bf16[512,512]{1,0:T(8,128)(2,1)}, bf16[512,512]{1,0:T(8,128)(2,1)S(1)}, u32[]{:S(2)}, u32[]{:S(2)}) %collective-permute-start.1) | collective-permute-done | bytes 524320 | tf_op jit(solution)/shard_map/ppermute | solution.py:171
  29.6 1.3 collective-permute-start.13
  31.0 7.6 %collective-permute-done.2.refs_3_ = bf16[512,512]{1,0:T(8,128)(2,1)S(1)} collective-permute-done((bf16[512,512]{1,0:T(8,128)(2,1)}, bf16[512,512]{1,0:T(8,128)(2,1)S(1)}, u32[]{:S(2)}, u32[]{:S(2)}) %collective-permute-start.2) | collective-permute-done | bytes 524320 | tf_op jit(solution)/shard_map/ppermute | solution.py:171
  39.3 8.2 %collective-permute-done.14.refs_16_ = bf16[512,512]{1,0:T(8,128)(2,1)S(1)} collective-permute-done((bf16[512,512]{1,0:T(8,128)(2,1)}, bf16[512,512]{1,0:T(8,128)(2,1)S(1)}, u32[]{:S(2)}, u32[]{:S(2)}) %collective-permute-start.14) | collective-permute-done | bytes 524320 | tf_op jit(solution)/shard_map/ppermute | solution.py:171
  47.5 1.3 collective-permute-start.6
  48.8 1.3 slice_bitcast_fusion
  50.1 1.5 collective-permute-done.15.refs_17_
  53.0 1.3 collective-permute-start.19
  54.3 0.8 copy-done.9
  55.8 26.8 %collective-permute-done.6.refs_7_ = bf16[512,512]{1,0:T(8,128)(2,1)} collective-permute-done((bf16[512,512]{1,0:T(8,128)(2,1)S(1)}, bf16[512,512]{1,0:T(8,128)(2,1)}, u32[]{:S(2)}, u32[]{:S(2)}) %collective-permute-start.6) | collective-permute-done | bytes 524320 | tf_op jit(solution)/shard_map/ppermute | solution.py:171
  82.6 3.6 %collective-permute-start.17 = (bf16[512,512]{1,0:T(8,128)(2,1)S(1)}, bf16[512,512]{1,0:T(8,128)(2,1)S(1)}, u32[]{:S(2)}, u32[]{:S(2)}) collective-permute-start(bf16[512,512]{1,0:T(8,128)(2,1)S(1)} %collective-permute-done.15.refs_17_), channel_id=1, source_target_pairs={{0,2},{1,3},{2,0},{3,1},{4,6},{5,7},{6,4},{7,5},{8,10},{9,11},{10,... | collective-permute-start | bytes 1572872 | tf_op jit(solution)/shard_map/ppermute | solution.py:160
  86.9 9.8 %collective-permute-done.19.refs_21_ = bf16[512,512]{1,0:T(8,128)(2,1)S(1)} collective-permute-done((bf16[512,512]{1,0:T(8,128)(2,1)S(1)}, bf16[512,512]{1,0:T(8,128)(2,1)S(1)}, u32[]{:S(2)}, u32[]{:S(2)}) %collective-permute-start.19) | collective-permute-done | bytes 524320 | tf_op jit(solution)/shard_map/ppermute | solution.py:171
  96.6 3.4 %collective-permute-start.4 = (bf16[512,512]{1,0:T(8,128)(2,1)S(1)}, bf16[512,512]{1,0:T(8,128)(2,1)S(1)}, u32[]{:S(2)}, u32[]{:S(2)}) collective-permute-start(bf16[512,512]{1,0:T(8,128)(2,1)S(1)} %collective-permute-done.2.refs_3_), channel_id=1, source_target_pairs={{0,2},{1,3},{2,0},{3,1},{4,6},{5,7},{6,4},{7,5},{8,10},{9,11},{10,... | collective-permute-start | bytes 1572872 | tf_op jit(solution)/shard_map/ppermute | solution.py:160
  100.9 1.4 collective-permute-start.9
  102.3 0.8 copy-done.22
  103.1 1.3 collective-permute-start.10
  105.2 1.5 collective-permute-start.22
  106.7 16.9 %collective-permute-done.4.refs_5_ = bf16[512,512]{1,0:T(8,128)(2,1)S(1)} collective-permute-done((bf16[512,512]{1,0:T(8,128)(2,1)S(1)}, bf16[512,512]{1,0:T(8,128)(2,1)S(1)}, u32[]{:S(2)}, u32[]{:S(2)}) %collective-permute-start.4) | collective-permute-done | bytes 524320 | tf_op jit(solution)/shard_map/ppermute | solution.py:160
  124.3 1.3 collective-permute-start.23
  125.6 1.0 copy-done.36
  127.3 0.8 copy-done.14
  128.1 3.4 %collective-permute-start.21 = (bf16[512,512]{1,0:T(8,128)(2,1)S(1)}, bf16[512,512]{1,0:T(8,128)(2,1)S(1)}, u32[]{:S(2)}, u32[]{:S(2)}) collective-permute-start(bf16[512,512]{1,0:T(8,128)(2,1)S(1)} %collective-permute-done.19.refs_21_), channel_id=1, source_target_pairs={{0,2},{1,3},{2,0},{3,1},{4,6},{5,7},{6,4},{7,5},{16,18},{17,19},{1... | collective-permute-start | bytes 1572872 | tf_op jit(solution)/shard_map/ppermute | solution.py:160
  131.6 0.8 copy-done.16
  132.4 1.5 collective-permute-done.10.refs_11_
  134.6 0.8 copy-done.12
  135.4 4.2 %collective-permute-start.8 = (bf16[512,512]{1,0:T(8,128)(2,1)}, bf16[512,512]{1,0:T(8,128)(2,1)}, u32[]{:S(2)}, u32[]{:S(2)}) collective-permute-start(bf16[512,512]{1,0:T(8,128)(2,1)} %collective-permute-done.6.refs_7_), channel_id=1, source_target_pairs={{0,2},{1,3},{2,0},{3,1},{4,6},{5,7},{6,4},{7,5},{16,18},{17,19},{1... | collective-permute-start | bytes 1572872 | tf_op jit(solution)/shard_map/ppermute | solution.py:160
  139.5 34.8 %collective-permute-done.23.refs_25_ = bf16[512,512]{1,0:T(8,128)(2,1)} collective-permute-done((bf16[512,512]{1,0:T(8,128)(2,1)S(1)}, bf16[512,512]{1,0:T(8,128)(2,1)}, u32[]{:S(2)}, u32[]{:S(2)}) %collective-permute-start.23) | collective-permute-done | bytes 524320 | tf_op jit(solution)/shard_map/ppermute | solution.py:171
  174.4 1.5 collective-permute-start.11
  176.6 2.9 %collective-permute-start.12 = (bf16[512,512]{1,0:T(8,128)(2,1)}, bf16[512,512]{1,0:T(8,128)(2,1)}, u32[]{:S(2)}, u32[]{:S(2)}) collective-permute-start(bf16[512,512]{1,0:T(8,128)(2,1)} %collective-permute-done.10.refs_11_), channel_id=1, source_target_pairs={{0,2},{1,3},{2,0},{3,1},{16,18},{17,19},{18,16},{19,17}} | collective-permute-start | bytes 1572872 | tf_op jit(solution)/shard_map/ppermute | solution.py:160
  180.3 1.4 collective-permute-start.24
  181.8 0.8 copy-done.32
  182.6 2.9 %collective-permute-start.25 = (bf16[512,512]{1,0:T(8,128)(2,1)}, bf16[512,512]{1,0:T(8,128)(2,1)}, u32[]{:S(2)}, u32[]{:S(2)}) collective-permute-start(bf16[512,512]{1,0:T(8,128)(2,1)} %collective-permute-done.23.refs_25_), channel_id=1, source_target_pairs={{0,2},{1,3},{2,0},{3,1},{16,18},{17,19},{18,16},{19,17}} | collective-permute-start | bytes 1572872 | tf_op jit(solution)/shard_map/ppermute | solution.py:160
  185.7 2.3 collective-permute-done.12.refs_13_
  188.0 6.0 %collective-permute-done.25.refs_27_ = bf16[512,512]{1,0:T(8,128)(2,1)} collective-permute-done((bf16[512,512]{1,0:T(8,128)(2,1)}, bf16[512,512]{1,0:T(8,128)(2,1)}, u32[]{:S(2)}, u32[]{:S(2)}) %collective-permute-start.25) | collective-permute-done | bytes 524320 | tf_op jit(solution)/shard_map/ppermute | solution.py:160
  194.0 1.0 copy-done.2
  195.0 1.0 copy-done.4
  196.1 1.0 copy-done.7
  197.1 1.0 copy-done.10
  198.2 1.0 copy-done.13
  199.2 1.0 copy-done.15
  200.2 1.0 copy-done.17
  201.3 1.0 copy-done.20
  202.3 1.0 copy-done.23
  203.4 1.0 copy-done.25
  204.4 1.0 copy-done.27
  205.5 1.0 copy-done.29
  206.5 1.0 copy-done.31
  207.5 1.0 copy-done.33
  208.6 1.2 copy-done.37
  209.8 18.4 %shard_map.56 = bf16[2,128,2048]{2,1,0:T(8,128)(2,1)S(1)} custom-call(s32[3]{0:T(128)S(1)} %pad_add_fusion.where_ref, s32[4,8]{1,0:T(4,128)S(1)} %collective-permute-done.26.table_ref, bf16[2,128,2048]{2,1,0:T(8,128)(2,1)S(1)} %copy-done.37, bf16[512,512]{1,0:T(8,128)(2,1)S(1)} %copy-done.2, bf16[512,512]{1,0:T(8,128)(2,1)S(1)} %copy-done.7, ...), custom_call_target="tpu_custom_call" | custom-call | flops 2147483648 | bytes 6291456 | tf_op jit(solution)/shard_map/pallas_call | solution.py:85
  228.4 18.4 %shard_map.55.even_ref = bf16[2,128,2048]{2,1,0:T(8,128)(2,1)S(1)} custom-call(s32[3]{0:T(128)S(1)} %pad_add_fusion.where_ref, s32[4,8]{1,0:T(4,128)S(1)} %copy-done.38, bf16[4,128,2048]{2,1,0:T(8,128)(2,1)S(1)} %bitcast.11, bf16[512,512]{1,0:T(8,128)(2,1)S(1)} %copy-done.3, bf16[512,512]{1,0:T(8,128)(2,1)S(1)} %copy-done.8, ...), custom_call_target="tpu_custom_call" | custom-call | flops 2147483648 | bytes 6291456 | tf_op jit(solution)/shard_map/pallas_call | solution.py:85
  246.9 1.0 copy-done.34
  247.8 1.0 copy-done.40
  248.8 1.2 copy-done.35
  250.1 5.8 %copy-done.39 = bf16[4096,2048]{1,0:T(8,128)(2,1)S(1)} copy-done((bf16[4096,2048]{1,0:T(8,128)(2,1)S(1)}, bf16[4096,2048]{1,0:T(8,128)(2,1)}, u32[]{:S(2)}) %copy-start.39) | copy-done | bytes 16777240
  255.8 1.2 copy-done.41
  257.1 12.4 %shard_map.57 = bf16[512,4096]{1,0:T(8,128)(2,1)} custom-call(bf16[2,128,2048]{2,1,0:T(8,128)(2,1)S(1)} %copy-done.35, bf16[2,128,2048]{2,1,0:T(8,128)(2,1)S(1)} %copy-done.41, bf16[2,2048,2048]{2,1,0:T(8,128)(2,1)S(1)} %bitcast.12), custom_call_target="tpu_custom_call" | custom-call | flops 8589934592 | bytes 23068672 | tf_op jit(solution)/shard_map/pallas_call | solution.py:125
  (87 shorter events, 9.2 us)
Async XLA Ops:
  6.5 1.2 copy-start
  6.5 242.3 %all-gather.2.cloned.1.call-start = ((), (), s32[]{:S(2)}) async-start(), calls=%async_computation | async-start | bytes 17301504 | tf_op jit(solution)/shard_map/all_gather | solution.py:188
  8.6 21.0 %collective-permute-start.1 = (bf16[512,512]{1,0:T(8,128)(2,1)}, bf16[512,512]{1,0:T(8,128)(2,1)S(1)}, u32[]{:S(2)}, u32[]{:S(2)}) collective-permute-start(bf16[512,512]{1,0:T(8,128)(2,1)} %refs_0_.3), channel_id=1, source_target_pairs={{0,4},{1,5},{2,6},{3,7},{4,8},{5,9},{6,10},{7,11},{8,12},{9,13},{1... | collective-permute-start | bytes 1572872 | tf_op jit(solution)/shard_map/ppermute | solution.py:171
  13.6 25.0 %collective-permute-start.2 = (bf16[512,512]{1,0:T(8,128)(2,1)}, bf16[512,512]{1,0:T(8,128)(2,1)S(1)}, u32[]{:S(2)}, u32[]{:S(2)}) collective-permute-start(bf16[512,512]{1,0:T(8,128)(2,1)} %refs_0_.3), channel_id=1, source_target_pairs={{4,0},{5,1},{6,2},{7,3},{8,4},{9,5},{10,6},{11,7},{12,8},{13,9},{1... | collective-permute-start | bytes 1572872 | tf_op jit(solution)/shard_map/ppermute | solution.py:171
  14.9 32.6 %collective-permute-start.14 = (bf16[512,512]{1,0:T(8,128)(2,1)}, bf16[512,512]{1,0:T(8,128)(2,1)S(1)}, u32[]{:S(2)}, u32[]{:S(2)}) collective-permute-start(bf16[512,512]{1,0:T(8,128)(2,1)} %refs_14_.3), channel_id=1, source_target_pairs={{0,4},{1,5},{2,6},{3,7},{4,8},{5,9},{6,10},{7,11},{8,12},{9,13},{1... | collective-permute-start | bytes 1572872 | tf_op jit(solution)/shard_map/ppermute | solution.py:171
  19.5 1.4 collective-permute-start.26
  19.6 31.9 %collective-permute-start.15 = (bf16[512,512]{1,0:T(8,128)(2,1)}, bf16[512,512]{1,0:T(8,128)(2,1)S(1)}, u32[]{:S(2)}, u32[]{:S(2)}) collective-permute-start(bf16[512,512]{1,0:T(8,128)(2,1)} %refs_14_.3), channel_id=1, source_target_pairs={{4,0},{5,1},{6,2},{7,3},{8,4},{9,5},{10,6},{11,7},{12,8},{13,9},{1... | collective-permute-start | bytes 1572872 | tf_op jit(solution)/shard_map/ppermute | solution.py:171
  20.9 31.3 %collective-permute-start = (bf16[512,512]{1,0:T(8,128)(2,1)}, bf16[512,512]{1,0:T(8,128)(2,1)S(1)}, u32[]{:S(2)}, u32[]{:S(2)}) collective-permute-start(bf16[512,512]{1,0:T(8,128)(2,1)} %refs_0_.3), channel_id=1, source_target_pairs={{0,2},{1,3},{2,0},{3,1},{4,6},{5,7},{6,4},{7,5},{8,10},{9,11},{10,... | collective-permute-start | bytes 1572872 | tf_op jit(solution)/shard_map/ppermute | solution.py:160
  29.6 24.6 %collective-permute-start.13 = (bf16[512,512]{1,0:T(8,128)(2,1)}, bf16[512,512]{1,0:T(8,128)(2,1)S(1)}, u32[]{:S(2)}, u32[]{:S(2)}) collective-permute-start(bf16[512,512]{1,0:T(8,128)(2,1)} %refs_14_.3), channel_id=1, source_target_pairs={{0,2},{1,3},{2,0},{3,1},{4,6},{5,7},{6,4},{7,5},{8,10},{9,11},{10,... | collective-permute-start | bytes 1572872 | tf_op jit(solution)/shard_map/ppermute | solution.py:160
  38.6 16.5 %collective-permute-start.5 = (bf16[512,512]{1,0:T(8,128)(2,1)S(1)}, bf16[512,512]{1,0:T(8,128)(2,1)S(1)}, u32[]{:S(2)}, u32[]{:S(2)}) collective-permute-start(bf16[512,512]{1,0:T(8,128)(2,1)S(1)} %collective-permute-done.1.refs_2_), channel_id=1, source_target_pairs={{4,8},{5,9},{6,10},{7,11},{8,12},{9,13},{10,14},{11,15},{20,24},{2... | collective-permute-start | bytes 1572872 | tf_op jit(solution)/shard_map/ppermute | solution.py:171
  47.5 35.1 %collective-permute-start.6 = (bf16[512,512]{1,0:T(8,128)(2,1)S(1)}, bf16[512,512]{1,0:T(8,128)(2,1)}, u32[]{:S(2)}, u32[]{:S(2)}) collective-permute-start(bf16[512,512]{1,0:T(8,128)(2,1)S(1)} %collective-permute-done.2.refs_3_), channel_id=1, source_target_pairs={{4,0},{5,1},{6,2},{7,3},{8,4},{9,5},{10,6},{11,7},{20,16},{21,17},... | collective-permute-start | bytes 1572872 | tf_op jit(solution)/shard_map/ppermute | solution.py:171
  51.5 34.6 %collective-permute-start.18 = (bf16[512,512]{1,0:T(8,128)(2,1)S(1)}, bf16[512,512]{1,0:T(8,128)(2,1)S(1)}, u32[]{:S(2)}, u32[]{:S(2)}) collective-permute-start(bf16[512,512]{1,0:T(8,128)(2,1)S(1)} %collective-permute-done.14.refs_16_), channel_id=1, source_target_pairs={{4,8},{5,9},{6,10},{7,11},{8,12},{9,13},{10,14},{11,15},{20,24},{2... | collective-permute-start | bytes 1572872 | tf_op jit(solution)/shard_map/ppermute | solution.py:171
  53.0 43.6 %collective-permute-start.19 = (bf16[512,512]{1,0:T(8,128)(2,1)S(1)}, bf16[512,512]{1,0:T(8,128)(2,1)S(1)}, u32[]{:S(2)}, u32[]{:S(2)}) collective-permute-start(bf16[512,512]{1,0:T(8,128)(2,1)S(1)} %collective-permute-done.15.refs_17_), channel_id=1, source_target_pairs={{4,0},{5,1},{6,2},{7,3},{8,4},{9,5},{10,6},{11,7},{20,16},{21,17},... | collective-permute-start | bytes 1572872 | tf_op jit(solution)/shard_map/ppermute | solution.py:171
  55.1 70.5 %collective-permute-start.27 = (bf16[2,128,2048]{2,1,0:T(8,128)(2,1)S(1)}, bf16[2,128,2048]{2,1,0:T(8,128)(2,1)S(1)}, u32[]{:S(2)}, u32[]{:S(2)}) collective-permute-start(bf16[2,128,2048]{2,1,0:T(8,128)(2,1)S(1)} %slice_bitcast_fusion), channel_id=1, source_target_pairs={{0,1},{1,0},{2,3},{3,2},{4,5},{5,4},{6,7},{7,6},{8,9},{9,8},{10,11... | collective-permute-start | bytes 3145736 | tf_op jit(solution)/shard_map/ppermute | solution.py:155
  55.1 44.9 %collective-permute-start.16 = (bf16[512,512]{1,0:T(8,128)(2,1)S(1)}, bf16[512,512]{1,0:T(8,128)(2,1)S(1)}, u32[]{:S(2)}, u32[]{:S(2)}) collective-permute-start(bf16[512,512]{1,0:T(8,128)(2,1)S(1)} %collective-permute-done.14.refs_16_), channel_id=1, source_target_pairs={{4,6},{5,7},{6,4},{7,5},{8,10},{9,11},{10,8},{11,9},{12,14},{13,15... | collective-permute-start | bytes 1572872 | tf_op jit(solution)/shard_map/ppermute | solution.py:160
  82.6 19.7 %collective-permute-start.17 = (bf16[512,512]{1,0:T(8,128)(2,1)S(1)}, bf16[512,512]{1,0:T(8,128)(2,1)S(1)}, u32[]{:S(2)}, u32[]{:S(2)}) collective-permute-start(bf16[512,512]{1,0:T(8,128)(2,1)S(1)} %collective-permute-done.15.refs_17_), channel_id=1, source_target_pairs={{0,2},{1,3},{2,0},{3,1},{4,6},{5,7},{6,4},{7,5},{8,10},{9,11},{10,... | collective-permute-start | bytes 1572872 | tf_op jit(solution)/shard_map/ppermute | solution.py:160
  86.2 18.3 %collective-permute-start.3 = (bf16[512,512]{1,0:T(8,128)(2,1)S(1)}, bf16[512,512]{1,0:T(8,128)(2,1)S(1)}, u32[]{:S(2)}, u32[]{:S(2)}) collective-permute-start(bf16[512,512]{1,0:T(8,128)(2,1)S(1)} %collective-permute-done.1.refs_2_), channel_id=1, source_target_pairs={{4,6},{5,7},{6,4},{7,5},{8,10},{9,11},{10,8},{11,9},{12,14},{13,15... | collective-permute-start | bytes 1572872 | tf_op jit(solution)/shard_map/ppermute | solution.py:160
  96.6 26.9 %collective-permute-start.4 = (bf16[512,512]{1,0:T(8,128)(2,1)S(1)}, bf16[512,512]{1,0:T(8,128)(2,1)S(1)}, u32[]{:S(2)}, u32[]{:S(2)}) collective-permute-start(bf16[512,512]{1,0:T(8,128)(2,1)S(1)} %collective-permute-done.2.refs_3_), channel_id=1, source_target_pairs={{0,2},{1,3},{2,0},{3,1},{4,6},{5,7},{6,4},{7,5},{8,10},{9,11},{10,... | collective-permute-start | bytes 1572872 | tf_op jit(solution)/shard_map/ppermute | solution.py:160
  100.9 27.2 %collective-permute-start.9 = (bf16[512,512]{1,0:T(8,128)(2,1)S(1)}, bf16[512,512]{1,0:T(8,128)(2,1)}, u32[]{:S(2)}, u32[]{:S(2)}) collective-permute-start(bf16[512,512]{1,0:T(8,128)(2,1)S(1)} %collective-permute-done.5.refs_6_), channel_id=1, source_target_pairs={{8,12},{9,13},{10,14},{11,15},{24,28},{25,29},{26,30},{27,31}} | collective-permute-start | bytes 1572872 | tf_op jit(solution)/shard_map/ppermute | solution.py:171
  102.3 0.8 copy-start.22
  103.1 30.7 %collective-permute-start.10 = (bf16[512,512]{1,0:T(8,128)(2,1)}, bf16[512,512]{1,0:T(8,128)(2,1)}, u32[]{:S(2)}, u32[]{:S(2)}) collective-permute-start(bf16[512,512]{1,0:T(8,128)(2,1)} %collective-permute-done.6.refs_7_), channel_id=1, source_target_pairs={{4,0},{5,1},{6,2},{7,3},{20,16},{21,17},{22,18},{23,19}} | collective-permute-start | bytes 1572872 | tf_op jit(solution)/shard_map/ppermute | solution.py:171
  105.2 30.1 %collective-permute-start.22 = (bf16[512,512]{1,0:T(8,128)(2,1)S(1)}, bf16[512,512]{1,0:T(8,128)(2,1)}, u32[]{:S(2)}, u32[]{:S(2)}) collective-permute-start(bf16[512,512]{1,0:T(8,128)(2,1)S(1)} %collective-permute-done.18.refs_20_), channel_id=1, source_target_pairs={{8,12},{9,13},{10,14},{11,15},{24,28},{25,29},{26,30},{27,31}} | collective-permute-start | bytes 1572872 | tf_op jit(solution)/shard_map/ppermute | solution.py:171
  124.3 50.0 %collective-permute-start.23 = (bf16[512,512]{1,0:T(8,128)(2,1)S(1)}, bf16[512,512]{1,0:T(8,128)(2,1)}, u32[]{:S(2)}, u32[]{:S(2)}) collective-permute-start(bf16[512,512]{1,0:T(8,128)(2,1)S(1)} %collective-permute-done.19.refs_21_), channel_id=1, source_target_pairs={{4,0},{5,1},{6,2},{7,3},{20,16},{21,17},{22,18},{23,19}} | collective-permute-start | bytes 1572872 | tf_op jit(solution)/shard_map/ppermute | solution.py:171
  125.6 1.0 copy-start.36
  126.6 49.2 %collective-permute-start.20 = (bf16[512,512]{1,0:T(8,128)(2,1)S(1)}, bf16[512,512]{1,0:T(8,128)(2,1)S(1)}, u32[]{:S(2)}, u32[]{:S(2)}) collective-permute-start(bf16[512,512]{1,0:T(8,128)(2,1)S(1)} %collective-permute-done.18.refs_20_), channel_id=1, source_target_pairs={{8,10},{9,11},{10,8},{11,9},{12,14},{13,15},{14,12},{15,13},{24,26... | collective-permute-start | bytes 1572872 | tf_op jit(solution)/shard_map/ppermute | solution.py:160
  127.3 0.8 copy-start.14
  128.1 51.4 %collective-permute-start.21 = (bf16[512,512]{1,0:T(8,128)(2,1)S(1)}, bf16[512,512]{1,0:T(8,128)(2,1)S(1)}, u32[]{:S(2)}, u32[]{:S(2)}) collective-permute-start(bf16[512,512]{1,0:T(8,128)(2,1)S(1)} %collective-permute-done.19.refs_21_), channel_id=1, source_target_pairs={{0,2},{1,3},{2,0},{3,1},{4,6},{5,7},{6,4},{7,5},{16,18},{17,19},{1... | collective-permute-start | bytes 1572872 | tf_op jit(solution)/shard_map/ppermute | solution.py:160
  131.5 0.8 copy-start.16
  133.9 47.9 %collective-permute-start.7 = (bf16[512,512]{1,0:T(8,128)(2,1)S(1)}, bf16[512,512]{1,0:T(8,128)(2,1)S(1)}, u32[]{:S(2)}, u32[]{:S(2)}) collective-permute-start(bf16[512,512]{1,0:T(8,128)(2,1)S(1)} %collective-permute-done.5.refs_6_), channel_id=1, source_target_pairs={{8,10},{9,11},{10,8},{11,9},{12,14},{13,15},{14,12},{15,13},{24,26... | collective-permute-start | bytes 1572872 | tf_op jit(solution)/shard_map/ppermute | solution.py:160
  135.4 50.3 %collective-permute-start.8 = (bf16[512,512]{1,0:T(8,128)(2,1)}, bf16[512,512]{1,0:T(8,128)(2,1)}, u32[]{:S(2)}, u32[]{:S(2)}) collective-permute-start(bf16[512,512]{1,0:T(8,128)(2,1)} %collective-permute-done.6.refs_7_), channel_id=1, source_target_pairs={{0,2},{1,3},{2,0},{3,1},{4,6},{5,7},{6,4},{7,5},{16,18},{17,19},{1... | collective-permute-start | bytes 1572872 | tf_op jit(solution)/shard_map/ppermute | solution.py:160
  174.4 11.3 %collective-permute-start.11 = (bf16[512,512]{1,0:T(8,128)(2,1)}, bf16[512,512]{1,0:T(8,128)(2,1)}, u32[]{:S(2)}, u32[]{:S(2)}) collective-permute-start(bf16[512,512]{1,0:T(8,128)(2,1)} %collective-permute-done.9.refs_10_), channel_id=1, source_target_pairs={{12,14},{13,15},{14,12},{15,13},{28,30},{29,31},{30,28},{31,29}} | collective-permute-start | bytes 1572872 | tf_op jit(solution)/shard_map/ppermute | solution.py:160
  176.6 11.4 %collective-permute-start.12 = (bf16[512,512]{1,0:T(8,128)(2,1)}, bf16[512,512]{1,0:T(8,128)(2,1)}, u32[]{:S(2)}, u32[]{:S(2)}) collective-permute-start(bf16[512,512]{1,0:T(8,128)(2,1)} %collective-permute-done.10.refs_11_), channel_id=1, source_target_pairs={{0,2},{1,3},{2,0},{3,1},{16,18},{17,19},{18,16},{19,17}} | collective-permute-start | bytes 1572872 | tf_op jit(solution)/shard_map/ppermute | solution.py:160
  180.3 7.7 %collective-permute-start.24 = (bf16[512,512]{1,0:T(8,128)(2,1)}, bf16[512,512]{1,0:T(8,128)(2,1)}, u32[]{:S(2)}, u32[]{:S(2)}) collective-permute-start(bf16[512,512]{1,0:T(8,128)(2,1)} %collective-permute-done.22.refs_24_), channel_id=1, source_target_pairs={{12,14},{13,15},{14,12},{15,13},{28,30},{29,31},{30,28},{31,29}} | collective-permute-start | bytes 1572872 | tf_op jit(solution)/shard_map/ppermute | solution.py:160
  181.8 0.8 copy-start.32
  182.6 11.4 %collective-permute-start.25 = (bf16[512,512]{1,0:T(8,128)(2,1)}, bf16[512,512]{1,0:T(8,128)(2,1)}, u32[]{:S(2)}, u32[]{:S(2)}) collective-permute-start(bf16[512,512]{1,0:T(8,128)(2,1)} %collective-permute-done.23.refs_25_), channel_id=1, source_target_pairs={{0,2},{1,3},{2,0},{3,1},{16,18},{17,19},{18,16},{19,17}} | collective-permute-start | bytes 1572872 | tf_op jit(solution)/shard_map/ppermute | solution.py:160
  185.6 42.8 %copy-start.38 = (s32[4,8]{1,0:T(4,128)S(1)}, s32[4,8]{1,0:T(4,128)}, u32[]{:S(2)}) copy-start(s32[4,8]{1,0:T(4,128)} %table_ref.1) | copy-start | bytes 388
  185.7 42.7 %copy-start.1 = (bf16[512,2048]{1,0:T(8,128)(2,1)S(1)}, bf16[512,2048]{1,0:T(8,128)(2,1)}, u32[]{:S(2)}) copy-start(bf16[512,2048]{1,0:T(8,128)(2,1)} %param.5) | copy-start | bytes 6291460
  194.0 1.0 copy-start.2
  195.0 1.0 copy-start.4
  196.1 1.0 copy-start.7
  197.1 1.0 copy-start.10
  198.2 1.0 copy-start.13
  199.2 1.0 copy-start.15
  200.2 1.0 copy-start.17
  201.3 1.0 copy-start.20
  202.3 1.0 copy-start.23
  203.4 1.0 copy-start.25
  204.4 1.0 copy-start.27
  205.5 1.0 copy-start.29
  206.5 1.0 copy-start.31
  207.5 1.0 copy-start.33
  208.6 1.2 copy-start.37
  209.8 18.6 %copy-start.3 = (bf16[512,512]{1,0:T(8,128)(2,1)S(1)}, bf16[512,512]{1,0:T(8,128)(2,1)}, u32[]{:S(2)}) copy-start(bf16[512,512]{1,0:T(8,128)(2,1)} %refs_0_.3) | copy-start | bytes 1572868
  209.8 18.6 %copy-start.5 = (bf16[512,512]{1,0:T(8,128)(2,1)S(1)}, bf16[512,512]{1,0:T(8,128)(2,1)}, u32[]{:S(2)}) copy-start(bf16[512,512]{1,0:T(8,128)(2,1)} %refs_14_.3) | copy-start | bytes 1572868
  209.8 18.6 %copy-start.8 = (bf16[512,512]{1,0:T(8,128)(2,1)S(1)}, bf16[512,512]{1,0:T(8,128)(2,1)}, u32[]{:S(2)}) copy-start(bf16[512,512]{1,0:T(8,128)(2,1)} %copy-done.6) | copy-start | bytes 1572868
  209.8 18.6 %copy-start.11 = (bf16[512,512]{1,0:T(8,128)(2,1)S(1)}, bf16[512,512]{1,0:T(8,128)(2,1)}, u32[]{:S(2)}) copy-start(bf16[512,512]{1,0:T(8,128)(2,1)} %copy-done.9) | copy-start | bytes 1572868
  209.8 18.6 %copy-start.18 = (bf16[512,512]{1,0:T(8,128)(2,1)S(1)}, bf16[512,512]{1,0:T(8,128)(2,1)}, u32[]{:S(2)}) copy-start(bf16[512,512]{1,0:T(8,128)(2,1)} %copy-done.16) | copy-start | bytes 1572868
  209.8 18.6 %copy-start.21 = (bf16[512,512]{1,0:T(8,128)(2,1)S(1)}, bf16[512,512]{1,0:T(8,128)(2,1)}, u32[]{:S(2)}) copy-start(bf16[512,512]{1,0:T(8,128)(2,1)} %copy-done.19) | copy-start | bytes 1572868
  228.3 19.6 %collective-permute-start.28 = (bf16[2,128,2048]{2,1,0:T(8,128)(2,1)S(1)}, bf16[2,128,2048]{2,1,0:T(8,128)(2,1)S(1)}, u32[]{:S(2)}, u32[]{:S(2)}) collective-permute-start(bf16[2,128,2048]{2,1,0:T(8,128)(2,1)S(1)} %shard_map.56), channel_id=1, source_target_pairs={{0,1},{1,0},{2,3},{3,2},{4,5},{5,4},{6,7},{7,6},{8,9},{9,8},{10,11... | collective-permute-start | bytes 3145736 | tf_op jit(solution)/shard_map/ppermute | solution.py:155
  246.8 1.0 copy-start.34
  247.8 1.0 copy-start.40
  248.8 1.2 copy-start.35
  250.1 5.8 %copy-start.39 = (bf16[4096,2048]{1,0:T(8,128)(2,1)S(1)}, bf16[4096,2048]{1,0:T(8,128)(2,1)}, u32[]{:S(2)}) copy-start(bf16[4096,2048]{1,0:T(8,128)(2,1)} %all-gather.2.cloned.1.call-done) | copy-start | bytes 50331652
  255.8 1.2 copy-start.41
  (8 other events, 6.4 us)
Sparse Core Ops, SparseCore 0:
  10.2 165.6 all-gather.1
where the time goes:
time: 278 us; the launch traced here: 276 us
  waiting for transfers between devices  123 us (44%)
  starting transfers between devices  50.6 us (18%)
  Pallas kernels  49.2 us (18%)
  local copies, waits for them, and re-layouts  39.9 us (14%)
  between operations  13.9 us (5%)
    ppermute x12, waiting for transfers between devices, move(): lax.ppermute(array, 'seq', [(index(o, s, c), index(o + way, s, c)) for o,...  97.3 us
    unnamed x84, local copies, waits for them, and re-layouts  37.8 us
    pallas_call x2, Pallas kernels, attention(): pl.pallas_call(functools.partial(attention_kernel, n_chip, hops, odd), ou...  36.8 us
    ppermute x14, starting transfers between devices, swap_side(): lax.ppermute(array, 'seq', [(index(o, s, c), index(o, 1 - s, c)) for o, s...  28.9 us
    ppermute x14, waiting for transfers between devices, swap_side(): lax.ppermute(array, 'seq', [(index(o, s, c), index(o, 1 - s, c)) for o, s...  25.2 us
    ppermute x12, starting transfers between devices, move(): lax.ppermute(array, 'seq', [(index(o, s, c), index(o + way, s, c)) for o,...  21.5 us
    pallas_call x1, Pallas kernels, project(): pl.pallas_call(project_kernel, out_shape=jax.ShapeDtypeStruct((4 * QB, pa...  12.4 us
  transfers between devices with their start and end apart: 30, of which 12 were waited for; matrix products, arithmetic and copies ran while one was open for 0% of the time, Pallas kernels for 13%

commit v1 on v0

v1 whole, which is shorter than its diff:
```python
import functools

import jax
import jax.numpy as jnp
import numpy as np
from jax import lax
from jax.experimental import pallas as pl
from jax.experimental.pallas import tpu as pltpu
from jax.sharding import PartitionSpec as P

H = 16
KVH = 4
HD = 128
QB = 128
ENTRIES = 8
GROUP = H // KVH
SCALE_LOG2 = HD ** (-0.5) * 1.4426950408889634
NT = (((1,), (1,)), ((), ()))


def arrivals(n_outer):
    rows = []
    for place in range(n_outer):
        row = [0]
        for hop in range(1, n_outer):
            if place - hop >= 0:
                row.append(-hop)
            if place + hop < n_outer:
                row.append(hop)
        rows.append(row)
    return rows


def attention_kernel(n_chip, odd, where_ref, order_ref, table_ref, q_ref, *refs):
    n_outer = n_chip // 2
    pieces = refs[: 2 * n_outer]
    o_ref, kbuf, vbuf, sems = refs[2 * n_outer :]
    step = pl.program_id(0)
    head = pl.program_id(1)
    per_entry = n_chip // ENTRIES
    outer, side, core = where_ref[0], where_ref[1], where_ref[2]
    chip = outer * 2 + side

    @pl.when((step == 0) & (head == 0))
    def _():
        for at in range(2 * n_outer):
            source_side = side if at < n_outer else 1 - side
            source = order_ref[outer, at % n_outer] * 2 + source_side
            ahead = source - chip + (core if odd else 0)
            ahead = lax.rem(ahead + 2 * n_chip, n_chip)
            entry = ahead // per_entry

            def fetch():
                for block in range(2):
                    row = table_ref[2 * block + (1 if odd else 0), entry] & 3
                    slot = pl.ds(pl.multiple_of(entry * QB, QB), QB)
                    for half, buf in enumerate((kbuf, vbuf)):
                        rows = pl.ds(pl.multiple_of((half * 4 + row) * QB, QB), QB)
                        pltpu.make_async_copy(
                            pieces[at].at[rows, :], buf.at[block, slot, :], sems.at[block, half]
                        ).start()

            if per_entry > 1:
                pl.when(lax.rem(ahead, per_entry) == 0)(fetch)
            else:
                fetch()

    @pl.when(head == 0)
    def _():
        pltpu.make_async_copy(kbuf.at[step], kbuf.at[step], sems.at[step, 0]).wait()
        pltpu.make_async_copy(vbuf.at[step], vbuf.at[step], sems.at[step, 1]).wait()

    columns = pl.ds(pl.multiple_of(head * HD, HD), HD)
    keys = kbuf[step, :, columns]
    values = vbuf[step, :, columns]
    scores = [
        lax.dot_general(
            q_ref[0, :, g * HD : (g + 1) * HD], keys, NT, preferred_element_type=jnp.float32
        )
        for g in range(GROUP)
    ]
    rounded, totals = [], []
    for s in scores:
        weights = jnp.exp2((s - jnp.max(s, axis=-1, keepdims=True)) * SCALE_LOG2)
        totals.append(jnp.sum(weights, axis=-1, keepdims=True))
        rounded.append(weights.astype(jnp.bfloat16))
    for g in range(GROUP):
        mixed = jnp.dot(rounded[g], values, preferred_element_type=jnp.float32)
        o_ref[0, :, g * HD : (g + 1) * HD] = (mixed / totals[g]).astype(jnp.bfloat16)


def attention(queries, where, order, table, pieces, n_chip, odd):
    spread = queries.shape[0] // 2
    width = GROUP * HD
    rows = ENTRIES * QB
    hbm = pl.BlockSpec(memory_space=pltpu.HBM)
    return pl.pallas_call(
        functools.partial(attention_kernel, n_chip, odd),
        out_shape=jax.ShapeDtypeStruct((2, QB, H * HD), jnp.bfloat16),
        grid_spec=pltpu.PrefetchScalarGridSpec(
            num_scalar_prefetch=3,
            grid=(2, KVH),
            in_specs=[pl.BlockSpec((1, QB, width), lambda b, h, *_: (b * spread, 0, h))]
            + [hbm] * len(pieces),
            out_specs=pl.BlockSpec((1, QB, width), lambda b, h, *_: (b, 0, h)),
            scratch_shapes=[
                pltpu.VMEM((2, rows, KVH * HD), jnp.bfloat16),
                pltpu.VMEM((2, rows, KVH * HD), jnp.bfloat16),
                pltpu.SemaphoreType.DMA((2, 2)),
            ],
        ),
        compiler_params=pltpu.CompilerParams(vmem_limit_bytes=32 * 1024 * 1024),
        cost_estimate=pl.CostEstimate(
            flops=4 * 2 * QB * rows * H * HD,
            bytes_accessed=2 * rows * 2 * KVH * HD * 2 + 4 * QB * H * HD * 2,
            transcendentals=2 * QB * rows * H,
        ),
    )(where, order, table, queries, *pieces)


def project_kernel(n_outer, parts, depth, where_ref, order_ref, even_ref, odd_ref, *refs):
    sets = [refs[p * n_outer : (p + 1) * n_outer] for p in range(parts)]
    o_ref, rows, wbuf, sems = refs[-4:]
    part, half = pl.program_id(0), pl.program_id(1)
    step = part * 2 + half
    outer, side = where_ref[0], where_ref[1]

    def fetch(into, p, h):
        for at in range(n_outer):
            chip = order_ref[outer, at] * 2
            for source_side, first in ((side, (0, 1)[h]), (1 - side, (3, 2)[h])):
                to = pl.ds(pl.multiple_of((chip + source_side) * depth, depth), depth)
                pltpu.make_async_copy(
                    sets[p][at].at[first * depth : (first + 1) * depth, :],
                    wbuf.at[into, to, :],
                    sems.at[into],
                ).start()

    @pl.when(step == 0)
    def _():
        fetch(0, 0, 0)
        for block in range(2):
            rows[2 * block * QB : (2 * block + 1) * QB, :] = even_ref[block]
            rows[(2 * block + 1) * QB : (2 * block + 2) * QB, :] = odd_ref[block]

    for later in range(1, 2 * parts):

        @pl.when(step == later - 1)
        def _():
            fetch(later % 2, later // 2, later % 2)

    pltpu.make_async_copy(wbuf.at[half], wbuf.at[half], sems.at[half]).wait()
    o_ref[...] = jnp.dot(
        rows[...], wbuf[half], preferred_element_type=jnp.float32
    ).astype(jnp.bfloat16)


def project(even, odd, where, order, places, sets, columns, before=None):
    parts, n_outer = len(sets), len(sets[0])
    depth, half = sets[0][0].shape[0] // 4, sets[0][0].shape[1]
    total = H * HD
    whole = pl.BlockSpec((2, QB, total), lambda p, h, *_: (0, 0, 0))
    hbm = pl.BlockSpec(memory_space=pltpu.HBM)
    count = 3 + 2 + parts * n_outer
    kernel = functools.partial(project_kernel, n_outer, parts, depth)
    if before is not None:
        inner = kernel

        def kernel(where_ref, order_ref, places_ref, e, o, *refs):
            inner(where_ref, order_ref, e, o, *refs[: parts * n_outer], *refs[-4:])

    else:
        inner = kernel

        def kernel(where_ref, order_ref, places_ref, e, o, *refs):
            inner(where_ref, order_ref, e, o, *refs)

    return pl.pallas_call(
        kernel,
        out_shape=jax.ShapeDtypeStruct((4 * QB, columns), jnp.bfloat16),
        grid_spec=pltpu.PrefetchScalarGridSpec(
            num_scalar_prefetch=3,
            grid=(parts, 2),
            in_specs=[whole, whole]
            + [hbm] * (parts * n_outer)
            + ([] if before is None else [hbm]),
            out_specs=pl.BlockSpec((4 * QB, half), lambda p, h, w, r, q: (0, q[p] * 2 + h)),
            scratch_shapes=[
                pltpu.VMEM((4 * QB, total), jnp.bfloat16),
                pltpu.VMEM((2, total, half), jnp.bfloat16),
                pltpu.SemaphoreType.DMA((2,)),
            ],
        ),
        input_output_aliases={} if before is None else {count: 0},
        compiler_params=pltpu.CompilerParams(vmem_limit_bytes=32 * 1024 * 1024),
        cost_estimate=pl.CostEstimate(
            flops=2 * 4 * QB * total * parts * 2 * half,
            bytes_accessed=2 * (total * parts * 2 * half + 4 * QB * (total + parts * 2 * half)),
            transcendentals=0,
        ),
    )(
        where,
        order,
        places,
        even,
        odd,
        *[piece for pieces in sets for piece in pieces],
        *([] if before is None else [before]),
    )


def body(n_groups, n_seq, queries, keys, values, block_table, out_weight):
    n_chip = n_seq // 2
    n_outer = n_chip // 2
    order_rows = arrivals(n_outer)

    def index(outer, side, core):
        return (outer * 2 + side) * 2 + core

    spots = [(o, s, c) for o in range(n_outer) for s in range(2) for c in range(2)]
    me = lax.axis_index("seq")
    group = lax.axis_index("groups")
    outer, side, core = me // 4, (me // 2) % 2, me % 2
    where = jnp.stack([outer, side, core]).astype(jnp.int32)
    order = jnp.asarray(
        np.array([[p + d for d in row] for p, row in enumerate(order_rows)], np.int32)
    )

    def swap_core(array):
        return lax.ppermute(
            array, "seq", [(index(o, s, c), index(o, s, 1 - c)) for o, s, c in spots]
        )

    def swap_side(array):
        return lax.ppermute(
            array, "seq", [(index(o, s, c), index(o, 1 - s, c)) for o, s, c in spots]
        )

    def move(array, hop, way):
        return lax.ppermute(
            array,
            "seq",
            [
                (index(o, s, c), index(o + way, s, c))
                for o, s, c in spots
                if 0 <= o + way < n_outer and 0 <= o - (hop - 1) * way < n_outer
            ],
        )

    def line(array):
        got = {0: array}
        for hop in range(1, n_outer):
            for way in (1, -1):
                got[-way * hop] = move(got[-way * (hop - 1)], hop, way)
        return got

    def pick(got, k):
        wanted = [row[k] for row in order_rows]
        result = got[wanted[0]]
        for offset in sorted(set(wanted[1:])):
            mask = functools.reduce(
                jnp.logical_or, [outer == p for p in range(n_outer) if wanted[p] == offset]
            )
            if offset != wanted[0]:
                result = jnp.where(mask, got[offset], result)
        return result

    query_blocks = queries.reshape(4, QB, H * HD)
    far_queries = swap_core(query_blocks.reshape(2, 2, QB, H * HD)[:, 1])
    far_table = swap_core(block_table)

    got = line(jnp.concatenate([keys, values], 0))
    near = [got[0]] + [pick(got, k) for k in range(1, n_outer)]
    pieces = near + [swap_side(piece) for piece in near]

    quarter = out_weight.shape[1] // (2 * n_groups)
    half = quarter // 2
    mine = lax.dynamic_slice_in_dim(out_weight, (group * 2 + core) * quarter, quarter, 1)
    theirs = lax.dynamic_slice_in_dim(out_weight, (group * 2 + 1 - core) * quarter, quarter, 1)
    theirs = swap_core(theirs)
    first = jnp.where(core == 0, mine, theirs)
    second = jnp.where(core == 0, theirs, mine)
    early = jnp.concatenate([first[:, half:], second[:, half:]], 0)
    late = jnp.concatenate([first[:, :half], second[:, :half]], 0)
    depth = late.shape[0]
    wgot = line(jnp.concatenate([late, early, swap_side(early)], 0))
    wnear = [wgot[0]] + [pick(wgot, k) for k in range(1, n_outer)]
    own = [jnp.concatenate([w, swap_side(w[:depth])], 0) for w in wnear]

    far = attention(far_queries, where, order, far_table, pieces, n_chip, True)
    odd = swap_core(far)
    even = attention(query_blocks, where, order, block_table, pieces, n_chip, False)

    sets = [own]
    for shift in range(1, n_groups):
        turn = [(g, (g + shift) % n_groups) for g in range(n_groups)]
        sets.append([lax.ppermute(w, "groups", turn) for w in own])
    groups = [(group - shift + n_groups) % n_groups for shift in range(n_groups)]
    columns = out_weight.shape[1]
    near_places = jnp.stack([g * 2 + core for g in groups]).astype(jnp.int32)
    far_places = jnp.stack([g * 2 + 1 - core for g in groups]).astype(jnp.int32)
    out = project(even, odd, where, order, near_places, sets, columns)
    far_sets = [[swap_core(w) for w in pieces_of] for pieces_of in sets]
    return project(even, odd, where, order, far_places, far_sets, columns, out)


def solution(mesh):
    in_specs = (
        P(("groups", "seq"), None),
        P(("groups", "seq"), None),
        P(("groups", "seq"), None),
        P(("groups", "seq"), None),
        P("seq", None),
    )
    out_specs = P(("groups", "seq"), None)
    run = functools.partial(body, mesh.shape["groups"], mesh.shape["seq"])
    return jax.shard_map(run, mesh=mesh, in_specs=in_specs, out_specs=out_specs, check_vma=False)
```

time: 278 us -> 278 us (level)
  waiting for transfers between devices: 123 us -> 162 us
  local copies, waits for them, and re-layouts: 39.9 us -> 18.5 us
  between operations: 13.9 us -> 0.55 us
  starting transfers between devices: 50.6 us -> 40.4 us
  other arithmetic: 0.08 us -> 10.2 us
  Pallas kernels: 49.2 us -> 45.6 us
    ppermute x14 -> x9, waiting for transfers between devices: 25.2 us -> 65.5 us  [swap_side(): lax.ppermute(array, 'seq', [(index(o, s, c), index(o, 1 - s, c)) for o, s...]
    unnamed x84 -> x71, local copies, waits for them, and re-layouts: 37.8 us -> 12.5 us
    ppermute x14 -> x9, starting transfers between devices: 28.9 us -> 10.8 us  [swap_side(): lax.ppermute(array, 'seq', [(index(o, s, c), index(o, 1 - s, c)) for o, s...]
    ppermute x12, waiting for transfers between devices: 97.3 us -> 90.1 us  [move(): lax.ppermute(array, 'seq', [(index(o, s, c), index(o + way, s, c)) for o,...]
    select_n x0 -> x3, other arithmetic: none -> 6.53 us  [the longest x2 5.45 us: pick(): result = jnp.where(mask, got[offset], result)]
    ppermute x0 -> x4, starting transfers between devices: none -> 5.96 us  [body(): sets.append([lax.ppermute(w, 'groups', turn) for w in own])]
    ppermute x0 -> x4, waiting for transfers between devices: none -> 5.68 us  [body(): sets.append([lax.ppermute(w, 'groups', turn) for w in own])]
    pallas_call x3 -> x4, Pallas kernels: 49.2 us -> 45.6 us  [the longest x2 28.7 us: attention(): pl.pallas_call(functools.partial(attention_kernel, n_chip, odd), out_shap...]
  transfers between devices with their start and end apart: 30 -> 37, of which waited for: 12 -> 12; matrix products, arithmetic and copies ran while one was open for 0% -> 7% of each run, Pallas kernels for 13% -> 13%
where the time goes in v1:
time: 278 us; the launch traced here: 277 us
  waiting for transfers between devices  162 us (58%)
  Pallas kernels  45.6 us (16%)
  starting transfers between devices  40.4 us (15%)
  local copies, waits for them, and re-layouts  18.5 us (7%)
  other arithmetic  10.2 us (4%)
    ppermute x12, waiting for transfers between devices, move(): lax.ppermute(array, 'seq', [(index(o, s, c), index(o + way, s, c)) for o,...  90.1 us
    ppermute x9, waiting for transfers between devices, swap_side(): lax.ppermute(array, 'seq', [(index(o, s, c), index(o, 1 - s, c)) for o, s...  65.5 us
    pallas_call x2, Pallas kernels, attention(): pl.pallas_call(functools.partial(attention_kernel, n_chip, odd), out_shap...  28.7 us
    ppermute x12, starting transfers between devices, move(): lax.ppermute(array, 'seq', [(index(o, s, c), index(o + way, s, c)) for o,...  21.4 us
    pallas_call x2, Pallas kernels, project(): pl.pallas_call(kernel, out_shape=jax.ShapeDtypeStruct((4 * QB, columns),...  16.9 us
    unnamed x71, local copies, waits for them, and re-layouts  12.5 us
    ppermute x9, starting transfers between devices, swap_side(): lax.ppermute(array, 'seq', [(index(o, s, c), index(o, 1 - s, c)) for o, s...  10.8 us
    ppermute x4, starting transfers between devices, body(): sets.append([lax.ppermute(w, 'groups', turn) for w in own])  5.96 us
  transfers between devices with their start and end apart: 37, of which 12 were waited for; matrix products, arithmetic and copies ran while one was open for 7% of the time, Pallas kernels for 13%

profile of v1, /device:TPU:0, one launch (start us, length us, event | category | flops | bytes accessed | tf_op | source)
XLA Modules:
  0.0 277.0 jit_solution(12585576848923072106)
XLA Ops:
  0.0 1.0 constant_dynamic-slice_fusion
  1.0 0.5 collective-permute-start.13
  1.5 1.1 constant_dynamic-update-slice_fusion.1
  2.6 1.1 constant_dynamic-update-slice_fusion.refs_0_
  3.7 4.6 %collective-permute-start = (bf16[1024,512]{1,0:T(8,128)(2,1)S(1)}, bf16[1024,512]{1,0:T(8,128)(2,1)S(1)}, u32[]{:S(2)}, u32[]{:S(2)}) collective-permute-start(bf16[1024,512]{1,0:T(8,128)(2,1)S(1)} %constant_dynamic-update-slice_fusion.refs_0_), channel_id=1, source_target_pairs={{0,4},{1,5},{2,6},{3,7},{4,8},{5,9},{6,10},{7,11},{8,12},{9,13},{1... | collective-permute-start | bytes 3145736 | tf_op jit(solution)/shard_map/ppermute | solution.py:240
  8.2 1.3 collective-permute-start.1
  9.5 1.1 broadcast_select_fusion.2
  10.7 0.7 constant_dynamic-update-slice_fusion.10
  11.4 0.7 constant_dynamic-update-slice_fusion.9
  12.1 1.6 collective-permute-start.14
  13.7 0.7 constant_dynamic-update-slice_fusion.5
  14.4 0.7 constant_dynamic-update-slice_fusion.4
  15.1 5.5 %collective-permute-done.14 = bf16[256,512]{1,0:T(8,128)(2,1)S(1)} collective-permute-done((bf16[256,512]{1,0:T(8,128)(2,1)S(1)}, bf16[256,512]{1,0:T(8,128)(2,1)S(1)}, u32[]{:S(2)}, u32[]{:S(2)}) %collective-permute-start.14) | collective-permute-done | bytes 262176 | tf_op jit(solution)/shard_map/ppermute | solution.py:235
  20.6 0.7 constant_dynamic-update-slice_fusion.8
  21.3 4.3 %collective-permute-start.17 = (bf16[768,512]{1,0:T(8,128)(2,1)S(1)}, bf16[768,512]{1,0:T(8,128)(2,1)S(1)}, u32[]{:S(2)}, u32[]{:S(2)}) collective-permute-start(bf16[768,512]{1,0:T(8,128)(2,1)S(1)} %get-tuple-element.13), channel_id=1, source_target_pairs={{0,4},{1,5},{2,6},{3,7},{4,8},{5,9},{6,10},{7,11},{8,12},{9,13},{1... | collective-permute-start | bytes 2359304 | tf_op jit(solution)/shard_map/ppermute | solution.py:240
  25.6 1.3 collective-permute-start.18
  26.9 21.1 %collective-permute-done.17 = bf16[768,512]{1,0:T(8,128)(2,1)S(1)} collective-permute-done((bf16[768,512]{1,0:T(8,128)(2,1)S(1)}, bf16[768,512]{1,0:T(8,128)(2,1)S(1)}, u32[]{:S(2)}, u32[]{:S(2)}) %collective-permute-start.17) | collective-permute-done | bytes 786464 | tf_op jit(solution)/shard_map/ppermute | solution.py:240
  48.1 0.7 collective-permute-start.21
  48.8 1.7 collective-permute-start.2
  50.5 1.3 collective-permute-start.3
  52.3 1.3 collective-permute-start.22
  53.7 0.7 collective-permute-start.25
  54.8 1.5 collective-permute-start.15
  56.3 43.7 %collective-permute-done.22 = bf16[768,512]{1,0:T(8,128)(2,1)S(1)} collective-permute-done((bf16[768,512]{1,0:T(8,128)(2,1)S(1)}, bf16[768,512]{1,0:T(8,128)(2,1)S(1)}, u32[]{:S(2)}, u32[]{:S(2)}) %collective-permute-start.22) | collective-permute-done | bytes 786464 | tf_op jit(solution)/shard_map/ppermute | solution.py:240
  100.0 1.3 collective-permute-start.26
  101.3 1.6 collective-permute-start.6
  102.9 1.7 collective-permute-start.4
  104.6 1.3 collective-permute-start.5
  105.9 1.1 slice_bitcast_fusion
  107.1 0.8 constant_dynamic-update-slice_fusion.2.refs_0_
  107.9 14.4 %collective-permute-done.26 = bf16[768,512]{1,0:T(8,128)(2,1)S(1)} collective-permute-done((bf16[768,512]{1,0:T(8,128)(2,1)S(1)}, bf16[768,512]{1,0:T(8,128)(2,1)S(1)}, u32[]{:S(2)}, u32[]{:S(2)}) %collective-permute-start.26) | collective-permute-done | bytes 786464 | tf_op jit(solution)/shard_map/ppermute | solution.py:240
  122.4 0.9 copy-done.27
  123.3 1.5 collective-permute-start.29
  124.8 3.0 %select_select_fusion.2 = (bf16[768,512]{1,0:T(8,128)(2,1)}, bf16[768,512]{1,0:T(8,128)(2,1)S(1)}, bf16[768,512]{1,0:T(8,128)(2,1)S(1)}) fusion(bf16[768,512]{1,0:T(8,128)(2,1)} %copy-done.25, bf16[768,512]{1,0:T(8,128)(2,1)} %copy-done.24, bf16[768,512]{1,0:T(8,128)(2,1)} %copy-done.26, bf16[768,512]{1,0:T(8,128)(2,1)} %copy-done.27, pred[]{:T(512)S(6)} %eq.14, ...), kind=kLoop, calls=%fused_computation.7 | loop fusion | flops 2359296 | bytes 7077893 | tf_op jit(solution)/shard_map/jit(_where)/select_n | solution.py:265
  127.7 1.3 slice.39
  129.1 0.9 copy-done.5
  130.0 1.5 collective-permute-start.27
  131.5 0.5 collective-permute-start.23
  132.0 10.4 %collective-permute-done.5 = bf16[1024,512]{1,0:T(8,128)(2,1)} collective-permute-done((bf16[1024,512]{1,0:T(8,128)(2,1)}, bf16[1024,512]{1,0:T(8,128)(2,1)}, u32[]{:S(2)}, u32[]{:S(2)}) %collective-permute-start.5) | collective-permute-done | bytes 1048608 | tf_op jit(solution)/shard_map/ppermute | solution.py:240
  142.4 1.6 collective-permute-start.19
  144.0 2.5 select_select_fusion
  146.5 0.5 collective-permute-start.7
  147.0 1.6 collective-permute-start.8
  149.1 2.2 collective-permute-done.19
  151.2 0.7 copy-done.30
  152.0 1.3 pad_maximum_fusion.2.refs_3_
  153.4 1.0 pad_maximum_fusion.1.refs_2_
  154.5 1.0 pad_maximum_fusion.refs_1_
  155.5 18.3 %collective-permute-done.7.refs_5_ = bf16[1024,512]{1,0:T(8,128)(2,1)} collective-permute-done((bf16[1024,512]{1,0:T(8,128)(2,1)S(1)}, bf16[1024,512]{1,0:T(8,128)(2,1)}, u32[]{:S(2)}, u32[]{:S(2)}) %collective-permute-start.7) | collective-permute-done | bytes 1048608 | tf_op jit(solution)/shard_map/ppermute | solution.py:235
  173.8 1.5 collective-permute-start.35
  175.3 21.0 %collective-permute-done.8.refs_6_ = bf16[1024,512]{1,0:T(8,128)(2,1)} collective-permute-done((bf16[1024,512]{1,0:T(8,128)(2,1)S(1)}, bf16[1024,512]{1,0:T(8,128)(2,1)}, u32[]{:S(2)}, u32[]{:S(2)}) %collective-permute-start.8) | collective-permute-done | bytes 1048608 | tf_op jit(solution)/shard_map/ppermute | solution.py:235
  196.3 1.5 collective-permute-start.33
  197.8 18.5 %collective-permute-done.9.refs_7_ = bf16[1024,512]{1,0:T(8,128)(2,1)} collective-permute-done((bf16[1024,512]{1,0:T(8,128)(2,1)S(1)}, bf16[1024,512]{1,0:T(8,128)(2,1)}, u32[]{:S(2)}, u32[]{:S(2)}) %collective-permute-start.9) | collective-permute-done | bytes 1048608 | tf_op jit(solution)/shard_map/ppermute | solution.py:235
  216.3 1.5 collective-permute-start.31
  217.8 14.7 %shard_map.65 = bf16[2,128,2048]{2,1,0:T(8,128)(2,1)S(1)} custom-call(s32[3]{0:T(128)S(1)} %pad_add_fusion.where_ref, s32[4,4]{1,0:T(4,128)S(1)} %copy-done.14, s32[4,8]{1,0:T(4,128)S(1)} %collective-permute-done.10.table_ref, bf16[2,128,2048]{2,1,0:T(8,128)(2,1)} %collective-permute-done.11.q_ref, bf16[1024,512]{1,0:T(8,128)(2,1)S(1)} %copy-done.1, ...), custom_call_target="tpu_custom_call" | custom-call | flops 2147483648 | bytes 6291456 | tf_op jit(solution)/shard_map/pallas_call | solution.py:97
  233.7 5.7 %collective-permute-done.31.refs_5_ = bf16[1024,512]{1,0:T(8,128)(2,1)} collective-permute-done((bf16[1024,512]{1,0:T(8,128)(2,1)}, bf16[1024,512]{1,0:T(8,128)(2,1)}, u32[]{:S(2)}, u32[]{:S(2)}) %collective-permute-start.31) | collective-permute-done | bytes 1048608 | tf_op jit(solution)/shard_map/ppermute | solution.py:297
  239.3 1.0 copy-done.8
  240.8 1.0 copy-done.10
  242.0 1.2 copy-done.2
  243.2 1.6 copy-done.4
  244.8 1.2 copy-done.7
  246.0 14.0 %shard_map.64.e = bf16[2,128,2048]{2,1,0:T(8,128)(2,1)S(1)} custom-call(s32[3]{0:T(128)S(1)} %pad_add_fusion.where_ref, s32[4,4]{1,0:T(4,128)S(1)} %copy-done.14, s32[4,8]{1,0:T(4,128)S(1)} %copy-done.15, bf16[4,128,2048]{2,1,0:T(8,128)(2,1)S(1)} %bitcast.14, bf16[1024,512]{1,0:T(8,128)(2,1)S(1)} %copy-done.2, ...), custom_call_target="tpu_custom_call" | custom-call | flops 2147483648 | bytes 6291456 | tf_op jit(solution)/shard_map/pallas_call | solution.py:97
  260.0 8.4 %shard_map.66.refs_8_ = bf16[512,4096]{1,0:T(8,128)(2,1)} custom-call(s32[3]{0:T(128)S(1)} %pad_add_fusion.where_ref, s32[4,4]{1,0:T(4,128)S(1)} %copy-done.14, s32[2]{0:T(128)S(1)} %pad_add_fusion.2.places_ref, bf16[2,128,2048]{2,1,0:T(8,128)(2,1)S(1)} %shard_map.64.e, bf16[2,128,2048]{2,1,0:T(8,128)(2,1)S(1)} %copy-done.11, ...), custom_call_target="tpu_custom_call" | custom-call | flops 4294967296 | bytes 12582912 | tf_op jit(solution)/shard_map/pallas_call | solution.py:178
  268.5 8.4 %shard_map.67 = bf16[512,4096]{1,0:T(8,128)(2,1)} custom-call(s32[3]{0:T(128)S(1)} %pad_add_fusion.where_ref, s32[4,4]{1,0:T(4,128)S(1)} %copy-done.14, s32[2]{0:T(128)S(1)} %pad_add_fusion.1.places_ref, bf16[2,128,2048]{2,1,0:T(8,128)(2,1)S(1)} %shard_map.64.e, bf16[2,128,2048]{2,1,0:T(8,128)(2,1)S(1)} %copy-done.11, ...), custom_call_target="tpu_custom_call", output_to_operand_aliasing={{}: (13, {})} | custom-call | flops 4294967296 | bytes 12582912 | tf_op jit(solution)/shard_map/pallas_call | solution.py:178
  (104 shorter events, 3.6 us)
Async XLA Ops:
  1.0 8.6 %collective-permute-start.13 = (bf16[128,1024]{1,0:T(8,128)(2,1)S(1)}, bf16[128,1024]{1,0:T(8,128)(2,1)S(1)}, u32[]{:S(2)}, u32[]{:S(2)}) collective-permute-start(bf16[128,1024]{1,0:T(8,128)(2,1)S(1)} %constant_dynamic-slice_fusion), channel_id=1, source_target_pairs={{0,1},{1,0},{2,3},{3,2},{4,5},{5,4},{6,7},{7,6},{8,9},{9,8},{10,11... | collective-permute-start | bytes 786440 | tf_op jit(solution)/shard_map/ppermute | solution.py:230
  3.6 97.6 %copy-start = (bf16[1024,512]{1,0:T(8,128)(2,1)}, bf16[1024,512]{1,0:T(8,128)(2,1)S(1)}, u32[]{:S(2)}) copy-start(bf16[1024,512]{1,0:T(8,128)(2,1)S(1)} %constant_dynamic-update-slice_fusion.refs_0_) | copy-start | bytes 3145732
  3.7 45.1 %collective-permute-start = (bf16[1024,512]{1,0:T(8,128)(2,1)S(1)}, bf16[1024,512]{1,0:T(8,128)(2,1)S(1)}, u32[]{:S(2)}, u32[]{:S(2)}) collective-permute-start(bf16[1024,512]{1,0:T(8,128)(2,1)S(1)} %constant_dynamic-update-slice_fusion.refs_0_), channel_id=1, source_target_pairs={{0,4},{1,5},{2,6},{3,7},{4,8},{5,9},{6,10},{7,11},{8,12},{9,13},{1... | collective-permute-start | bytes 3145736 | tf_op jit(solution)/shard_map/ppermute | solution.py:240
  8.2 42.2 %collective-permute-start.1 = (bf16[1024,512]{1,0:T(8,128)(2,1)S(1)}, bf16[1024,512]{1,0:T(8,128)(2,1)}, u32[]{:S(2)}, u32[]{:S(2)}) collective-permute-start(bf16[1024,512]{1,0:T(8,128)(2,1)S(1)} %constant_dynamic-update-slice_fusion.refs_0_), channel_id=1, source_target_pairs={{4,0},{5,1},{6,2},{7,3},{8,4},{9,5},{10,6},{11,7},{12,8},{13,9},{1... | collective-permute-start | bytes 3145736 | tf_op jit(solution)/shard_map/ppermute | solution.py:240
  10.6 42.9 %copy-start.15 = (s32[4,8]{1,0:T(4,128)S(1)}, s32[4,8]{1,0:T(4,128)}, u32[]{:S(2)}) copy-start(s32[4,8]{1,0:T(4,128)} %table_ref.1) | copy-start | bytes 388
  10.7 95.3 %copy-start.3 = (bf16[512,2048]{1,0:T(8,128)(2,1)S(1)}, bf16[512,2048]{1,0:T(8,128)(2,1)}, u32[]{:S(2)}) copy-start(bf16[512,2048]{1,0:T(8,128)(2,1)} %param.6) | copy-start | bytes 6291460
  12.1 8.5 %collective-permute-start.14 = (bf16[256,512]{1,0:T(8,128)(2,1)S(1)}, bf16[256,512]{1,0:T(8,128)(2,1)S(1)}, u32[]{:S(2)}, u32[]{:S(2)}) collective-permute-start(bf16[256,512]{1,0:T(8,128)(2,1)S(1)} %pad_maximum_fusion.3), channel_id=1, source_target_pairs={{0,2},{1,3},{2,0},{3,1},{4,6},{5,7},{6,4},{7,5},{8,10},{9,11},{10,... | collective-permute-start | bytes 786440 | tf_op jit(solution)/shard_map/ppermute | solution.py:235
  21.3 26.7 %collective-permute-start.17 = (bf16[768,512]{1,0:T(8,128)(2,1)S(1)}, bf16[768,512]{1,0:T(8,128)(2,1)S(1)}, u32[]{:S(2)}, u32[]{:S(2)}) collective-permute-start(bf16[768,512]{1,0:T(8,128)(2,1)S(1)} %get-tuple-element.13), channel_id=1, source_target_pairs={{0,4},{1,5},{2,6},{3,7},{4,8},{5,9},{6,10},{7,11},{8,12},{9,13},{1... | collective-permute-start | bytes 2359304 | tf_op jit(solution)/shard_map/ppermute | solution.py:240
  25.6 26.6 %collective-permute-start.18 = (bf16[768,512]{1,0:T(8,128)(2,1)S(1)}, bf16[768,512]{1,0:T(8,128)(2,1)S(1)}, u32[]{:S(2)}, u32[]{:S(2)}) collective-permute-start(bf16[768,512]{1,0:T(8,128)(2,1)S(1)} %get-tuple-element.13), channel_id=1, source_target_pairs={{4,0},{5,1},{6,2},{7,3},{8,4},{9,5},{10,6},{11,7},{12,8},{13,9},{1... | collective-permute-start | bytes 2359304 | tf_op jit(solution)/shard_map/ppermute | solution.py:240
  48.1 53.2 %copy-start.22 = (bf16[768,512]{1,0:T(8,128)(2,1)}, bf16[768,512]{1,0:T(8,128)(2,1)S(1)}, u32[]{:S(2)}) copy-start(bf16[768,512]{1,0:T(8,128)(2,1)S(1)} %collective-permute-done.17) | copy-start | bytes 2359300
  48.1 5.6 %collective-permute-start.21 = (bf16[768,512]{1,0:T(8,128)(2,1)S(1)}, bf16[768,512]{1,0:T(8,128)(2,1)S(1)}, u32[]{:S(2)}, u32[]{:S(2)}) collective-permute-start(bf16[768,512]{1,0:T(8,128)(2,1)S(1)} %collective-permute-done.17), channel_id=1, source_target_pairs={{4,8},{5,9},{6,10},{7,11},{8,12},{9,13},{10,14},{11,15},{20,24},{2... | collective-permute-start | bytes 2359304 | tf_op jit(solution)/shard_map/ppermute | solution.py:240
  48.8 76.0 %copy-start.20 = (bf16[1024,512]{1,0:T(8,128)(2,1)}, bf16[1024,512]{1,0:T(8,128)(2,1)S(1)}, u32[]{:S(2)}) copy-start(bf16[1024,512]{1,0:T(8,128)(2,1)S(1)} %collective-permute-done) | copy-start | bytes 3145732
  48.8 54.1 %collective-permute-start.2 = (bf16[1024,512]{1,0:T(8,128)(2,1)S(1)}, bf16[1024,512]{1,0:T(8,128)(2,1)}, u32[]{:S(2)}, u32[]{:S(2)}) collective-permute-start(bf16[1024,512]{1,0:T(8,128)(2,1)S(1)} %collective-permute-done), channel_id=1, source_target_pairs={{4,8},{5,9},{6,10},{7,11},{8,12},{9,13},{10,14},{11,15},{20,24},{2... | collective-permute-start | bytes 3145736 | tf_op jit(solution)/shard_map/ppermute | solution.py:240
  50.5 54.2 %collective-permute-start.3 = (bf16[1024,512]{1,0:T(8,128)(2,1)}, bf16[1024,512]{1,0:T(8,128)(2,1)}, u32[]{:S(2)}, u32[]{:S(2)}) collective-permute-start(bf16[1024,512]{1,0:T(8,128)(2,1)} %collective-permute-done.1), channel_id=1, source_target_pairs={{4,0},{5,1},{6,2},{7,3},{8,4},{9,5},{10,6},{11,7},{20,16},{21,17},... | collective-permute-start | bytes 3145736 | tf_op jit(solution)/shard_map/ppermute | solution.py:240
  52.3 50.6 %copy-start.23 = (bf16[768,512]{1,0:T(8,128)(2,1)}, bf16[768,512]{1,0:T(8,128)(2,1)S(1)}, u32[]{:S(2)}) copy-start(bf16[768,512]{1,0:T(8,128)(2,1)S(1)} %collective-permute-done.18) | copy-start | bytes 2359300
  52.3 47.7 %collective-permute-start.22 = (bf16[768,512]{1,0:T(8,128)(2,1)S(1)}, bf16[768,512]{1,0:T(8,128)(2,1)S(1)}, u32[]{:S(2)}, u32[]{:S(2)}) collective-permute-start(bf16[768,512]{1,0:T(8,128)(2,1)S(1)} %collective-permute-done.18), channel_id=1, source_target_pairs={{4,0},{5,1},{6,2},{7,3},{8,4},{9,5},{10,6},{11,7},{20,16},{21,17},... | collective-permute-start | bytes 2359304 | tf_op jit(solution)/shard_map/ppermute | solution.py:240
  53.6 1.2 collective-permute-start.10
  53.6 53.3 %copy-start.24 = (bf16[768,512]{1,0:T(8,128)(2,1)}, bf16[768,512]{1,0:T(8,128)(2,1)S(1)}, u32[]{:S(2)}) copy-start(bf16[768,512]{1,0:T(8,128)(2,1)S(1)} %collective-permute-done.21) | copy-start | bytes 2359300
  53.7 53.3 %collective-permute-start.25 = (bf16[768,512]{1,0:T(8,128)(2,1)S(1)}, bf16[768,512]{1,0:T(8,128)(2,1)S(1)}, u32[]{:S(2)}, u32[]{:S(2)}) collective-permute-start(bf16[768,512]{1,0:T(8,128)(2,1)S(1)} %collective-permute-done.21), channel_id=1, source_target_pairs={{8,12},{9,13},{10,14},{11,15},{24,28},{25,29},{26,30},{27,31}} | collective-permute-start | bytes 2359304 | tf_op jit(solution)/shard_map/ppermute | solution.py:240
  54.8 46.5 %collective-permute-start.15 = (bf16[256,512]{1,0:T(8,128)(2,1)S(1)}, bf16[256,512]{1,0:T(8,128)(2,1)S(1)}, u32[]{:S(2)}, u32[]{:S(2)}) collective-permute-start(bf16[256,512]{1,0:T(8,128)(2,1)S(1)} %pad_maximum_fusion.4), channel_id=1, source_target_pairs={{0,2},{1,3},{2,0},{3,1},{4,6},{5,7},{6,4},{7,5},{8,10},{9,11},{10,... | collective-permute-start | bytes 786440 | tf_op jit(solution)/shard_map/ppermute | solution.py:235
  100.0 7.0 %copy-start.25 = (bf16[768,512]{1,0:T(8,128)(2,1)}, bf16[768,512]{1,0:T(8,128)(2,1)S(1)}, u32[]{:S(2)}) copy-start(bf16[768,512]{1,0:T(8,128)(2,1)S(1)} %collective-permute-done.22) | copy-start | bytes 2359300
  100.0 22.4 %collective-permute-start.26 = (bf16[768,512]{1,0:T(8,128)(2,1)S(1)}, bf16[768,512]{1,0:T(8,128)(2,1)S(1)}, u32[]{:S(2)}, u32[]{:S(2)}) collective-permute-start(bf16[768,512]{1,0:T(8,128)(2,1)S(1)} %collective-permute-done.22), channel_id=1, source_target_pairs={{4,0},{5,1},{6,2},{7,3},{20,16},{21,17},{22,18},{23,19}} | collective-permute-start | bytes 2359304 | tf_op jit(solution)/shard_map/ppermute | solution.py:240
  101.3 27.7 %collective-permute-start.6 = (bf16[1024,512]{1,0:T(8,128)(2,1)S(1)}, bf16[1024,512]{1,0:T(8,128)(2,1)S(1)}, u32[]{:S(2)}, u32[]{:S(2)}) collective-permute-start(bf16[1024,512]{1,0:T(8,128)(2,1)S(1)} %constant_dynamic-update-slice_fusion.refs_0_), channel_id=1, source_target_pairs={{0,2},{1,3},{2,0},{3,1},{4,6},{5,7},{6,4},{7,5},{8,10},{9,11},{10,... | collective-permute-start | bytes 3145736 | tf_op jit(solution)/shard_map/ppermute | solution.py:235
  102.9 28.6 %collective-permute-start.4 = (bf16[1024,512]{1,0:T(8,128)(2,1)}, bf16[1024,512]{1,0:T(8,128)(2,1)}, u32[]{:S(2)}, u32[]{:S(2)}) collective-permute-start(bf16[1024,512]{1,0:T(8,128)(2,1)} %collective-permute-done.2), channel_id=1, source_target_pairs={{8,12},{9,13},{10,14},{11,15},{24,28},{25,29},{26,30},{27,31}} | collective-permute-start | bytes 3145736 | tf_op jit(solution)/shard_map/ppermute | solution.py:240
  104.6 37.8 %collective-permute-start.5 = (bf16[1024,512]{1,0:T(8,128)(2,1)}, bf16[1024,512]{1,0:T(8,128)(2,1)}, u32[]{:S(2)}, u32[]{:S(2)}) collective-permute-start(bf16[1024,512]{1,0:T(8,128)(2,1)} %collective-permute-done.3), channel_id=1, source_target_pairs={{4,0},{5,1},{6,2},{7,3},{20,16},{21,17},{22,18},{23,19}} | collective-permute-start | bytes 3145736 | tf_op jit(solution)/shard_map/ppermute | solution.py:240
  107.0 15.4 %copy-start.26 = (bf16[768,512]{1,0:T(8,128)(2,1)}, bf16[768,512]{1,0:T(8,128)(2,1)S(1)}, u32[]{:S(2)}) copy-start(bf16[768,512]{1,0:T(8,128)(2,1)S(1)} %collective-permute-done.25) | copy-start | bytes 2359300
  107.0 39.5 %collective-permute-start.11 = (bf16[2,128,2048]{2,1,0:T(8,128)(2,1)}, bf16[2,128,2048]{2,1,0:T(8,128)(2,1)}, u32[]{:S(2)}, u32[]{:S(2)}) collective-permute-start(bf16[2,128,2048]{2,1,0:T(8,128)(2,1)} %slice_bitcast_fusion), channel_id=1, source_target_pairs={{0,1},{1,0},{2,3},{3,2},{4,5},{5,4},{6,7},{7,6},{8,9},{9,8},{10,11... | collective-permute-start | bytes 3145736 | tf_op jit(solution)/shard_map/ppermute | solution.py:230
  123.3 23.8 %collective-permute-start.29 = (bf16[1024,512]{1,0:T(8,128)(2,1)}, bf16[1024,512]{1,0:T(8,128)(2,1)}, u32[]{:S(2)}, u32[]{:S(2)}) collective-permute-start(bf16[1024,512]{1,0:T(8,128)(2,1)} %constant_dynamic-update-slice_fusion.2.refs_0_), channel_id=1, source_target_pairs={{0,16},{16,0},{1,17},{17,1},{2,18},{18,2},{3,19},{19,3},{4,20},{20... | collective-permute-start | bytes 3145736 | tf_op jit(solution)/shard_map/ppermute | solution.py:297
  127.7 14.7 %copy-start.16 = (bf16[768,512]{1,0:T(8,128)(2,1)}, bf16[768,512]{1,0:T(8,128)(2,1)S(1)}, u32[]{:S(2)}) copy-start(bf16[768,512]{1,0:T(8,128)(2,1)S(1)} %get-tuple-element.12) | copy-start | bytes 2359300
  127.7 14.7 %copy-start.18 = (bf16[768,512]{1,0:T(8,128)(2,1)}, bf16[768,512]{1,0:T(8,128)(2,1)S(1)}, u32[]{:S(2)}) copy-start(bf16[768,512]{1,0:T(8,128)(2,1)S(1)} %get-tuple-element.8) | copy-start | bytes 2359300
  127.7 16.2 %copy-start.21 = (bf16[1024,512]{1,0:T(8,128)(2,1)S(1)}, bf16[1024,512]{1,0:T(8,128)(2,1)}, u32[]{:S(2)}) copy-start(bf16[1024,512]{1,0:T(8,128)(2,1)} %copy-done.20) | copy-start | bytes 3145732
  130.0 18.6 %collective-permute-start.27 = (bf16[256,512]{1,0:T(8,128)(2,1)S(1)}, bf16[256,512]{1,0:T(8,128)(2,1)S(1)}, u32[]{:S(2)}, u32[]{:S(2)}) collective-permute-start(bf16[256,512]{1,0:T(8,128)(2,1)S(1)} %slice.39), channel_id=1, source_target_pairs={{0,2},{1,3},{2,0},{3,1},{4,6},{5,7},{6,4},{7,5},{8,10},{9,11},{10,... | collective-permute-start | bytes 786440 | tf_op jit(solution)/shard_map/ppermute | solution.py:235
  131.5 17.5 %collective-permute-start.23 = (bf16[256,512]{1,0:T(8,128)(2,1)S(1)}, bf16[256,512]{1,0:T(8,128)(2,1)S(1)}, u32[]{:S(2)}, u32[]{:S(2)}) collective-permute-start(bf16[256,512]{1,0:T(8,128)(2,1)S(1)} %slice.38), channel_id=1, source_target_pairs={{0,2},{1,3},{2,0},{3,1},{4,6},{5,7},{6,4},{7,5},{8,10},{9,11},{10,... | collective-permute-start | bytes 786440 | tf_op jit(solution)/shard_map/ppermute | solution.py:235
  142.4 8.8 %collective-permute-start.19 = (bf16[256,512]{1,0:T(8,128)(2,1)S(1)}, bf16[256,512]{1,0:T(8,128)(2,1)S(1)}, u32[]{:S(2)}, u32[]{:S(2)}) collective-permute-start(bf16[256,512]{1,0:T(8,128)(2,1)S(1)} %slice.37), channel_id=1, source_target_pairs={{0,2},{1,3},{2,0},{3,1},{4,6},{5,7},{6,4},{7,5},{8,10},{9,11},{10,... | collective-permute-start | bytes 786440 | tf_op jit(solution)/shard_map/ppermute | solution.py:235
  146.5 27.3 %collective-permute-start.7 = (bf16[1024,512]{1,0:T(8,128)(2,1)S(1)}, bf16[1024,512]{1,0:T(8,128)(2,1)}, u32[]{:S(2)}, u32[]{:S(2)}) collective-permute-start(bf16[1024,512]{1,0:T(8,128)(2,1)S(1)} %get-tuple-element.11.refs_1_), channel_id=1, source_target_pairs={{0,2},{1,3},{2,0},{3,1},{4,6},{5,7},{6,4},{7,5},{8,10},{9,11},{10,... | collective-permute-start | bytes 3145736 | tf_op jit(solution)/shard_map/ppermute | solution.py:235
  147.0 49.3 %collective-permute-start.8 = (bf16[1024,512]{1,0:T(8,128)(2,1)S(1)}, bf16[1024,512]{1,0:T(8,128)(2,1)}, u32[]{:S(2)}, u32[]{:S(2)}) collective-permute-start(bf16[1024,512]{1,0:T(8,128)(2,1)S(1)} %get-tuple-element.6.refs_2_), channel_id=1, source_target_pairs={{0,2},{1,3},{2,0},{3,1},{4,6},{5,7},{6,4},{7,5},{8,10},{9,11},{10,... | collective-permute-start | bytes 3145736 | tf_op jit(solution)/shard_map/ppermute | solution.py:235
  148.6 67.7 %collective-permute-start.9 = (bf16[1024,512]{1,0:T(8,128)(2,1)S(1)}, bf16[1024,512]{1,0:T(8,128)(2,1)}, u32[]{:S(2)}, u32[]{:S(2)}) collective-permute-start(bf16[1024,512]{1,0:T(8,128)(2,1)S(1)} %get-tuple-element.5.refs_3_), channel_id=1, source_target_pairs={{0,2},{1,3},{2,0},{3,1},{4,6},{5,7},{6,4},{7,5},{8,10},{9,11},{10,... | collective-permute-start | bytes 3145736 | tf_op jit(solution)/shard_map/ppermute | solution.py:235
  149.0 2.2 copy-start.28
  149.0 83.5 %collective-permute-start.16 = (bf16[1024,512]{1,0:T(8,128)(2,1)}, bf16[1024,512]{1,0:T(8,128)(2,1)}, u32[]{:S(2)}, u32[]{:S(2)}) collective-permute-start(bf16[1024,512]{1,0:T(8,128)(2,1)} %constant_dynamic-update-slice_fusion.2.refs_0_), channel_id=1, source_target_pairs={{0,1},{1,0},{2,3},{3,2},{4,5},{5,4},{6,7},{7,6},{8,9},{9,8},{10,11... | collective-permute-start | bytes 3145736 | tf_op jit(solution)/shard_map/ppermute | solution.py:230
  151.9 80.7 %collective-permute-start.30 = (bf16[1024,512]{1,0:T(8,128)(2,1)}, bf16[1024,512]{1,0:T(8,128)(2,1)}, u32[]{:S(2)}, u32[]{:S(2)}) collective-permute-start(bf16[1024,512]{1,0:T(8,128)(2,1)} %collective-permute-done.29.refs_4_), channel_id=1, source_target_pairs={{0,1},{1,0},{2,3},{3,2},{4,5},{5,4},{6,7},{7,6},{8,9},{9,8},{10,11... | collective-permute-start | bytes 3145736 | tf_op jit(solution)/shard_map/ppermute | solution.py:230
  152.0 1.4 copy-start.19
  152.0 1.4 copy-start.29
  152.0 2.4 copy-start.17
  152.0 2.4 copy-start.31
  153.4 79.2 %copy-start.12 = (bf16[1024,512]{1,0:T(8,128)(2,1)}, bf16[1024,512]{1,0:T(8,128)(2,1)S(1)}, u32[]{:S(2)}) copy-start(bf16[1024,512]{1,0:T(8,128)(2,1)S(1)} %pad_maximum_fusion.2.refs_3_) | copy-start | bytes 3145732
  153.4 64.4 %copy-start.1 = (bf16[1024,512]{1,0:T(8,128)(2,1)S(1)}, bf16[1024,512]{1,0:T(8,128)(2,1)}, u32[]{:S(2)}) copy-start(bf16[1024,512]{1,0:T(8,128)(2,1)} %copy-done) | copy-start | bytes 3145732
  153.4 64.4 %copy-start.6 = (bf16[1024,512]{1,0:T(8,128)(2,1)S(1)}, bf16[1024,512]{1,0:T(8,128)(2,1)}, u32[]{:S(2)}) copy-start(bf16[1024,512]{1,0:T(8,128)(2,1)} %copy-done.5) | copy-start | bytes 3145732
  153.4 64.4 %copy-start.14 = (s32[4,4]{1,0:T(4,128)S(1)}, s32[4,4]{1,0:T(4,128)}, u32[]{:S(2)}) copy-start(s32[4,4]{1,0:T(4,128)} %constant.66.clone.order_ref) | copy-start | bytes 196
  173.8 59.3 %collective-permute-start.35 = (bf16[1024,512]{1,0:T(8,128)(2,1)S(1)}, bf16[1024,512]{1,0:T(8,128)(2,1)}, u32[]{:S(2)}, u32[]{:S(2)}) collective-permute-start(bf16[1024,512]{1,0:T(8,128)(2,1)S(1)} %pad_maximum_fusion.2.refs_3_), channel_id=1, source_target_pairs={{0,16},{16,0},{1,17},{17,1},{2,18},{18,2},{3,19},{19,3},{4,20},{20... | collective-permute-start | bytes 3145736 | tf_op jit(solution)/shard_map/ppermute | solution.py:297
  196.3 37.0 %collective-permute-start.33 = (bf16[1024,512]{1,0:T(8,128)(2,1)}, bf16[1024,512]{1,0:T(8,128)(2,1)}, u32[]{:S(2)}, u32[]{:S(2)}) collective-permute-start(bf16[1024,512]{1,0:T(8,128)(2,1)} %pad_maximum_fusion.1.refs_2_), channel_id=1, source_target_pairs={{0,16},{16,0},{1,17},{17,1},{2,18},{18,2},{3,19},{19,3},{4,20},{20... | collective-permute-start | bytes 3145736 | tf_op jit(solution)/shard_map/ppermute | solution.py:297
  216.3 23.0 %collective-permute-start.31 = (bf16[1024,512]{1,0:T(8,128)(2,1)}, bf16[1024,512]{1,0:T(8,128)(2,1)}, u32[]{:S(2)}, u32[]{:S(2)}) collective-permute-start(bf16[1024,512]{1,0:T(8,128)(2,1)} %pad_maximum_fusion.refs_1_), channel_id=1, source_target_pairs={{0,16},{16,0},{1,17},{17,1},{2,18},{18,2},{3,19},{19,3},{4,20},{20... | collective-permute-start | bytes 3145736 | tf_op jit(solution)/shard_map/ppermute | solution.py:297
  232.6 6.8 %collective-permute-start.28 = (bf16[1024,512]{1,0:T(8,128)(2,1)S(1)}, bf16[1024,512]{1,0:T(8,128)(2,1)S(1)}, u32[]{:S(2)}, u32[]{:S(2)}) collective-permute-start(bf16[1024,512]{1,0:T(8,128)(2,1)S(1)} %pad_maximum_fusion.2.refs_3_), channel_id=1, source_target_pairs={{0,1},{1,0},{2,3},{3,2},{4,5},{5,4},{6,7},{7,6},{8,9},{9,8},{10,11... | collective-permute-start | bytes 3145736 | tf_op jit(solution)/shard_map/ppermute | solution.py:230
  232.7 8.2 %collective-permute-start.12 = (bf16[2,128,2048]{2,1,0:T(8,128)(2,1)S(1)}, bf16[2,128,2048]{2,1,0:T(8,128)(2,1)S(1)}, u32[]{:S(2)}, u32[]{:S(2)}) collective-permute-start(bf16[2,128,2048]{2,1,0:T(8,128)(2,1)S(1)} %shard_map.65), channel_id=1, source_target_pairs={{0,1},{1,0},{2,3},{3,2},{4,5},{5,4},{6,7},{7,6},{8,9},{9,8},{10,11... | collective-permute-start | bytes 3145736 | tf_op jit(solution)/shard_map/ppermute | solution.py:230
  233.2 35.3 %collective-permute-start.24 = (bf16[1024,512]{1,0:T(8,128)(2,1)}, bf16[1024,512]{1,0:T(8,128)(2,1)}, u32[]{:S(2)}, u32[]{:S(2)}) collective-permute-start(bf16[1024,512]{1,0:T(8,128)(2,1)} %pad_maximum_fusion.1.refs_2_), channel_id=1, source_target_pairs={{0,1},{1,0},{2,3},{3,2},{4,5},{5,4},{6,7},{7,6},{8,9},{9,8},{10,11... | collective-permute-start | bytes 3145736 | tf_op jit(solution)/shard_map/ppermute | solution.py:230
  233.2 35.3 %collective-permute-start.20 = (bf16[1024,512]{1,0:T(8,128)(2,1)}, bf16[1024,512]{1,0:T(8,128)(2,1)}, u32[]{:S(2)}, u32[]{:S(2)}) collective-permute-start(bf16[1024,512]{1,0:T(8,128)(2,1)} %pad_maximum_fusion.refs_1_), channel_id=1, source_target_pairs={{0,1},{1,0},{2,3},{3,2},{4,5},{5,4},{6,7},{7,6},{8,9},{9,8},{10,11... | collective-permute-start | bytes 3145736 | tf_op jit(solution)/shard_map/ppermute | solution.py:230
  239.3 29.2 %collective-permute-start.36 = (bf16[1024,512]{1,0:T(8,128)(2,1)}, bf16[1024,512]{1,0:T(8,128)(2,1)}, u32[]{:S(2)}, u32[]{:S(2)}) collective-permute-start(bf16[1024,512]{1,0:T(8,128)(2,1)} %collective-permute-done.35.refs_7_), channel_id=1, source_target_pairs={{0,1},{1,0},{2,3},{3,2},{4,5},{5,4},{6,7},{7,6},{8,9},{9,8},{10,11... | collective-permute-start | bytes 3145736 | tf_op jit(solution)/shard_map/ppermute | solution.py:230
  240.3 28.2 %collective-permute-start.34 = (bf16[1024,512]{1,0:T(8,128)(2,1)}, bf16[1024,512]{1,0:T(8,128)(2,1)}, u32[]{:S(2)}, u32[]{:S(2)}) collective-permute-start(bf16[1024,512]{1,0:T(8,128)(2,1)} %collective-permute-done.33.refs_6_), channel_id=1, source_target_pairs={{0,1},{1,0},{2,3},{3,2},{4,5},{5,4},{6,7},{7,6},{8,9},{9,8},{10,11... | collective-permute-start | bytes 3145736 | tf_op jit(solution)/shard_map/ppermute | solution.py:230
  241.8 26.7 %collective-permute-start.32 = (bf16[1024,512]{1,0:T(8,128)(2,1)}, bf16[1024,512]{1,0:T(8,128)(2,1)}, u32[]{:S(2)}, u32[]{:S(2)}) collective-permute-start(bf16[1024,512]{1,0:T(8,128)(2,1)} %collective-permute-done.31.refs_5_), channel_id=1, source_target_pairs={{0,1},{1,0},{2,3},{3,2},{4,5},{5,4},{6,7},{7,6},{8,9},{9,8},{10,11... | collective-permute-start | bytes 3145736 | tf_op jit(solution)/shard_map/ppermute | solution.py:230
  242.0 1.2 copy-start.2
  243.2 1.6 copy-start.4
  244.8 1.2 copy-start.7
  246.0 14.0 %copy-start.11 = (bf16[2,128,2048]{2,1,0:T(8,128)(2,1)S(1)}, bf16[2,128,2048]{2,1,0:T(8,128)(2,1)}, u32[]{:S(2)}) copy-start(bf16[2,128,2048]{2,1,0:T(8,128)(2,1)} %copy-done.10) | copy-start | bytes 3145732
  246.0 14.0 %copy-start.13 = (bf16[1024,512]{1,0:T(8,128)(2,1)S(1)}, bf16[1024,512]{1,0:T(8,128)(2,1)}, u32[]{:S(2)}) copy-start(bf16[1024,512]{1,0:T(8,128)(2,1)} %copy-done.12) | copy-start | bytes 3145732
  260.0 8.5 %copy-start.9 = (bf16[1024,512]{1,0:T(8,128)(2,1)S(1)}, bf16[1024,512]{1,0:T(8,128)(2,1)}, u32[]{:S(2)}) copy-start(bf16[1024,512]{1,0:T(8,128)(2,1)} %copy-done.8) | copy-start | bytes 3145732
  (5 other events, 4.5 us)

commit v2 on v1

--- a/solution.py
+++ b/solution.py
@@ -16,6 +16,7 @@
 GROUP = H // KVH
 SCALE_LOG2 = HD ** (-0.5) * 1.4426950408889634
 NT = (((1,), (1,)), ((), ()))
+VMEM_LIMIT = 40 * 1024 * 1024
 
 
 def arrivals(n_outer):
@@ -33,52 +34,40 @@
 
 def attention_kernel(n_chip, odd, where_ref, order_ref, table_ref, q_ref, *refs):
     n_outer = n_chip // 2
-    pieces = refs[: 2 * n_outer]
-    o_ref, kbuf, vbuf, sems = refs[2 * n_outer :]
+    pieces, o_ref = refs[:-1], refs[-1]
     step = pl.program_id(0)
     head = pl.program_id(1)
     per_entry = n_chip // ENTRIES
     outer, side, core = where_ref[0], where_ref[1], where_ref[2]
     chip = outer * 2 + side
-
-    @pl.when((step == 0) & (head == 0))
-    def _():
-        for at in range(2 * n_outer):
-            source_side = side if at < n_outer else 1 - side
-            source = order_ref[outer, at % n_outer] * 2 + source_side
-            ahead = source - chip + (core if odd else 0)
-            ahead = lax.rem(ahead + 2 * n_chip, n_chip)
-            entry = ahead // per_entry
-
-            def fetch():
-                for block in range(2):
-                    row = table_ref[2 * block + (1 if odd else 0), entry] & 3
-                    slot = pl.ds(pl.multiple_of(entry * QB, QB), QB)
-                    for half, buf in enumerate((kbuf, vbuf)):
-                        rows = pl.ds(pl.multiple_of((half * 4 + row) * QB, QB), QB)
-                        pltpu.make_async_copy(
-                            pieces[at].at[rows, :], buf.at[block, slot, :], sems.at[block, half]
-                        ).start()
-
-            if per_entry > 1:
-                pl.when(lax.rem(ahead, per_entry) == 0)(fetch)
-            else:
-                fetch()
-
-    @pl.when(head == 0)
-    def _():
-        pltpu.make_async_copy(kbuf.at[step], kbuf.at[step], sems.at[step, 0]).wait()
-        pltpu.make_async_copy(vbuf.at[step], vbuf.at[step], sems.at[step, 1]).wait()
-
     columns = pl.ds(pl.multiple_of(head * HD, HD), HD)
-    keys = kbuf[step, :, columns]
-    values = vbuf[step, :, columns]
-    scores = [
-        lax.dot_general(
+
+    keys, values, usable = [], [], []
+    for at, piece in enumerate(pieces):
+        source_side = side if at < n_outer else 1 - side
+        source = order_ref[outer, at % n_outer] * 2 + source_side
+        ahead = lax.rem(source - chip + (core if odd else 0) + 2 * n_chip, n_chip)
+        row = table_ref[2 * step + (1 if odd else 0), ahead // per_entry] & 3
+        keys.append(piece[pl.ds(pl.multiple_of(row * QB, QB), QB), columns])
+        values.append(piece[pl.ds(pl.multiple_of((4 + row) * QB, QB), QB), columns])
+        usable.append(lax.rem(ahead, per_entry) == 0)
+    keys = jnp.concatenate(keys, 0)
+    values = jnp.concatenate(values, 0)
+
+    scores = []
+    for g in range(GROUP):
+        s = lax.dot_general(
             q_ref[0, :, g * HD : (g + 1) * HD], keys, NT, preferred_element_type=jnp.float32
         )
-        for g in range(GROUP)
-    ]
+        if per_entry > 1:
+            s = jnp.concatenate(
+                [
+                    jnp.where(ok, s[:, at * QB : (at + 1) * QB], -1e30)
+                    for at, ok in enumerate(usable)
+                ],
+                1,
+            )
+        scores.append(s)
     rounded, totals = [], []
     for s in scores:
         weights = jnp.exp2((s - jnp.max(s, axis=-1, keepdims=True)) * SCALE_LOG2)
@@ -93,7 +82,7 @@
     spread = queries.shape[0] // 2
     width = GROUP * HD
     rows = ENTRIES * QB
-    hbm = pl.BlockSpec(memory_space=pltpu.HBM)
+    whole = pl.BlockSpec(memory_space=pltpu.VMEM)
     return pl.pallas_call(
         functools.partial(attention_kernel, n_chip, odd),
         out_shape=jax.ShapeDtypeStruct((2, QB, H * HD), jnp.bfloat16),
@@ -101,15 +90,10 @@
             num_scalar_prefetch=3,
             grid=(2, KVH),
             in_specs=[pl.BlockSpec((1, QB, width), lambda b, h, *_: (b * spread, 0, h))]
-            + [hbm] * len(pieces),
+            + [whole] * len(pieces),
             out_specs=pl.BlockSpec((1, QB, width), lambda b, h, *_: (b, 0, h)),
-            scratch_shapes=[
-                pltpu.VMEM((2, rows, KVH * HD), jnp.bfloat16),
-                pltpu.VMEM((2, rows, KVH * HD), jnp.bfloat16),
-                pltpu.SemaphoreType.DMA((2, 2)),
-            ],
         ),
-        compiler_params=pltpu.CompilerParams(vmem_limit_bytes=32 * 1024 * 1024),
+        compiler_params=pltpu.CompilerParams(vmem_limit_bytes=VMEM_LIMIT),
         cost_estimate=pl.CostEstimate(
             flops=4 * 2 * QB * rows * H * HD,
             bytes_accessed=2 * rows * 2 * KVH * HD * 2 + 4 * QB * H * HD * 2,
@@ -160,6 +144,7 @@
     depth, half = sets[0][0].shape[0] // 4, sets[0][0].shape[1]
     total = H * HD
     whole = pl.BlockSpec((2, QB, total), lambda p, h, *_: (0, 0, 0))
+    inside = pl.BlockSpec(memory_space=pltpu.VMEM)
     hbm = pl.BlockSpec(memory_space=pltpu.HBM)
     count = 3 + 2 + parts * n_outer
     kernel = functools.partial(project_kernel, n_outer, parts, depth)
@@ -182,7 +167,7 @@
             num_scalar_prefetch=3,
             grid=(parts, 2),
             in_specs=[whole, whole]
-            + [hbm] * (parts * n_outer)
+            + [inside] * (parts * n_outer)
             + ([] if before is None else [hbm]),
             out_specs=pl.BlockSpec((4 * QB, half), lambda p, h, w, r, q: (0, q[p] * 2 + h)),
             scratch_shapes=[
@@ -192,7 +177,7 @@
             ],
         ),
         input_output_aliases={} if before is None else {count: 0},
-        compiler_params=pltpu.CompilerParams(vmem_limit_bytes=32 * 1024 * 1024),
+        compiler_params=pltpu.CompilerParams(vmem_limit_bytes=VMEM_LIMIT),
         cost_estimate=pl.CostEstimate(
             flops=2 * 4 * QB * total * parts * 2 * half,
             bytes_accessed=2 * (total * parts * 2 * half + 4 * QB * (total + parts * 2 * half)),
@@ -265,27 +250,49 @@
                 result = jnp.where(mask, got[offset], result)
         return result
 
+    def after(array, *others):
+        return lax.optimization_barrier((array, *others))[0]
+
+    got = line(jnp.concatenate([keys, values], 0))
+    near, across = [got[0]], [swap_side(got[0])]
+    for k in range(1, n_outer):
+        tied = {
+            d: after(got[d], near[-1])
+            for d in sorted({row[k] for row in order_rows})
+        }
+        near.append(pick(tied, k))
+        across.append(swap_side(after(near[-1], across[-1])))
+    pieces = near + across
+
     query_blocks = queries.reshape(4, QB, H * HD)
-    far_queries = swap_core(query_blocks.reshape(2, 2, QB, H * HD)[:, 1])
     far_table = swap_core(block_table)
-
-    got = line(jnp.concatenate([keys, values], 0))
-    near = [got[0]] + [pick(got, k) for k in range(1, n_outer)]
-    pieces = near + [swap_side(piece) for piece in near]
 
     quarter = out_weight.shape[1] // (2 * n_groups)
     half = quarter // 2
     mine = lax.dynamic_slice_in_dim(out_weight, (group * 2 + core) * quarter, quarter, 1)
     theirs = lax.dynamic_slice_in_dim(out_weight, (group * 2 + 1 - core) * quarter, quarter, 1)
     theirs = swap_core(theirs)
+    far_queries = swap_core(
+        after(query_blocks.reshape(2, 2, QB, H * HD)[:, 1], theirs)
+    )
     first = jnp.where(core == 0, mine, theirs)
     second = jnp.where(core == 0, theirs, mine)
     early = jnp.concatenate([first[:, half:], second[:, half:]], 0)
     late = jnp.concatenate([first[:, :half], second[:, :half]], 0)
     depth = late.shape[0]
-    wgot = line(jnp.concatenate([late, early, swap_side(early)], 0))
-    wnear = [wgot[0]] + [pick(wgot, k) for k in range(1, n_outer)]
-    own = [jnp.concatenate([w, swap_side(w[:depth])], 0) for w in wnear]
+    ends = [got[d] for d in (1 - n_outer, n_outer - 1)]
+    wgot = line(after(jnp.concatenate([late, early, swap_side(early)], 0), *ends))
+    own = []
+    last = across[-1]
+    for k in range(n_outer):
+        if k == 0:
+            w = wgot[0]
+        else:
+            w = pick(
+                {d: after(wgot[d], own[-1]) for d in sorted({row[k] for row in order_rows})}, k
+            )
+        last = swap_side(after(w[:depth], last))
+        own.append(jnp.concatenate([w, last], 0))
 
     far = attention(far_queries, where, order, far_table, pieces, n_chip, True)
     odd = swap_core(far)

time: 278 us -> 316 us (1.14)
  waiting for transfers between devices: 162 us -> 193 us
  starting transfers between devices: 40.4 us -> 46.6 us
  Pallas kernels: 45.6 us -> 41.6 us
    ppermute x4, waiting for transfers between devices: 5.68 us -> 74.6 us  [body(): sets.append([lax.ppermute(w, 'groups', turn) for w in own])]
    ppermute x9, waiting for transfers between devices: 65.5 us -> 38.6 us  [swap_side(): lax.ppermute(array, 'seq', [(index(o, s, c), index(o, 1 - s, c)) for o, s...]
    ppermute x12, waiting for transfers between devices: 90.1 us -> 79.9 us  [move(): lax.ppermute(array, 'seq', [(index(o, s, c), index(o + way, s, c)) for o,...]
    pallas_call x2, Pallas kernels: 28.7 us -> 21.2 us  [attention(): pl.pallas_call(functools.partial(attention_kernel, n_chip, odd), out_shap...]
    ppermute x12, starting transfers between devices: 21.4 us -> 27.3 us  [move(): lax.ppermute(array, 'seq', [(index(o, s, c), index(o + way, s, c)) for o,...]
    pallas_call x2, Pallas kernels: 16.9 us -> 20.4 us  [project(): pl.pallas_call(kernel, out_shape=jax.ShapeDtypeStruct((4 * QB, columns),...]
    unnamed x71 -> x62, local copies, waits for them, and re-layouts: 12.5 us -> 14.4 us
    select_n x2 -> x6, other arithmetic: 5.45 us -> 7.17 us  [pick(): result = jnp.where(mask, got[offset], result)]
  transfers between devices with their start and end apart: 37 -> 37, of which waited for: 12 -> 12; matrix products, arithmetic and copies ran while one was open for 7% -> 5% of each run, Pallas kernels for 13% -> 10%
where the time goes in v2:
time: 316 us; the launch traced here: 312 us
  waiting for transfers between devices  193 us (61%)
  starting transfers between devices  46.6 us (15%)
  Pallas kernels  41.6 us (13%)
  local copies, waits for them, and re-layouts  19.1 us (6%)
  other arithmetic  11 us (3%)
    ppermute x12, waiting for transfers between devices, move(): lax.ppermute(array, 'seq', [(index(o, s, c), index(o + way, s, c)) for o,...  79.9 us
    ppermute x4, waiting for transfers between devices, body(): sets.append([lax.ppermute(w, 'groups', turn) for w in own])  74.6 us
    ppermute x9, waiting for transfers between devices, swap_side(): lax.ppermute(array, 'seq', [(index(o, s, c), index(o, 1 - s, c)) for o, s...  38.6 us
    ppermute x12, starting transfers between devices, move(): lax.ppermute(array, 'seq', [(index(o, s, c), index(o + way, s, c)) for o,...  27.3 us
    pallas_call x2, Pallas kernels, attention(): pl.pallas_call(functools.partial(attention_kernel, n_chip, odd), out_shap...  21.2 us
    pallas_call x2, Pallas kernels, project(): pl.pallas_call(kernel, out_shape=jax.ShapeDtypeStruct((4 * QB, columns),...  20.4 us
    unnamed x62, local copies, waits for them, and re-layouts  14.4 us
    ppermute x9, starting transfers between devices, swap_side(): lax.ppermute(array, 'seq', [(index(o, s, c), index(o, 1 - s, c)) for o, s...  13 us
  transfers between devices with their start and end apart: 37, of which 12 were waited for; matrix products, arithmetic and copies ran while one was open for 5% of the time, Pallas kernels for 10%

profile of v2, /device:TPU:0, one launch (start us, length us, event | category | flops | bytes accessed | tf_op | source)
XLA Modules:
  0.0 311.9 jit_solution(10961036204291388136)
XLA Ops:
  0.0 1.1 constant_dynamic-update-slice_fusion.1
  1.1 1.1 constant_dynamic-update-slice_fusion.refs_0_
  2.2 1.3 collective-permute-start.1
  3.5 6.6 %collective-permute-start = (bf16[1024,512]{1,0:T(8,128)(2,1)S(1)}, bf16[1024,512]{1,0:T(8,128)(2,1)}, u32[]{:S(2)}, u32[]{:S(2)}) collective-permute-start(bf16[1024,512]{1,0:T(8,128)(2,1)S(1)} %constant_dynamic-update-slice_fusion.refs_0_), channel_id=1, source_target_pairs={{0,4},{1,5},{2,6},{3,7},{4,8},{5,9},{6,10},{7,11},{8,12},{9,13},{1... | collective-permute-start | bytes 3145736 | tf_op jit(solution)/shard_map/ppermute | solution.py:225
  10.0 2.0 collective-permute-start.6
  12.0 18.4 %collective-permute-done.1 = bf16[1024,512]{1,0:T(8,128)(2,1)} collective-permute-done((bf16[1024,512]{1,0:T(8,128)(2,1)S(1)}, bf16[1024,512]{1,0:T(8,128)(2,1)}, u32[]{:S(2)}, u32[]{:S(2)}) %collective-permute-start.1) | collective-permute-done | bytes 1048608 | tf_op jit(solution)/shard_map/ppermute | solution.py:225
  30.4 1.3 collective-permute-start.3
  31.7 1.7 collective-permute-start.2
  33.3 1.3 broadcast_select_fusion.refs_1_
  34.7 1.7 collective-permute-start.7
  36.4 20.5 %collective-permute-done.3 = bf16[1024,512]{1,0:T(8,128)(2,1)} collective-permute-done((bf16[1024,512]{1,0:T(8,128)(2,1)}, bf16[1024,512]{1,0:T(8,128)(2,1)}, u32[]{:S(2)}, u32[]{:S(2)}) %collective-permute-start.3) | collective-permute-done | bytes 1048608 | tf_op jit(solution)/shard_map/ppermute | solution.py:225
  56.9 1.3 collective-permute-start.5
  58.2 1.7 collective-permute-start.4
  59.9 1.7 constant_dynamic-slice_fusion
  61.6 1.4 select_select_fusion.1.refs_2_
  63.0 1.4 collective-permute-start.8
  64.4 1.1 broadcast_select_fusion.2
  65.5 17.0 %collective-permute-done.5 = bf16[1024,512]{1,0:T(8,128)(2,1)} collective-permute-done((bf16[1024,512]{1,0:T(8,128)(2,1)}, bf16[1024,512]{1,0:T(8,128)(2,1)}, u32[]{:S(2)}, u32[]{:S(2)}) %collective-permute-start.5) | collective-permute-done | bytes 1048608 | tf_op jit(solution)/shard_map/ppermute | solution.py:225
  82.5 1.4 select_select_fusion.refs_3_
  84.0 4.6 %collective-permute-done.8.refs_6_ = bf16[1024,512]{1,0:T(8,128)(2,1)S(1)} collective-permute-done((bf16[1024,512]{1,0:T(8,128)(2,1)S(1)}, bf16[1024,512]{1,0:T(8,128)(2,1)S(1)}, u32[]{:S(2)}, u32[]{:S(2)}) %collective-permute-start.8) | collective-permute-done | bytes 1048608 | tf_op jit(solution)/shard_map/ppermute | solution.py:220
  88.6 1.4 collective-permute-start.9
  90.0 0.7 collective-permute-start.14
  90.8 28.2 %collective-permute-done.14 = bf16[256,512]{1,0:T(8,128)(2,1)S(1)} collective-permute-done((bf16[256,512]{1,0:T(8,128)(2,1)S(1)}, bf16[256,512]{1,0:T(8,128)(2,1)S(1)}, u32[]{:S(2)}, u32[]{:S(2)}) %collective-permute-start.14) | collective-permute-done | bytes 262176 | tf_op jit(solution)/shard_map/ppermute | solution.py:220
  119.0 1.3 collective-permute-start.18
  120.3 7.4 %collective-permute-start.17 = (bf16[768,512]{1,0:T(8,128)(2,1)S(1)}, bf16[768,512]{1,0:T(8,128)(2,1)}, u32[]{:S(2)}, u32[]{:S(2)}) collective-permute-start(bf16[768,512]{1,0:T(8,128)(2,1)S(1)} %constant_dynamic-update-slice_fusion.2), channel_id=1, source_target_pairs={{0,4},{1,5},{2,6},{3,7},{4,8},{5,9},{6,10},{7,11},{8,12},{9,13},{1... | collective-permute-start | bytes 2359304 | tf_op jit(solution)/shard_map/ppermute | solution.py:225
  127.8 1.0 copy-done.11
  128.7 1.4 collective-permute-start.15
  130.1 1.1 slice_bitcast_fusion
  131.2 10.3 %collective-permute-done.18 = bf16[768,512]{1,0:T(8,128)(2,1)} collective-permute-done((bf16[768,512]{1,0:T(8,128)(2,1)S(1)}, bf16[768,512]{1,0:T(8,128)(2,1)}, u32[]{:S(2)}, u32[]{:S(2)}) %collective-permute-start.18) | collective-permute-done | bytes 786464 | tf_op jit(solution)/shard_map/ppermute | solution.py:225
  141.5 1.3 collective-permute-start.22
  142.8 1.6 collective-permute-start.21
  144.4 1.0 constant_dynamic-update-slice_fusion.6
  145.4 0.7 constant_dynamic-update-slice_fusion.5.refs_0_
  146.1 1.2 broadcast_select_fusion.1
  147.4 0.8 copy-done.28
  148.2 1.4 collective-permute-start.19
  149.6 13.7 %collective-permute-done.22 = bf16[768,512]{1,0:T(8,128)(2,1)} collective-permute-done((bf16[768,512]{1,0:T(8,128)(2,1)}, bf16[768,512]{1,0:T(8,128)(2,1)}, u32[]{:S(2)}, u32[]{:S(2)}) %collective-permute-start.22) | collective-permute-done | bytes 786464 | tf_op jit(solution)/shard_map/ppermute | solution.py:225
  163.2 1.3 collective-permute-start.26
  165.3 1.4 pad_maximum_fusion.refs_1_
  166.7 1.7 select_select_fusion.3
  168.4 1.6 collective-permute-start.23
  170.1 10.4 %shard_map.65 = bf16[2,128,2048]{2,1,0:T(8,128)(2,1)S(1)} custom-call(s32[3]{0:T(128)S(1)} %pad_add_fusion.where_ref, s32[4,4]{1,0:T(4,128)S(1)} %copy-done.26, s32[4,8]{1,0:T(4,128)S(1)} %collective-permute-done.10.table_ref, bf16[2,128,2048]{2,1,0:T(8,128)(2,1)} %collective-permute-done.12.q_ref, bf16[1024,512]{1,0:T(8,128)(2,1)S(1)} %copy-done.1, ...), custom_call_target="tpu_custom_call" | custom-call | flops 2147483648 | bytes 6291456 | tf_op jit(solution)/shard_map/pallas_call | solution.py:86
  180.6 1.5 collective-permute-start.29
  182.6 1.5 collective-permute-start.27
  184.1 1.5 collective-permute-start.31
  185.6 5.7 %collective-permute-done.27 = bf16[256,512]{1,0:T(8,128)(2,1)S(1)} collective-permute-done((bf16[256,512]{1,0:T(8,128)(2,1)S(1)}, bf16[256,512]{1,0:T(8,128)(2,1)S(1)}, u32[]{:S(2)}, u32[]{:S(2)}) %collective-permute-start.27) | collective-permute-done | bytes 262176 | tf_op jit(solution)/shard_map/ppermute | solution.py:220
  191.3 1.0 pad_maximum_fusion.2.refs_3_
  192.3 1.0 copy-done.14
  193.8 13.1 %collective-permute-done.29.refs_4_ = bf16[1024,512]{1,0:T(8,128)(2,1)} collective-permute-done((bf16[1024,512]{1,0:T(8,128)(2,1)}, bf16[1024,512]{1,0:T(8,128)(2,1)}, u32[]{:S(2)}, u32[]{:S(2)}) %collective-permute-start.29) | collective-permute-done | bytes 1048608 | tf_op jit(solution)/shard_map/ppermute | solution.py:304
  207.0 0.9 copy-done.16
  207.9 1.5 collective-permute-start.35
  209.4 20.0 %collective-permute-done.31.refs_5_ = bf16[1024,512]{1,0:T(8,128)(2,1)} collective-permute-done((bf16[1024,512]{1,0:T(8,128)(2,1)S(1)}, bf16[1024,512]{1,0:T(8,128)(2,1)}, u32[]{:S(2)}, u32[]{:S(2)}) %collective-permute-start.31) | collective-permute-done | bytes 1048608 | tf_op jit(solution)/shard_map/ppermute | solution.py:304
  229.4 1.0 copy-done.18
  231.0 20.9 %collective-permute-done.33.refs_6_ = bf16[1024,512]{1,0:T(8,128)(2,1)} collective-permute-done((bf16[1024,512]{1,0:T(8,128)(2,1)S(1)}, bf16[1024,512]{1,0:T(8,128)(2,1)}, u32[]{:S(2)}, u32[]{:S(2)}) %collective-permute-start.33) | collective-permute-done | bytes 1048608 | tf_op jit(solution)/shard_map/ppermute | solution.py:304
  251.9 1.0 copy-done.20
  253.4 20.5 %collective-permute-done.35.refs_7_ = bf16[1024,512]{1,0:T(8,128)(2,1)} collective-permute-done((bf16[1024,512]{1,0:T(8,128)(2,1)}, bf16[1024,512]{1,0:T(8,128)(2,1)}, u32[]{:S(2)}, u32[]{:S(2)}) %collective-permute-start.35) | collective-permute-done | bytes 1048608 | tf_op jit(solution)/shard_map/ppermute | solution.py:304
  274.1 1.2 copy-done.2
  275.3 1.6 copy-done.4
  276.9 1.2 copy-done.7
  278.1 1.2 copy-done.10
  279.3 1.2 copy-done.13
  280.6 10.7 %shard_map.64.e = bf16[2,128,2048]{2,1,0:T(8,128)(2,1)S(1)} custom-call(s32[3]{0:T(128)S(1)} %pad_add_fusion.where_ref, s32[4,4]{1,0:T(4,128)S(1)} %copy-done.26, s32[4,8]{1,0:T(4,128)S(1)} %copy-done.27, bf16[4,128,2048]{2,1,0:T(8,128)(2,1)S(1)} %bitcast.14, bf16[1024,512]{1,0:T(8,128)(2,1)S(1)} %copy-done.2, ...), custom_call_target="tpu_custom_call" | custom-call | flops 2147483648 | bytes 6291456 | tf_op jit(solution)/shard_map/pallas_call | solution.py:86
  291.4 10.5 %shard_map.66.refs_8_ = bf16[512,4096]{1,0:T(8,128)(2,1)} custom-call(s32[3]{0:T(128)S(1)} %pad_add_fusion.where_ref, s32[4,4]{1,0:T(4,128)S(1)} %copy-done.26, s32[2]{0:T(128)S(1)} %pad_add_fusion.2.places_ref, bf16[2,128,2048]{2,1,0:T(8,128)(2,1)S(1)} %shard_map.64.e, bf16[2,128,2048]{2,1,0:T(8,128)(2,1)S(1)} %copy-done.15, ...), custom_call_target="tpu_custom_call" | custom-call | flops 4294967296 | bytes 12582912 | tf_op jit(solution)/shard_map/pallas_call | solution.py:163
  302.0 9.9 %shard_map.67 = bf16[512,4096]{1,0:T(8,128)(2,1)} custom-call(s32[3]{0:T(128)S(1)} %pad_add_fusion.where_ref, s32[4,4]{1,0:T(4,128)S(1)} %copy-done.26, s32[2]{0:T(128)S(1)} %pad_add_fusion.1.places_ref, bf16[2,128,2048]{2,1,0:T(8,128)(2,1)S(1)} %shard_map.64.e, bf16[2,128,2048]{2,1,0:T(8,128)(2,1)S(1)} %copy-done.15, ...), custom_call_target="tpu_custom_call", output_to_operand_aliasing={{}: (13, {})} | custom-call | flops 4294967296 | bytes 12582912 | tf_op jit(solution)/shard_map/pallas_call | solution.py:163
  (101 shorter events, 3.3 us)
Async XLA Ops:
  2.2 59.4 %copy-start = (bf16[1024,512]{1,0:T(8,128)(2,1)}, bf16[1024,512]{1,0:T(8,128)(2,1)S(1)}, u32[]{:S(2)}) copy-start(bf16[1024,512]{1,0:T(8,128)(2,1)S(1)} %constant_dynamic-update-slice_fusion.refs_0_) | copy-start | bytes 3145732
  2.2 28.2 %collective-permute-start.1 = (bf16[1024,512]{1,0:T(8,128)(2,1)S(1)}, bf16[1024,512]{1,0:T(8,128)(2,1)}, u32[]{:S(2)}, u32[]{:S(2)}) collective-permute-start(bf16[1024,512]{1,0:T(8,128)(2,1)S(1)} %constant_dynamic-update-slice_fusion.refs_0_), channel_id=1, source_target_pairs={{4,0},{5,1},{6,2},{7,3},{8,4},{9,5},{10,6},{11,7},{12,8},{13,9},{1... | collective-permute-start | bytes 3145736 | tf_op jit(solution)/shard_map/ppermute | solution.py:225
  3.5 28.2 %collective-permute-start = (bf16[1024,512]{1,0:T(8,128)(2,1)S(1)}, bf16[1024,512]{1,0:T(8,128)(2,1)}, u32[]{:S(2)}, u32[]{:S(2)}) collective-permute-start(bf16[1024,512]{1,0:T(8,128)(2,1)S(1)} %constant_dynamic-update-slice_fusion.refs_0_), channel_id=1, source_target_pairs={{0,4},{1,5},{2,6},{3,7},{4,8},{5,9},{6,10},{7,11},{8,12},{9,13},{1... | collective-permute-start | bytes 3145736 | tf_op jit(solution)/shard_map/ppermute | solution.py:225
  10.0 24.6 %collective-permute-start.6 = (bf16[1024,512]{1,0:T(8,128)(2,1)S(1)}, bf16[1024,512]{1,0:T(8,128)(2,1)S(1)}, u32[]{:S(2)}, u32[]{:S(2)}) collective-permute-start(bf16[1024,512]{1,0:T(8,128)(2,1)S(1)} %constant_dynamic-update-slice_fusion.refs_0_), channel_id=1, source_target_pairs={{0,2},{1,3},{2,0},{3,1},{4,6},{5,7},{6,4},{7,5},{8,10},{9,11},{10,... | collective-permute-start | bytes 3145736 | tf_op jit(solution)/shard_map/ppermute | solution.py:220
  30.4 26.5 %collective-permute-start.3 = (bf16[1024,512]{1,0:T(8,128)(2,1)}, bf16[1024,512]{1,0:T(8,128)(2,1)}, u32[]{:S(2)}, u32[]{:S(2)}) collective-permute-start(bf16[1024,512]{1,0:T(8,128)(2,1)} %collective-permute-done.1), channel_id=1, source_target_pairs={{4,0},{5,1},{6,2},{7,3},{8,4},{9,5},{10,6},{11,7},{20,16},{21,17},... | collective-permute-start | bytes 3145736 | tf_op jit(solution)/shard_map/ppermute | solution.py:225
  31.7 26.5 %collective-permute-start.2 = (bf16[1024,512]{1,0:T(8,128)(2,1)}, bf16[1024,512]{1,0:T(8,128)(2,1)}, u32[]{:S(2)}, u32[]{:S(2)}) collective-permute-start(bf16[1024,512]{1,0:T(8,128)(2,1)} %collective-permute-done), channel_id=1, source_target_pairs={{4,8},{5,9},{6,10},{7,11},{8,12},{9,13},{10,14},{11,15},{20,24},{2... | collective-permute-start | bytes 3145736 | tf_op jit(solution)/shard_map/ppermute | solution.py:225
  34.7 28.3 %copy-start.5 = (bf16[1024,512]{1,0:T(8,128)(2,1)}, bf16[1024,512]{1,0:T(8,128)(2,1)S(1)}, u32[]{:S(2)}) copy-start(bf16[1024,512]{1,0:T(8,128)(2,1)S(1)} %collective-permute-done.6.refs_4_) | copy-start | bytes 3145732
  34.7 28.3 %collective-permute-start.7 = (bf16[1024,512]{1,0:T(8,128)(2,1)S(1)}, bf16[1024,512]{1,0:T(8,128)(2,1)}, u32[]{:S(2)}, u32[]{:S(2)}) collective-permute-start(bf16[1024,512]{1,0:T(8,128)(2,1)S(1)} %broadcast_select_fusion.refs_1_), channel_id=1, source_target_pairs={{0,2},{1,3},{2,0},{3,1},{4,6},{5,7},{6,4},{7,5},{8,10},{9,11},{10,... | collective-permute-start | bytes 3145736 | tf_op jit(solution)/shard_map/ppermute | solution.py:220
  56.9 25.6 %collective-permute-start.5 = (bf16[1024,512]{1,0:T(8,128)(2,1)}, bf16[1024,512]{1,0:T(8,128)(2,1)}, u32[]{:S(2)}, u32[]{:S(2)}) collective-permute-start(bf16[1024,512]{1,0:T(8,128)(2,1)} %collective-permute-done.3), channel_id=1, source_target_pairs={{4,0},{5,1},{6,2},{7,3},{20,16},{21,17},{22,18},{23,19}} | collective-permute-start | bytes 3145736 | tf_op jit(solution)/shard_map/ppermute | solution.py:225
  58.2 24.3 %collective-permute-start.4 = (bf16[1024,512]{1,0:T(8,128)(2,1)}, bf16[1024,512]{1,0:T(8,128)(2,1)}, u32[]{:S(2)}, u32[]{:S(2)}) collective-permute-start(bf16[1024,512]{1,0:T(8,128)(2,1)} %collective-permute-done.2), channel_id=1, source_target_pairs={{8,12},{9,13},{10,14},{11,15},{24,28},{25,29},{26,30},{27,31}} | collective-permute-start | bytes 3145736 | tf_op jit(solution)/shard_map/ppermute | solution.py:225
  61.6 2.8 collective-permute-start.11
  63.0 25.6 %collective-permute-start.8 = (bf16[1024,512]{1,0:T(8,128)(2,1)S(1)}, bf16[1024,512]{1,0:T(8,128)(2,1)S(1)}, u32[]{:S(2)}, u32[]{:S(2)}) collective-permute-start(bf16[1024,512]{1,0:T(8,128)(2,1)S(1)} %select_select_fusion.1.refs_2_), channel_id=1, source_target_pairs={{0,2},{1,3},{2,0},{3,1},{4,6},{5,7},{6,4},{7,5},{8,10},{9,11},{10,... | collective-permute-start | bytes 3145736 | tf_op jit(solution)/shard_map/ppermute | solution.py:220
  84.0 46.1 %copy-start.3 = (bf16[512,2048]{1,0:T(8,128)(2,1)S(1)}, bf16[512,2048]{1,0:T(8,128)(2,1)}, u32[]{:S(2)}) copy-start(bf16[512,2048]{1,0:T(8,128)(2,1)} %param.6) | copy-start | bytes 6291460
  88.6 42.6 %copy-start.8 = (bf16[1024,512]{1,0:T(8,128)(2,1)}, bf16[1024,512]{1,0:T(8,128)(2,1)S(1)}, u32[]{:S(2)}) copy-start(bf16[1024,512]{1,0:T(8,128)(2,1)S(1)} %collective-permute-done.8.refs_6_) | copy-start | bytes 3145732
  88.6 39.2 %collective-permute-start.9 = (bf16[1024,512]{1,0:T(8,128)(2,1)S(1)}, bf16[1024,512]{1,0:T(8,128)(2,1)S(1)}, u32[]{:S(2)}, u32[]{:S(2)}) collective-permute-start(bf16[1024,512]{1,0:T(8,128)(2,1)S(1)} %select_select_fusion.refs_3_), channel_id=1, source_target_pairs={{0,2},{1,3},{2,0},{3,1},{4,6},{5,7},{6,4},{7,5},{8,10},{9,11},{10,... | collective-permute-start | bytes 3145736 | tf_op jit(solution)/shard_map/ppermute | solution.py:220
  90.0 29.0 %collective-permute-start.14 = (bf16[256,512]{1,0:T(8,128)(2,1)S(1)}, bf16[256,512]{1,0:T(8,128)(2,1)S(1)}, u32[]{:S(2)}, u32[]{:S(2)}) collective-permute-start(bf16[256,512]{1,0:T(8,128)(2,1)S(1)} %pad_maximum_fusion.3), channel_id=1, source_target_pairs={{0,2},{1,3},{2,0},{3,1},{4,6},{5,7},{6,4},{7,5},{8,10},{9,11},{10,... | collective-permute-start | bytes 786440 | tf_op jit(solution)/shard_map/ppermute | solution.py:220
  119.0 22.5 %collective-permute-start.18 = (bf16[768,512]{1,0:T(8,128)(2,1)S(1)}, bf16[768,512]{1,0:T(8,128)(2,1)}, u32[]{:S(2)}, u32[]{:S(2)}) collective-permute-start(bf16[768,512]{1,0:T(8,128)(2,1)S(1)} %constant_dynamic-update-slice_fusion.2), channel_id=1, source_target_pairs={{4,0},{5,1},{6,2},{7,3},{8,4},{9,5},{10,6},{11,7},{12,8},{13,9},{1... | collective-permute-start | bytes 2359304 | tf_op jit(solution)/shard_map/ppermute | solution.py:225
  120.3 22.5 %collective-permute-start.17 = (bf16[768,512]{1,0:T(8,128)(2,1)S(1)}, bf16[768,512]{1,0:T(8,128)(2,1)}, u32[]{:S(2)}, u32[]{:S(2)}) collective-permute-start(bf16[768,512]{1,0:T(8,128)(2,1)S(1)} %constant_dynamic-update-slice_fusion.2), channel_id=1, source_target_pairs={{0,4},{1,5},{2,6},{3,7},{4,8},{5,9},{6,10},{7,11},{8,12},{9,13},{1... | collective-permute-start | bytes 2359304 | tf_op jit(solution)/shard_map/ppermute | solution.py:225
  127.8 1.0 copy-start.11
  128.7 16.6 %collective-permute-start.15 = (bf16[256,512]{1,0:T(8,128)(2,1)S(1)}, bf16[256,512]{1,0:T(8,128)(2,1)S(1)}, u32[]{:S(2)}, u32[]{:S(2)}) collective-permute-start(bf16[256,512]{1,0:T(8,128)(2,1)S(1)} %slice.32), channel_id=1, source_target_pairs={{0,2},{1,3},{2,0},{3,1},{4,6},{5,7},{6,4},{7,5},{8,10},{9,11},{10,... | collective-permute-start | bytes 786440 | tf_op jit(solution)/shard_map/ppermute | solution.py:220
  131.2 38.9 %collective-permute-start.12 = (bf16[2,128,2048]{2,1,0:T(8,128)(2,1)}, bf16[2,128,2048]{2,1,0:T(8,128)(2,1)}, u32[]{:S(2)}, u32[]{:S(2)}) collective-permute-start(bf16[2,128,2048]{2,1,0:T(8,128)(2,1)} %slice_bitcast_fusion), channel_id=1, source_target_pairs={{0,1},{1,0},{2,3},{3,2},{4,5},{5,4},{6,7},{7,6},{8,9},{9,8},{10,11... | collective-permute-start | bytes 3145736 | tf_op jit(solution)/shard_map/ppermute | solution.py:215
  141.5 21.7 %collective-permute-start.22 = (bf16[768,512]{1,0:T(8,128)(2,1)}, bf16[768,512]{1,0:T(8,128)(2,1)}, u32[]{:S(2)}, u32[]{:S(2)}) collective-permute-start(bf16[768,512]{1,0:T(8,128)(2,1)} %collective-permute-done.18), channel_id=1, source_target_pairs={{4,0},{5,1},{6,2},{7,3},{8,4},{9,5},{10,6},{11,7},{20,16},{21,17},... | collective-permute-start | bytes 2359304 | tf_op jit(solution)/shard_map/ppermute | solution.py:225
  142.8 21.7 %collective-permute-start.21 = (bf16[768,512]{1,0:T(8,128)(2,1)}, bf16[768,512]{1,0:T(8,128)(2,1)}, u32[]{:S(2)}, u32[]{:S(2)}) collective-permute-start(bf16[768,512]{1,0:T(8,128)(2,1)} %collective-permute-done.17), channel_id=1, source_target_pairs={{4,8},{5,9},{6,10},{7,11},{8,12},{9,13},{10,14},{11,15},{20,24},{2... | collective-permute-start | bytes 2359304 | tf_op jit(solution)/shard_map/ppermute | solution.py:225
  145.4 4.2 %copy-start.27 = (s32[4,8]{1,0:T(4,128)S(1)}, s32[4,8]{1,0:T(4,128)}, u32[]{:S(2)}) copy-start(s32[4,8]{1,0:T(4,128)} %table_ref.1) | copy-start | bytes 388
  148.2 17.0 %collective-permute-start.19 = (bf16[256,512]{1,0:T(8,128)(2,1)S(1)}, bf16[256,512]{1,0:T(8,128)(2,1)}, u32[]{:S(2)}, u32[]{:S(2)}) collective-permute-start(bf16[256,512]{1,0:T(8,128)(2,1)S(1)} %slice.41), channel_id=1, source_target_pairs={{0,2},{1,3},{2,0},{3,1},{4,6},{5,7},{6,4},{7,5},{8,10},{9,11},{10,... | collective-permute-start | bytes 786440 | tf_op jit(solution)/shard_map/ppermute | solution.py:220
  149.6 20.5 %collective-permute-start.10 = (s32[4,8]{1,0:T(4,128)S(1)}, s32[4,8]{1,0:T(4,128)S(1)}, u32[]{:S(2)}, u32[]{:S(2)}) collective-permute-start(s32[4,8]{1,0:T(4,128)S(1)} %copy-done.27), channel_id=1, source_target_pairs={{0,1},{1,0},{2,3},{3,2},{4,5},{5,4},{6,7},{7,6},{8,9},{9,8},{10,11... | collective-permute-start | bytes 392 | tf_op jit(solution)/shard_map/ppermute | solution.py:215
  163.2 19.2 %collective-permute-start.26 = (bf16[768,512]{1,0:T(8,128)(2,1)}, bf16[768,512]{1,0:T(8,128)(2,1)S(1)}, u32[]{:S(2)}, u32[]{:S(2)}) collective-permute-start(bf16[768,512]{1,0:T(8,128)(2,1)} %collective-permute-done.22), channel_id=1, source_target_pairs={{4,0},{5,1},{6,2},{7,3},{20,16},{21,17},{22,18},{23,19}} | collective-permute-start | bytes 2359304 | tf_op jit(solution)/shard_map/ppermute | solution.py:225
  164.5 17.9 %collective-permute-start.25 = (bf16[768,512]{1,0:T(8,128)(2,1)}, bf16[768,512]{1,0:T(8,128)(2,1)S(1)}, u32[]{:S(2)}, u32[]{:S(2)}) collective-permute-start(bf16[768,512]{1,0:T(8,128)(2,1)} %collective-permute-done.21), channel_id=1, source_target_pairs={{8,12},{9,13},{10,14},{11,15},{24,28},{25,29},{26,30},{27,31}} | collective-permute-start | bytes 2359304 | tf_op jit(solution)/shard_map/ppermute | solution.py:225
  165.3 4.8 %copy-start.12 = (bf16[1024,512]{1,0:T(8,128)(2,1)S(1)}, bf16[1024,512]{1,0:T(8,128)(2,1)}, u32[]{:S(2)}) copy-start(bf16[1024,512]{1,0:T(8,128)(2,1)} %copy-done.11) | copy-start | bytes 3145732
  166.6 24.6 %copy-start.22 = (bf16[1024,512]{1,0:T(8,128)(2,1)}, bf16[1024,512]{1,0:T(8,128)(2,1)S(1)}, u32[]{:S(2)}) copy-start(bf16[1024,512]{1,0:T(8,128)(2,1)S(1)} %pad_maximum_fusion.refs_1_) | copy-start | bytes 3145732
  166.7 3.4 %copy-start.1 = (bf16[1024,512]{1,0:T(8,128)(2,1)S(1)}, bf16[1024,512]{1,0:T(8,128)(2,1)}, u32[]{:S(2)}) copy-start(bf16[1024,512]{1,0:T(8,128)(2,1)} %copy-done) | copy-start | bytes 3145732
  166.7 3.4 %copy-start.6 = (bf16[1024,512]{1,0:T(8,128)(2,1)S(1)}, bf16[1024,512]{1,0:T(8,128)(2,1)}, u32[]{:S(2)}) copy-start(bf16[1024,512]{1,0:T(8,128)(2,1)} %copy-done.5) | copy-start | bytes 3145732
  166.7 3.4 %copy-start.9 = (bf16[1024,512]{1,0:T(8,128)(2,1)S(1)}, bf16[1024,512]{1,0:T(8,128)(2,1)}, u32[]{:S(2)}) copy-start(bf16[1024,512]{1,0:T(8,128)(2,1)} %copy-done.8) | copy-start | bytes 3145732
  166.7 3.4 %copy-start.26 = (s32[4,4]{1,0:T(4,128)S(1)}, s32[4,4]{1,0:T(4,128)}, u32[]{:S(2)}) copy-start(s32[4,4]{1,0:T(4,128)} %constant.66.clone.order_ref) | copy-start | bytes 196
  168.4 13.8 %collective-permute-start.23 = (bf16[256,512]{1,0:T(8,128)(2,1)S(1)}, bf16[256,512]{1,0:T(8,128)(2,1)S(1)}, u32[]{:S(2)}, u32[]{:S(2)}) collective-permute-start(bf16[256,512]{1,0:T(8,128)(2,1)S(1)} %slice.42), channel_id=1, source_target_pairs={{0,2},{1,3},{2,0},{3,1},{4,6},{5,7},{6,4},{7,5},{8,10},{9,11},{10,... | collective-permute-start | bytes 786440 | tf_op jit(solution)/shard_map/ppermute | solution.py:220
  180.5 11.8 %collective-permute-start.13 = (bf16[2,128,2048]{2,1,0:T(8,128)(2,1)S(1)}, bf16[2,128,2048]{2,1,0:T(8,128)(2,1)S(1)}, u32[]{:S(2)}, u32[]{:S(2)}) collective-permute-start(bf16[2,128,2048]{2,1,0:T(8,128)(2,1)S(1)} %shard_map.65), channel_id=1, source_target_pairs={{0,1},{1,0},{2,3},{3,2},{4,5},{5,4},{6,7},{7,6},{8,9},{9,8},{10,11... | collective-permute-start | bytes 3145736 | tf_op jit(solution)/shard_map/ppermute | solution.py:215
  180.6 26.3 %collective-permute-start.29 = (bf16[1024,512]{1,0:T(8,128)(2,1)}, bf16[1024,512]{1,0:T(8,128)(2,1)}, u32[]{:S(2)}, u32[]{:S(2)}) collective-permute-start(bf16[1024,512]{1,0:T(8,128)(2,1)} %constant_dynamic-update-slice_fusion.5.refs_0_), channel_id=1, source_target_pairs={{0,16},{16,0},{1,17},{17,1},{2,18},{18,2},{3,19},{19,3},{4,20},{20... | collective-permute-start | bytes 3145736 | tf_op jit(solution)/shard_map/ppermute | solution.py:304
  182.2 24.8 %collective-permute-start.16 = (bf16[1024,512]{1,0:T(8,128)(2,1)}, bf16[1024,512]{1,0:T(8,128)(2,1)S(1)}, u32[]{:S(2)}, u32[]{:S(2)}) collective-permute-start(bf16[1024,512]{1,0:T(8,128)(2,1)} %constant_dynamic-update-slice_fusion.5.refs_0_), channel_id=1, source_target_pairs={{0,1},{1,0},{2,3},{3,2},{4,5},{5,4},{6,7},{7,6},{8,9},{9,8},{10,11... | collective-permute-start | bytes 3145736 | tf_op jit(solution)/shard_map/ppermute | solution.py:215
  182.4 24.6 %copy-start.24 = (bf16[1024,512]{1,0:T(8,128)(2,1)}, bf16[1024,512]{1,0:T(8,128)(2,1)S(1)}, u32[]{:S(2)}) copy-start(bf16[1024,512]{1,0:T(8,128)(2,1)S(1)} %pad_maximum_fusion.1.refs_2_) | copy-start | bytes 3145732
  182.6 8.6 %collective-permute-start.27 = (bf16[256,512]{1,0:T(8,128)(2,1)S(1)}, bf16[256,512]{1,0:T(8,128)(2,1)S(1)}, u32[]{:S(2)}, u32[]{:S(2)}) collective-permute-start(bf16[256,512]{1,0:T(8,128)(2,1)S(1)} %slice.43), channel_id=1, source_target_pairs={{0,2},{1,3},{2,0},{3,1},{4,6},{5,7},{6,4},{7,5},{8,10},{9,11},{10,... | collective-permute-start | bytes 786440 | tf_op jit(solution)/shard_map/ppermute | solution.py:220
  184.1 45.3 %collective-permute-start.31 = (bf16[1024,512]{1,0:T(8,128)(2,1)S(1)}, bf16[1024,512]{1,0:T(8,128)(2,1)}, u32[]{:S(2)}, u32[]{:S(2)}) collective-permute-start(bf16[1024,512]{1,0:T(8,128)(2,1)S(1)} %pad_maximum_fusion.refs_1_), channel_id=1, source_target_pairs={{0,16},{16,0},{1,17},{17,1},{2,18},{18,2},{3,19},{19,3},{4,20},{20... | collective-permute-start | bytes 3145736 | tf_op jit(solution)/shard_map/ppermute | solution.py:304
  191.3 38.2 %collective-permute-start.20 = (bf16[1024,512]{1,0:T(8,128)(2,1)S(1)}, bf16[1024,512]{1,0:T(8,128)(2,1)S(1)}, u32[]{:S(2)}, u32[]{:S(2)}) collective-permute-start(bf16[1024,512]{1,0:T(8,128)(2,1)S(1)} %pad_maximum_fusion.refs_1_), channel_id=1, source_target_pairs={{0,1},{1,0},{2,3},{3,2},{4,5},{5,4},{6,7},{7,6},{8,9},{9,8},{10,11... | collective-permute-start | bytes 3145736 | tf_op jit(solution)/shard_map/ppermute | solution.py:215
  192.3 1.0 copy-start.14
  193.3 58.6 %collective-permute-start.33 = (bf16[1024,512]{1,0:T(8,128)(2,1)S(1)}, bf16[1024,512]{1,0:T(8,128)(2,1)}, u32[]{:S(2)}, u32[]{:S(2)}) collective-permute-start(bf16[1024,512]{1,0:T(8,128)(2,1)S(1)} %pad_maximum_fusion.1.refs_2_), channel_id=1, source_target_pairs={{0,16},{16,0},{1,17},{17,1},{2,18},{18,2},{3,19},{19,3},{4,20},{20... | collective-permute-start | bytes 3145736 | tf_op jit(solution)/shard_map/ppermute | solution.py:304
  207.0 44.9 %collective-permute-start.24 = (bf16[1024,512]{1,0:T(8,128)(2,1)S(1)}, bf16[1024,512]{1,0:T(8,128)(2,1)S(1)}, u32[]{:S(2)}, u32[]{:S(2)}) collective-permute-start(bf16[1024,512]{1,0:T(8,128)(2,1)S(1)} %pad_maximum_fusion.1.refs_2_), channel_id=1, source_target_pairs={{0,1},{1,0},{2,3},{3,2},{4,5},{5,4},{6,7},{7,6},{8,9},{9,8},{10,11... | collective-permute-start | bytes 3145736 | tf_op jit(solution)/shard_map/ppermute | solution.py:215
  207.9 66.0 %collective-permute-start.35 = (bf16[1024,512]{1,0:T(8,128)(2,1)}, bf16[1024,512]{1,0:T(8,128)(2,1)}, u32[]{:S(2)}, u32[]{:S(2)}) collective-permute-start(bf16[1024,512]{1,0:T(8,128)(2,1)} %pad_maximum_fusion.2.refs_3_), channel_id=1, source_target_pairs={{0,16},{16,0},{1,17},{17,1},{2,18},{18,2},{3,19},{19,3},{4,20},{20... | collective-permute-start | bytes 3145736 | tf_op jit(solution)/shard_map/ppermute | solution.py:304
  229.4 72.5 %collective-permute-start.30 = (bf16[1024,512]{1,0:T(8,128)(2,1)}, bf16[1024,512]{1,0:T(8,128)(2,1)}, u32[]{:S(2)}, u32[]{:S(2)}) collective-permute-start(bf16[1024,512]{1,0:T(8,128)(2,1)} %collective-permute-done.29.refs_4_), channel_id=1, source_target_pairs={{0,1},{1,0},{2,3},{3,2},{4,5},{5,4},{6,7},{7,6},{8,9},{9,8},{10,11... | collective-permute-start | bytes 3145736 | tf_op jit(solution)/shard_map/ppermute | solution.py:215
  229.4 1.0 copy-start.18
  230.5 71.5 %collective-permute-start.28 = (bf16[1024,512]{1,0:T(8,128)(2,1)}, bf16[1024,512]{1,0:T(8,128)(2,1)}, u32[]{:S(2)}, u32[]{:S(2)}) collective-permute-start(bf16[1024,512]{1,0:T(8,128)(2,1)} %pad_maximum_fusion.2.refs_3_), channel_id=1, source_target_pairs={{0,1},{1,0},{2,3},{3,2},{4,5},{5,4},{6,7},{7,6},{8,9},{9,8},{10,11... | collective-permute-start | bytes 3145736 | tf_op jit(solution)/shard_map/ppermute | solution.py:215
  251.9 50.0 %collective-permute-start.32 = (bf16[1024,512]{1,0:T(8,128)(2,1)}, bf16[1024,512]{1,0:T(8,128)(2,1)}, u32[]{:S(2)}, u32[]{:S(2)}) collective-permute-start(bf16[1024,512]{1,0:T(8,128)(2,1)} %collective-permute-done.31.refs_5_), channel_id=1, source_target_pairs={{0,1},{1,0},{2,3},{3,2},{4,5},{5,4},{6,7},{7,6},{8,9},{9,8},{10,11... | collective-permute-start | bytes 3145736 | tf_op jit(solution)/shard_map/ppermute | solution.py:215
  251.9 1.0 copy-start.20
  252.9 49.0 %collective-permute-start.34 = (bf16[1024,512]{1,0:T(8,128)(2,1)}, bf16[1024,512]{1,0:T(8,128)(2,1)}, u32[]{:S(2)}, u32[]{:S(2)}) collective-permute-start(bf16[1024,512]{1,0:T(8,128)(2,1)} %collective-permute-done.33.refs_6_), channel_id=1, source_target_pairs={{0,1},{1,0},{2,3},{3,2},{4,5},{5,4},{6,7},{7,6},{8,9},{9,8},{10,11... | collective-permute-start | bytes 3145736 | tf_op jit(solution)/shard_map/ppermute | solution.py:215
  273.9 28.0 %collective-permute-start.36 = (bf16[1024,512]{1,0:T(8,128)(2,1)}, bf16[1024,512]{1,0:T(8,128)(2,1)}, u32[]{:S(2)}, u32[]{:S(2)}) collective-permute-start(bf16[1024,512]{1,0:T(8,128)(2,1)} %collective-permute-done.35.refs_7_), channel_id=1, source_target_pairs={{0,1},{1,0},{2,3},{3,2},{4,5},{5,4},{6,7},{7,6},{8,9},{9,8},{10,11... | collective-permute-start | bytes 3145736 | tf_op jit(solution)/shard_map/ppermute | solution.py:215
  274.1 1.2 copy-start.2
  275.3 1.6 copy-start.4
  276.9 1.2 copy-start.7
  278.1 1.2 copy-start.10
  279.3 1.2 copy-start.13
  280.6 10.7 %copy-start.15 = (bf16[2,128,2048]{2,1,0:T(8,128)(2,1)S(1)}, bf16[2,128,2048]{2,1,0:T(8,128)(2,1)}, u32[]{:S(2)}) copy-start(bf16[2,128,2048]{2,1,0:T(8,128)(2,1)} %copy-done.14) | copy-start | bytes 3145732
  280.6 10.8 %copy-start.23 = (bf16[1024,512]{1,0:T(8,128)(2,1)S(1)}, bf16[1024,512]{1,0:T(8,128)(2,1)}, u32[]{:S(2)}) copy-start(bf16[1024,512]{1,0:T(8,128)(2,1)} %copy-done.22) | copy-start | bytes 3145732
  280.6 10.8 %copy-start.25 = (bf16[1024,512]{1,0:T(8,128)(2,1)S(1)}, bf16[1024,512]{1,0:T(8,128)(2,1)}, u32[]{:S(2)}) copy-start(bf16[1024,512]{1,0:T(8,128)(2,1)} %copy-done.24) | copy-start | bytes 3145732
  291.3 10.6 %copy-start.17 = (bf16[1024,512]{1,0:T(8,128)(2,1)S(1)}, bf16[1024,512]{1,0:T(8,128)(2,1)}, u32[]{:S(2)}) copy-start(bf16[1024,512]{1,0:T(8,128)(2,1)} %copy-done.16) | copy-start | bytes 3145732
  291.4 10.6 %copy-start.19 = (bf16[1024,512]{1,0:T(8,128)(2,1)S(1)}, bf16[1024,512]{1,0:T(8,128)(2,1)}, u32[]{:S(2)}) copy-start(bf16[1024,512]{1,0:T(8,128)(2,1)} %copy-done.18) | copy-start | bytes 3145732
  291.4 10.6 %copy-start.21 = (bf16[1024,512]{1,0:T(8,128)(2,1)S(1)}, bf16[1024,512]{1,0:T(8,128)(2,1)}, u32[]{:S(2)}) copy-start(bf16[1024,512]{1,0:T(8,128)(2,1)} %copy-done.20) | copy-start | bytes 3145732
  (2 other events, 1.8 us)

commit v3 on v2

v3 whole, which is shorter than its diff:
```python
import functools

import jax
import jax.numpy as jnp
import numpy as np
from jax import lax
from jax.experimental import pallas as pl
from jax.experimental.pallas import tpu as pltpu
from jax.sharding import PartitionSpec as P

H = 16
KVH = 4
HD = 128
QB = 128
ENTRIES = 8
GROUP = H // KVH
SCALE_LOG2 = HD ** (-0.5) * 1.4426950408889634
NT = (((1,), (1,)), ((), ()))
VMEM_LIMIT = 40 * 1024 * 1024


def arrivals(n_outer):
    rows = []
    for place in range(n_outer):
        row = [0]
        for hop in range(1, n_outer):
            if place - hop >= 0:
                row.append(-hop)
            if place + hop < n_outer:
                row.append(hop)
        rows.append(row)
    return rows


def attention_kernel(
    n_chip, where_ref, order_ref, table_ref, far_table_ref, q_ref, far_q_ref, *refs
):
    n_outer = n_chip // 2
    pieces, o_ref, far_o_ref = refs[:-2], refs[-2], refs[-1]
    step = pl.program_id(0)
    head = pl.program_id(1)
    per_entry = n_chip // ENTRIES
    outer, side, core = where_ref[0], where_ref[1], where_ref[2]
    chip = outer * 2 + side
    odd = step < 2
    columns = pl.ds(pl.multiple_of(head * HD, HD), HD)

    keys, values, usable = [], [], []
    for at, piece in enumerate(pieces):
        source_side = side if at < n_outer else 1 - side
        source = order_ref[outer, at % n_outer] * 2 + source_side
        ahead = lax.rem(source - chip + jnp.where(odd, core, 0) + 2 * n_chip, n_chip)
        entry = ahead // per_entry
        row = (
            jnp.where(
                odd,
                far_table_ref[2 * lax.rem(step, 2) + 1, entry],
                table_ref[2 * lax.rem(step, 2), entry],
            )
            & 3
        )
        keys.append(piece[pl.ds(pl.multiple_of(row * QB, QB), QB), columns])
        values.append(piece[pl.ds(pl.multiple_of((4 + row) * QB, QB), QB), columns])
        usable.append(lax.rem(ahead, per_entry) == 0)
    keys = jnp.concatenate(keys, 0)
    values = jnp.concatenate(values, 0)
    queries = jnp.where(odd, far_q_ref[0], q_ref[0])

    scores = []
    for g in range(GROUP):
        s = lax.dot_general(
            queries[:, g * HD : (g + 1) * HD], keys, NT, preferred_element_type=jnp.float32
        )
        if per_entry > 1:
            s = jnp.concatenate(
                [
                    jnp.where(ok, s[:, at * QB : (at + 1) * QB], -1e30)
                    for at, ok in enumerate(usable)
                ],
                1,
            )
        scores.append(s)
    rounded, totals = [], []
    for s in scores:
        weights = jnp.exp2((s - jnp.max(s, axis=-1, keepdims=True)) * SCALE_LOG2)
        totals.append(jnp.sum(weights, axis=-1, keepdims=True))
        rounded.append(weights.astype(jnp.bfloat16))
    mixed = [
        (jnp.dot(rounded[g], values, preferred_element_type=jnp.float32) / totals[g]).astype(
            jnp.bfloat16
        )
        for g in range(GROUP)
    ]
    result = jnp.concatenate(mixed, 1)

    @pl.when(odd)
    def _():
        far_o_ref[0] = result

    @pl.when(jnp.logical_not(odd))
    def _():
        o_ref[0] = result


def attention(queries, far_queries, where, order, table, far_table, pieces, n_chip):
    width = GROUP * HD
    rows = ENTRIES * QB
    whole = pl.BlockSpec(memory_space=pltpu.VMEM)
    last = KVH - 1

    def near_at(spread):
        return lambda b, h, *_: (
            jnp.where(b < 2, 0, b - 2) * spread, 0, jnp.where(b < 2, 0, h)
        )

    def far_at(b, h, *_):
        return (jnp.where(b < 2, b, 1), 0, jnp.where(b < 2, h, last))

    block = (1, QB, width)
    shape = jax.ShapeDtypeStruct((2, QB, H * HD), jnp.bfloat16)
    return pl.pallas_call(
        functools.partial(attention_kernel, n_chip),
        out_shape=(shape, shape),
        grid_spec=pltpu.PrefetchScalarGridSpec(
            num_scalar_prefetch=4,
            grid=(4, KVH),
            in_specs=[pl.BlockSpec(block, near_at(2)), pl.BlockSpec(block, far_at)]
            + [whole] * len(pieces),
            out_specs=(pl.BlockSpec(block, near_at(1)), pl.BlockSpec(block, far_at)),
        ),
        compiler_params=pltpu.CompilerParams(vmem_limit_bytes=VMEM_LIMIT),
        cost_estimate=pl.CostEstimate(
            flops=4 * 4 * QB * rows * H * HD,
            bytes_accessed=4 * rows * 2 * KVH * HD * 2 + 8 * QB * H * HD * 2,
            transcendentals=4 * QB * rows * H,
        ),
    )(where, order, table, far_table, queries, far_queries, *pieces)


def project_kernel(even_ref, odd_ref, w_ref, o_ref, rows):
    @pl.when((pl.program_id(0) == 0) & (pl.program_id(1) == 0))
    def _():
        for block in range(2):
            rows[2 * block * QB : (2 * block + 1) * QB, :] = even_ref[block]
            rows[(2 * block + 1) * QB : (2 * block + 2) * QB, :] = odd_ref[block]

    o_ref[...] = jnp.dot(
        rows[...], w_ref[0], preferred_element_type=jnp.float32
    ).astype(jnp.bfloat16)


def project(even, odd, weights, tile=512):
    parts, depth, columns = weights.shape
    tiles = columns // tile
    whole = pl.BlockSpec((2, QB, depth), lambda p, t: (0, 0, 0))
    return pl.pallas_call(
        project_kernel,
        out_shape=jax.ShapeDtypeStruct((4 * QB, parts * columns), jnp.bfloat16),
        grid_spec=pl.GridSpec(
            grid=(parts, tiles),
            in_specs=[whole, whole, pl.BlockSpec((1, depth, tile), lambda p, t: (p, 0, t))],
            out_specs=pl.BlockSpec((4 * QB, tile), lambda p, t: (0, p * tiles + t)),
            scratch_shapes=[pltpu.VMEM((4 * QB, depth), jnp.bfloat16)],
        ),
        compiler_params=pltpu.CompilerParams(vmem_limit_bytes=VMEM_LIMIT),
        cost_estimate=pl.CostEstimate(
            flops=2 * 4 * QB * depth * parts * columns,
            bytes_accessed=2 * (depth * parts * columns + 4 * QB * (depth + parts * columns)),
            transcendentals=0,
        ),
    )(even, odd, weights)


def body(n_groups, n_seq, queries, keys, values, block_table, out_weight):
    n_chip = n_seq // 2
    n_outer = n_chip // 2
    order_rows = arrivals(n_outer)

    def index(outer, side, core):
        return (outer * 2 + side) * 2 + core

    spots = [(o, s, c) for o in range(n_outer) for s in range(2) for c in range(2)]
    me = lax.axis_index("seq")
    group = lax.axis_index("groups")
    outer, side, core = me // 4, (me // 2) % 2, me % 2
    where = jnp.stack([outer, side, core]).astype(jnp.int32)
    order = jnp.asarray(
        np.array([[p + d for d in row] for p, row in enumerate(order_rows)], np.int32)
    )

    def swap_core(array):
        return lax.ppermute(
            array, "seq", [(index(o, s, c), index(o, s, 1 - c)) for o, s, c in spots]
        )

    def swap_side(array):
        return lax.ppermute(
            array, "seq", [(index(o, s, c), index(o, 1 - s, c)) for o, s, c in spots]
        )

    def move(array, hop, way):
        return lax.ppermute(
            array,
            "seq",
            [
                (index(o, s, c), index(o + way, s, c))
                for o, s, c in spots
                if 0 <= o + way < n_outer and 0 <= o - (hop - 1) * way < n_outer
            ],
        )

    def line(array):
        got = {0: array}
        for hop in range(1, n_outer):
            for way in (1, -1):
                got[-way * hop] = move(got[-way * (hop - 1)], hop, way)
        return got

    def pick(got, k):
        wanted = [row[k] for row in order_rows]
        result = got[wanted[0]]
        for offset in sorted(set(wanted[1:])):
            mask = functools.reduce(
                jnp.logical_or, [outer == p for p in range(n_outer) if wanted[p] == offset]
            )
            if offset != wanted[0]:
                result = jnp.where(mask, got[offset], result)
        return result

    def after(array, *others):
        return lax.optimization_barrier((array, *others))[0]

    got = line(jnp.concatenate([keys, values], 0))
    near, across = [got[0]], [swap_side(got[0])]
    for k in range(1, n_outer):
        tied = {
            d: after(got[d], near[-1])
            for d in sorted({row[k] for row in order_rows})
        }
        near.append(pick(tied, k))
        across.append(swap_side(after(near[-1], across[-1])))
    pieces = near + across

    query_blocks = queries.reshape(4, QB, H * HD)
    far_table = swap_core(block_table)

    part = out_weight.shape[1] // n_groups
    mine = lax.dynamic_slice_in_dim(out_weight, group * part, part, 1)
    gathered = lax.all_gather(mine, ("groups", "seq"), axis=0, tiled=True)
    gathered = gathered.reshape(n_groups, n_seq * out_weight.shape[0], part)
    far_queries = swap_core(query_blocks.reshape(2, 2, QB, H * HD)[:, 1])

    even, far = attention(
        query_blocks, far_queries, where, order, block_table, far_table, pieces, n_chip
    )
    return project(even, swap_core(far), gathered)


def solution(mesh):
    in_specs = (
        P(("groups", "seq"), None),
        P(("groups", "seq"), None),
        P(("groups", "seq"), None),
        P(("groups", "seq"), None),
        P("seq", None),
    )
    out_specs = P(("groups", "seq"), None)
    run = functools.partial(body, mesh.shape["groups"], mesh.shape["seq"])
    return jax.shard_map(run, mesh=mesh, in_specs=in_specs, out_specs=out_specs, check_vma=False)
```

time: 316 us -> 246 us (0.78); the launches traced: 312 us -> 245 us
  waiting for transfers between devices: 193 us -> 157 us
  starting transfers between devices: 46.6 us -> 19.3 us
  between operations: 0.59 us -> 13.5 us
  other arithmetic: 11 us -> 4.17 us
  Pallas kernels: 41.6 us -> 35.3 us
    ppermute x4 -> x0, waiting for transfers between devices: 74.6 us -> none  [body(): sets.append([lax.ppermute(w, 'groups', turn) for w in own])]
    ppermute x12 -> x6, waiting for transfers between devices: 79.9 us -> 132 us  [move(): lax.ppermute(array, 'seq', [(index(o, s, c), index(o + way, s, c)) for o,...]
    ppermute x9 -> x4, waiting for transfers between devices: 38.6 us -> 21.4 us  [swap_side(): lax.ppermute(array, 'seq', [(index(o, s, c), index(o, 1 - s, c)) for o, s...]
    ppermute x12 -> x6, starting transfers between devices: 27.3 us -> 12.8 us  [move(): lax.ppermute(array, 'seq', [(index(o, s, c), index(o + way, s, c)) for o,...]
    ppermute x9 -> x4, starting transfers between devices: 13 us -> 6.54 us  [swap_side(): lax.ppermute(array, 'seq', [(index(o, s, c), index(o, 1 - s, c)) for o, s...]
    pallas_call x4 -> x2, Pallas kernels: 41.6 us -> 35.3 us  [the longest x1 20.8 us: attention(): pl.pallas_call(functools.partial(attention_kernel, n_chip), out_shape=(sh...]
    ppermute x4 -> x0, starting transfers between devices: 5.06 us -> none  [body(): sets.append([lax.ppermute(w, 'groups', turn) for w in own])]
    ppermute x12 -> x3, waiting for transfers between devices: 0.03 us -> 3.74 us  [swap_core(): lax.ppermute(array, 'seq', [(index(o, s, c), index(o, s, 1 - c)) for o, s...]
  transfers between devices with their start and end apart: 37 -> 14, of which waited for: 12 -> 6; matrix products, arithmetic and copies ran while one was open for 5% -> 4% of each run, Pallas kernels for 10% -> 8%
where the time goes in v3:
time: 246 us; the launch traced here: 245 us
  waiting for transfers between devices  157 us (64%)
  Pallas kernels  35.3 us (14%)
  starting transfers between devices  19.3 us (8%)
  local copies, waits for them, and re-layouts  16 us (7%)
  between operations  13.5 us (5%)
  other arithmetic  4.17 us (2%)
    ppermute x6, waiting for transfers between devices, move(): lax.ppermute(array, 'seq', [(index(o, s, c), index(o + way, s, c)) for o,...  132 us
    ppermute x4, waiting for transfers between devices, swap_side(): lax.ppermute(array, 'seq', [(index(o, s, c), index(o, 1 - s, c)) for o, s...  21.4 us
    pallas_call x1, Pallas kernels, attention(): pl.pallas_call(functools.partial(attention_kernel, n_chip), out_shape=(sh...  20.8 us
    pallas_call x1, Pallas kernels, project(): pl.pallas_call(project_kernel, out_shape=jax.ShapeDtypeStruct((4 * QB, pa...  14.5 us
    ppermute x6, starting transfers between devices, move(): lax.ppermute(array, 'seq', [(index(o, s, c), index(o + way, s, c)) for o,...  12.8 us
    unnamed x25, local copies, waits for them, and re-layouts  11.7 us
    ppermute x4, starting transfers between devices, swap_side(): lax.ppermute(array, 'seq', [(index(o, s, c), index(o, 1 - s, c)) for o, s...  6.54 us
  transfers between devices with their start and end apart: 14, of which 6 were waited for; matrix products, arithmetic and copies ran while one was open for 4% of the time, Pallas kernels for 8%

profile of v3, /device:TPU:0, one launch (start us, length us, event | category | flops | bytes accessed | tf_op | source)
XLA Modules:
  0.0 245.2 jit_solution(16952176397170259811)
XLA Ops:
  6.5 0.0 copy-start
  6.5 0.0 all-gather.2.cloned.1.call-start
  6.5 1.2 copy-done
  7.8 0.9 constant_dynamic-slice_fusion
  8.6 0.0 all-gather.2.cloned.1.call-update
  8.6 1.1 constant_dynamic-update-slice_fusion.1
  9.7 1.1 constant_dynamic-update-slice_fusion.refs_0_
  10.8 0.0 copy-start.2
  10.8 1.3 collective-permute-start.3
  12.1 6.5 %collective-permute-start.2 = (bf16[1024,512]{1,0:T(8,128)(2,1)S(1)}, bf16[1024,512]{1,0:T(8,128)(2,1)}, u32[]{:S(2)}, u32[]{:S(2)}) collective-permute-start(bf16[1024,512]{1,0:T(8,128)(2,1)S(1)} %constant_dynamic-update-slice_fusion.refs_0_), channel_id=1, source_target_pairs={{0,4},{1,5},{2,6},{3,7},{4,8},{5,9},{6,10},{7,11},{8,12},{9,13},{1... | collective-permute-start | bytes 3145736 | tf_op jit(solution)/shard_map/ppermute | solution.py:202
  18.7 2.0 collective-permute-start.8
  20.6 29.6 %collective-permute-done.3 = bf16[1024,512]{1,0:T(8,128)(2,1)} collective-permute-done((bf16[1024,512]{1,0:T(8,128)(2,1)S(1)}, bf16[1024,512]{1,0:T(8,128)(2,1)}, u32[]{:S(2)}, u32[]{:S(2)}) %collective-permute-start.3) | collective-permute-done | bytes 1048608 | tf_op jit(solution)/shard_map/ppermute | solution.py:202
  50.2 1.3 collective-permute-start.5
  51.5 0.0 collective-permute-done.2
  51.5 1.6 collective-permute-start.4
  53.1 1.4 broadcast_select_fusion.refs_1_
  54.5 0.0 collective-permute-done.8.refs_4_
  54.5 1.8 collective-permute-start.9
  56.3 49.7 %collective-permute-done.5 = bf16[1024,512]{1,0:T(8,128)(2,1)} collective-permute-done((bf16[1024,512]{1,0:T(8,128)(2,1)}, bf16[1024,512]{1,0:T(8,128)(2,1)}, u32[]{:S(2)}, u32[]{:S(2)}) %collective-permute-start.5) | collective-permute-done | bytes 1048608 | tf_op jit(solution)/shard_map/ppermute | solution.py:202
  106.0 1.3 collective-permute-start.7
  107.3 0.0 collective-permute-done.4
  107.3 0.0 copy-done.2
  107.3 0.7 collective-permute-start.6
  108.0 1.4 select_select_fusion.1.refs_2_
  109.4 0.0 copy-start.8
  109.4 0.0 copy-start.9
  109.5 0.0 collective-permute-done.9.refs_5_
  109.5 0.0 copy-start.4
  109.5 1.0 copy-done.4
  110.5 1.4 collective-permute-start.10
  111.9 2.3 slice_bitcast_fusion
  114.2 0.0 collective-permute-start.1
  114.2 52.4 %collective-permute-done.7 = bf16[1024,512]{1,0:T(8,128)(2,1)S(1)} collective-permute-done((bf16[1024,512]{1,0:T(8,128)(2,1)}, bf16[1024,512]{1,0:T(8,128)(2,1)S(1)}, u32[]{:S(2)}, u32[]{:S(2)}) %collective-permute-start.7) | collective-permute-done | bytes 1048608 | tf_op jit(solution)/shard_map/ppermute | solution.py:202
  166.6 0.0 collective-permute-done.6
  166.7 1.3 select_select_fusion.refs_3_
  168.0 0.0 collective-permute-done.10.refs_6_
  168.0 0.0 copy-start.6
  168.0 1.0 copy-done.6
  169.0 1.4 collective-permute-start.11
  170.3 0.0 copy-done.8
  170.3 0.0 collective-permute-start
  170.3 0.1 pad_add_fusion.where_ref
  170.4 1.1 collective-permute-done.far_table_ref
  171.5 0.0 collective-permute-done.1.far_q_ref
  171.5 21.4 %collective-permute-done.11.refs_7_ = bf16[1024,512]{1,0:T(8,128)(2,1)} collective-permute-done((bf16[1024,512]{1,0:T(8,128)(2,1)}, bf16[1024,512]{1,0:T(8,128)(2,1)}, u32[]{:S(2)}, u32[]{:S(2)}) %collective-permute-start.11) | collective-permute-done | bytes 1048608 | tf_op jit(solution)/shard_map/ppermute | solution.py:197
  192.9 0.0 copy-done.9
  192.9 0.0 copy-start.1
  192.9 1.6 copy-done.1
  194.5 0.0 copy-start.3
  194.5 1.2 copy-done.3
  195.7 0.0 copy-start.5
  195.7 1.2 copy-done.5
  197.0 0.0 copy-start.7
  197.0 1.2 copy-done.7
  198.2 20.8 %shard_map.64 = (bf16[2,128,2048]{2,1,0:T(8,128)(2,1)S(1)}, bf16[2,128,2048]{2,1,0:T(8,128)(2,1)S(1)}) custom-call(s32[3]{0:T(128)S(1)} %pad_add_fusion.where_ref, s32[4,4]{1,0:T(4,128)S(1)} %copy-done.9, s32[4,8]{1,0:T(4,128)S(1)} %copy-done.8, s32[4,8]{1,0:T(4,128)S(1)} %collective-permute-done.far_table_ref, bf16[4,128,2048]{2,1,0:T(8,128)(2,1)S(1)} %bitcast.11, ...), custom_call_target="tpu_custom_call" | custom-call | flops 4294967296 | bytes 12582912 | tf_op jit(solution)/shard_map/pallas_call | solution.py:121
  219.0 0.0 copy-start.10
  219.0 1.0 copy-done.10
  219.9 0.0 collective-permute-start.12
  219.9 2.7 %collective-permute-done.12.odd_ref = bf16[2,128,2048]{2,1,0:T(8,128)(2,1)S(1)} collective-permute-done((bf16[2,128,2048]{2,1,0:T(8,128)(2,1)S(1)}, bf16[2,128,2048]{2,1,0:T(8,128)(2,1)S(1)}, u32[]{:S(2)}, u32[]{:S(2)}) %collective-permute-start.12) | collective-permute-done | bytes 1048608 | tf_op jit(solution)/shard_map/ppermute | solution.py:192
  222.6 0.0 all-gather.2.cloned.1.call-done
  222.6 0.0 copy-start.11
  222.6 1.2 copy-done.11
  223.8 14.5 %shard_map.65 = bf16[512,4096]{1,0:T(8,128)(2,1)} custom-call(bf16[2,128,2048]{2,1,0:T(8,128)(2,1)S(1)} %copy-done.11, bf16[2,128,2048]{2,1,0:T(8,128)(2,1)S(1)} %collective-permute-done.12.odd_ref, bf16[2,2048,2048]{2,1,0:T(8,128)(2,1)} %bitcast.12), custom_call_target="tpu_custom_call" | custom-call | flops 8589934592 | bytes 23068672 | tf_op jit(solution)/shard_map/pallas_call | solution.py:156
Async XLA Ops:
  6.5 1.2 copy-start
  6.5 216.1 %all-gather.2.cloned.1.call-start = ((), (), s32[]{:S(2)}) async-start(), calls=%async_computation | async-start | bytes 17301504 | tf_op jit(solution)/shard_map/all_gather | solution.py:249
  10.8 96.5 %copy-start.2 = (bf16[1024,512]{1,0:T(8,128)(2,1)}, bf16[1024,512]{1,0:T(8,128)(2,1)S(1)}, u32[]{:S(2)}) copy-start(bf16[1024,512]{1,0:T(8,128)(2,1)S(1)} %constant_dynamic-update-slice_fusion.refs_0_) | copy-start | bytes 3145732
  10.8 39.4 %collective-permute-start.3 = (bf16[1024,512]{1,0:T(8,128)(2,1)S(1)}, bf16[1024,512]{1,0:T(8,128)(2,1)}, u32[]{:S(2)}, u32[]{:S(2)}) collective-permute-start(bf16[1024,512]{1,0:T(8,128)(2,1)S(1)} %constant_dynamic-update-slice_fusion.refs_0_), channel_id=1, source_target_pairs={{4,0},{5,1},{6,2},{7,3},{8,4},{9,5},{10,6},{11,7},{12,8},{13,9},{1... | collective-permute-start | bytes 3145736 | tf_op jit(solution)/shard_map/ppermute | solution.py:202
  12.1 39.4 %collective-permute-start.2 = (bf16[1024,512]{1,0:T(8,128)(2,1)S(1)}, bf16[1024,512]{1,0:T(8,128)(2,1)}, u32[]{:S(2)}, u32[]{:S(2)}) collective-permute-start(bf16[1024,512]{1,0:T(8,128)(2,1)S(1)} %constant_dynamic-update-slice_fusion.refs_0_), channel_id=1, source_target_pairs={{0,4},{1,5},{2,6},{3,7},{4,8},{5,9},{6,10},{7,11},{8,12},{9,13},{1... | collective-permute-start | bytes 3145736 | tf_op jit(solution)/shard_map/ppermute | solution.py:202
  18.7 35.9 %collective-permute-start.8 = (bf16[1024,512]{1,0:T(8,128)(2,1)S(1)}, bf16[1024,512]{1,0:T(8,128)(2,1)}, u32[]{:S(2)}, u32[]{:S(2)}) collective-permute-start(bf16[1024,512]{1,0:T(8,128)(2,1)S(1)} %constant_dynamic-update-slice_fusion.refs_0_), channel_id=1, source_target_pairs={{0,2},{1,3},{2,0},{3,1},{4,6},{5,7},{6,4},{7,5},{8,10},{9,11},{10,... | collective-permute-start | bytes 3145736 | tf_op jit(solution)/shard_map/ppermute | solution.py:197
  50.2 55.8 %collective-permute-start.5 = (bf16[1024,512]{1,0:T(8,128)(2,1)}, bf16[1024,512]{1,0:T(8,128)(2,1)}, u32[]{:S(2)}, u32[]{:S(2)}) collective-permute-start(bf16[1024,512]{1,0:T(8,128)(2,1)} %collective-permute-done.3), channel_id=1, source_target_pairs={{4,0},{5,1},{6,2},{7,3},{8,4},{9,5},{10,6},{11,7},{20,16},{21,17},... | collective-permute-start | bytes 3145736 | tf_op jit(solution)/shard_map/ppermute | solution.py:202
  51.5 55.8 %collective-permute-start.4 = (bf16[1024,512]{1,0:T(8,128)(2,1)}, bf16[1024,512]{1,0:T(8,128)(2,1)}, u32[]{:S(2)}, u32[]{:S(2)}) collective-permute-start(bf16[1024,512]{1,0:T(8,128)(2,1)} %collective-permute-done.2), channel_id=1, source_target_pairs={{4,8},{5,9},{6,10},{7,11},{8,12},{9,13},{10,14},{11,15},{20,24},{2... | collective-permute-start | bytes 3145736 | tf_op jit(solution)/shard_map/ppermute | solution.py:202
  54.5 54.9 %collective-permute-start.9 = (bf16[1024,512]{1,0:T(8,128)(2,1)S(1)}, bf16[1024,512]{1,0:T(8,128)(2,1)S(1)}, u32[]{:S(2)}, u32[]{:S(2)}) collective-permute-start(bf16[1024,512]{1,0:T(8,128)(2,1)S(1)} %broadcast_select_fusion.refs_1_), channel_id=1, source_target_pairs={{0,2},{1,3},{2,0},{3,1},{4,6},{5,7},{6,4},{7,5},{8,10},{9,11},{10,... | collective-permute-start | bytes 3145736 | tf_op jit(solution)/shard_map/ppermute | solution.py:197
  106.0 60.6 %collective-permute-start.7 = (bf16[1024,512]{1,0:T(8,128)(2,1)}, bf16[1024,512]{1,0:T(8,128)(2,1)S(1)}, u32[]{:S(2)}, u32[]{:S(2)}) collective-permute-start(bf16[1024,512]{1,0:T(8,128)(2,1)} %collective-permute-done.5), channel_id=1, source_target_pairs={{4,0},{5,1},{6,2},{7,3},{20,16},{21,17},{22,18},{23,19}} | collective-permute-start | bytes 3145736 | tf_op jit(solution)/shard_map/ppermute | solution.py:202
  107.3 59.3 %collective-permute-start.6 = (bf16[1024,512]{1,0:T(8,128)(2,1)}, bf16[1024,512]{1,0:T(8,128)(2,1)S(1)}, u32[]{:S(2)}, u32[]{:S(2)}) collective-permute-start(bf16[1024,512]{1,0:T(8,128)(2,1)} %collective-permute-done.4), channel_id=1, source_target_pairs={{8,12},{9,13},{10,14},{11,15},{24,28},{25,29},{26,30},{27,31}} | collective-permute-start | bytes 3145736 | tf_op jit(solution)/shard_map/ppermute | solution.py:202
  109.4 60.9 %copy-start.8 = (s32[4,8]{1,0:T(4,128)S(1)}, s32[4,8]{1,0:T(4,128)}, u32[]{:S(2)}) copy-start(s32[4,8]{1,0:T(4,128)} %table_ref.1) | copy-start | bytes 388
  109.4 83.5 %copy-start.9 = (s32[4,4]{1,0:T(4,128)S(1)}, s32[4,4]{1,0:T(4,128)}, u32[]{:S(2)}) copy-start(s32[4,4]{1,0:T(4,128)} %constant.56.clone.order_ref) | copy-start | bytes 196
  109.5 1.0 copy-start.4
  110.5 57.5 %collective-permute-start.10 = (bf16[1024,512]{1,0:T(8,128)(2,1)S(1)}, bf16[1024,512]{1,0:T(8,128)(2,1)S(1)}, u32[]{:S(2)}, u32[]{:S(2)}) collective-permute-start(bf16[1024,512]{1,0:T(8,128)(2,1)S(1)} %select_select_fusion.1.refs_2_), channel_id=1, source_target_pairs={{0,2},{1,3},{2,0},{3,1},{4,6},{5,7},{6,4},{7,5},{8,10},{9,11},{10,... | collective-permute-start | bytes 3145736 | tf_op jit(solution)/shard_map/ppermute | solution.py:197
  114.2 57.3 %collective-permute-start.1 = (bf16[2,128,2048]{2,1,0:T(8,128)(2,1)}, bf16[2,128,2048]{2,1,0:T(8,128)(2,1)}, u32[]{:S(2)}, u32[]{:S(2)}) collective-permute-start(bf16[2,128,2048]{2,1,0:T(8,128)(2,1)} %slice_bitcast_fusion), channel_id=1, source_target_pairs={{0,1},{1,0},{2,3},{3,2},{4,5},{5,4},{6,7},{7,6},{8,9},{9,8},{10,11... | collective-permute-start | bytes 3145736 | tf_op jit(solution)/shard_map/ppermute | solution.py:192
  168.0 1.0 copy-start.6
  169.0 24.0 %collective-permute-start.11 = (bf16[1024,512]{1,0:T(8,128)(2,1)}, bf16[1024,512]{1,0:T(8,128)(2,1)}, u32[]{:S(2)}, u32[]{:S(2)}) collective-permute-start(bf16[1024,512]{1,0:T(8,128)(2,1)} %select_select_fusion.refs_3_), channel_id=1, source_target_pairs={{0,2},{1,3},{2,0},{3,1},{4,6},{5,7},{6,4},{7,5},{8,10},{9,11},{10,... | collective-permute-start | bytes 3145736 | tf_op jit(solution)/shard_map/ppermute | solution.py:197
  170.3 1.2 collective-permute-start
  192.9 1.6 copy-start.1
  194.5 1.2 copy-start.3
  195.7 1.2 copy-start.5
  197.0 1.2 copy-start.7
  219.0 1.0 copy-start.10
  219.9 2.7 %collective-permute-start.12 = (bf16[2,128,2048]{2,1,0:T(8,128)(2,1)S(1)}, bf16[2,128,2048]{2,1,0:T(8,128)(2,1)S(1)}, u32[]{:S(2)}, u32[]{:S(2)}) collective-permute-start(bf16[2,128,2048]{2,1,0:T(8,128)(2,1)S(1)} %get-tuple-element.32), channel_id=1, source_target_pairs={{0,1},{1,0},{2,3},{3,2},{4,5},{5,4},{6,7},{7,6},{8,9},{9,8},{10,11... | collective-permute-start | bytes 3145736 | tf_op jit(solution)/shard_map/ppermute | solution.py:192
  222.6 1.2 copy-start.11
Sparse Core Ops, SparseCore 0:
  10.2 151.8 all-gather.1

commit v4 on v3

v4 whole, which is shorter than its diff:
```python
import functools

import jax
import jax.numpy as jnp
import numpy as np
from jax import lax
from jax.experimental import pallas as pl
from jax.experimental.pallas import tpu as pltpu
from jax.sharding import PartitionSpec as P

H = 16
KVH = 4
HD = 128
QB = 128
ENTRIES = 8
GROUP = H // KVH
SCALE_LOG2 = HD ** (-0.5) * 1.4426950408889634
NT = (((1,), (1,)), ((), ()))
VMEM_LIMIT = 40 * 1024 * 1024


def arrivals(n_outer):
    rows = []
    for place in range(n_outer):
        row = [0]
        for hop in range(1, n_outer):
            if place - hop >= 0:
                row.append(-hop)
            if place + hop < n_outer:
                row.append(hop)
        rows.append(row)
    return rows


def attention_kernel(n_chip, where_ref, order_ref, table_ref, q_ref, *refs):
    n_outer = n_chip // 2
    pieces, o_ref = refs[:-1], refs[-1]
    step = pl.program_id(0)
    head = pl.program_id(1)
    per_entry = n_chip // ENTRIES
    outer, side, core, asking = where_ref[0], where_ref[1], where_ref[2], where_ref[3]
    chip = outer * 2 + asking
    turn = jnp.where(step < 2, 0, core) + 2 * n_chip - chip
    columns = pl.ds(pl.multiple_of(head * HD, HD), HD)

    keys, values, usable = [], [], []
    for at, piece in enumerate(pieces):
        source_side = side if at < n_outer else 1 - side
        source = order_ref[outer, at % n_outer] * 2 + source_side
        ahead = lax.rem(source + turn, n_chip)
        row = table_ref[step, ahead // per_entry] & 3
        keys.append(piece[pl.ds(pl.multiple_of(row * QB, QB), QB), columns])
        values.append(piece[pl.ds(pl.multiple_of((4 + row) * QB, QB), QB), columns])
        usable.append(lax.rem(ahead, per_entry) == 0)
    keys = jnp.concatenate(keys, 0)
    values = jnp.concatenate(values, 0)

    scores = []
    for g in range(GROUP):
        s = lax.dot_general(
            q_ref[0, :, g * HD : (g + 1) * HD], keys, NT, preferred_element_type=jnp.float32
        )
        if per_entry > 1:
            s = jnp.concatenate(
                [
                    jnp.where(ok, s[:, at * QB : (at + 1) * QB], -1e30)
                    for at, ok in enumerate(usable)
                ],
                1,
            )
        scores.append(s)
    rounded, totals = [], []
    for s in scores:
        weights = jnp.exp2((s - jnp.max(s, axis=-1, keepdims=True)) * SCALE_LOG2)
        totals.append(jnp.sum(weights, axis=-1, keepdims=True))
        rounded.append(weights.astype(jnp.bfloat16))
    for g in range(GROUP):
        mixed = jnp.dot(rounded[g], values, preferred_element_type=jnp.float32)
        o_ref[0, :, g * HD : (g + 1) * HD] = (mixed / totals[g]).astype(jnp.bfloat16)


def attention(queries, where, order, table, pieces, n_chip):
    width = GROUP * HD
    blocks, _, columns = queries.shape
    rows = len(pieces) * QB
    whole = pl.BlockSpec(memory_space=pltpu.VMEM)
    tile = pl.BlockSpec((1, QB, width), lambda b, h, *_: (b, 0, h))
    return pl.pallas_call(
        functools.partial(attention_kernel, n_chip),
        out_shape=jax.ShapeDtypeStruct(queries.shape, jnp.bfloat16),
        grid_spec=pltpu.PrefetchScalarGridSpec(
            num_scalar_prefetch=3,
            grid=(blocks, columns // width),
            in_specs=[tile] + [whole] * len(pieces),
            out_specs=tile,
        ),
        compiler_params=pltpu.CompilerParams(vmem_limit_bytes=VMEM_LIMIT),
        cost_estimate=pl.CostEstimate(
            flops=4 * blocks * QB * rows * columns,
            bytes_accessed=2 * blocks * (rows * columns // 2 + 2 * QB * columns),
            transcendentals=blocks * QB * rows * columns // HD,
        ),
    )(where, order, table, queries, *pieces)


def project_kernel(where_ref, near_ref, across_ref, far_ref, far_across_ref, w_ref, o_ref, rows):
    side = where_ref[1]

    @pl.when((pl.program_id(0) == 0) & (pl.program_id(1) == 0))
    def _():
        width = near_ref.shape[-1]
        here = pl.ds(pl.multiple_of(side * width, width), width)
        there = pl.ds(pl.multiple_of((1 - side) * width, width), width)
        for block in range(2):
            even = slice(2 * block * QB, (2 * block + 1) * QB)
            odd = slice((2 * block + 1) * QB, (2 * block + 2) * QB)
            rows[even, here] = near_ref[block]
            rows[even, there] = across_ref[block]
            rows[odd, here] = far_ref[block]
            rows[odd, there] = far_across_ref[block]

    o_ref[...] = jnp.dot(
        rows[...], w_ref[0], preferred_element_type=jnp.float32
    ).astype(jnp.bfloat16)


def project(where, near, across, far, far_across, weights, tile=512):
    parts, depth, columns = weights.shape
    tiles = columns // tile
    half = pl.BlockSpec((2, QB, depth // 2), lambda p, t, *_: (0, 0, 0))
    return pl.pallas_call(
        project_kernel,
        out_shape=jax.ShapeDtypeStruct((4 * QB, parts * columns), jnp.bfloat16),
        grid_spec=pltpu.PrefetchScalarGridSpec(
            num_scalar_prefetch=1,
            grid=(parts, tiles),
            in_specs=[half] * 4 + [pl.BlockSpec((1, depth, tile), lambda p, t, *_: (p, 0, t))],
            out_specs=pl.BlockSpec((4 * QB, tile), lambda p, t, *_: (0, p * tiles + t)),
            scratch_shapes=[pltpu.VMEM((4 * QB, depth), jnp.bfloat16)],
        ),
        compiler_params=pltpu.CompilerParams(vmem_limit_bytes=VMEM_LIMIT),
        cost_estimate=pl.CostEstimate(
            flops=2 * 4 * QB * depth * parts * columns,
            bytes_accessed=2 * (depth * parts * columns + 4 * QB * (depth + parts * columns)),
            transcendentals=0,
        ),
    )(where, near, across, far, far_across, weights)


def body(n_groups, n_seq, queries, keys, values, block_table, out_weight):
    n_chip = n_seq // 2
    n_outer = n_chip // 2
    order_rows = arrivals(n_outer)

    def index(outer, side, core):
        return (outer * 2 + side) * 2 + core

    spots = [(o, s, c) for o in range(n_outer) for s in range(2) for c in range(2)]
    me = lax.axis_index("seq")
    group = lax.axis_index("groups")
    outer, side, core = me // 4, (me // 2) % 2, me % 2
    where = jnp.stack([outer, side, core, side]).astype(jnp.int32)
    where_across = jnp.stack([outer, side, core, 1 - side]).astype(jnp.int32)
    order = jnp.asarray(
        np.array([[p + d for d in row] for p, row in enumerate(order_rows)], np.int32)
    )

    def swap_core(array):
        return lax.ppermute(
            array, "seq", [(index(o, s, c), index(o, s, 1 - c)) for o, s, c in spots]
        )

    def swap_side(array):
        return lax.ppermute(
            array, "seq", [(index(o, s, c), index(o, 1 - s, c)) for o, s, c in spots]
        )

    def move(array, hop, way):
        return lax.ppermute(
            array,
            "seq",
            [
                (index(o, s, c), index(o + way, s, c))
                for o, s, c in spots
                if 0 <= o + way < n_outer and 0 <= o - (hop - 1) * way < n_outer
            ],
        )

    def line(array):
        got = {0: array}
        for hop in range(1, n_outer):
            for way in (1, -1):
                got[-way * hop] = move(got[-way * (hop - 1)], hop, way)
        return got

    def pick(got, k):
        wanted = [row[k] for row in order_rows]
        result = got[wanted[0]]
        for offset in sorted(set(wanted[1:])):
            mask = functools.reduce(
                jnp.logical_or, [outer == p for p in range(n_outer) if wanted[p] == offset]
            )
            if offset != wanted[0]:
                result = jnp.where(mask, got[offset], result)
        return result

    def after(array, *others):
        return lax.optimization_barrier((array, *others))[0]

    def half_of(array, which):
        width = array.shape[-1] // 2
        return lax.dynamic_slice_in_dim(array, which * width, width, array.ndim - 1)

    mine = jnp.concatenate([half_of(keys, side), half_of(values, side)], 0)
    theirs = jnp.concatenate([half_of(keys, 1 - side), half_of(values, 1 - side)], 0)
    theirs = swap_side(theirs)
    pieces = []
    for chain in (mine, theirs):
        got = line(chain)
        near = [got[0]]
        for k in range(1, n_outer):
            tied = {d: after(got[d], near[-1]) for d in sorted({row[k] for row in order_rows})}
            near.append(pick(tied, k))
        pieces += near

    part = out_weight.shape[1] // n_groups
    columns = lax.dynamic_slice_in_dim(out_weight, group * part, part, 1)
    gathered = lax.all_gather(columns, ("groups", "seq"), axis=0, tiled=True)
    gathered = gathered.reshape(n_groups, n_seq * out_weight.shape[0], part)

    query_blocks = queries.reshape(2, 2, QB, H * HD)
    far_queries = swap_core(query_blocks[:, 1])
    far_table = swap_core(block_table)
    table = jnp.concatenate([block_table[0::2], far_table[1::2]], 0)
    near_queries = query_blocks[:, 0]

    def my_blocks(which):
        return jnp.concatenate([half_of(near_queries, which), half_of(far_queries, which)], 0)

    across_queries = swap_side(my_blocks(1 - side))
    across_table = swap_side(table)

    across = attention(across_queries, where_across, order, across_table, pieces, n_chip)
    across = swap_side(across)
    near = attention(my_blocks(side), where, order, table, pieces, n_chip)
    far = swap_core(near[2:])
    far_across = swap_core(across[2:])
    return project(where, near, across, far, far_across, gathered)


def solution(mesh):
    in_specs = (
        P(("groups", "seq"), None),
        P(("groups", "seq"), None),
        P(("groups", "seq"), None),
        P(("groups", "seq"), None),
        P("seq", None),
    )
    out_specs = P(("groups", "seq"), None)
    run = functools.partial(body, mesh.shape["groups"], mesh.shape["seq"])
    return jax.shard_map(run, mesh=mesh, in_specs=in_specs, out_specs=out_specs, check_vma=False)
```

time: 246 us -> 227 us (0.923); the launches traced: 245 us -> 223 us
  waiting for transfers between devices: 157 us -> 135 us
  starting transfers between devices: 19.3 us -> 28.3 us
  local copies, waits for them, and re-layouts: 16 us -> 8.66 us
    ppermute x6 -> x12, waiting for transfers between devices: 132 us -> 110 us  [move(): lax.ppermute(array, 'seq', [(index(o, s, c), index(o + way, s, c)) for o,...]
    unnamed x25 -> x16, local copies, waits for them, and re-layouts: 11.7 us -> 2.48 us
    ppermute x6 -> x12, starting transfers between devices: 12.8 us -> 21.4 us  [move(): lax.ppermute(array, 'seq', [(index(o, s, c), index(o + way, s, c)) for o,...]
    dynamic_slice x1 -> x4, local copies, waits for them, and re-layouts: 0.85 us -> 4.9 us  [the longest x3 4.07 us: half_of(): return lax.dynamic_slice_in_dim(array, which * width, width, array.ndim - 1)]
    pallas_call x1 -> x2, Pallas kernels: 20.8 us -> 18.4 us  [attention(): pl.pallas_call(functools.partial(attention_kernel, n_chip), out_shape=jax...]
  transfers between devices with their start and end apart: 14 -> 21, of which waited for: 6 -> 9; matrix products, arithmetic and copies ran while one was open for 4% -> 4% of each run, Pallas kernels for 8% -> 8%
where the time goes in v4:
time: 227 us; the launch traced here: 223 us
  waiting for transfers between devices  135 us (59%)
  Pallas kernels  33.5 us (15%)
  starting transfers between devices  28.3 us (12%)
  between operations  13.7 us (6%)
  local copies, waits for them, and re-layouts  8.66 us (4%)
  other arithmetic  3.99 us (2%)
    ppermute x12, waiting for transfers between devices, move(): lax.ppermute(array, 'seq', [(index(o, s, c), index(o + way, s, c)) for o,...  110 us
    ppermute x4, waiting for transfers between devices, swap_side(): lax.ppermute(array, 'seq', [(index(o, s, c), index(o, 1 - s, c)) for o, s...  22.7 us
    ppermute x12, starting transfers between devices, move(): lax.ppermute(array, 'seq', [(index(o, s, c), index(o + way, s, c)) for o,...  21.4 us
    pallas_call x2, Pallas kernels, attention(): pl.pallas_call(functools.partial(attention_kernel, n_chip), out_shape=jax...  18.4 us
    pallas_call x1, Pallas kernels, project(): pl.pallas_call(project_kernel, out_shape=jax.ShapeDtypeStruct((4 * QB, pa...  15.1 us
    ppermute x4, starting transfers between devices, swap_side(): lax.ppermute(array, 'seq', [(index(o, s, c), index(o, 1 - s, c)) for o, s...  6.23 us
  transfers between devices with their start and end apart: 21, of which 9 were waited for; matrix products, arithmetic and copies ran while one was open for 4% of the time, Pallas kernels for 8%

profile of v4, /device:TPU:0, one launch (start us, length us, event | category | flops | bytes accessed | tf_op | source)
XLA Modules:
  0.0 223.0 jit_solution(16312794865579750089)
XLA Ops:
  6.5 1.2 copy-done
  7.8 0.8 constant_dynamic-slice_fusion
  8.6 0.0 all-gather.2.cloned.1.call-update
  8.7 0.0 copy-start.4
  8.7 0.0 copy-start.7
  8.7 1.4 constant_dynamic-slice_fusion.2
  10.1 5.8 %collective-permute-start.2 = (bf16[1024,256]{1,0:T(8,128)(2,1)S(1)}, bf16[1024,256]{1,0:T(8,128)(2,1)}, u32[]{:S(2)}, u32[]{:S(2)}) collective-permute-start(bf16[1024,256]{1,0:T(8,128)(2,1)S(1)} %pad_maximum_fusion.2.refs_0_), channel_id=1, source_target_pairs={{0,4},{1,5},{2,6},{3,7},{4,8},{5,9},{6,10},{7,11},{8,12},{9,13},{1... | collective-permute-start | bytes 1572872 | tf_op jit(solution)/shard_map/ppermute | solution.py:179
  15.9 1.3 collective-permute-start.3
  17.2 0.8 pad_maximum_fusion.3
  18.0 1.5 collective-permute-start.8
  19.5 1.2 fusion
  20.7 0.0 collective-permute-start.1
  20.7 0.5 collective-permute-start
  21.2 14.2 %collective-permute-done.8.refs_4_ = bf16[1024,256]{1,0:T(8,128)(2,1)S(1)} collective-permute-done((bf16[1024,256]{1,0:T(8,128)(2,1)}, bf16[1024,256]{1,0:T(8,128)(2,1)S(1)}, u32[]{:S(2)}, u32[]{:S(2)}) %collective-permute-start.8) | collective-permute-done | bytes 524320 | tf_op jit(solution)/shard_map/ppermute | solution.py:174
  35.4 5.1 %collective-permute-start.9 = (bf16[1024,256]{1,0:T(8,128)(2,1)S(1)}, bf16[1024,256]{1,0:T(8,128)(2,1)}, u32[]{:S(2)}, u32[]{:S(2)}) collective-permute-start(bf16[1024,256]{1,0:T(8,128)(2,1)S(1)} %collective-permute-done.8.refs_4_), channel_id=1, source_target_pairs={{0,4},{1,5},{2,6},{3,7},{4,8},{5,9},{6,10},{7,11},{8,12},{9,13},{1... | collective-permute-start | bytes 1572872 | tf_op jit(solution)/shard_map/ppermute | solution.py:179
  40.4 0.0 collective-permute-done
  40.4 1.3 collective-permute-start.10
  41.7 0.1 pad_add_fusion.3
  41.8 1.1 dynamic-slice_bitcast_fusion
  42.9 0.0 collective-permute-done.2
  42.9 0.0 collective-permute-done.3
  42.9 1.4 collective-permute-start.5
  44.4 0.7 collective-permute-start.4
  45.1 1.1 broadcast_select_fusion.1.refs_1_
  46.2 6.4 %collective-permute-done.9 = bf16[1024,256]{1,0:T(8,128)(2,1)} collective-permute-done((bf16[1024,256]{1,0:T(8,128)(2,1)S(1)}, bf16[1024,256]{1,0:T(8,128)(2,1)}, u32[]{:S(2)}, u32[]{:S(2)}) %collective-permute-start.9) | collective-permute-done | bytes 524320 | tf_op jit(solution)/shard_map/ppermute | solution.py:179
  52.6 16.6 %collective-permute-done.10 = bf16[1024,256]{1,0:T(8,128)(2,1)} collective-permute-done((bf16[1024,256]{1,0:T(8,128)(2,1)S(1)}, bf16[1024,256]{1,0:T(8,128)(2,1)}, u32[]{:S(2)}, u32[]{:S(2)}) %collective-permute-start.10) | collective-permute-done | bytes 524320 | tf_op jit(solution)/shard_map/ppermute | solution.py:179
  69.2 1.1 broadcast_select_fusion.refs_5_
  70.3 17.7 %collective-permute-done.5 = bf16[1024,256]{1,0:T(8,128)(2,1)S(1)} collective-permute-done((bf16[1024,256]{1,0:T(8,128)(2,1)}, bf16[1024,256]{1,0:T(8,128)(2,1)S(1)}, u32[]{:S(2)}, u32[]{:S(2)}) %collective-permute-start.5) | collective-permute-done | bytes 524320 | tf_op jit(solution)/shard_map/ppermute | solution.py:179
  88.1 0.0 collective-permute-done.4
  88.1 1.3 collective-permute-start.12
  89.3 0.7 collective-permute-start.11
  90.0 0.0 collective-permute-done.1
  90.1 1.6 constant_dynamic-slice_fusion.1
  91.7 0.1 pad_maximum_fusion.1
  91.8 1.6 collective-permute-start.16
  93.3 1.3 collective-permute-start.7
  94.6 0.7 collective-permute-start.6
  95.3 0.1 select_select_fusion.3.refs_2_
  95.5 33.4 %collective-permute-done.12 = bf16[1024,256]{1,0:T(8,128)(2,1)S(1)} collective-permute-done((bf16[1024,256]{1,0:T(8,128)(2,1)}, bf16[1024,256]{1,0:T(8,128)(2,1)S(1)}, u32[]{:S(2)}, u32[]{:S(2)}) %collective-permute-start.12) | collective-permute-done | bytes 524320 | tf_op jit(solution)/shard_map/ppermute | solution.py:179
  128.9 0.0 collective-permute-done.11
  128.9 1.3 collective-permute-start.14
  130.2 0.7 collective-permute-start.13
  130.9 0.1 select_select_fusion.1.refs_6_
  131.0 14.1 %collective-permute-done.7 = bf16[1024,256]{1,0:T(8,128)(2,1)S(1)} collective-permute-done((bf16[1024,256]{1,0:T(8,128)(2,1)S(1)}, bf16[1024,256]{1,0:T(8,128)(2,1)S(1)}, u32[]{:S(2)}, u32[]{:S(2)}) %collective-permute-start.7) | collective-permute-done | bytes 524320 | tf_op jit(solution)/shard_map/ppermute | solution.py:179
  145.1 1.5 collective-permute-start.15
  146.6 0.0 collective-permute-done.6
  146.6 0.2 select_select_fusion.2.refs_3_
  146.8 21.9 %collective-permute-done.14 = bf16[1024,256]{1,0:T(8,128)(2,1)S(1)} collective-permute-done((bf16[1024,256]{1,0:T(8,128)(2,1)S(1)}, bf16[1024,256]{1,0:T(8,128)(2,1)S(1)}, u32[]{:S(2)}, u32[]{:S(2)}) %collective-permute-start.14) | collective-permute-done | bytes 524320 | tf_op jit(solution)/shard_map/ppermute | solution.py:179
  168.7 0.0 collective-permute-done.13
  168.7 0.1 select_select_fusion.refs_7_
  168.9 0.0 collective-permute-done.16.q_ref
  168.9 9.2 %shard_map.65 = bf16[4,128,1024]{2,1,0:T(8,128)(2,1)S(1)} custom-call(s32[4]{0:T(128)S(1)} %get-tuple-element.41.where_ref, s32[4,4]{1,0:T(4,128)S(1)} %copy-done.3, s32[4,8]{1,0:T(4,128)S(1)} %collective-permute-done.15.table_ref, bf16[4,128,1024]{2,1,0:T(8,128)(2,1)S(1)} %collective-permute-done.16.q_ref, bf16[1024,256]{1,0:T(8,128)(2,1)S(1)} %pad_maximum_fusion.2.refs_0_, ...), custom_call_target="tpu_custom_call" | custom-call | flops 2147483648 | bytes 6291456 | tf_op jit(solution)/shard_map/pallas_call | solution.py:88
  178.1 1.6 collective-permute-start.17
  179.7 0.1 pad_add_fusion.1.where_ref
  179.8 0.1 pad_maximum_fusion.q_ref
  179.9 9.2 %shard_map.64.near_ref = bf16[4,128,1024]{2,1,0:T(8,128)(2,1)S(1)} custom-call(s32[4]{0:T(128)S(1)} %pad_add_fusion.1.where_ref, s32[4,4]{1,0:T(4,128)S(1)} %copy-done.3, s32[4,8]{1,0:T(4,128)S(1)} %pad_add_fusion.table_ref, bf16[4,128,1024]{2,1,0:T(8,128)(2,1)S(1)} %pad_maximum_fusion.q_ref, bf16[1024,256]{1,0:T(8,128)(2,1)S(1)} %pad_maximum_fusion.2.refs_0_, ...), custom_call_target="tpu_custom_call" | custom-call | flops 2147483648 | bytes 6291456 | tf_op jit(solution)/shard_map/pallas_call | solution.py:88
  189.1 0.0 copy-start.1
  189.2 0.1 collective-permute-start.18
  189.3 8.6 %collective-permute-done.17.across_ref = bf16[4,128,1024]{2,1,0:T(8,128)(2,1)S(1)} collective-permute-done((bf16[4,128,1024]{2,1,0:T(8,128)(2,1)S(1)}, bf16[4,128,1024]{2,1,0:T(8,128)(2,1)S(1)}, u32[]{:S(2)}, u32[]{:S(2)}) %collective-permute-start.17) | collective-permute-done | bytes 1048608 | tf_op jit(solution)/shard_map/ppermute | solution.py:174
  197.9 0.1 collective-permute-start.19
  197.9 0.0 collective-permute-done.18.far_ref
  197.9 1.9 collective-permute-done.19.far_across_ref
  199.8 1.2 copy-done.2
  201.1 15.1 %shard_map.66 = bf16[512,4096]{1,0:T(8,128)(2,1)} custom-call(s32[4]{0:T(128)S(1)} %pad_add_fusion.1.where_ref, bf16[4,128,1024]{2,1,0:T(8,128)(2,1)S(1)} %copy-done.2, bf16[4,128,1024]{2,1,0:T(8,128)(2,1)S(1)} %collective-permute-done.17.across_ref, bf16[2,128,1024]{2,1,0:T(8,128)(2,1)S(1)} %collective-permute-done.18.far_ref, ...), custom_call_target="tpu_custom_call" | custom-call | flops 8589934592 | bytes 23068672 | tf_op jit(solution)/shard_map/pallas_call | solution.py:131
  (20 shorter events, 0.2 us)
Async XLA Ops:
  6.5 1.2 copy-start
  6.5 193.3 %all-gather.2.cloned.1.call-start = ((), (), s32[]{:S(2)}) async-start(), calls=%async_computation | async-start | bytes 17301504 | tf_op jit(solution)/shard_map/all_gather | solution.py:228
  8.7 10.9 %copy-start.4 = (bf16[512,2048]{1,0:T(8,128)(2,1)S(1)}, bf16[512,2048]{1,0:T(8,128)(2,1)}, u32[]{:S(2)}) copy-start(bf16[512,2048]{1,0:T(8,128)(2,1)} %param.6) | copy-start | bytes 6291460
  8.7 12.0 %copy-start.7 = (s32[4,8]{1,0:T(4,128)S(1)}, s32[4,8]{1,0:T(4,128)}, u32[]{:S(2)}) copy-start(s32[4,8]{1,0:T(4,128)} %param.9) | copy-start | bytes 388
  10.1 32.8 %collective-permute-start.2 = (bf16[1024,256]{1,0:T(8,128)(2,1)S(1)}, bf16[1024,256]{1,0:T(8,128)(2,1)}, u32[]{:S(2)}, u32[]{:S(2)}) collective-permute-start(bf16[1024,256]{1,0:T(8,128)(2,1)S(1)} %pad_maximum_fusion.2.refs_0_), channel_id=1, source_target_pairs={{0,4},{1,5},{2,6},{3,7},{4,8},{5,9},{6,10},{7,11},{8,12},{9,13},{1... | collective-permute-start | bytes 1572872 | tf_op jit(solution)/shard_map/ppermute | solution.py:179
  15.9 27.0 %collective-permute-start.3 = (bf16[1024,256]{1,0:T(8,128)(2,1)S(1)}, bf16[1024,256]{1,0:T(8,128)(2,1)}, u32[]{:S(2)}, u32[]{:S(2)}) collective-permute-start(bf16[1024,256]{1,0:T(8,128)(2,1)S(1)} %pad_maximum_fusion.2.refs_0_), channel_id=1, source_target_pairs={{4,0},{5,1},{6,2},{7,3},{8,4},{9,5},{10,6},{11,7},{12,8},{13,9},{1... | collective-permute-start | bytes 1572872 | tf_op jit(solution)/shard_map/ppermute | solution.py:179
  18.0 17.3 %collective-permute-start.8 = (bf16[1024,256]{1,0:T(8,128)(2,1)}, bf16[1024,256]{1,0:T(8,128)(2,1)S(1)}, u32[]{:S(2)}, u32[]{:S(2)}) collective-permute-start(bf16[1024,256]{1,0:T(8,128)(2,1)} %pad_maximum_fusion.3), channel_id=1, source_target_pairs={{0,2},{1,3},{2,0},{3,1},{4,6},{5,7},{6,4},{7,5},{8,10},{9,11},{10,... | collective-permute-start | bytes 1572872 | tf_op jit(solution)/shard_map/ppermute | solution.py:174
  20.7 69.4 %collective-permute-start.1 = (bf16[2,128,2048]{2,1,0:T(8,128)(2,1)}, bf16[2,128,2048]{2,1,0:T(8,128)(2,1)}, u32[]{:S(2)}, u32[]{:S(2)}) collective-permute-start(bf16[2,128,2048]{2,1,0:T(8,128)(2,1)} %get-tuple-element.44), channel_id=1, source_target_pairs={{0,1},{1,0},{2,3},{3,2},{4,5},{5,4},{6,7},{7,6},{8,9},{9,8},{10,11... | collective-permute-start | bytes 3145736 | tf_op jit(solution)/shard_map/ppermute | solution.py:169
  20.7 19.7 %collective-permute-start = (s32[4,8]{1,0:T(4,128)S(1)}, s32[4,8]{1,0:T(4,128)S(1)}, u32[]{:S(2)}, u32[]{:S(2)}) collective-permute-start(s32[4,8]{1,0:T(4,128)S(1)} %copy-done.7), channel_id=1, source_target_pairs={{0,1},{1,0},{2,3},{3,2},{4,5},{5,4},{6,7},{7,6},{8,9},{9,8},{10,11... | collective-permute-start | bytes 392 | tf_op jit(solution)/shard_map/ppermute | solution.py:169
  35.4 17.3 %collective-permute-start.9 = (bf16[1024,256]{1,0:T(8,128)(2,1)S(1)}, bf16[1024,256]{1,0:T(8,128)(2,1)}, u32[]{:S(2)}, u32[]{:S(2)}) collective-permute-start(bf16[1024,256]{1,0:T(8,128)(2,1)S(1)} %collective-permute-done.8.refs_4_), channel_id=1, source_target_pairs={{0,4},{1,5},{2,6},{3,7},{4,8},{5,9},{6,10},{7,11},{8,12},{9,13},{1... | collective-permute-start | bytes 1572872 | tf_op jit(solution)/shard_map/ppermute | solution.py:179
  40.4 28.8 %collective-permute-start.10 = (bf16[1024,256]{1,0:T(8,128)(2,1)S(1)}, bf16[1024,256]{1,0:T(8,128)(2,1)}, u32[]{:S(2)}, u32[]{:S(2)}) collective-permute-start(bf16[1024,256]{1,0:T(8,128)(2,1)S(1)} %collective-permute-done.8.refs_4_), channel_id=1, source_target_pairs={{4,0},{5,1},{6,2},{7,3},{8,4},{9,5},{10,6},{11,7},{12,8},{13,9},{1... | collective-permute-start | bytes 1572872 | tf_op jit(solution)/shard_map/ppermute | solution.py:179
  42.9 48.8 %copy-start.6 = (bf16[2,128,1024]{2,1,0:T(8,128)(2,1)S(1)}, bf16[2,128,1024]{2,1,0:T(8,128)(2,1)}, u32[]{:S(2)}) copy-start(bf16[2,128,1024]{2,1,0:T(8,128)(2,1)} %get-tuple-element.45) | copy-start | bytes 1572868
  42.9 45.1 %collective-permute-start.5 = (bf16[1024,256]{1,0:T(8,128)(2,1)}, bf16[1024,256]{1,0:T(8,128)(2,1)S(1)}, u32[]{:S(2)}, u32[]{:S(2)}) collective-permute-start(bf16[1024,256]{1,0:T(8,128)(2,1)} %collective-permute-done.3), channel_id=1, source_target_pairs={{4,0},{5,1},{6,2},{7,3},{8,4},{9,5},{10,6},{11,7},{20,16},{21,17},... | collective-permute-start | bytes 1572872 | tf_op jit(solution)/shard_map/ppermute | solution.py:179
  44.4 43.7 %collective-permute-start.4 = (bf16[1024,256]{1,0:T(8,128)(2,1)}, bf16[1024,256]{1,0:T(8,128)(2,1)S(1)}, u32[]{:S(2)}, u32[]{:S(2)}) collective-permute-start(bf16[1024,256]{1,0:T(8,128)(2,1)} %collective-permute-done.2), channel_id=1, source_target_pairs={{4,8},{5,9},{6,10},{7,11},{8,12},{9,13},{10,14},{11,15},{20,24},{2... | collective-permute-start | bytes 1572872 | tf_op jit(solution)/shard_map/ppermute | solution.py:179
  88.1 40.8 %collective-permute-start.12 = (bf16[1024,256]{1,0:T(8,128)(2,1)}, bf16[1024,256]{1,0:T(8,128)(2,1)S(1)}, u32[]{:S(2)}, u32[]{:S(2)}) collective-permute-start(bf16[1024,256]{1,0:T(8,128)(2,1)} %collective-permute-done.10), channel_id=1, source_target_pairs={{4,0},{5,1},{6,2},{7,3},{8,4},{9,5},{10,6},{11,7},{20,16},{21,17},... | collective-permute-start | bytes 1572872 | tf_op jit(solution)/shard_map/ppermute | solution.py:179
  89.3 39.5 %collective-permute-start.11 = (bf16[1024,256]{1,0:T(8,128)(2,1)}, bf16[1024,256]{1,0:T(8,128)(2,1)S(1)}, u32[]{:S(2)}, u32[]{:S(2)}) collective-permute-start(bf16[1024,256]{1,0:T(8,128)(2,1)} %collective-permute-done.9), channel_id=1, source_target_pairs={{4,8},{5,9},{6,10},{7,11},{8,12},{9,13},{10,14},{11,15},{20,24},{2... | collective-permute-start | bytes 1572872 | tf_op jit(solution)/shard_map/ppermute | solution.py:179
  91.8 77.1 %collective-permute-start.16 = (bf16[4,128,1024]{2,1,0:T(8,128)(2,1)S(1)}, bf16[4,128,1024]{2,1,0:T(8,128)(2,1)S(1)}, u32[]{:S(2)}, u32[]{:S(2)}) collective-permute-start(bf16[4,128,1024]{2,1,0:T(8,128)(2,1)S(1)} %pad_maximum_fusion.1), channel_id=1, source_target_pairs={{0,2},{1,3},{2,0},{3,1},{4,6},{5,7},{6,4},{7,5},{8,10},{9,11},{10,... | collective-permute-start | bytes 3145736 | tf_op jit(solution)/shard_map/ppermute | solution.py:174
  93.3 51.8 %collective-permute-start.7 = (bf16[1024,256]{1,0:T(8,128)(2,1)S(1)}, bf16[1024,256]{1,0:T(8,128)(2,1)S(1)}, u32[]{:S(2)}, u32[]{:S(2)}) collective-permute-start(bf16[1024,256]{1,0:T(8,128)(2,1)S(1)} %collective-permute-done.5), channel_id=1, source_target_pairs={{4,0},{5,1},{6,2},{7,3},{20,16},{21,17},{22,18},{23,19}} | collective-permute-start | bytes 1572872 | tf_op jit(solution)/shard_map/ppermute | solution.py:179
  94.6 52.0 %collective-permute-start.6 = (bf16[1024,256]{1,0:T(8,128)(2,1)S(1)}, bf16[1024,256]{1,0:T(8,128)(2,1)S(1)}, u32[]{:S(2)}, u32[]{:S(2)}) collective-permute-start(bf16[1024,256]{1,0:T(8,128)(2,1)S(1)} %collective-permute-done.4), channel_id=1, source_target_pairs={{8,12},{9,13},{10,14},{11,15},{24,28},{25,29},{26,30},{27,31}} | collective-permute-start | bytes 1572872 | tf_op jit(solution)/shard_map/ppermute | solution.py:179
  95.5 73.4 %copy-start.3 = (s32[4,4]{1,0:T(4,128)S(1)}, s32[4,4]{1,0:T(4,128)}, u32[]{:S(2)}) copy-start(s32[4,4]{1,0:T(4,128)} %constant.64.clone.order_ref) | copy-start | bytes 196
  128.9 39.9 %collective-permute-start.14 = (bf16[1024,256]{1,0:T(8,128)(2,1)S(1)}, bf16[1024,256]{1,0:T(8,128)(2,1)S(1)}, u32[]{:S(2)}, u32[]{:S(2)}) collective-permute-start(bf16[1024,256]{1,0:T(8,128)(2,1)S(1)} %collective-permute-done.12), channel_id=1, source_target_pairs={{4,0},{5,1},{6,2},{7,3},{20,16},{21,17},{22,18},{23,19}} | collective-permute-start | bytes 1572872 | tf_op jit(solution)/shard_map/ppermute | solution.py:179
  130.2 38.6 %collective-permute-start.13 = (bf16[1024,256]{1,0:T(8,128)(2,1)S(1)}, bf16[1024,256]{1,0:T(8,128)(2,1)S(1)}, u32[]{:S(2)}, u32[]{:S(2)}) collective-permute-start(bf16[1024,256]{1,0:T(8,128)(2,1)S(1)} %collective-permute-done.11), channel_id=1, source_target_pairs={{8,12},{9,13},{10,14},{11,15},{24,28},{25,29},{26,30},{27,31}} | collective-permute-start | bytes 1572872 | tf_op jit(solution)/shard_map/ppermute | solution.py:179
  145.1 23.7 %collective-permute-start.15 = (s32[4,8]{1,0:T(4,128)S(1)}, s32[4,8]{1,0:T(4,128)S(1)}, u32[]{:S(2)}, u32[]{:S(2)}) collective-permute-start(s32[4,8]{1,0:T(4,128)S(1)} %pad_add_fusion.table_ref), channel_id=1, source_target_pairs={{0,2},{1,3},{2,0},{3,1},{4,6},{5,7},{6,4},{7,5},{8,10},{9,11},{10,... | collective-permute-start | bytes 392 | tf_op jit(solution)/shard_map/ppermute | solution.py:174
  168.8 11.0 %copy-start.5 = (bf16[2,128,1024]{2,1,0:T(8,128)(2,1)S(1)}, bf16[2,128,1024]{2,1,0:T(8,128)(2,1)}, u32[]{:S(2)}) copy-start(bf16[2,128,1024]{2,1,0:T(8,128)(2,1)} %get-tuple-element.46) | copy-start | bytes 1572868
  178.1 19.7 %collective-permute-start.17 = (bf16[4,128,1024]{2,1,0:T(8,128)(2,1)S(1)}, bf16[4,128,1024]{2,1,0:T(8,128)(2,1)S(1)}, u32[]{:S(2)}, u32[]{:S(2)}) collective-permute-start(bf16[4,128,1024]{2,1,0:T(8,128)(2,1)S(1)} %shard_map.65), channel_id=1, source_target_pairs={{0,2},{1,3},{2,0},{3,1},{4,6},{5,7},{6,4},{7,5},{8,10},{9,11},{10,... | collective-permute-start | bytes 3145736 | tf_op jit(solution)/shard_map/ppermute | solution.py:174
  189.1 8.7 %copy-start.1 = (bf16[4,128,1024]{2,1,0:T(8,128)(2,1)}, bf16[4,128,1024]{2,1,0:T(8,128)(2,1)S(1)}, u32[]{:S(2)}) copy-start(bf16[4,128,1024]{2,1,0:T(8,128)(2,1)S(1)} %shard_map.64.near_ref) | copy-start | bytes 3145732
  189.2 8.8 %collective-permute-start.18 = (bf16[2,128,1024]{2,1,0:T(8,128)(2,1)S(1)}, bf16[2,128,1024]{2,1,0:T(8,128)(2,1)S(1)}, u32[]{:S(2)}, u32[]{:S(2)}) collective-permute-start(bf16[2,128,1024]{2,1,0:T(8,128)(2,1)S(1)} %slice.26), channel_id=1, source_target_pairs={{0,1},{1,0},{2,3},{3,2},{4,5},{5,4},{6,7},{7,6},{8,9},{9,8},{10,11... | collective-permute-start | bytes 1572872 | tf_op jit(solution)/shard_map/ppermute | solution.py:169
  197.9 2.0 collective-permute-start.19
  199.8 1.2 copy-start.2
Sparse Core Ops, SparseCore 0:
  10.2 160.5 all-gather.1

commit v5 on v4

--- a/solution.py
+++ b/solution.py
@@ -6,6 +6,7 @@
 from jax import lax
 from jax.experimental import pallas as pl
 from jax.experimental.pallas import tpu as pltpu
+from jax.sharding import Mesh
 from jax.sharding import PartitionSpec as P
 
 H = 16
@@ -103,33 +104,42 @@
     )(where, order, table, queries, *pieces)
 
 
-def project_kernel(where_ref, near_ref, across_ref, far_ref, far_across_ref, w_ref, o_ref, rows):
+def project_kernel(
+    n_outer, where_ref, near_ref, across_ref, far_ref, far_across_ref, w_ref, o_ref, rows
+):
     side = where_ref[1]
 
     @pl.when((pl.program_id(0) == 0) & (pl.program_id(1) == 0))
     def _():
-        width = near_ref.shape[-1]
-        here = pl.ds(pl.multiple_of(side * width, width), width)
-        there = pl.ds(pl.multiple_of((1 - side) * width, width), width)
+        heads = H // 2
         for block in range(2):
             even = slice(2 * block * QB, (2 * block + 1) * QB)
             odd = slice((2 * block + 1) * QB, (2 * block + 2) * QB)
-            rows[even, here] = near_ref[block]
-            rows[even, there] = across_ref[block]
-            rows[odd, here] = far_ref[block]
-            rows[odd, there] = far_across_ref[block]
+            for which, even_ref, odd_ref in (
+                (side, near_ref, far_ref),
+                (1 - side, across_ref, far_across_ref),
+            ):
+                for h in range(heads):
+                    at = slice(h * HD, (h + 1) * HD)
+                    if n_outer:
+                        to = (h % 4) * n_outer + h // 4 + which * (heads // 4)
+                    else:
+                        to = h + which * heads
+                    to = pl.ds(pl.multiple_of(to * HD, HD), HD)
+                    rows[even, to] = even_ref[block, :, at]
+                    rows[odd, to] = odd_ref[block, :, at]
 
     o_ref[...] = jnp.dot(
         rows[...], w_ref[0], preferred_element_type=jnp.float32
     ).astype(jnp.bfloat16)
 
 
-def project(where, near, across, far, far_across, weights, tile=512):
+def project(n_outer, where, near, across, far, far_across, weights, tile=512):
     parts, depth, columns = weights.shape
     tiles = columns // tile
     half = pl.BlockSpec((2, QB, depth // 2), lambda p, t, *_: (0, 0, 0))
     return pl.pallas_call(
-        project_kernel,
+        functools.partial(project_kernel, n_outer),
         out_shape=jax.ShapeDtypeStruct((4 * QB, parts * columns), jnp.bfloat16),
         grid_spec=pltpu.PrefetchScalarGridSpec(
             num_scalar_prefetch=1,
@@ -147,18 +157,21 @@
     )(where, near, across, far, far_across, weights)
 
 
-def body(n_groups, n_seq, queries, keys, values, block_table, out_weight):
-    n_chip = n_seq // 2
-    n_outer = n_chip // 2
+LINE = "outer"
+PLANE = ("groups", "side", "core")
+SEQ = ("outer", "side", "core")
+
+
+def body(n_groups, n_outer, queries, keys, values, block_table, out_weight):
+    n_chip = n_outer * 2
     order_rows = arrivals(n_outer)
 
     def index(outer, side, core):
         return (outer * 2 + side) * 2 + core
 
     spots = [(o, s, c) for o in range(n_outer) for s in range(2) for c in range(2)]
-    me = lax.axis_index("seq")
     group = lax.axis_index("groups")
-    outer, side, core = me // 4, (me // 2) % 2, me % 2
+    outer, side, core = (lax.axis_index(name) for name in SEQ)
     where = jnp.stack([outer, side, core, side]).astype(jnp.int32)
     where_across = jnp.stack([outer, side, core, 1 - side]).astype(jnp.int32)
     order = jnp.asarray(
@@ -167,18 +180,18 @@
 
     def swap_core(array):
         return lax.ppermute(
-            array, "seq", [(index(o, s, c), index(o, s, 1 - c)) for o, s, c in spots]
+            array, SEQ, [(index(o, s, c), index(o, s, 1 - c)) for o, s, c in spots]
         )
 
     def swap_side(array):
         return lax.ppermute(
-            array, "seq", [(index(o, s, c), index(o, 1 - s, c)) for o, s, c in spots]
+            array, SEQ, [(index(o, s, c), index(o, 1 - s, c)) for o, s, c in spots]
         )
 
     def move(array, hop, way):
         return lax.ppermute(
             array,
-            "seq",
+            SEQ,
             [
                 (index(o, s, c), index(o + way, s, c))
                 for o, s, c in spots
@@ -211,9 +224,37 @@
         width = array.shape[-1] // 2
         return lax.dynamic_slice_in_dim(array, which * width, width, array.ndim - 1)
 
+    part = out_weight.shape[1] // n_groups
+    columns = lax.dynamic_slice_in_dim(out_weight, group * part, part, 1)
+    gathered = lax.all_gather(columns, LINE, axis=0, tiled=True)
+
     mine = jnp.concatenate([half_of(keys, side), half_of(values, side)], 0)
     theirs = jnp.concatenate([half_of(keys, 1 - side), half_of(values, 1 - side)], 0)
     theirs = swap_side(theirs)
+
+    query_blocks = queries.reshape(2, 2, QB, H * HD)
+    far_queries = swap_core(query_blocks[:, 1])
+    far_table = swap_core(block_table)
+    table = jnp.concatenate([block_table[0::2], far_table[1::2]], 0)
+    near_queries = query_blocks[:, 0]
+
+    def my_blocks(which):
+        return jnp.concatenate([half_of(near_queries, which), half_of(far_queries, which)], 0)
+
+    across_queries = swap_side(my_blocks(1 - side))
+    across_table = swap_side(table)
+
+    gathered = after(gathered, theirs, across_queries, across_table)
+    mine, theirs = after(mine, gathered), after(theirs, gathered)
+    gathered = lax.all_gather(gathered, PLANE, axis=0, tiled=True)
+    held = out_weight.shape[0]
+    order_of_rows = n_outer
+    if held != HD:
+        gathered = gathered.reshape(n_groups, 2, 2, n_outer, held, part)
+        gathered = jnp.transpose(gathered, (0, 3, 1, 2, 4, 5))
+        order_of_rows = 0
+    gathered = gathered.reshape(n_groups, H * HD, part)
+
     pieces = []
     for chain in (mine, theirs):
         got = line(chain)
@@ -223,39 +264,19 @@
             near.append(pick(tied, k))
         pieces += near
 
-    part = out_weight.shape[1] // n_groups
-    columns = lax.dynamic_slice_in_dim(out_weight, group * part, part, 1)
-    gathered = lax.all_gather(columns, ("groups", "seq"), axis=0, tiled=True)
-    gathered = gathered.reshape(n_groups, n_seq * out_weight.shape[0], part)
-
-    query_blocks = queries.reshape(2, 2, QB, H * HD)
-    far_queries = swap_core(query_blocks[:, 1])
-    far_table = swap_core(block_table)
-    table = jnp.concatenate([block_table[0::2], far_table[1::2]], 0)
-    near_queries = query_blocks[:, 0]
-
-    def my_blocks(which):
-        return jnp.concatenate([half_of(near_queries, which), half_of(far_queries, which)], 0)
-
-    across_queries = swap_side(my_blocks(1 - side))
-    across_table = swap_side(table)
-
     across = attention(across_queries, where_across, order, across_table, pieces, n_chip)
     across = swap_side(across)
     near = attention(my_blocks(side), where, order, table, pieces, n_chip)
     far = swap_core(near[2:])
     far_across = swap_core(across[2:])
-    return project(where, near, across, far, far_across, gathered)
+    return project(order_of_rows, where, near, across, far, far_across, gathered)
 
 
 def solution(mesh):
-    in_specs = (
-        P(("groups", "seq"), None),
-        P(("groups", "seq"), None),
-        P(("groups", "seq"), None),
-        P(("groups", "seq"), None),
-        P("seq", None),
-    )
-    out_specs = P(("groups", "seq"), None)
-    run = functools.partial(body, mesh.shape["groups"], mesh.shape["seq"])
-    return jax.shard_map(run, mesh=mesh, in_specs=in_specs, out_specs=out_specs, check_vma=False)
+    n_groups, n_seq = mesh.shape["groups"], mesh.shape["seq"]
+    n_outer = n_seq // 4
+    split = Mesh(mesh.devices.reshape(n_groups, n_outer, 2, 2), ("groups", *SEQ))
+    rows = P(("groups", *SEQ), None)
+    in_specs = (rows, rows, rows, rows, P(SEQ, None))
+    run = functools.partial(body, n_groups, n_outer)
+    return jax.shard_map(run, mesh=split, in_specs=in_specs, out_specs=rows, check_vma=False)

time: 227 us -> 194 us (0.85); the launches traced: 223 us -> 194 us
  waiting for transfers between devices: 135 us -> 103 us
    ppermute x20, waiting for transfers between devices: 135 us -> 99.1 us  [the longest x4 47.6 us: swap_side(): lax.ppermute(array, SEQ, [(index(o, s, c), index(o, 1 - s, c)) for o, s,...]
    all_gather x1 -> x2, waiting for transfers between devices: 0.01 us -> 3.4 us  [the longest x1 3.4 us: body(): gathered = lax.all_gather(columns, LINE, axis=0, tiled=True)]
  transfers between devices with their start and end apart: 21 -> 22, of which waited for: 9 -> 13; matrix products, arithmetic and copies ran while one was open for 4% -> 6% of each run, Pallas kernels for 8% -> 10%
where the time goes in v5:
time: 194 us
  waiting for transfers between devices  103 us (53%)
  Pallas kernels  34 us (18%)
  starting transfers between devices  28.4 us (15%)
  between operations  13.7 us (7%)
  local copies, waits for them, and re-layouts  9.95 us (5%)
  other arithmetic  4.96 us (3%)
    ppermute x4, waiting for transfers between devices, swap_side(): lax.ppermute(array, SEQ, [(index(o, s, c), index(o, 1 - s, c)) for o, s,...  47.6 us
    ppermute x12, waiting for transfers between devices, move(): lax.ppermute(array, SEQ, [(index(o, s, c), index(o + way, s, c)) for o, s...  46.9 us
    ppermute x12, starting transfers between devices, move(): lax.ppermute(array, SEQ, [(index(o, s, c), index(o + way, s, c)) for o, s...  21.2 us
    pallas_call x2, Pallas kernels, attention(): pl.pallas_call(functools.partial(attention_kernel, n_chip), out_shape=jax...  18.6 us
    pallas_call x1, Pallas kernels, project(): pl.pallas_call(functools.partial(project_kernel, n_outer), out_shape=jax....  15.4 us
    ppermute x4, starting transfers between devices, swap_side(): lax.ppermute(array, SEQ, [(index(o, s, c), index(o, 1 - s, c)) for o, s,...  6.54 us
    ppermute x4, waiting for transfers between devices, swap_core(): lax.ppermute(array, SEQ, [(index(o, s, c), index(o, s, 1 - c)) for o, s,...  4.62 us
  transfers between devices with their start and end apart: 22, of which 13 were waited for; matrix products, arithmetic and copies ran while one was open for 6% of the time, Pallas kernels for 10%

profile of v5, /device:TPU:0, one launch (start us, length us, event | category | flops | bytes accessed | tf_op | source)
XLA Modules:
  0.0 193.5 jit_solution(10759289649985964218)
XLA Ops:
  6.5 1.2 copy-done
  7.8 0.8 constant_dynamic-slice_fusion.3
  8.6 0.0 all-gather.3.cloned.1.call-update
  8.6 0.0 all-gather.5.cloned.1.call-start
  8.7 2.8 %fusion = (bf16[2,1,128,2048]{3,2,1,0:T(8,128)(2,1)S(1)}, bf16[2,128,2048]{2,1,0:T(8,128)(2,1)}) fusion(bf16[2,2,128,2048]{3,2,1,0:T(8,128)(2,1)} %bitcast.14), kind=kLoop, calls=%fused_computation.24 | loop fusion | bytes 4194304 | tf_op jit(solution)/shard_map/slice | solution.py:239
  11.4 0.5 collective-permute-start.1
  11.9 0.9 dynamic-slice_bitcast_fusion
  12.8 1.6 collective-permute-done.1
  14.4 0.9 constant_dynamic-slice_fusion
  15.3 1.1 pad_maximum_fusion.1
  16.4 2.9 %collective-permute-start.3 = (bf16[4,128,1024]{2,1,0:T(8,128)(2,1)}, bf16[4,128,1024]{2,1,0:T(8,128)(2,1)S(1)}, u32[]{:S(2)}, u32[]{:S(2)}) collective-permute-start(bf16[4,128,1024]{2,1,0:T(8,128)(2,1)} %pad_maximum_fusion.1), channel_id=1, source_target_pairs={{0,2},{1,3},{2,0},{3,1},{4,6},{5,7},{6,4},{7,5},{8,10},{9,11},{10,... | collective-permute-start | bytes 3145736 | tf_op jit(solution)/shard_map/ppermute | solution.py:187
  19.2 2.0 %constant_dynamic-slice_fusion.1 = (bf16[512,256]{1,0:T(8,128)(2,1)S(1)}, bf16[512,256]{1,0:T(8,128)(2,1)S(1)}, bf16[512,256]{1,0:T(8,128)(2,1)}, bf16[512,256]{1,0:T(8,128)(2,1)S(1)}) fusion(bf16[512,512]{1,0:T(8,128)(2,1)} %param.8, s32[]{:T(128)S(6)} %select_n.82, s32[]{:T(128)S(6)} %select_n.80, bf16[512,512]{1,0:T(8,128)(2,1)} %param.7), kind=kLoop, calls=%fused_computation.14 | loop fusion | bytes 2097160 | tf_op jit(solution)/shard_map/dynamic_slice | solution.py:225
  21.3 0.1 collective-permute-start.2
  21.4 0.0 collective-permute-start
  21.4 1.1 collective-permute-done
  22.6 2.0 %collective-permute-start.4 = (s32[4,8]{1,0:T(4,128)S(1)}, s32[4,8]{1,0:T(4,128)S(1)}, u32[]{:S(2)}, u32[]{:S(2)}) collective-permute-start(s32[4,8]{1,0:T(4,128)S(1)} %pad_add_fusion.table_ref), channel_id=1, source_target_pairs={{0,2},{1,3},{2,0},{3,1},{4,6},{5,7},{6,4},{7,5},{8,10},{9,11},{10,... | collective-permute-start | bytes 392 | tf_op jit(solution)/shard_map/ppermute | solution.py:187
  24.6 29.6 %collective-permute-done.4.table_ref = s32[4,8]{1,0:T(4,128)S(1)} collective-permute-done((s32[4,8]{1,0:T(4,128)S(1)}, s32[4,8]{1,0:T(4,128)S(1)}, u32[]{:S(2)}, u32[]{:S(2)}) %collective-permute-start.4) | collective-permute-done | bytes 160 | tf_op jit(solution)/shard_map/ppermute | solution.py:187
  54.2 0.0 collective-permute-done.2.refs_4_
  54.2 3.4 %all-gather.3.cloned.1.call-done = bf16[512,2048]{1,0:T(8,128)(2,1)} async-done(((bf16[128,2048]{1,0:T(8,128)(2,1)}), bf16[512,2048]{1,0:T(8,128)(2,1)}) %all-gather.3.cloned.1.call-update) | async-done | bytes 2097168 | tf_op jit(solution)/shard_map/all_gather | solution.py:229
  57.6 0.0 all-gather.5.cloned.1.call-update
  57.6 1.3 collective-permute-start.12
  58.9 5.4 %collective-permute-start.11 = (bf16[1024,256]{1,0:T(8,128)(2,1)S(1)}, bf16[1024,256]{1,0:T(8,128)(2,1)}, u32[]{:S(2)}, u32[]{:S(2)}) collective-permute-start(bf16[1024,256]{1,0:T(8,128)(2,1)S(1)} %collective-permute-done.2.refs_4_), channel_id=1, source_target_pairs={{0,4},{1,5},{2,6},{3,7},{4,8},{5,9},{6,10},{7,11},{8,12},{9,13},{1... | collective-permute-start | bytes 1572872 | tf_op jit(solution)/shard_map/ppermute | solution.py:192
  64.3 1.0 pad_maximum_fusion.2.refs_0_
  65.3 1.3 collective-permute-start.6
  66.6 5.4 %collective-permute-start.5 = (bf16[1024,256]{1,0:T(8,128)(2,1)S(1)}, bf16[1024,256]{1,0:T(8,128)(2,1)}, u32[]{:S(2)}, u32[]{:S(2)}) collective-permute-start(bf16[1024,256]{1,0:T(8,128)(2,1)S(1)} %pad_maximum_fusion.2.refs_0_), channel_id=1, source_target_pairs={{0,4},{1,5},{2,6},{3,7},{4,8},{5,9},{6,10},{7,11},{8,12},{9,13},{1... | collective-permute-start | bytes 1572872 | tf_op jit(solution)/shard_map/ppermute | solution.py:192
  72.0 0.1 pad_add_fusion.3
  72.1 2.4 %collective-permute-done.12 = bf16[1024,256]{1,0:T(8,128)(2,1)} collective-permute-done((bf16[1024,256]{1,0:T(8,128)(2,1)S(1)}, bf16[1024,256]{1,0:T(8,128)(2,1)}, u32[]{:S(2)}, u32[]{:S(2)}) %collective-permute-start.12) | collective-permute-done | bytes 524320 | tf_op jit(solution)/shard_map/ppermute | solution.py:192
  74.4 1.4 collective-permute-done.11
  75.8 1.3 collective-permute-start.14
  77.1 0.7 collective-permute-start.13
  77.8 7.8 %collective-permute-done.6 = bf16[1024,256]{1,0:T(8,128)(2,1)} collective-permute-done((bf16[1024,256]{1,0:T(8,128)(2,1)S(1)}, bf16[1024,256]{1,0:T(8,128)(2,1)}, u32[]{:S(2)}, u32[]{:S(2)}) %collective-permute-start.6) | collective-permute-done | bytes 524320 | tf_op jit(solution)/shard_map/ppermute | solution.py:192
  85.7 1.3 collective-permute-start.8
  87.0 0.0 collective-permute-done.5
  87.0 0.7 collective-permute-start.7
  87.7 1.1 broadcast_select_fusion.refs_5_
  88.8 1.1 broadcast_select_fusion.1.refs_1_
  89.9 6.9 %collective-permute-done.14 = bf16[1024,256]{1,0:T(8,128)(2,1)S(1)} collective-permute-done((bf16[1024,256]{1,0:T(8,128)(2,1)}, bf16[1024,256]{1,0:T(8,128)(2,1)S(1)}, u32[]{:S(2)}, u32[]{:S(2)}) %collective-permute-start.14) | collective-permute-done | bytes 524320 | tf_op jit(solution)/shard_map/ppermute | solution.py:192
  96.8 1.3 collective-permute-start.16
  98.1 0.7 collective-permute-start.15
  98.8 9.2 %collective-permute-done.8 = bf16[1024,256]{1,0:T(8,128)(2,1)S(1)} collective-permute-done((bf16[1024,256]{1,0:T(8,128)(2,1)}, bf16[1024,256]{1,0:T(8,128)(2,1)S(1)}, u32[]{:S(2)}, u32[]{:S(2)}) %collective-permute-start.8) | collective-permute-done | bytes 524320 | tf_op jit(solution)/shard_map/ppermute | solution.py:192
  108.0 1.3 collective-permute-start.10
  109.3 0.0 collective-permute-done.7
  109.3 0.7 collective-permute-start.9
  110.0 0.1 select_select_fusion.1.refs_6_
  110.1 0.1 select_select_fusion.3.refs_2_
  110.2 0.0 copy-start.3
  110.2 9.0 %collective-permute-done.16 = bf16[1024,256]{1,0:T(8,128)(2,1)S(1)} collective-permute-done((bf16[1024,256]{1,0:T(8,128)(2,1)S(1)}, bf16[1024,256]{1,0:T(8,128)(2,1)S(1)}, u32[]{:S(2)}, u32[]{:S(2)}) %collective-permute-start.16) | collective-permute-done | bytes 524320 | tf_op jit(solution)/shard_map/ppermute | solution.py:192
  119.3 0.0 collective-permute-done.15
  119.3 10.1 %collective-permute-done.10 = bf16[1024,256]{1,0:T(8,128)(2,1)S(1)} collective-permute-done((bf16[1024,256]{1,0:T(8,128)(2,1)S(1)}, bf16[1024,256]{1,0:T(8,128)(2,1)S(1)}, u32[]{:S(2)}, u32[]{:S(2)}) %collective-permute-start.10) | collective-permute-done | bytes 524320 | tf_op jit(solution)/shard_map/ppermute | solution.py:192
  129.4 0.0 collective-permute-done.9
  129.4 0.1 select_select_fusion.refs_7_
  129.5 0.1 select_select_fusion.2.refs_3_
  129.6 9.3 %shard_map.65 = bf16[4,128,1024]{2,1,0:T(8,128)(2,1)S(1)} custom-call(s32[4]{0:T(128)S(1)} %get-tuple-element.47.where_ref, s32[4,4]{1,0:T(4,128)S(1)} %copy-done.3, s32[4,8]{1,0:T(4,128)S(1)} %collective-permute-done.4.table_ref, bf16[4,128,1024]{2,1,0:T(8,128)(2,1)S(1)} %collective-permute-done.3.q_ref, bf16[1024,256]{1,0:T(8,128)(2,1)S(1)} %pad_maximum_fusion.2.refs_0_, ...), custom_call_target="tpu_custom_call" | custom-call | flops 2147483648 | bytes 6291456 | tf_op jit(solution)/shard_map/pallas_call | solution.py:89
  138.9 1.5 collective-permute-start.17
  140.4 0.1 pad_add_fusion.1.where_ref
  140.5 0.1 pad_maximum_fusion.q_ref
  140.6 9.3 %shard_map.64.near_ref = bf16[4,128,1024]{2,1,0:T(8,128)(2,1)S(1)} custom-call(s32[4]{0:T(128)S(1)} %pad_add_fusion.1.where_ref, s32[4,4]{1,0:T(4,128)S(1)} %copy-done.3, s32[4,8]{1,0:T(4,128)S(1)} %pad_add_fusion.table_ref, bf16[4,128,1024]{2,1,0:T(8,128)(2,1)S(1)} %pad_maximum_fusion.q_ref, bf16[1024,256]{1,0:T(8,128)(2,1)S(1)} %pad_maximum_fusion.2.refs_0_, ...), custom_call_target="tpu_custom_call" | custom-call | flops 2147483648 | bytes 6291456 | tf_op jit(solution)/shard_map/pallas_call | solution.py:89
  149.9 0.0 copy-start.1
  149.9 0.1 collective-permute-start.18
  150.0 18.0 %collective-permute-done.17.across_ref = bf16[4,128,1024]{2,1,0:T(8,128)(2,1)S(1)} collective-permute-done((bf16[4,128,1024]{2,1,0:T(8,128)(2,1)S(1)}, bf16[4,128,1024]{2,1,0:T(8,128)(2,1)S(1)}, u32[]{:S(2)}, u32[]{:S(2)}) %collective-permute-start.17) | collective-permute-done | bytes 1048608 | tf_op jit(solution)/shard_map/ppermute | solution.py:187
  168.0 0.1 collective-permute-start.19
  168.1 1.9 collective-permute-done.19.far_across_ref
  170.0 1.2 copy-done.2
  171.2 15.4 %shard_map.66 = bf16[512,4096]{1,0:T(8,128)(2,1)} custom-call(s32[4]{0:T(128)S(1)} %pad_add_fusion.1.where_ref, bf16[4,128,1024]{2,1,0:T(8,128)(2,1)S(1)} %copy-done.2, bf16[4,128,1024]{2,1,0:T(8,128)(2,1)S(1)} %collective-permute-done.17.across_ref, bf16[2,128,1024]{2,1,0:T(8,128)(2,1)S(1)} %collective-permute-done.18.far_ref, ...), custom_call_target="tpu_custom_call" | custom-call | flops 8589934592 | bytes 23068672 | tf_op jit(solution)/shard_map/pallas_call | solution.py:141
  (21 shorter events, 0.2 us)
Async XLA Ops:
  6.5 1.2 copy-start
  6.5 51.1 %all-gather.3.cloned.1.call-start = ((), (), s32[]{:S(2)}) async-start(), calls=%async_computation | async-start | bytes 2621440 | tf_op jit(solution)/shard_map/all_gather | solution.py:229
  8.6 161.4 %all-gather.5.cloned.1.call-start = ((), (), s32[]{:S(2)}) async-start(), calls=%async_computation.1 | async-start | bytes 18874368 | tf_op jit(solution)/shard_map/all_gather | solution.py:249
  11.4 3.0 %collective-permute-start.1 = (bf16[2,128,2048]{2,1,0:T(8,128)(2,1)}, bf16[2,128,2048]{2,1,0:T(8,128)(2,1)S(1)}, u32[]{:S(2)}, u32[]{:S(2)}) collective-permute-start(bf16[2,128,2048]{2,1,0:T(8,128)(2,1)} %get-tuple-element.50), channel_id=1, source_target_pairs={{0,1},{1,0},{2,3},{3,2},{4,5},{5,4},{6,7},{7,6},{8,9},{9,8},{10,11... | collective-permute-start | bytes 3145736 | tf_op jit(solution)/shard_map/ppermute | solution.py:182
  16.4 5.0 %copy-start.6 = (s32[4,8]{1,0:T(4,128)S(1)}, s32[4,8]{1,0:T(4,128)}, u32[]{:S(2)}) copy-start(s32[4,8]{1,0:T(4,128)} %param.9) | copy-start | bytes 388
  16.4 37.8 %collective-permute-start.3 = (bf16[4,128,1024]{2,1,0:T(8,128)(2,1)}, bf16[4,128,1024]{2,1,0:T(8,128)(2,1)S(1)}, u32[]{:S(2)}, u32[]{:S(2)}) collective-permute-start(bf16[4,128,1024]{2,1,0:T(8,128)(2,1)} %pad_maximum_fusion.1), channel_id=1, source_target_pairs={{0,2},{1,3},{2,0},{3,1},{4,6},{5,7},{6,4},{7,5},{8,10},{9,11},{10,... | collective-permute-start | bytes 3145736 | tf_op jit(solution)/shard_map/ppermute | solution.py:187
  21.3 32.9 %collective-permute-start.2 = (bf16[1024,256]{1,0:T(8,128)(2,1)S(1)}, bf16[1024,256]{1,0:T(8,128)(2,1)S(1)}, u32[]{:S(2)}, u32[]{:S(2)}) collective-permute-start(bf16[1024,256]{1,0:T(8,128)(2,1)S(1)} %pad_maximum_fusion.3), channel_id=1, source_target_pairs={{0,2},{1,3},{2,0},{3,1},{4,6},{5,7},{6,4},{7,5},{8,10},{9,11},{10,... | collective-permute-start | bytes 1572872 | tf_op jit(solution)/shard_map/ppermute | solution.py:187
  21.4 1.2 collective-permute-start
  22.6 31.6 %collective-permute-start.4 = (s32[4,8]{1,0:T(4,128)S(1)}, s32[4,8]{1,0:T(4,128)S(1)}, u32[]{:S(2)}, u32[]{:S(2)}) collective-permute-start(s32[4,8]{1,0:T(4,128)S(1)} %pad_add_fusion.table_ref), channel_id=1, source_target_pairs={{0,2},{1,3},{2,0},{3,1},{4,6},{5,7},{6,4},{7,5},{8,10},{9,11},{10,... | collective-permute-start | bytes 392 | tf_op jit(solution)/shard_map/ppermute | solution.py:187
  57.6 16.8 %collective-permute-start.12 = (bf16[1024,256]{1,0:T(8,128)(2,1)S(1)}, bf16[1024,256]{1,0:T(8,128)(2,1)}, u32[]{:S(2)}, u32[]{:S(2)}) collective-permute-start(bf16[1024,256]{1,0:T(8,128)(2,1)S(1)} %collective-permute-done.2.refs_4_), channel_id=1, source_target_pairs={{4,0},{5,1},{6,2},{7,3},{8,4},{9,5},{10,6},{11,7},{12,8},{13,9},{1... | collective-permute-start | bytes 1572872 | tf_op jit(solution)/shard_map/ppermute | solution.py:192
  58.9 16.9 %collective-permute-start.11 = (bf16[1024,256]{1,0:T(8,128)(2,1)S(1)}, bf16[1024,256]{1,0:T(8,128)(2,1)}, u32[]{:S(2)}, u32[]{:S(2)}) collective-permute-start(bf16[1024,256]{1,0:T(8,128)(2,1)S(1)} %collective-permute-done.2.refs_4_), channel_id=1, source_target_pairs={{0,4},{1,5},{2,6},{3,7},{4,8},{5,9},{6,10},{7,11},{8,12},{9,13},{1... | collective-permute-start | bytes 1572872 | tf_op jit(solution)/shard_map/ppermute | solution.py:192
  65.3 20.4 %collective-permute-start.6 = (bf16[1024,256]{1,0:T(8,128)(2,1)S(1)}, bf16[1024,256]{1,0:T(8,128)(2,1)}, u32[]{:S(2)}, u32[]{:S(2)}) collective-permute-start(bf16[1024,256]{1,0:T(8,128)(2,1)S(1)} %pad_maximum_fusion.2.refs_0_), channel_id=1, source_target_pairs={{4,0},{5,1},{6,2},{7,3},{8,4},{9,5},{10,6},{11,7},{12,8},{13,9},{1... | collective-permute-start | bytes 1572872 | tf_op jit(solution)/shard_map/ppermute | solution.py:192
  66.6 20.3 %collective-permute-start.5 = (bf16[1024,256]{1,0:T(8,128)(2,1)S(1)}, bf16[1024,256]{1,0:T(8,128)(2,1)}, u32[]{:S(2)}, u32[]{:S(2)}) collective-permute-start(bf16[1024,256]{1,0:T(8,128)(2,1)S(1)} %pad_maximum_fusion.2.refs_0_), channel_id=1, source_target_pairs={{0,4},{1,5},{2,6},{3,7},{4,8},{5,9},{6,10},{7,11},{8,12},{9,13},{1... | collective-permute-start | bytes 1572872 | tf_op jit(solution)/shard_map/ppermute | solution.py:192
  75.8 21.0 %collective-permute-start.14 = (bf16[1024,256]{1,0:T(8,128)(2,1)}, bf16[1024,256]{1,0:T(8,128)(2,1)S(1)}, u32[]{:S(2)}, u32[]{:S(2)}) collective-permute-start(bf16[1024,256]{1,0:T(8,128)(2,1)} %collective-permute-done.12), channel_id=1, source_target_pairs={{4,0},{5,1},{6,2},{7,3},{8,4},{9,5},{10,6},{11,7},{20,16},{21,17},... | collective-permute-start | bytes 1572872 | tf_op jit(solution)/shard_map/ppermute | solution.py:192
  77.1 19.7 %collective-permute-start.13 = (bf16[1024,256]{1,0:T(8,128)(2,1)}, bf16[1024,256]{1,0:T(8,128)(2,1)S(1)}, u32[]{:S(2)}, u32[]{:S(2)}) collective-permute-start(bf16[1024,256]{1,0:T(8,128)(2,1)} %collective-permute-done.11), channel_id=1, source_target_pairs={{4,8},{5,9},{6,10},{7,11},{8,12},{9,13},{10,14},{11,15},{20,24},{2... | collective-permute-start | bytes 1572872 | tf_op jit(solution)/shard_map/ppermute | solution.py:192
  85.7 22.4 %collective-permute-start.8 = (bf16[1024,256]{1,0:T(8,128)(2,1)}, bf16[1024,256]{1,0:T(8,128)(2,1)S(1)}, u32[]{:S(2)}, u32[]{:S(2)}) collective-permute-start(bf16[1024,256]{1,0:T(8,128)(2,1)} %collective-permute-done.6), channel_id=1, source_target_pairs={{4,0},{5,1},{6,2},{7,3},{8,4},{9,5},{10,6},{11,7},{20,16},{21,17},... | collective-permute-start | bytes 1572872 | tf_op jit(solution)/shard_map/ppermute | solution.py:192
  87.0 22.4 %collective-permute-start.7 = (bf16[1024,256]{1,0:T(8,128)(2,1)}, bf16[1024,256]{1,0:T(8,128)(2,1)S(1)}, u32[]{:S(2)}, u32[]{:S(2)}) collective-permute-start(bf16[1024,256]{1,0:T(8,128)(2,1)} %collective-permute-done.5), channel_id=1, source_target_pairs={{4,8},{5,9},{6,10},{7,11},{8,12},{9,13},{10,14},{11,15},{20,24},{2... | collective-permute-start | bytes 1572872 | tf_op jit(solution)/shard_map/ppermute | solution.py:192
  96.8 22.5 %collective-permute-start.16 = (bf16[1024,256]{1,0:T(8,128)(2,1)S(1)}, bf16[1024,256]{1,0:T(8,128)(2,1)S(1)}, u32[]{:S(2)}, u32[]{:S(2)}) collective-permute-start(bf16[1024,256]{1,0:T(8,128)(2,1)S(1)} %collective-permute-done.14), channel_id=1, source_target_pairs={{4,0},{5,1},{6,2},{7,3},{20,16},{21,17},{22,18},{23,19}} | collective-permute-start | bytes 1572872 | tf_op jit(solution)/shard_map/ppermute | solution.py:192
  98.1 21.2 %collective-permute-start.15 = (bf16[1024,256]{1,0:T(8,128)(2,1)S(1)}, bf16[1024,256]{1,0:T(8,128)(2,1)S(1)}, u32[]{:S(2)}, u32[]{:S(2)}) collective-permute-start(bf16[1024,256]{1,0:T(8,128)(2,1)S(1)} %collective-permute-done.13), channel_id=1, source_target_pairs={{8,12},{9,13},{10,14},{11,15},{24,28},{25,29},{26,30},{27,31}} | collective-permute-start | bytes 1572872 | tf_op jit(solution)/shard_map/ppermute | solution.py:192
  108.0 21.3 %collective-permute-start.10 = (bf16[1024,256]{1,0:T(8,128)(2,1)S(1)}, bf16[1024,256]{1,0:T(8,128)(2,1)S(1)}, u32[]{:S(2)}, u32[]{:S(2)}) collective-permute-start(bf16[1024,256]{1,0:T(8,128)(2,1)S(1)} %collective-permute-done.8), channel_id=1, source_target_pairs={{4,0},{5,1},{6,2},{7,3},{20,16},{21,17},{22,18},{23,19}} | collective-permute-start | bytes 1572872 | tf_op jit(solution)/shard_map/ppermute | solution.py:192
  109.3 20.0 %collective-permute-start.9 = (bf16[1024,256]{1,0:T(8,128)(2,1)S(1)}, bf16[1024,256]{1,0:T(8,128)(2,1)S(1)}, u32[]{:S(2)}, u32[]{:S(2)}) collective-permute-start(bf16[1024,256]{1,0:T(8,128)(2,1)S(1)} %collective-permute-done.7), channel_id=1, source_target_pairs={{8,12},{9,13},{10,14},{11,15},{24,28},{25,29},{26,30},{27,31}} | collective-permute-start | bytes 1572872 | tf_op jit(solution)/shard_map/ppermute | solution.py:192
  110.2 19.3 %copy-start.3 = (s32[4,4]{1,0:T(4,128)S(1)}, s32[4,4]{1,0:T(4,128)}, u32[]{:S(2)}) copy-start(s32[4,4]{1,0:T(4,128)} %constant.37.clone.order_ref) | copy-start | bytes 196
  129.6 10.9 %copy-start.4 = (bf16[2,128,1024]{2,1,0:T(8,128)(2,1)S(1)}, bf16[2,128,1024]{2,1,0:T(8,128)(2,1)}, u32[]{:S(2)}) copy-start(bf16[2,128,1024]{2,1,0:T(8,128)(2,1)} %get-tuple-element.52) | copy-start | bytes 1572868
  129.6 10.9 %copy-start.5 = (bf16[2,128,1024]{2,1,0:T(8,128)(2,1)S(1)}, bf16[2,128,1024]{2,1,0:T(8,128)(2,1)}, u32[]{:S(2)}) copy-start(bf16[2,128,1024]{2,1,0:T(8,128)(2,1)} %get-tuple-element.54) | copy-start | bytes 1572868
  138.9 29.1 %collective-permute-start.17 = (bf16[4,128,1024]{2,1,0:T(8,128)(2,1)S(1)}, bf16[4,128,1024]{2,1,0:T(8,128)(2,1)S(1)}, u32[]{:S(2)}, u32[]{:S(2)}) collective-permute-start(bf16[4,128,1024]{2,1,0:T(8,128)(2,1)S(1)} %shard_map.65), channel_id=1, source_target_pairs={{0,2},{1,3},{2,0},{3,1},{4,6},{5,7},{6,4},{7,5},{8,10},{9,11},{10,... | collective-permute-start | bytes 3145736 | tf_op jit(solution)/shard_map/ppermute | solution.py:187
  149.9 18.1 %copy-start.1 = (bf16[4,128,1024]{2,1,0:T(8,128)(2,1)}, bf16[4,128,1024]{2,1,0:T(8,128)(2,1)S(1)}, u32[]{:S(2)}) copy-start(bf16[4,128,1024]{2,1,0:T(8,128)(2,1)S(1)} %shard_map.64.near_ref) | copy-start | bytes 3145732
  149.9 18.2 %collective-permute-start.18 = (bf16[2,128,1024]{2,1,0:T(8,128)(2,1)S(1)}, bf16[2,128,1024]{2,1,0:T(8,128)(2,1)S(1)}, u32[]{:S(2)}, u32[]{:S(2)}) collective-permute-start(bf16[2,128,1024]{2,1,0:T(8,128)(2,1)S(1)} %slice.26), channel_id=1, source_target_pairs={{0,1},{1,0},{2,3},{3,2},{4,5},{5,4},{6,7},{7,6},{8,9},{9,8},{10,11... | collective-permute-start | bytes 1572872 | tf_op jit(solution)/shard_map/ppermute | solution.py:182
  168.0 2.0 %collective-permute-start.19 = (bf16[2,128,1024]{2,1,0:T(8,128)(2,1)S(1)}, bf16[2,128,1024]{2,1,0:T(8,128)(2,1)S(1)}, u32[]{:S(2)}, u32[]{:S(2)}) collective-permute-start(bf16[2,128,1024]{2,1,0:T(8,128)(2,1)S(1)} %slice.27), channel_id=1, source_target_pairs={{0,1},{1,0},{2,3},{3,2},{4,5},{5,4},{6,7},{7,6},{8,9},{9,8},{10,11... | collective-permute-start | bytes 1572872 | tf_op jit(solution)/shard_map/ppermute | solution.py:182
  170.0 1.2 copy-start.2
Sparse Core Ops, SparseCore 0:
  8.9 48.6 all-gather.2
  59.5 93.3 all-gather.4

commit v6 on v5

--- a/solution.py
+++ b/solution.py
@@ -199,11 +199,17 @@
             ],
         )
 
-    def line(array):
+    def after(array, *others):
+        return lax.optimization_barrier((array, *others))[0]
+
+    def line(array, gates={}):
         got = {0: array}
         for hop in range(1, n_outer):
             for way in (1, -1):
-                got[-way * hop] = move(got[-way * (hop - 1)], hop, way)
+                sent = got[-way * (hop - 1)]
+                if hop in gates:
+                    sent = after(sent, *gates[hop])
+                got[-way * hop] = move(sent, hop, way)
         return got
 
     def pick(got, k):
@@ -217,20 +223,9 @@
                 result = jnp.where(mask, got[offset], result)
         return result
 
-    def after(array, *others):
-        return lax.optimization_barrier((array, *others))[0]
-
     def half_of(array, which):
         width = array.shape[-1] // 2
         return lax.dynamic_slice_in_dim(array, which * width, width, array.ndim - 1)
-
-    part = out_weight.shape[1] // n_groups
-    columns = lax.dynamic_slice_in_dim(out_weight, group * part, part, 1)
-    gathered = lax.all_gather(columns, LINE, axis=0, tiled=True)
-
-    mine = jnp.concatenate([half_of(keys, side), half_of(values, side)], 0)
-    theirs = jnp.concatenate([half_of(keys, 1 - side), half_of(values, 1 - side)], 0)
-    theirs = swap_side(theirs)
 
     query_blocks = queries.reshape(2, 2, QB, H * HD)
     far_queries = swap_core(query_blocks[:, 1])
@@ -241,13 +236,33 @@
     def my_blocks(which):
         return jnp.concatenate([half_of(near_queries, which), half_of(far_queries, which)], 0)
 
-    across_queries = swap_side(my_blocks(1 - side))
+    sent_queries = my_blocks(1 - side)
+
+    mine = jnp.concatenate([half_of(keys, side), half_of(values, side)], 0)
+    theirs = jnp.concatenate([half_of(keys, 1 - side), half_of(values, 1 - side)], 0)
+    theirs = swap_side(theirs)
+
+    part = out_weight.shape[1] // n_groups
+    columns = lax.dynamic_slice_in_dim(out_weight, group * part, part, 1)
+    held = out_weight.shape[0]
+    strip = held // 2
+    gates = {2: (far_queries, far_table), 3: (theirs, mine, sent_queries, table)}
+    strips = [line(columns[:strip], gates), line(columns[strip:], gates)]
+
+    across_queries = swap_side(after(sent_queries, theirs))
     across_table = swap_side(table)
 
-    gathered = after(gathered, theirs, across_queries, across_table)
-    mine, theirs = after(mine, gathered), after(theirs, gathered)
+    gathered = jnp.zeros((n_outer * held, part), columns.dtype)
+    for k in range(n_outer):
+        for at, got in enumerate(strips):
+            rows = (order[outer, k] * 2 + at) * strip
+            piece = pick({d: after(got[d], gathered) for d in {row[k] for row in order_rows}}, k)
+            gathered = lax.dynamic_update_slice_in_dim(gathered, piece, rows, 0)
+
+    ends = (1 - n_outer, n_outer - 1)
+    mine = after(mine, *[strips[0][d] for d in ends])
+    theirs = after(theirs, *[strips[1][d] for d in ends])
     gathered = lax.all_gather(gathered, PLANE, axis=0, tiled=True)
-    held = out_weight.shape[0]
     order_of_rows = n_outer
     if held != HD:
         gathered = gathered.reshape(n_groups, 2, 2, n_outer, held, part)
@@ -257,7 +272,7 @@
 
     pieces = []
     for chain in (mine, theirs):
-        got = line(chain)
+        got = line(chain, {2: (across_queries, across_table)})
         near = [got[0]]
         for k in range(1, n_outer):
             tied = {d: after(got[d], near[-1]) for d in sorted({row[k] for row in order_rows})}

time: 194 us -> 219 us (1.13)
  starting transfers between devices: 28.4 us -> 46.4 us
  between operations: 13.7 us -> 19.3 us
  local copies, waits for them, and re-layouts: 9.95 us -> 14.6 us
  waiting for transfers between devices: 103 us -> 99 us
    ppermute x12 -> x24, starting transfers between devices: 21.2 us -> 39.4 us  [move(): lax.ppermute(array, SEQ, [(index(o, s, c), index(o + way, s, c)) for o, s...]
    ppermute x12 -> x24, waiting for transfers between devices: 46.9 us -> 59.8 us  [move(): lax.ppermute(array, SEQ, [(index(o, s, c), index(o + way, s, c)) for o, s...]
    ppermute x4, waiting for transfers between devices: 47.6 us -> 37.3 us  [swap_side(): lax.ppermute(array, SEQ, [(index(o, s, c), index(o, 1 - s, c)) for o, s,...]
    all_gather x1 -> x0, waiting for transfers between devices: 3.4 us -> none  [body(): gathered = lax.all_gather(columns, LINE, axis=0, tiled=True)]
    ppermute x4, waiting for transfers between devices: 4.62 us -> 1.89 us  [swap_core(): lax.ppermute(array, SEQ, [(index(o, s, c), index(o, s, 1 - c)) for o, s,...]
    dynamic_update_slice x0 -> x6, other arithmetic: none -> 2.56 us  [body(): gathered = lax.dynamic_update_slice_in_dim(gathered, piece, rows, 0)]
  transfers between devices with their start and end apart: 22 -> 33, of which waited for: 13 -> 14; matrix products, arithmetic and copies ran while one was open for 6% -> 8% of each run, Pallas kernels for 10% -> 8%
where the time goes in v6:
time: 219 us; the launch traced here: 218 us
  waiting for transfers between devices  99 us (45%)
  starting transfers between devices  46.4 us (21%)
  Pallas kernels  33.7 us (15%)
  between operations  19.3 us (9%)
  local copies, waits for them, and re-layouts  14.6 us (7%)
  other arithmetic  5.32 us (2%)
    ppermute x24, waiting for transfers between devices, move(): lax.ppermute(array, SEQ, [(index(o, s, c), index(o + way, s, c)) for o, s...  59.8 us
    ppermute x24, starting transfers between devices, move(): lax.ppermute(array, SEQ, [(index(o, s, c), index(o + way, s, c)) for o, s...  39.4 us
    ppermute x4, waiting for transfers between devices, swap_side(): lax.ppermute(array, SEQ, [(index(o, s, c), index(o, 1 - s, c)) for o, s,...  37.3 us
    pallas_call x2, Pallas kernels, attention(): pl.pallas_call(functools.partial(attention_kernel, n_chip), out_shape=jax...  18.3 us
    pallas_call x1, Pallas kernels, project(): pl.pallas_call(functools.partial(project_kernel, n_outer), out_shape=jax....  15.4 us
    ppermute x4, starting transfers between devices, swap_side(): lax.ppermute(array, SEQ, [(index(o, s, c), index(o, 1 - s, c)) for o, s,...  6.3 us
    dynamic_slice x3, local copies, waits for them, and re-layouts, half_of(): return lax.dynamic_slice_in_dim(array, which * width, width, array.ndim - 1)  5.46 us
  transfers between devices with their start and end apart: 33, of which 14 were waited for; matrix products, arithmetic and copies ran while one was open for 8% of the time, Pallas kernels for 8%

profile of v6, /device:TPU:0, one launch (start us, length us, event | category | flops | bytes accessed | tf_op | source)
XLA Modules:
  0.0 218.2 jit_solution(14271934088477216505)
XLA Ops:
  6.5 1.8 fusion.1
  8.3 5.6 %collective-permute-start.2 = (bf16[64,2048]{1,0:T(8,128)(2,1)}, bf16[64,2048]{1,0:T(8,128)(2,1)}, u32[]{:S(2)}, u32[]{:S(2)}) collective-permute-start(bf16[64,2048]{1,0:T(8,128)(2,1)} %get-tuple-element.91), channel_id=1, source_target_pairs={{0,4},{1,5},{2,6},{3,7},{4,8},{5,9},{6,10},{7,11},{8,12},{9,13},{1... | collective-permute-start | bytes 786440 | tf_op jit(solution)/shard_map/ppermute | solution.py:192
  13.9 1.3 collective-permute-start.6
  15.2 5.3 %collective-permute-start.17 = (bf16[64,2048]{1,0:T(8,128)(2,1)S(1)}, bf16[64,2048]{1,0:T(8,128)(2,1)}, u32[]{:S(2)}, u32[]{:S(2)}) collective-permute-start(bf16[64,2048]{1,0:T(8,128)(2,1)S(1)} %get-tuple-element.92), channel_id=1, source_target_pairs={{0,4},{1,5},{2,6},{3,7},{4,8},{5,9},{6,10},{7,11},{8,12},{9,13},{1... | collective-permute-start | bytes 786440 | tf_op jit(solution)/shard_map/ppermute | solution.py:192
  20.5 1.3 collective-permute-start.20
  21.9 1.5 constant_dynamic-slice_fusion.8
  24.7 3.1 %fusion = (bf16[2,1,128,2048]{3,2,1,0:T(8,128)(2,1)}, bf16[2,128,2048]{2,1,0:T(8,128)(2,1)}) fusion(bf16[2,2,128,2048]{3,2,1,0:T(8,128)(2,1)} %bitcast.22), kind=kLoop, calls=%fused_computation.36 | loop fusion | bytes 4194304 | tf_op jit(solution)/shard_map/slice | solution.py:234
  27.8 0.2 broadcast_in_dim.3
  28.1 1.0 constant_dynamic-update-slice_fusion.1
  29.1 1.1 constant_dynamic-slice_fusion.3
  30.3 0.8 pad_maximum_fusion.3
  35.2 2.2 %dynamic-slice_bitcast_fusion = (bf16[2,128,1024]{2,1,0:T(8,128)(2,1)}, bf16[2,128,1024]{2,1,0:T(8,128)(2,1)}) fusion(bf16[2,1,128,2048]{3,2,1,0:T(8,128)(2,1)} %get-tuple-element.113, s32[]{:T(128)S(6)} %select_n.177, s32[]{:T(128)S(6)} %select_n.173), kind=kLoop, calls=%fused_computation.9 | loop fusion | bytes 2097160 | tf_op jit(solution)/shard_map/dynamic_slice | solution.py:228
  37.5 0.5 collective-permute-start.1
  38.0 1.6 collective-permute-start.4
  39.6 1.0 select_dynamic-update-slice_fusion.5
  40.6 1.0 select_dynamic-update-slice_fusion.4
  41.7 0.7 collective-permute-start.3
  42.3 1.3 collective-permute-start.7
  43.6 0.7 collective-permute-start.18
  44.3 1.3 collective-permute-start.21
  45.6 2.1 constant_dynamic-slice_fusion.2
  47.7 1.1 pad_maximum_fusion.1
  48.8 3.3 %collective-permute-done.4.refs_4_ = bf16[1024,256]{1,0:T(8,128)(2,1)S(1)} collective-permute-done((bf16[1024,256]{1,0:T(8,128)(2,1)}, bf16[1024,256]{1,0:T(8,128)(2,1)S(1)}, u32[]{:S(2)}, u32[]{:S(2)}) %collective-permute-start.4) | collective-permute-done | bytes 524320 | tf_op jit(solution)/shard_map/ppermute | solution.py:187
  52.1 0.7 collective-permute-start.5
  52.8 1.9 collective-permute-done.7
  54.7 1.3 collective-permute-start.8
  56.0 0.7 collective-permute-start.19
  56.7 4.3 %collective-permute-done.21 = bf16[64,2048]{1,0:T(8,128)(2,1)S(1)} collective-permute-done((bf16[64,2048]{1,0:T(8,128)(2,1)}, bf16[64,2048]{1,0:T(8,128)(2,1)S(1)}, u32[]{:S(2)}, u32[]{:S(2)}) %collective-permute-start.21) | collective-permute-done | bytes 262176 | tf_op jit(solution)/shard_map/ppermute | solution.py:192
  61.0 1.3 collective-permute-start.22
  62.3 0.1 select_dynamic-update-slice_fusion.3
  62.4 0.1 select_dynamic-update-slice_fusion.2
  62.5 4.4 %collective-permute-done.8 = bf16[64,2048]{1,0:T(8,128)(2,1)S(1)} collective-permute-done((bf16[64,2048]{1,0:T(8,128)(2,1)S(1)}, bf16[64,2048]{1,0:T(8,128)(2,1)S(1)}, u32[]{:S(2)}, u32[]{:S(2)}) %collective-permute-start.8) | collective-permute-done | bytes 262176 | tf_op jit(solution)/shard_map/ppermute | solution.py:192
  66.9 0.1 select_dynamic-update-slice_fusion.1
  67.0 4.6 %collective-permute-done.22 = bf16[64,2048]{1,0:T(8,128)(2,1)S(1)} collective-permute-done((bf16[64,2048]{1,0:T(8,128)(2,1)S(1)}, bf16[64,2048]{1,0:T(8,128)(2,1)S(1)}, u32[]{:S(2)}, u32[]{:S(2)}) %collective-permute-start.22) | collective-permute-done | bytes 262176 | tf_op jit(solution)/shard_map/ppermute | solution.py:192
  71.6 0.1 select_dynamic-update-slice_fusion
  71.8 1.3 copy-done.1
  73.1 1.1 collective-permute-start.11
  74.2 2.3 %collective-permute-start.9 = (bf16[1024,256]{1,0:T(8,128)(2,1)S(1)}, bf16[1024,256]{1,0:T(8,128)(2,1)}, u32[]{:S(2)}, u32[]{:S(2)}) collective-permute-start(bf16[1024,256]{1,0:T(8,128)(2,1)S(1)} %pad_maximum_fusion.2.refs_0_), channel_id=1, source_target_pairs={{0,4},{1,5},{2,6},{3,7},{4,8},{5,9},{6,10},{7,11},{8,12},{9,13},{1... | collective-permute-start | bytes 1572872 | tf_op jit(solution)/shard_map/ppermute | solution.py:192
  76.4 1.3 collective-permute-start.10
  77.7 5.4 %collective-permute-start.23 = (bf16[1024,256]{1,0:T(8,128)(2,1)S(1)}, bf16[1024,256]{1,0:T(8,128)(2,1)}, u32[]{:S(2)}, u32[]{:S(2)}) collective-permute-start(bf16[1024,256]{1,0:T(8,128)(2,1)S(1)} %collective-permute-done.4.refs_4_), channel_id=1, source_target_pairs={{0,4},{1,5},{2,6},{3,7},{4,8},{5,9},{6,10},{7,11},{8,12},{9,13},{1... | collective-permute-start | bytes 1572872 | tf_op jit(solution)/shard_map/ppermute | solution.py:192
  83.1 1.3 collective-permute-start.24
  84.5 3.5 %collective-permute-done.9 = bf16[1024,256]{1,0:T(8,128)(2,1)} collective-permute-done((bf16[1024,256]{1,0:T(8,128)(2,1)S(1)}, bf16[1024,256]{1,0:T(8,128)(2,1)}, u32[]{:S(2)}, u32[]{:S(2)}) %collective-permute-start.9) | collective-permute-done | bytes 524320 | tf_op jit(solution)/shard_map/ppermute | solution.py:192
  88.0 1.0 collective-permute-start.12
  89.0 4.2 %collective-permute-done.10 = bf16[1024,256]{1,0:T(8,128)(2,1)S(1)} collective-permute-done((bf16[1024,256]{1,0:T(8,128)(2,1)S(1)}, bf16[1024,256]{1,0:T(8,128)(2,1)S(1)}, u32[]{:S(2)}, u32[]{:S(2)}) %collective-permute-start.10) | collective-permute-done | bytes 524320 | tf_op jit(solution)/shard_map/ppermute | solution.py:192
  93.2 19.6 %collective-permute-done.12.table_ref = s32[4,8]{1,0:T(4,128)S(1)} collective-permute-done((s32[4,8]{1,0:T(4,128)S(1)}, s32[4,8]{1,0:T(4,128)S(1)}, u32[]{:S(2)}, u32[]{:S(2)}) %collective-permute-start.12) | collective-permute-done | bytes 160 | tf_op jit(solution)/shard_map/ppermute | solution.py:187
  112.8 0.7 collective-permute-start.13
  113.5 1.3 collective-permute-start.14
  114.8 0.7 collective-permute-start.25
  115.5 1.3 collective-permute-start.26
  117.0 13.3 %collective-permute-done.14 = bf16[1024,256]{1,0:T(8,128)(2,1)S(1)} collective-permute-done((bf16[1024,256]{1,0:T(8,128)(2,1)S(1)}, bf16[1024,256]{1,0:T(8,128)(2,1)S(1)}, u32[]{:S(2)}, u32[]{:S(2)}) %collective-permute-start.14) | collective-permute-done | bytes 524320 | tf_op jit(solution)/shard_map/ppermute | solution.py:192
  130.3 0.7 collective-permute-start.15
  130.9 1.3 collective-permute-start.16
  132.3 0.7 collective-permute-start.27
  133.0 8.5 %collective-permute-done.26 = bf16[1024,256]{1,0:T(8,128)(2,1)S(1)} collective-permute-done((bf16[1024,256]{1,0:T(8,128)(2,1)S(1)}, bf16[1024,256]{1,0:T(8,128)(2,1)S(1)}, u32[]{:S(2)}, u32[]{:S(2)}) %collective-permute-start.26) | collective-permute-done | bytes 524320 | tf_op jit(solution)/shard_map/ppermute | solution.py:192
  141.5 1.3 collective-permute-start.28
  142.9 0.1 select_select_fusion.1.refs_6_
  143.0 9.5 %collective-permute-done.16 = bf16[1024,256]{1,0:T(8,128)(2,1)S(1)} collective-permute-done((bf16[1024,256]{1,0:T(8,128)(2,1)S(1)}, bf16[1024,256]{1,0:T(8,128)(2,1)S(1)}, u32[]{:S(2)}, u32[]{:S(2)}) %collective-permute-start.16) | collective-permute-done | bytes 524320 | tf_op jit(solution)/shard_map/ppermute | solution.py:192
  152.5 5.6 %collective-permute-done.28 = bf16[1024,256]{1,0:T(8,128)(2,1)S(1)} collective-permute-done((bf16[1024,256]{1,0:T(8,128)(2,1)S(1)}, bf16[1024,256]{1,0:T(8,128)(2,1)S(1)}, u32[]{:S(2)}, u32[]{:S(2)}) %collective-permute-start.28) | collective-permute-done | bytes 524320 | tf_op jit(solution)/shard_map/ppermute | solution.py:192
  158.3 9.1 %shard_map.65 = bf16[4,128,1024]{2,1,0:T(8,128)(2,1)S(1)} custom-call(s32[4]{0:T(128)S(1)} %get-tuple-element.111.where_ref, s32[4,4]{1,0:T(4,128)S(1)} %copy-done, s32[4,8]{1,0:T(4,128)S(1)} %collective-permute-done.12.table_ref, bf16[4,128,1024]{2,1,0:T(8,128)(2,1)S(1)} %collective-permute-done.11.q_ref, bf16[1024,256]{1,0:T(8,128)(2,1)S(1)} %pad_maximum_fusion.2.refs_0_, ...), custom_call_target="tpu_custom_call" | custom-call | flops 2147483648 | bytes 6291456 | tf_op jit(solution)/shard_map/pallas_call | solution.py:89
  167.5 2.6 %collective-permute-start.29 = (bf16[4,128,1024]{2,1,0:T(8,128)(2,1)S(1)}, bf16[4,128,1024]{2,1,0:T(8,128)(2,1)S(1)}, u32[]{:S(2)}, u32[]{:S(2)}) collective-permute-start(bf16[4,128,1024]{2,1,0:T(8,128)(2,1)S(1)} %shard_map.65), channel_id=1, source_target_pairs={{0,2},{1,3},{2,0},{3,1},{4,6},{5,7},{6,4},{7,5},{8,10},{9,11},{10,... | collective-permute-start | bytes 3145736 | tf_op jit(solution)/shard_map/ppermute | solution.py:187
  170.3 9.1 %shard_map.64.near_ref = bf16[4,128,1024]{2,1,0:T(8,128)(2,1)S(1)} custom-call(s32[4]{0:T(128)S(1)} %pad_add_fusion.1.where_ref, s32[4,4]{1,0:T(4,128)S(1)} %copy-done, s32[4,8]{1,0:T(4,128)S(1)} %pad_add_fusion.table_ref, bf16[4,128,1024]{2,1,0:T(8,128)(2,1)S(1)} %pad_maximum_fusion.q_ref, bf16[1024,256]{1,0:T(8,128)(2,1)S(1)} %pad_maximum_fusion.2.refs_0_, ...), custom_call_target="tpu_custom_call" | custom-call | flops 2147483648 | bytes 6291456 | tf_op jit(solution)/shard_map/pallas_call | solution.py:89
  179.6 14.4 %collective-permute-done.29.across_ref = bf16[4,128,1024]{2,1,0:T(8,128)(2,1)S(1)} collective-permute-done((bf16[4,128,1024]{2,1,0:T(8,128)(2,1)S(1)}, bf16[4,128,1024]{2,1,0:T(8,128)(2,1)S(1)}, u32[]{:S(2)}, u32[]{:S(2)}) %collective-permute-start.29) | collective-permute-done | bytes 1048608 | tf_op jit(solution)/shard_map/ppermute | solution.py:187
  194.0 1.9 collective-permute-done.31.far_across_ref
  195.9 15.4 %shard_map.66 = bf16[512,4096]{1,0:T(8,128)(2,1)} custom-call(s32[4]{0:T(128)S(1)} %pad_add_fusion.1.where_ref, bf16[4,128,1024]{2,1,0:T(8,128)(2,1)S(1)} %shard_map.64.near_ref, bf16[4,128,1024]{2,1,0:T(8,128)(2,1)S(1)} %collective-permute-done.29.across_ref, bf16[2,128,1024]{2,1,0:T(8,128)(2,1)S(1)} %collective-permute-done.30.far_ref, ...), custom_call_target="tpu_custom_call" | custom-call | flops 8589934592 | bytes 23068672 | tf_op jit(solution)/shard_map/pallas_call | solution.py:141
  (52 shorter events, 1.1 us)
Async XLA Ops:
  6.5 189.4 %all-gather.2.cloned.1.call-start = ((), (), s32[]{:S(2)}) async-start(), calls=%async_computation | async-start | bytes 18874368 | tf_op jit(solution)/shard_map/all_gather | solution.py:265
  8.3 29.7 %collective-permute-start.2 = (bf16[64,2048]{1,0:T(8,128)(2,1)}, bf16[64,2048]{1,0:T(8,128)(2,1)}, u32[]{:S(2)}, u32[]{:S(2)}) collective-permute-start(bf16[64,2048]{1,0:T(8,128)(2,1)} %get-tuple-element.91), channel_id=1, source_target_pairs={{0,4},{1,5},{2,6},{3,7},{4,8},{5,9},{6,10},{7,11},{8,12},{9,13},{1... | collective-permute-start | bytes 786440 | tf_op jit(solution)/shard_map/ppermute | solution.py:192
  13.9 25.6 %collective-permute-start.6 = (bf16[64,2048]{1,0:T(8,128)(2,1)}, bf16[64,2048]{1,0:T(8,128)(2,1)}, u32[]{:S(2)}, u32[]{:S(2)}) collective-permute-start(bf16[64,2048]{1,0:T(8,128)(2,1)} %get-tuple-element.91), channel_id=1, source_target_pairs={{4,0},{5,1},{6,2},{7,3},{8,4},{9,5},{10,6},{11,7},{12,8},{13,9},{1... | collective-permute-start | bytes 786440 | tf_op jit(solution)/shard_map/ppermute | solution.py:192
  15.2 25.4 %collective-permute-start.17 = (bf16[64,2048]{1,0:T(8,128)(2,1)S(1)}, bf16[64,2048]{1,0:T(8,128)(2,1)}, u32[]{:S(2)}, u32[]{:S(2)}) collective-permute-start(bf16[64,2048]{1,0:T(8,128)(2,1)S(1)} %get-tuple-element.92), channel_id=1, source_target_pairs={{0,4},{1,5},{2,6},{3,7},{4,8},{5,9},{6,10},{7,11},{8,12},{9,13},{1... | collective-permute-start | bytes 786440 | tf_op jit(solution)/shard_map/ppermute | solution.py:192
  20.5 20.1 %collective-permute-start.20 = (bf16[64,2048]{1,0:T(8,128)(2,1)S(1)}, bf16[64,2048]{1,0:T(8,128)(2,1)}, u32[]{:S(2)}, u32[]{:S(2)}) collective-permute-start(bf16[64,2048]{1,0:T(8,128)(2,1)S(1)} %get-tuple-element.92), channel_id=1, source_target_pairs={{4,0},{5,1},{6,2},{7,3},{8,4},{9,5},{10,6},{11,7},{12,8},{13,9},{1... | collective-permute-start | bytes 786440 | tf_op jit(solution)/shard_map/ppermute | solution.py:192
  21.8 15.7 %collective-permute-start = (s32[4,8]{1,0:T(4,128)}, s32[4,8]{1,0:T(4,128)S(1)}, u32[]{:S(2)}, u32[]{:S(2)}) collective-permute-start(s32[4,8]{1,0:T(4,128)} %param.9), channel_id=1, source_target_pairs={{0,1},{1,0},{2,3},{3,2},{4,5},{5,4},{6,7},{7,6},{8,9},{9,8},{10,11... | collective-permute-start | bytes 392 | tf_op jit(solution)/shard_map/ppermute | solution.py:182
  27.8 1.2 copy-start.5
  29.1 2.1 copy-start.6
  37.5 4.2 %collective-permute-start.1 = (bf16[2,128,2048]{2,1,0:T(8,128)(2,1)}, bf16[2,128,2048]{2,1,0:T(8,128)(2,1)}, u32[]{:S(2)}, u32[]{:S(2)}) collective-permute-start(bf16[2,128,2048]{2,1,0:T(8,128)(2,1)} %get-tuple-element.114), channel_id=1, source_target_pairs={{0,1},{1,0},{2,3},{3,2},{4,5},{5,4},{6,7},{7,6},{8,9},{9,8},{10,11... | collective-permute-start | bytes 3145736 | tf_op jit(solution)/shard_map/ppermute | solution.py:182
  38.0 9.8 %copy-start.4 = (bf16[2,128,1024]{2,1,0:T(8,128)(2,1)S(1)}, bf16[2,128,1024]{2,1,0:T(8,128)(2,1)}, u32[]{:S(2)}) copy-start(bf16[2,128,1024]{2,1,0:T(8,128)(2,1)} %get-tuple-element.117) | copy-start | bytes 1572868
  38.0 14.1 %collective-permute-start.4 = (bf16[1024,256]{1,0:T(8,128)(2,1)}, bf16[1024,256]{1,0:T(8,128)(2,1)S(1)}, u32[]{:S(2)}, u32[]{:S(2)}) collective-permute-start(bf16[1024,256]{1,0:T(8,128)(2,1)} %pad_maximum_fusion.3), channel_id=1, source_target_pairs={{0,2},{1,3},{2,0},{3,1},{4,6},{5,7},{6,4},{7,5},{8,10},{9,11},{10,... | collective-permute-start | bytes 1572872 | tf_op jit(solution)/shard_map/ppermute | solution.py:187
  41.7 10.5 %collective-permute-start.3 = (bf16[64,2048]{1,0:T(8,128)(2,1)}, bf16[64,2048]{1,0:T(8,128)(2,1)S(1)}, u32[]{:S(2)}, u32[]{:S(2)}) collective-permute-start(bf16[64,2048]{1,0:T(8,128)(2,1)} %collective-permute-done.2), channel_id=1, source_target_pairs={{4,8},{5,9},{6,10},{7,11},{8,12},{9,13},{10,14},{11,15},{20,24},{2... | collective-permute-start | bytes 786440 | tf_op jit(solution)/shard_map/ppermute | solution.py:192
  42.3 12.4 %collective-permute-start.7 = (bf16[64,2048]{1,0:T(8,128)(2,1)}, bf16[64,2048]{1,0:T(8,128)(2,1)S(1)}, u32[]{:S(2)}, u32[]{:S(2)}) collective-permute-start(bf16[64,2048]{1,0:T(8,128)(2,1)} %collective-permute-done.6), channel_id=1, source_target_pairs={{4,0},{5,1},{6,2},{7,3},{8,4},{9,5},{10,6},{11,7},{20,16},{21,17},... | collective-permute-start | bytes 786440 | tf_op jit(solution)/shard_map/ppermute | solution.py:192
  43.6 12.4 %collective-permute-start.18 = (bf16[64,2048]{1,0:T(8,128)(2,1)}, bf16[64,2048]{1,0:T(8,128)(2,1)S(1)}, u32[]{:S(2)}, u32[]{:S(2)}) collective-permute-start(bf16[64,2048]{1,0:T(8,128)(2,1)} %collective-permute-done.17), channel_id=1, source_target_pairs={{4,8},{5,9},{6,10},{7,11},{8,12},{9,13},{10,14},{11,15},{20,24},{2... | collective-permute-start | bytes 786440 | tf_op jit(solution)/shard_map/ppermute | solution.py:192
  44.3 16.7 %collective-permute-start.21 = (bf16[64,2048]{1,0:T(8,128)(2,1)}, bf16[64,2048]{1,0:T(8,128)(2,1)S(1)}, u32[]{:S(2)}, u32[]{:S(2)}) collective-permute-start(bf16[64,2048]{1,0:T(8,128)(2,1)} %collective-permute-done.20), channel_id=1, source_target_pairs={{4,0},{5,1},{6,2},{7,3},{8,4},{9,5},{10,6},{11,7},{20,16},{21,17},... | collective-permute-start | bytes 786440 | tf_op jit(solution)/shard_map/ppermute | solution.py:192
  52.1 10.4 %collective-permute-start.5 = (bf16[64,2048]{1,0:T(8,128)(2,1)S(1)}, bf16[64,2048]{1,0:T(8,128)(2,1)S(1)}, u32[]{:S(2)}, u32[]{:S(2)}) collective-permute-start(bf16[64,2048]{1,0:T(8,128)(2,1)S(1)} %collective-permute-done.3), channel_id=1, source_target_pairs={{8,12},{9,13},{10,14},{11,15},{24,28},{25,29},{26,30},{27,31}} | collective-permute-start | bytes 786440 | tf_op jit(solution)/shard_map/ppermute | solution.py:192
  54.7 12.1 %collective-permute-start.8 = (bf16[64,2048]{1,0:T(8,128)(2,1)S(1)}, bf16[64,2048]{1,0:T(8,128)(2,1)S(1)}, u32[]{:S(2)}, u32[]{:S(2)}) collective-permute-start(bf16[64,2048]{1,0:T(8,128)(2,1)S(1)} %collective-permute-done.7), channel_id=1, source_target_pairs={{4,0},{5,1},{6,2},{7,3},{20,16},{21,17},{22,18},{23,19}} | collective-permute-start | bytes 786440 | tf_op jit(solution)/shard_map/ppermute | solution.py:192
  56.0 11.0 %collective-permute-start.19 = (bf16[64,2048]{1,0:T(8,128)(2,1)S(1)}, bf16[64,2048]{1,0:T(8,128)(2,1)S(1)}, u32[]{:S(2)}, u32[]{:S(2)}) collective-permute-start(bf16[64,2048]{1,0:T(8,128)(2,1)S(1)} %collective-permute-done.18), channel_id=1, source_target_pairs={{8,12},{9,13},{10,14},{11,15},{24,28},{25,29},{26,30},{27,31}} | collective-permute-start | bytes 786440 | tf_op jit(solution)/shard_map/ppermute | solution.py:192
  61.0 10.6 %collective-permute-start.22 = (bf16[64,2048]{1,0:T(8,128)(2,1)S(1)}, bf16[64,2048]{1,0:T(8,128)(2,1)S(1)}, u32[]{:S(2)}, u32[]{:S(2)}) collective-permute-start(bf16[64,2048]{1,0:T(8,128)(2,1)S(1)} %collective-permute-done.21), channel_id=1, source_target_pairs={{4,0},{5,1},{6,2},{7,3},{20,16},{21,17},{22,18},{23,19}} | collective-permute-start | bytes 786440 | tf_op jit(solution)/shard_map/ppermute | solution.py:192
  71.7 1.3 copy-start.1
  73.1 39.7 %collective-permute-start.11 = (bf16[4,128,1024]{2,1,0:T(8,128)(2,1)}, bf16[4,128,1024]{2,1,0:T(8,128)(2,1)S(1)}, u32[]{:S(2)}, u32[]{:S(2)}) collective-permute-start(bf16[4,128,1024]{2,1,0:T(8,128)(2,1)} %pad_maximum_fusion.1), channel_id=1, source_target_pairs={{0,2},{1,3},{2,0},{3,1},{4,6},{5,7},{6,4},{7,5},{8,10},{9,11},{10,... | collective-permute-start | bytes 3145736 | tf_op jit(solution)/shard_map/ppermute | solution.py:187
  74.2 13.8 %collective-permute-start.9 = (bf16[1024,256]{1,0:T(8,128)(2,1)S(1)}, bf16[1024,256]{1,0:T(8,128)(2,1)}, u32[]{:S(2)}, u32[]{:S(2)}) collective-permute-start(bf16[1024,256]{1,0:T(8,128)(2,1)S(1)} %pad_maximum_fusion.2.refs_0_), channel_id=1, source_target_pairs={{0,4},{1,5},{2,6},{3,7},{4,8},{5,9},{6,10},{7,11},{8,12},{9,13},{1... | collective-permute-start | bytes 1572872 | tf_op jit(solution)/shard_map/ppermute | solution.py:192
  76.4 16.7 %collective-permute-start.10 = (bf16[1024,256]{1,0:T(8,128)(2,1)S(1)}, bf16[1024,256]{1,0:T(8,128)(2,1)S(1)}, u32[]{:S(2)}, u32[]{:S(2)}) collective-permute-start(bf16[1024,256]{1,0:T(8,128)(2,1)S(1)} %pad_maximum_fusion.2.refs_0_), channel_id=1, source_target_pairs={{4,0},{5,1},{6,2},{7,3},{8,4},{9,5},{10,6},{11,7},{12,8},{13,9},{1... | collective-permute-start | bytes 1572872 | tf_op jit(solution)/shard_map/ppermute | solution.py:192
  77.7 37.1 %collective-permute-start.23 = (bf16[1024,256]{1,0:T(8,128)(2,1)S(1)}, bf16[1024,256]{1,0:T(8,128)(2,1)}, u32[]{:S(2)}, u32[]{:S(2)}) collective-permute-start(bf16[1024,256]{1,0:T(8,128)(2,1)S(1)} %collective-permute-done.4.refs_4_), channel_id=1, source_target_pairs={{0,4},{1,5},{2,6},{3,7},{4,8},{5,9},{6,10},{7,11},{8,12},{9,13},{1... | collective-permute-start | bytes 1572872 | tf_op jit(solution)/shard_map/ppermute | solution.py:192
  83.1 32.4 %collective-permute-start.24 = (bf16[1024,256]{1,0:T(8,128)(2,1)S(1)}, bf16[1024,256]{1,0:T(8,128)(2,1)S(1)}, u32[]{:S(2)}, u32[]{:S(2)}) collective-permute-start(bf16[1024,256]{1,0:T(8,128)(2,1)S(1)} %collective-permute-done.4.refs_4_), channel_id=1, source_target_pairs={{4,0},{5,1},{6,2},{7,3},{8,4},{9,5},{10,6},{11,7},{12,8},{13,9},{1... | collective-permute-start | bytes 1572872 | tf_op jit(solution)/shard_map/ppermute | solution.py:192
  88.0 24.8 %collective-permute-start.12 = (s32[4,8]{1,0:T(4,128)S(1)}, s32[4,8]{1,0:T(4,128)S(1)}, u32[]{:S(2)}, u32[]{:S(2)}) collective-permute-start(s32[4,8]{1,0:T(4,128)S(1)} %pad_add_fusion.table_ref), channel_id=1, source_target_pairs={{0,2},{1,3},{2,0},{3,1},{4,6},{5,7},{6,4},{7,5},{8,10},{9,11},{10,... | collective-permute-start | bytes 392 | tf_op jit(solution)/shard_map/ppermute | solution.py:187
  112.8 4.2 %collective-permute-start.13 = (bf16[1024,256]{1,0:T(8,128)(2,1)}, bf16[1024,256]{1,0:T(8,128)(2,1)S(1)}, u32[]{:S(2)}, u32[]{:S(2)}) collective-permute-start(bf16[1024,256]{1,0:T(8,128)(2,1)} %collective-permute-done.9), channel_id=1, source_target_pairs={{4,8},{5,9},{6,10},{7,11},{8,12},{9,13},{10,14},{11,15},{20,24},{2... | collective-permute-start | bytes 1572872 | tf_op jit(solution)/shard_map/ppermute | solution.py:192
  113.5 16.8 %collective-permute-start.14 = (bf16[1024,256]{1,0:T(8,128)(2,1)S(1)}, bf16[1024,256]{1,0:T(8,128)(2,1)S(1)}, u32[]{:S(2)}, u32[]{:S(2)}) collective-permute-start(bf16[1024,256]{1,0:T(8,128)(2,1)S(1)} %collective-permute-done.10), channel_id=1, source_target_pairs={{4,0},{5,1},{6,2},{7,3},{8,4},{9,5},{10,6},{11,7},{20,16},{21,17},... | collective-permute-start | bytes 1572872 | tf_op jit(solution)/shard_map/ppermute | solution.py:192
  114.8 17.4 %collective-permute-start.25 = (bf16[1024,256]{1,0:T(8,128)(2,1)}, bf16[1024,256]{1,0:T(8,128)(2,1)S(1)}, u32[]{:S(2)}, u32[]{:S(2)}) collective-permute-start(bf16[1024,256]{1,0:T(8,128)(2,1)} %collective-permute-done.23), channel_id=1, source_target_pairs={{4,8},{5,9},{6,10},{7,11},{8,12},{9,13},{10,14},{11,15},{20,24},{2... | collective-permute-start | bytes 1572872 | tf_op jit(solution)/shard_map/ppermute | solution.py:192
  115.5 26.0 %collective-permute-start.26 = (bf16[1024,256]{1,0:T(8,128)(2,1)S(1)}, bf16[1024,256]{1,0:T(8,128)(2,1)S(1)}, u32[]{:S(2)}, u32[]{:S(2)}) collective-permute-start(bf16[1024,256]{1,0:T(8,128)(2,1)S(1)} %collective-permute-done.24), channel_id=1, source_target_pairs={{4,0},{5,1},{6,2},{7,3},{8,4},{9,5},{10,6},{11,7},{20,16},{21,17},... | collective-permute-start | bytes 1572872 | tf_op jit(solution)/shard_map/ppermute | solution.py:192
  130.3 12.8 %collective-permute-start.15 = (bf16[1024,256]{1,0:T(8,128)(2,1)S(1)}, bf16[1024,256]{1,0:T(8,128)(2,1)S(1)}, u32[]{:S(2)}, u32[]{:S(2)}) collective-permute-start(bf16[1024,256]{1,0:T(8,128)(2,1)S(1)} %collective-permute-done.13), channel_id=1, source_target_pairs={{8,12},{9,13},{10,14},{11,15},{24,28},{25,29},{26,30},{27,31}} | collective-permute-start | bytes 1572872 | tf_op jit(solution)/shard_map/ppermute | solution.py:192
  130.9 21.5 %collective-permute-start.16 = (bf16[1024,256]{1,0:T(8,128)(2,1)S(1)}, bf16[1024,256]{1,0:T(8,128)(2,1)S(1)}, u32[]{:S(2)}, u32[]{:S(2)}) collective-permute-start(bf16[1024,256]{1,0:T(8,128)(2,1)S(1)} %collective-permute-done.14), channel_id=1, source_target_pairs={{4,0},{5,1},{6,2},{7,3},{20,16},{21,17},{22,18},{23,19}} | collective-permute-start | bytes 1572872 | tf_op jit(solution)/shard_map/ppermute | solution.py:192
  132.3 20.2 %collective-permute-start.27 = (bf16[1024,256]{1,0:T(8,128)(2,1)S(1)}, bf16[1024,256]{1,0:T(8,128)(2,1)S(1)}, u32[]{:S(2)}, u32[]{:S(2)}) collective-permute-start(bf16[1024,256]{1,0:T(8,128)(2,1)S(1)} %collective-permute-done.25), channel_id=1, source_target_pairs={{8,12},{9,13},{10,14},{11,15},{24,28},{25,29},{26,30},{27,31}} | collective-permute-start | bytes 1572872 | tf_op jit(solution)/shard_map/ppermute | solution.py:192
  141.5 16.6 %collective-permute-start.28 = (bf16[1024,256]{1,0:T(8,128)(2,1)S(1)}, bf16[1024,256]{1,0:T(8,128)(2,1)S(1)}, u32[]{:S(2)}, u32[]{:S(2)}) collective-permute-start(bf16[1024,256]{1,0:T(8,128)(2,1)S(1)} %collective-permute-done.26), channel_id=1, source_target_pairs={{4,0},{5,1},{6,2},{7,3},{20,16},{21,17},{22,18},{23,19}} | collective-permute-start | bytes 1572872 | tf_op jit(solution)/shard_map/ppermute | solution.py:192
  143.0 15.3 %copy-start = (s32[4,4]{1,0:T(4,128)S(1)}, s32[4,4]{1,0:T(4,128)}, u32[]{:S(2)}) copy-start(s32[4,4]{1,0:T(4,128)} %constant.66.clone.order_ref) | copy-start | bytes 196
  158.3 11.9 %copy-start.2 = (bf16[2,128,1024]{2,1,0:T(8,128)(2,1)S(1)}, bf16[2,128,1024]{2,1,0:T(8,128)(2,1)}, u32[]{:S(2)}) copy-start(bf16[2,128,1024]{2,1,0:T(8,128)(2,1)} %get-tuple-element.118) | copy-start | bytes 1572868
  158.3 11.9 %copy-start.3 = (bf16[2,128,1024]{2,1,0:T(8,128)(2,1)S(1)}, bf16[2,128,1024]{2,1,0:T(8,128)(2,1)}, u32[]{:S(2)}) copy-start(bf16[2,128,1024]{2,1,0:T(8,128)(2,1)} %get-tuple-element.120) | copy-start | bytes 1572868
  167.5 26.4 %collective-permute-start.29 = (bf16[4,128,1024]{2,1,0:T(8,128)(2,1)S(1)}, bf16[4,128,1024]{2,1,0:T(8,128)(2,1)S(1)}, u32[]{:S(2)}, u32[]{:S(2)}) collective-permute-start(bf16[4,128,1024]{2,1,0:T(8,128)(2,1)S(1)} %shard_map.65), channel_id=1, source_target_pairs={{0,2},{1,3},{2,0},{3,1},{4,6},{5,7},{6,4},{7,5},{8,10},{9,11},{10,... | collective-permute-start | bytes 3145736 | tf_op jit(solution)/shard_map/ppermute | solution.py:187
  179.5 14.6 %collective-permute-start.30 = (bf16[2,128,1024]{2,1,0:T(8,128)(2,1)S(1)}, bf16[2,128,1024]{2,1,0:T(8,128)(2,1)S(1)}, u32[]{:S(2)}, u32[]{:S(2)}) collective-permute-start(bf16[2,128,1024]{2,1,0:T(8,128)(2,1)S(1)} %slice.34), channel_id=1, source_target_pairs={{0,1},{1,0},{2,3},{3,2},{4,5},{5,4},{6,7},{7,6},{8,9},{9,8},{10,11... | collective-permute-start | bytes 1572872 | tf_op jit(solution)/shard_map/ppermute | solution.py:182
  194.0 2.0 collective-permute-start.31
Sparse Core Ops, SparseCore 0:
  73.2 104.6 all-gather.1

commit v7 on v5

--- a/solution.py
+++ b/solution.py
@@ -18,6 +18,7 @@
 SCALE_LOG2 = HD ** (-0.5) * 1.4426950408889634
 NT = (((1,), (1,)), ((), ()))
 VMEM_LIMIT = 40 * 1024 * 1024
+PROJECT_TILE = 512
 
 
 def arrivals(n_outer):
@@ -33,21 +34,21 @@
     return rows
 
 
-def attention_kernel(n_chip, where_ref, order_ref, table_ref, q_ref, *refs):
-    n_outer = n_chip // 2
-    pieces, o_ref = refs[:-1], refs[-1]
+def attention_kernel(n_chip, slots, first, last, where_ref, order_ref, table_ref, q_ref, *refs):
+    count = 2 * len(slots)
+    pieces = refs[:count]
+    before, after = ((), refs[count:]) if first else (refs[count : count + 2], refs[count + 2 :])
     step = pl.program_id(0)
     head = pl.program_id(1)
     per_entry = n_chip // ENTRIES
     outer, side, core, asking = where_ref[0], where_ref[1], where_ref[2], where_ref[3]
-    chip = outer * 2 + asking
-    turn = jnp.where(step < 2, 0, core) + 2 * n_chip - chip
+    turn = jnp.where(step < 2, 0, core) + 2 * n_chip - (outer * 2 + asking)
     columns = pl.ds(pl.multiple_of(head * HD, HD), HD)
 
     keys, values, usable = [], [], []
     for at, piece in enumerate(pieces):
-        source_side = side if at < n_outer else 1 - side
-        source = order_ref[outer, at % n_outer] * 2 + source_side
+        source_side = side if at < len(slots) else 1 - side
+        source = order_ref[outer, slots[at % len(slots)]] * 2 + source_side
         ahead = lax.rem(source + turn, n_chip)
         row = table_ref[step, ahead // per_entry] & 3
         keys.append(piece[pl.ds(pl.multiple_of(row * QB, QB), QB), columns])
@@ -70,91 +71,122 @@
                 1,
             )
         scores.append(s)
-    rounded, totals = [], []
-    for s in scores:
-        weights = jnp.exp2((s - jnp.max(s, axis=-1, keepdims=True)) * SCALE_LOG2)
-        totals.append(jnp.sum(weights, axis=-1, keepdims=True))
+    rounded, totals, highs, factors = [], [], [], []
+    for g, s in enumerate(scores):
+        high = jnp.max(s, axis=-1, keepdims=True)
+        if not first:
+            known = before[1][0, :, g * HD : g * HD + 1]
+            high = jnp.maximum(high, known)
+            factors.append(jnp.exp2((known - high) * SCALE_LOG2))
+        weights = jnp.exp2((s - high) * SCALE_LOG2)
+        total = jnp.sum(weights, axis=-1, keepdims=True)
+        if not first:
+            total += before[1][0, :, g * HD + HD // 2 : g * HD + HD // 2 + 1] * factors[g]
+        highs.append(high)
+        totals.append(total)
         rounded.append(weights.astype(jnp.bfloat16))
+    left = lax.broadcasted_iota(jnp.int32, (QB, HD), 1) < HD // 2
     for g in range(GROUP):
+        at = slice(g * HD, (g + 1) * HD)
         mixed = jnp.dot(rounded[g], values, preferred_element_type=jnp.float32)
-        o_ref[0, :, g * HD : (g + 1) * HD] = (mixed / totals[g]).astype(jnp.bfloat16)
-
-
-def attention(queries, where, order, table, pieces, n_chip):
+        if not first:
+            mixed += before[0][0, :, at] * factors[g]
+        if last:
+            after[0][0, :, at] = (mixed / totals[g]).astype(jnp.bfloat16)
+        else:
+            after[0][0, :, at] = mixed
+            after[1][0, :, at] = jnp.where(left, highs[g], totals[g])
+
+
+def attention(queries, where, order, table, pieces, slots, n_chip, state=None, last=True):
     width = GROUP * HD
     blocks, _, columns = queries.shape
     rows = len(pieces) * QB
     whole = pl.BlockSpec(memory_space=pltpu.VMEM)
     tile = pl.BlockSpec((1, QB, width), lambda b, h, *_: (b, 0, h))
+    state_shape = jax.ShapeDtypeStruct(queries.shape, jnp.float32)
+    done_shape = jax.ShapeDtypeStruct(queries.shape, jnp.bfloat16)
     return pl.pallas_call(
-        functools.partial(attention_kernel, n_chip),
-        out_shape=jax.ShapeDtypeStruct(queries.shape, jnp.bfloat16),
+        functools.partial(attention_kernel, n_chip, slots, state is None, last),
+        out_shape=done_shape if last else (state_shape, state_shape),
         grid_spec=pltpu.PrefetchScalarGridSpec(
             num_scalar_prefetch=3,
             grid=(blocks, columns // width),
-            in_specs=[tile] + [whole] * len(pieces),
-            out_specs=tile,
+            in_specs=[tile] + [whole] * len(pieces) + [tile] * (0 if state is None else 2),
+            out_specs=tile if last else (tile, tile),
         ),
         compiler_params=pltpu.CompilerParams(vmem_limit_bytes=VMEM_LIMIT),
         cost_estimate=pl.CostEstimate(
             flops=4 * blocks * QB * rows * columns,
-            bytes_accessed=2 * blocks * (rows * columns // 2 + 2 * QB * columns),
+            bytes_accessed=2 * blocks * (rows * columns // 2 + 6 * QB * columns),
             transcendentals=blocks * QB * rows * columns // HD,
         ),
-    )(where, order, table, queries, *pieces)
-
-
-def project_kernel(
-    n_outer, where_ref, near_ref, across_ref, far_ref, far_across_ref, w_ref, o_ref, rows
-):
+    )(where, order, table, queries, *pieces, *(state or ()))
+
+
+def lay_out_kernel(n_outer, where_ref, near_ref, across_ref, far_ref, far_across_ref, rows):
     side = where_ref[1]
-
-    @pl.when((pl.program_id(0) == 0) & (pl.program_id(1) == 0))
-    def _():
-        heads = H // 2
-        for block in range(2):
-            even = slice(2 * block * QB, (2 * block + 1) * QB)
-            odd = slice((2 * block + 1) * QB, (2 * block + 2) * QB)
-            for which, even_ref, odd_ref in (
-                (side, near_ref, far_ref),
-                (1 - side, across_ref, far_across_ref),
-            ):
-                for h in range(heads):
-                    at = slice(h * HD, (h + 1) * HD)
-                    if n_outer:
-                        to = (h % 4) * n_outer + h // 4 + which * (heads // 4)
-                    else:
-                        to = h + which * heads
-                    to = pl.ds(pl.multiple_of(to * HD, HD), HD)
-                    rows[even, to] = even_ref[block, :, at]
-                    rows[odd, to] = odd_ref[block, :, at]
-
+    heads = H // 2
+    for block in range(2):
+        even = slice(2 * block * QB, (2 * block + 1) * QB)
+        odd = slice((2 * block + 1) * QB, (2 * block + 2) * QB)
+        for which, even_ref, odd_ref in (
+            (side, near_ref, far_ref),
+            (1 - side, across_ref, far_across_ref),
+        ):
+            for h in range(heads):
+                at = slice(h * HD, (h + 1) * HD)
+                if n_outer:
+                    to = (h % 4) * n_outer + h // 4 + which * (heads // 4)
+                else:
+                    to = h + which * heads
+                to = pl.ds(pl.multiple_of(to * HD, HD), HD)
+                rows[even, to] = even_ref[block, :, at]
+                rows[odd, to] = odd_ref[block, :, at]
+
+
+def lay_out(n_outer, where, near, across, far, far_across):
+    half = pl.BlockSpec((2, QB, near.shape[-1]), lambda i, *_: (0, 0, 0))
+    return pl.pallas_call(
+        functools.partial(lay_out_kernel, n_outer),
+        out_shape=jax.ShapeDtypeStruct((4 * QB, H * HD), jnp.bfloat16),
+        grid_spec=pltpu.PrefetchScalarGridSpec(
+            num_scalar_prefetch=1,
+            grid=(1,),
+            in_specs=[half] * 4,
+            out_specs=pl.BlockSpec((4 * QB, H * HD), lambda i, *_: (0, 0)),
+        ),
+        compiler_params=pltpu.CompilerParams(vmem_limit_bytes=VMEM_LIMIT),
+    )(where, near, across, far, far_across)
+
+
+def project_kernel(rows_ref, w_ref, o_ref):
     o_ref[...] = jnp.dot(
-        rows[...], w_ref[0], preferred_element_type=jnp.float32
+        rows_ref[...], w_ref[0], preferred_element_type=jnp.float32
     ).astype(jnp.bfloat16)
 
 
-def project(n_outer, where, near, across, far, far_across, weights, tile=512):
+def project(rows, weights, tile=PROJECT_TILE):
     parts, depth, columns = weights.shape
     tiles = columns // tile
-    half = pl.BlockSpec((2, QB, depth // 2), lambda p, t, *_: (0, 0, 0))
     return pl.pallas_call(
-        functools.partial(project_kernel, n_outer),
-        out_shape=jax.ShapeDtypeStruct((4 * QB, parts * columns), jnp.bfloat16),
-        grid_spec=pltpu.PrefetchScalarGridSpec(
-            num_scalar_prefetch=1,
+        project_kernel,
+        out_shape=jax.ShapeDtypeStruct((rows.shape[0], parts * columns), jnp.bfloat16),
+        grid_spec=pl.GridSpec(
             grid=(parts, tiles),
-            in_specs=[half] * 4 + [pl.BlockSpec((1, depth, tile), lambda p, t, *_: (p, 0, t))],
-            out_specs=pl.BlockSpec((4 * QB, tile), lambda p, t, *_: (0, p * tiles + t)),
-            scratch_shapes=[pltpu.VMEM((4 * QB, depth), jnp.bfloat16)],
+            in_specs=[
+                pl.BlockSpec(rows.shape, lambda p, t: (0, 0)),
+                pl.BlockSpec((1, depth, tile), lambda p, t: (p, 0, t)),
+            ],
+            out_specs=pl.BlockSpec((rows.shape[0], tile), lambda p, t: (0, p * tiles + t)),
         ),
         compiler_params=pltpu.CompilerParams(vmem_limit_bytes=VMEM_LIMIT),
         cost_estimate=pl.CostEstimate(
-            flops=2 * 4 * QB * depth * parts * columns,
-            bytes_accessed=2 * (depth * parts * columns + 4 * QB * (depth + parts * columns)),
+            flops=2 * rows.shape[0] * depth * parts * columns,
+            bytes_accessed=2 * (depth * parts * columns + rows.shape[0] * (depth + parts * columns)),
             transcendentals=0,
         ),
-    )(where, near, across, far, far_across, weights)
+    )(rows, weights)
 
 
 LINE = "outer"
@@ -199,11 +231,17 @@
             ],
         )
 
-    def line(array):
+    def after(array, *others):
+        return lax.optimization_barrier((array, *others))[0]
+
+    def line(array, gates={}):
         got = {0: array}
         for hop in range(1, n_outer):
             for way in (1, -1):
-                got[-way * hop] = move(got[-way * (hop - 1)], hop, way)
+                sent = got[-way * (hop - 1)]
+                if hop in gates:
+                    sent = after(sent, *gates[hop])
+                got[-way * hop] = move(sent, hop, way)
         return got
 
     def pick(got, k):
@@ -217,9 +255,6 @@
                 result = jnp.where(mask, got[offset], result)
         return result
 
-    def after(array, *others):
-        return lax.optimization_barrier((array, *others))[0]
-
     def half_of(array, which):
         width = array.shape[-1] // 2
         return lax.dynamic_slice_in_dim(array, which * width, width, array.ndim - 1)
@@ -245,7 +280,7 @@
     across_table = swap_side(table)
 
     gathered = after(gathered, theirs, across_queries, across_table)
-    mine, theirs = after(mine, gathered), after(theirs, gathered)
+    gates = ({2: (gathered,)}, {1: (gathered,)})
     gathered = lax.all_gather(gathered, PLANE, axis=0, tiled=True)
     held = out_weight.shape[0]
     order_of_rows = n_outer
@@ -255,21 +290,30 @@
         order_of_rows = 0
     gathered = gathered.reshape(n_groups, H * HD, part)
 
-    pieces = []
-    for chain in (mine, theirs):
-        got = line(chain)
+    early, late = [], []
+    for chain, gate in zip((mine, theirs), gates):
+        got = line(chain, gate)
         near = [got[0]]
         for k in range(1, n_outer):
             tied = {d: after(got[d], near[-1]) for d in sorted({row[k] for row in order_rows})}
             near.append(pick(tied, k))
-        pieces += near
-
-    across = attention(across_queries, where_across, order, across_table, pieces, n_chip)
+        early += near[:-1]
+        late += near[-1:]
+
+    asks = (
+        (across_queries, where_across, order, across_table),
+        (my_blocks(side), where, order, table),
+    )
+    slots = tuple(range(n_outer))
+    states = [attention(*ask, early, slots[:-1], n_chip, last=False) for ask in asks]
+    across, near = (
+        attention(*ask, late, slots[-1:], n_chip, state) for ask, state in zip(asks, states)
+    )
     across = swap_side(across)
-    near = attention(my_blocks(side), where, order, table, pieces, n_chip)
     far = swap_core(near[2:])
     far_across = swap_core(across[2:])
-    return project(order_of_rows, where, near, across, far, far_across, gathered)
+    rows = lay_out(order_of_rows, where, near, across, far, far_across)
+    return project(rows, gathered)
 
 
 def solution(mesh):

time: 194 us -> 193 us (level)
  Pallas kernels: 34 us -> 48.7 us
  waiting for transfers between devices: 103 us -> 89.3 us
  starting transfers between devices: 28.4 us -> 26.2 us
    pallas_call x3 -> x6, Pallas kernels: 34 us -> 48.7 us  [the longest x4 33.3 us: attention(): pl.pallas_call(functools.partial(attention_kernel, n_chip, slots, state i...]
    ppermute x4, waiting for transfers between devices: 47.6 us -> 37.1 us  [swap_side(): lax.ppermute(array, SEQ, [(index(o, s, c), index(o, 1 - s, c)) for o, s,...]
    ppermute x12, waiting for transfers between devices: 46.9 us -> 44 us  [move(): lax.ppermute(array, SEQ, [(index(o, s, c), index(o + way, s, c)) for o, s...]
    ppermute x12, starting transfers between devices: 21.2 us -> 19.1 us  [move(): lax.ppermute(array, SEQ, [(index(o, s, c), index(o + way, s, c)) for o, s...]
  transfers between devices with their start and end apart: 22 -> 22, of which waited for: 13 -> 13; matrix products, arithmetic and copies ran while one was open for 6% -> 6% of each run, Pallas kernels for 10% -> 18%
where the time goes in v7:
time: 193 us; the launch traced here: 192 us
  waiting for transfers between devices  89.3 us (46%)
  Pallas kernels  48.7 us (25%)
  starting transfers between devices  26.2 us (14%)
  between operations  13.6 us (7%)
  local copies, waits for them, and re-layouts  8.63 us (4%)
  other arithmetic  5.85 us (3%)
    ppermute x12, waiting for transfers between devices, move(): lax.ppermute(array, SEQ, [(index(o, s, c), index(o + way, s, c)) for o, s...  44 us
    ppermute x4, waiting for transfers between devices, swap_side(): lax.ppermute(array, SEQ, [(index(o, s, c), index(o, 1 - s, c)) for o, s,...  37.1 us
    pallas_call x4, Pallas kernels, attention(): pl.pallas_call(functools.partial(attention_kernel, n_chip, slots, state i...  33.3 us
    ppermute x12, starting transfers between devices, move(): lax.ppermute(array, SEQ, [(index(o, s, c), index(o + way, s, c)) for o, s...  19.1 us
    pallas_call x1, Pallas kernels, project(): pl.pallas_call(project_kernel, out_shape=jax.ShapeDtypeStruct((rows.shape...  14.4 us
    ppermute x4, starting transfers between devices, swap_side(): lax.ppermute(array, SEQ, [(index(o, s, c), index(o, 1 - s, c)) for o, s,...  6.51 us
    ppermute x4, waiting for transfers between devices, swap_core(): lax.ppermute(array, SEQ, [(index(o, s, c), index(o, s, 1 - c)) for o, s,...  4.63 us
  transfers between devices with their start and end apart: 22, of which 13 were waited for; matrix products, arithmetic and copies ran while one was open for 6% of the time, Pallas kernels for 18%

profile of v7, /device:TPU:0, one launch (start us, length us, event | category | flops | bytes accessed | tf_op | source)
XLA Modules:
  0.0 192.3 jit_solution(16296761677829252497)
XLA Ops:
  6.5 1.2 copy-done
  7.8 0.8 constant_dynamic-slice_fusion.3
  8.6 0.0 all-gather.3.cloned.1.call-update
  8.6 0.0 all-gather.5.cloned.1.call-start
  8.7 2.7 %fusion = (bf16[2,1,128,2048]{3,2,1,0:T(8,128)(2,1)S(1)}, bf16[2,128,2048]{2,1,0:T(8,128)(2,1)}) fusion(bf16[2,2,128,2048]{3,2,1,0:T(8,128)(2,1)} %bitcast.14), kind=kLoop, calls=%fused_computation.24 | loop fusion | bytes 4194304 | tf_op jit(solution)/shard_map/slice | solution.py:274
  11.4 0.5 collective-permute-start.1
  11.8 0.9 dynamic-slice_bitcast_fusion
  12.7 1.6 collective-permute-done.1
  14.3 0.9 constant_dynamic-slice_fusion
  15.2 1.1 pad_maximum_fusion.1
  16.3 2.9 %collective-permute-start.4 = (bf16[4,128,1024]{2,1,0:T(8,128)(2,1)}, bf16[4,128,1024]{2,1,0:T(8,128)(2,1)S(1)}, u32[]{:S(2)}, u32[]{:S(2)}) collective-permute-start(bf16[4,128,1024]{2,1,0:T(8,128)(2,1)} %pad_maximum_fusion.1), channel_id=1, source_target_pairs={{0,2},{1,3},{2,0},{3,1},{4,6},{5,7},{6,4},{7,5},{8,10},{9,11},{10,... | collective-permute-start | bytes 3145736 | tf_op jit(solution)/shard_map/ppermute | solution.py:219
  19.2 2.0 %constant_dynamic-slice_fusion.1 = (bf16[512,256]{1,0:T(8,128)(2,1)S(1)}, bf16[512,256]{1,0:T(8,128)(2,1)S(1)}, bf16[512,256]{1,0:T(8,128)(2,1)}, bf16[512,256]{1,0:T(8,128)(2,1)S(1)}) fusion(bf16[512,512]{1,0:T(8,128)(2,1)} %param.8, s32[]{:T(128)S(6)} %select_n.83, s32[]{:T(128)S(6)} %select_n.81, bf16[512,512]{1,0:T(8,128)(2,1)} %param.7), kind=kLoop, calls=%fused_computation.14 | loop fusion | bytes 2097160 | tf_op jit(solution)/shard_map/dynamic_slice | solution.py:260
  21.1 0.8 pad_maximum_fusion.3
  22.0 0.1 collective-permute-start.3
  22.0 0.0 collective-permute-start
  22.1 1.1 collective-permute-done
  23.2 2.0 %collective-permute-start.5 = (s32[4,8]{1,0:T(4,128)S(1)}, s32[4,8]{1,0:T(4,128)S(1)}, u32[]{:S(2)}, u32[]{:S(2)}) collective-permute-start(s32[4,8]{1,0:T(4,128)S(1)} %pad_add_fusion.table_ref), channel_id=1, source_target_pairs={{0,2},{1,3},{2,0},{3,1},{4,6},{5,7},{6,4},{7,5},{8,10},{9,11},{10,... | collective-permute-start | bytes 392 | tf_op jit(solution)/shard_map/ppermute | solution.py:219
  25.3 28.9 %collective-permute-done.5.table_ref = s32[4,8]{1,0:T(4,128)S(1)} collective-permute-done((s32[4,8]{1,0:T(4,128)S(1)}, s32[4,8]{1,0:T(4,128)S(1)}, u32[]{:S(2)}, u32[]{:S(2)}) %collective-permute-start.5) | collective-permute-done | bytes 160 | tf_op jit(solution)/shard_map/ppermute | solution.py:219
  54.1 3.5 %all-gather.3.cloned.1.call-done = bf16[512,2048]{1,0:T(8,128)(2,1)} async-done(((bf16[128,2048]{1,0:T(8,128)(2,1)}), bf16[512,2048]{1,0:T(8,128)(2,1)}) %all-gather.3.cloned.1.call-update) | async-done | bytes 2097168 | tf_op jit(solution)/shard_map/all_gather | solution.py:264
  57.6 0.0 all-gather.5.cloned.1.call-update
  57.6 1.0 pad_maximum_fusion.2.refs_0_
  58.6 2.6 %collective-permute-start.7 = (bf16[1024,256]{1,0:T(8,128)(2,1)S(1)}, bf16[1024,256]{1,0:T(8,128)(2,1)}, u32[]{:S(2)}, u32[]{:S(2)}) collective-permute-start(bf16[1024,256]{1,0:T(8,128)(2,1)S(1)} %pad_maximum_fusion.2.refs_0_), channel_id=1, source_target_pairs={{0,4},{1,5},{2,6},{3,7},{4,8},{5,9},{6,10},{7,11},{8,12},{9,13},{1... | collective-permute-start | bytes 1572872 | tf_op jit(solution)/shard_map/ppermute | solution.py:224
  61.2 1.3 collective-permute-start.2
  62.5 1.3 collective-permute-start.11
  63.8 6.0 %collective-permute-start.13 = (bf16[1024,256]{1,0:T(8,128)(2,1)S(1)}, bf16[1024,256]{1,0:T(8,128)(2,1)}, u32[]{:S(2)}, u32[]{:S(2)}) collective-permute-start(bf16[1024,256]{1,0:T(8,128)(2,1)S(1)} %collective-permute-done.3.refs_3_), channel_id=1, source_target_pairs={{0,4},{1,5},{2,6},{3,7},{4,8},{5,9},{6,10},{7,11},{8,12},{9,13},{1... | collective-permute-start | bytes 1572872 | tf_op jit(solution)/shard_map/ppermute | solution.py:224
  69.8 0.1 pad_add_fusion.3
  69.9 2.9 %collective-permute-done.7 = bf16[1024,256]{1,0:T(8,128)(2,1)} collective-permute-done((bf16[1024,256]{1,0:T(8,128)(2,1)S(1)}, bf16[1024,256]{1,0:T(8,128)(2,1)}, u32[]{:S(2)}, u32[]{:S(2)}) %collective-permute-start.7) | collective-permute-done | bytes 524320 | tf_op jit(solution)/shard_map/ppermute | solution.py:224
  72.8 5.3 %collective-permute-done.2 = bf16[1024,256]{1,0:T(8,128)(2,1)} collective-permute-done((bf16[1024,256]{1,0:T(8,128)(2,1)S(1)}, bf16[1024,256]{1,0:T(8,128)(2,1)}, u32[]{:S(2)}, u32[]{:S(2)}) %collective-permute-start.2) | collective-permute-done | bytes 524320 | tf_op jit(solution)/shard_map/ppermute | solution.py:224
  78.1 1.3 collective-permute-start.6
  79.4 0.7 collective-permute-start.8
  80.1 1.1 broadcast_select_fusion.1.refs_1_
  81.2 8.1 %collective-permute-done.11 = bf16[1024,256]{1,0:T(8,128)(2,1)} collective-permute-done((bf16[1024,256]{1,0:T(8,128)(2,1)S(1)}, bf16[1024,256]{1,0:T(8,128)(2,1)}, u32[]{:S(2)}, u32[]{:S(2)}) %collective-permute-start.11) | collective-permute-done | bytes 524320 | tf_op jit(solution)/shard_map/ppermute | solution.py:224
  89.3 0.0 collective-permute-done.13
  89.3 1.3 collective-permute-start.12
  90.6 0.7 collective-permute-start.14
  91.3 1.1 broadcast_select_fusion.refs_4_
  92.4 0.0 copy-start.1
  92.4 8.0 %collective-permute-done.6 = bf16[1024,256]{1,0:T(8,128)(2,1)S(1)} collective-permute-done((bf16[1024,256]{1,0:T(8,128)(2,1)}, bf16[1024,256]{1,0:T(8,128)(2,1)S(1)}, u32[]{:S(2)}, u32[]{:S(2)}) %collective-permute-start.6) | collective-permute-done | bytes 524320 | tf_op jit(solution)/shard_map/ppermute | solution.py:224
  100.4 0.0 collective-permute-done.8
  100.4 1.3 collective-permute-start.10
  101.7 0.7 collective-permute-start.9
  102.4 0.1 select_select_fusion.3.refs_2_
  102.6 9.1 %collective-permute-done.12 = bf16[1024,256]{1,0:T(8,128)(2,1)S(1)} collective-permute-done((bf16[1024,256]{1,0:T(8,128)(2,1)}, bf16[1024,256]{1,0:T(8,128)(2,1)S(1)}, u32[]{:S(2)}, u32[]{:S(2)}) %collective-permute-start.12) | collective-permute-done | bytes 524320 | tf_op jit(solution)/shard_map/ppermute | solution.py:224
  111.7 1.3 collective-permute-start.16
  113.0 0.7 collective-permute-start.15
  113.7 0.1 select_select_fusion.1.refs_5_
  113.8 9.1 %collective-permute-done.10 = bf16[1024,256]{1,0:T(8,128)(2,1)S(1)} collective-permute-done((bf16[1024,256]{1,0:T(8,128)(2,1)S(1)}, bf16[1024,256]{1,0:T(8,128)(2,1)S(1)}, u32[]{:S(2)}, u32[]{:S(2)}) %collective-permute-start.10) | collective-permute-done | bytes 524320 | tf_op jit(solution)/shard_map/ppermute | solution.py:224
  122.9 7.9 %shard_map.66 = (f32[4,128,1024]{2,1,0:T(8,128)S(1)}, f32[4,128,1024]{2,1,0:T(8,128)S(1)}) custom-call(s32[4]{0:T(128)S(1)} %get-tuple-element.57.where_ref, s32[4,4]{1,0:T(4,128)S(1)} %copy-done.1, s32[4,8]{1,0:T(4,128)S(1)} %collective-permute-done.5.table_ref, bf16[4,128,1024]{2,1,0:T(8,128)(2,1)S(1)} %collective-permute-done.4.q_ref, ...), custom_call_target="tpu_custom_call" | custom-call | flops 1610612736 | bytes 9437184 | tf_op jit(solution)/shard_map/pallas_call | solution.py:109
  130.8 0.1 select_select_fusion.2.refs_0_
  130.9 1.5 collective-permute-done.16
  132.4 0.1 select_select_fusion.refs_1_
  132.6 8.7 %shard_map.67 = bf16[4,128,1024]{2,1,0:T(8,128)(2,1)S(1)} custom-call(s32[4]{0:T(128)S(1)} %get-tuple-element.57.where_ref, s32[4,4]{1,0:T(4,128)S(1)} %copy-done.1, s32[4,8]{1,0:T(4,128)S(1)} %collective-permute-done.5.table_ref, bf16[4,128,1024]{2,1,0:T(8,128)(2,1)S(1)} %collective-permute-done.4.q_ref, bf16[1024,256]{1,0:T(8,128)(2,1)S(1)} %select_select_fusion.2.refs_0_, ...), custom_call_target="tpu_custom_call" | custom-call | flops 536870912 | bytes 7340032 | tf_op jit(solution)/shard_map/pallas_call | solution.py:109
  141.3 1.5 collective-permute-start.17
  142.8 0.1 pad_add_fusion.1.where_ref
  142.9 0.1 pad_maximum_fusion.q_ref
  143.0 7.9 %shard_map.64 = (f32[4,128,1024]{2,1,0:T(8,128)S(1)}, f32[4,128,1024]{2,1,0:T(8,128)S(1)}) custom-call(s32[4]{0:T(128)S(1)} %pad_add_fusion.1.where_ref, s32[4,4]{1,0:T(4,128)S(1)} %copy-done.1, s32[4,8]{1,0:T(4,128)S(1)} %pad_add_fusion.table_ref, bf16[4,128,1024]{2,1,0:T(8,128)(2,1)S(1)} %pad_maximum_fusion.q_ref, ...), custom_call_target="tpu_custom_call" | custom-call | flops 1610612736 | bytes 9437184 | tf_op jit(solution)/shard_map/pallas_call | solution.py:109
  150.9 8.7 %shard_map.65.near_ref = bf16[4,128,1024]{2,1,0:T(8,128)(2,1)S(1)} custom-call(s32[4]{0:T(128)S(1)} %pad_add_fusion.1.where_ref, s32[4,4]{1,0:T(4,128)S(1)} %copy-done.1, s32[4,8]{1,0:T(4,128)S(1)} %pad_add_fusion.table_ref, bf16[4,128,1024]{2,1,0:T(8,128)(2,1)S(1)} %pad_maximum_fusion.q_ref, bf16[1024,256]{1,0:T(8,128)(2,1)S(1)} %select_select_fusion.2.refs_0_, ...), custom_call_target="tpu_custom_call" | custom-call | flops 536870912 | bytes 7340032 | tf_op jit(solution)/shard_map/pallas_call | solution.py:109
  159.7 0.1 collective-permute-start.18
  159.8 8.2 %collective-permute-done.17.across_ref = bf16[4,128,1024]{2,1,0:T(8,128)(2,1)S(1)} collective-permute-done((bf16[4,128,1024]{2,1,0:T(8,128)(2,1)S(1)}, bf16[4,128,1024]{2,1,0:T(8,128)(2,1)S(1)}, u32[]{:S(2)}, u32[]{:S(2)}) %collective-permute-start.17) | collective-permute-done | bytes 1048608 | tf_op jit(solution)/shard_map/ppermute | solution.py:219
  168.0 0.1 collective-permute-start.19
  168.1 1.9 collective-permute-done.19.far_across_ref
  170.0 1.0 shard_map.68.rows_ref
  171.0 0.0 all-gather.5.cloned.1.call-done
  171.1 14.4 %shard_map.69 = bf16[512,4096]{1,0:T(8,128)(2,1)} custom-call(bf16[512,2048]{1,0:T(8,128)(2,1)S(1)} %shard_map.68.rows_ref, bf16[2,2048,2048]{2,1,0:T(8,128)(2,1)} %bitcast.15), custom_call_target="tpu_custom_call" | custom-call | flops 8589934592 | bytes 23068672 | tf_op jit(solution)/shard_map/pallas_call | solution.py:172
  (20 shorter events, 0.2 us)
Async XLA Ops:
  6.5 1.2 copy-start
  6.5 51.1 %all-gather.3.cloned.1.call-start = ((), (), s32[]{:S(2)}) async-start(), calls=%async_computation | async-start | bytes 2621440 | tf_op jit(solution)/shard_map/all_gather | solution.py:264
  8.6 162.5 %all-gather.5.cloned.1.call-start = ((), (), s32[]{:S(2)}) async-start(), calls=%async_computation.1 | async-start | bytes 18874368 | tf_op jit(solution)/shard_map/all_gather | solution.py:284
  11.4 3.0 %collective-permute-start.1 = (bf16[2,128,2048]{2,1,0:T(8,128)(2,1)}, bf16[2,128,2048]{2,1,0:T(8,128)(2,1)S(1)}, u32[]{:S(2)}, u32[]{:S(2)}) collective-permute-start(bf16[2,128,2048]{2,1,0:T(8,128)(2,1)} %get-tuple-element.60), channel_id=1, source_target_pairs={{0,1},{1,0},{2,3},{3,2},{4,5},{5,4},{6,7},{7,6},{8,9},{9,8},{10,11... | collective-permute-start | bytes 3145736 | tf_op jit(solution)/shard_map/ppermute | solution.py:214
  16.3 5.7 %copy-start.4 = (s32[4,8]{1,0:T(4,128)S(1)}, s32[4,8]{1,0:T(4,128)}, u32[]{:S(2)}) copy-start(s32[4,8]{1,0:T(4,128)} %param.9) | copy-start | bytes 388
  16.3 37.8 %collective-permute-start.4 = (bf16[4,128,1024]{2,1,0:T(8,128)(2,1)}, bf16[4,128,1024]{2,1,0:T(8,128)(2,1)S(1)}, u32[]{:S(2)}, u32[]{:S(2)}) collective-permute-start(bf16[4,128,1024]{2,1,0:T(8,128)(2,1)} %pad_maximum_fusion.1), channel_id=1, source_target_pairs={{0,2},{1,3},{2,0},{3,1},{4,6},{5,7},{6,4},{7,5},{8,10},{9,11},{10,... | collective-permute-start | bytes 3145736 | tf_op jit(solution)/shard_map/ppermute | solution.py:219
  22.0 32.2 %collective-permute-start.3 = (bf16[1024,256]{1,0:T(8,128)(2,1)}, bf16[1024,256]{1,0:T(8,128)(2,1)S(1)}, u32[]{:S(2)}, u32[]{:S(2)}) collective-permute-start(bf16[1024,256]{1,0:T(8,128)(2,1)} %pad_maximum_fusion.3), channel_id=1, source_target_pairs={{0,2},{1,3},{2,0},{3,1},{4,6},{5,7},{6,4},{7,5},{8,10},{9,11},{10,... | collective-permute-start | bytes 1572872 | tf_op jit(solution)/shard_map/ppermute | solution.py:219
  22.0 1.2 collective-permute-start
  23.2 30.9 %collective-permute-start.5 = (s32[4,8]{1,0:T(4,128)S(1)}, s32[4,8]{1,0:T(4,128)S(1)}, u32[]{:S(2)}, u32[]{:S(2)}) collective-permute-start(s32[4,8]{1,0:T(4,128)S(1)} %pad_add_fusion.table_ref), channel_id=1, source_target_pairs={{0,2},{1,3},{2,0},{3,1},{4,6},{5,7},{6,4},{7,5},{8,10},{9,11},{10,... | collective-permute-start | bytes 392 | tf_op jit(solution)/shard_map/ppermute | solution.py:219
  58.6 14.2 %collective-permute-start.7 = (bf16[1024,256]{1,0:T(8,128)(2,1)S(1)}, bf16[1024,256]{1,0:T(8,128)(2,1)}, u32[]{:S(2)}, u32[]{:S(2)}) collective-permute-start(bf16[1024,256]{1,0:T(8,128)(2,1)S(1)} %pad_maximum_fusion.2.refs_0_), channel_id=1, source_target_pairs={{0,4},{1,5},{2,6},{3,7},{4,8},{5,9},{6,10},{7,11},{8,12},{9,13},{1... | collective-permute-start | bytes 1572872 | tf_op jit(solution)/shard_map/ppermute | solution.py:224
  61.2 16.8 %collective-permute-start.2 = (bf16[1024,256]{1,0:T(8,128)(2,1)S(1)}, bf16[1024,256]{1,0:T(8,128)(2,1)}, u32[]{:S(2)}, u32[]{:S(2)}) collective-permute-start(bf16[1024,256]{1,0:T(8,128)(2,1)S(1)} %pad_maximum_fusion.2.refs_0_), channel_id=1, source_target_pairs={{4,0},{5,1},{6,2},{7,3},{8,4},{9,5},{10,6},{11,7},{12,8},{13,9},{1... | collective-permute-start | bytes 1572872 | tf_op jit(solution)/shard_map/ppermute | solution.py:224
  62.5 26.8 %collective-permute-start.11 = (bf16[1024,256]{1,0:T(8,128)(2,1)S(1)}, bf16[1024,256]{1,0:T(8,128)(2,1)}, u32[]{:S(2)}, u32[]{:S(2)}) collective-permute-start(bf16[1024,256]{1,0:T(8,128)(2,1)S(1)} %collective-permute-done.3.refs_3_), channel_id=1, source_target_pairs={{4,0},{5,1},{6,2},{7,3},{8,4},{9,5},{10,6},{11,7},{12,8},{13,9},{1... | collective-permute-start | bytes 1572872 | tf_op jit(solution)/shard_map/ppermute | solution.py:224
  63.8 25.5 %collective-permute-start.13 = (bf16[1024,256]{1,0:T(8,128)(2,1)S(1)}, bf16[1024,256]{1,0:T(8,128)(2,1)}, u32[]{:S(2)}, u32[]{:S(2)}) collective-permute-start(bf16[1024,256]{1,0:T(8,128)(2,1)S(1)} %collective-permute-done.3.refs_3_), channel_id=1, source_target_pairs={{0,4},{1,5},{2,6},{3,7},{4,8},{5,9},{6,10},{7,11},{8,12},{9,13},{1... | collective-permute-start | bytes 1572872 | tf_op jit(solution)/shard_map/ppermute | solution.py:224
  78.1 22.4 %collective-permute-start.6 = (bf16[1024,256]{1,0:T(8,128)(2,1)}, bf16[1024,256]{1,0:T(8,128)(2,1)S(1)}, u32[]{:S(2)}, u32[]{:S(2)}) collective-permute-start(bf16[1024,256]{1,0:T(8,128)(2,1)} %collective-permute-done.2), channel_id=1, source_target_pairs={{4,0},{5,1},{6,2},{7,3},{8,4},{9,5},{10,6},{11,7},{20,16},{21,17},... | collective-permute-start | bytes 1572872 | tf_op jit(solution)/shard_map/ppermute | solution.py:224
  79.4 21.1 %collective-permute-start.8 = (bf16[1024,256]{1,0:T(8,128)(2,1)}, bf16[1024,256]{1,0:T(8,128)(2,1)S(1)}, u32[]{:S(2)}, u32[]{:S(2)}) collective-permute-start(bf16[1024,256]{1,0:T(8,128)(2,1)} %collective-permute-done.7), channel_id=1, source_target_pairs={{4,8},{5,9},{6,10},{7,11},{8,12},{9,13},{10,14},{11,15},{20,24},{2... | collective-permute-start | bytes 1572872 | tf_op jit(solution)/shard_map/ppermute | solution.py:224
  89.3 22.4 %collective-permute-start.12 = (bf16[1024,256]{1,0:T(8,128)(2,1)}, bf16[1024,256]{1,0:T(8,128)(2,1)S(1)}, u32[]{:S(2)}, u32[]{:S(2)}) collective-permute-start(bf16[1024,256]{1,0:T(8,128)(2,1)} %collective-permute-done.11), channel_id=1, source_target_pairs={{4,0},{5,1},{6,2},{7,3},{8,4},{9,5},{10,6},{11,7},{20,16},{21,17},... | collective-permute-start | bytes 1572872 | tf_op jit(solution)/shard_map/ppermute | solution.py:224
  90.6 21.1 %collective-permute-start.14 = (bf16[1024,256]{1,0:T(8,128)(2,1)}, bf16[1024,256]{1,0:T(8,128)(2,1)S(1)}, u32[]{:S(2)}, u32[]{:S(2)}) collective-permute-start(bf16[1024,256]{1,0:T(8,128)(2,1)} %collective-permute-done.13), channel_id=1, source_target_pairs={{4,8},{5,9},{6,10},{7,11},{8,12},{9,13},{10,14},{11,15},{20,24},{2... | collective-permute-start | bytes 1572872 | tf_op jit(solution)/shard_map/ppermute | solution.py:224
  92.4 30.5 %copy-start.1 = (s32[4,4]{1,0:T(4,128)S(1)}, s32[4,4]{1,0:T(4,128)}, u32[]{:S(2)}) copy-start(s32[4,4]{1,0:T(4,128)} %constant.37.clone.order_ref) | copy-start | bytes 196
  100.4 22.5 %collective-permute-start.10 = (bf16[1024,256]{1,0:T(8,128)(2,1)S(1)}, bf16[1024,256]{1,0:T(8,128)(2,1)S(1)}, u32[]{:S(2)}, u32[]{:S(2)}) collective-permute-start(bf16[1024,256]{1,0:T(8,128)(2,1)S(1)} %collective-permute-done.6), channel_id=1, source_target_pairs={{4,0},{5,1},{6,2},{7,3},{20,16},{21,17},{22,18},{23,19}} | collective-permute-start | bytes 1572872 | tf_op jit(solution)/shard_map/ppermute | solution.py:224
  101.7 21.2 %collective-permute-start.9 = (bf16[1024,256]{1,0:T(8,128)(2,1)S(1)}, bf16[1024,256]{1,0:T(8,128)(2,1)S(1)}, u32[]{:S(2)}, u32[]{:S(2)}) collective-permute-start(bf16[1024,256]{1,0:T(8,128)(2,1)S(1)} %collective-permute-done.8), channel_id=1, source_target_pairs={{8,12},{9,13},{10,14},{11,15},{24,28},{25,29},{26,30},{27,31}} | collective-permute-start | bytes 1572872 | tf_op jit(solution)/shard_map/ppermute | solution.py:224
  111.7 20.8 %collective-permute-start.16 = (bf16[1024,256]{1,0:T(8,128)(2,1)S(1)}, bf16[1024,256]{1,0:T(8,128)(2,1)S(1)}, u32[]{:S(2)}, u32[]{:S(2)}) collective-permute-start(bf16[1024,256]{1,0:T(8,128)(2,1)S(1)} %collective-permute-done.12), channel_id=1, source_target_pairs={{4,0},{5,1},{6,2},{7,3},{20,16},{21,17},{22,18},{23,19}} | collective-permute-start | bytes 1572872 | tf_op jit(solution)/shard_map/ppermute | solution.py:224
  113.0 19.5 %collective-permute-start.15 = (bf16[1024,256]{1,0:T(8,128)(2,1)S(1)}, bf16[1024,256]{1,0:T(8,128)(2,1)S(1)}, u32[]{:S(2)}, u32[]{:S(2)}) collective-permute-start(bf16[1024,256]{1,0:T(8,128)(2,1)S(1)} %collective-permute-done.14), channel_id=1, source_target_pairs={{8,12},{9,13},{10,14},{11,15},{24,28},{25,29},{26,30},{27,31}} | collective-permute-start | bytes 1572872 | tf_op jit(solution)/shard_map/ppermute | solution.py:224
  132.5 10.4 %copy-start.2 = (bf16[2,128,1024]{2,1,0:T(8,128)(2,1)S(1)}, bf16[2,128,1024]{2,1,0:T(8,128)(2,1)}, u32[]{:S(2)}) copy-start(bf16[2,128,1024]{2,1,0:T(8,128)(2,1)} %get-tuple-element.62) | copy-start | bytes 1572868
  132.6 10.4 %copy-start.3 = (bf16[2,128,1024]{2,1,0:T(8,128)(2,1)S(1)}, bf16[2,128,1024]{2,1,0:T(8,128)(2,1)}, u32[]{:S(2)}) copy-start(bf16[2,128,1024]{2,1,0:T(8,128)(2,1)} %get-tuple-element.64) | copy-start | bytes 1572868
  141.3 26.7 %collective-permute-start.17 = (bf16[4,128,1024]{2,1,0:T(8,128)(2,1)S(1)}, bf16[4,128,1024]{2,1,0:T(8,128)(2,1)S(1)}, u32[]{:S(2)}, u32[]{:S(2)}) collective-permute-start(bf16[4,128,1024]{2,1,0:T(8,128)(2,1)S(1)} %shard_map.67), channel_id=1, source_target_pairs={{0,2},{1,3},{2,0},{3,1},{4,6},{5,7},{6,4},{7,5},{8,10},{9,11},{10,... | collective-permute-start | bytes 3145736 | tf_op jit(solution)/shard_map/ppermute | solution.py:219
  159.7 8.4 %collective-permute-start.18 = (bf16[2,128,1024]{2,1,0:T(8,128)(2,1)S(1)}, bf16[2,128,1024]{2,1,0:T(8,128)(2,1)S(1)}, u32[]{:S(2)}, u32[]{:S(2)}) collective-permute-start(bf16[2,128,1024]{2,1,0:T(8,128)(2,1)S(1)} %slice.26), channel_id=1, source_target_pairs={{0,1},{1,0},{2,3},{3,2},{4,5},{5,4},{6,7},{7,6},{8,9},{9,8},{10,11... | collective-permute-start | bytes 1572872 | tf_op jit(solution)/shard_map/ppermute | solution.py:214
  168.0 2.0 %collective-permute-start.19 = (bf16[2,128,1024]{2,1,0:T(8,128)(2,1)S(1)}, bf16[2,128,1024]{2,1,0:T(8,128)(2,1)S(1)}, u32[]{:S(2)}, u32[]{:S(2)}) collective-permute-start(bf16[2,128,1024]{2,1,0:T(8,128)(2,1)S(1)} %slice.27), channel_id=1, source_target_pairs={{0,1},{1,0},{2,3},{3,2},{4,5},{5,4},{6,7},{7,6},{8,9},{9,8},{10,11... | collective-permute-start | bytes 1572872 | tf_op jit(solution)/shard_map/ppermute | solution.py:214
Sparse Core Ops, SparseCore 0:
  8.9 48.6 all-gather.2
  59.5 91.0 all-gather.4

commit v8 on v7

--- a/solution.py
+++ b/solution.py
@@ -18,7 +18,7 @@
 SCALE_LOG2 = HD ** (-0.5) * 1.4426950408889634
 NT = (((1,), (1,)), ((), ()))
 VMEM_LIMIT = 40 * 1024 * 1024
-PROJECT_TILE = 512
+PROJECT_TILE = 1024
 
 
 def arrivals(n_outer):
@@ -37,30 +37,41 @@
 def attention_kernel(n_chip, slots, first, last, where_ref, order_ref, table_ref, q_ref, *refs):
     count = 2 * len(slots)
     pieces = refs[:count]
-    before, after = ((), refs[count:]) if first else (refs[count : count + 2], refs[count + 2 :])
+    before, after = ((), refs[count:]) if first else (refs[count : count + 3], refs[count + 3 :])
     step = pl.program_id(0)
-    head = pl.program_id(1)
     per_entry = n_chip // ENTRIES
     outer, side, core, asking = where_ref[0], where_ref[1], where_ref[2], where_ref[3]
     turn = jnp.where(step < 2, 0, core) + 2 * n_chip - (outer * 2 + asking)
-    columns = pl.ds(pl.multiple_of(head * HD, HD), HD)
-
-    keys, values, usable = [], [], []
-    for at, piece in enumerate(pieces):
+
+    starts, usable = [], []
+    for at in range(count):
         source_side = side if at < len(slots) else 1 - side
         source = order_ref[outer, slots[at % len(slots)]] * 2 + source_side
         ahead = lax.rem(source + turn, n_chip)
         row = table_ref[step, ahead // per_entry] & 3
-        keys.append(piece[pl.ds(pl.multiple_of(row * QB, QB), QB), columns])
-        values.append(piece[pl.ds(pl.multiple_of((4 + row) * QB, QB), QB), columns])
+        starts.append(pl.multiple_of(row * QB, QB))
         usable.append(lax.rem(ahead, per_entry) == 0)
-    keys = jnp.concatenate(keys, 0)
-    values = jnp.concatenate(values, 0)
-
+
+    def gather(head, base):
+        columns = slice(head * HD, (head + 1) * HD)
+        return jnp.concatenate(
+            [
+                piece[pl.ds(start + base, QB), columns]
+                for piece, start in zip(pieces, starts)
+            ],
+            0,
+        )
+
+    def spread(column):
+        return jnp.broadcast_to(column, (QB, HD))
+
+    heads = q_ref.shape[-1] // HD
     scores = []
-    for g in range(GROUP):
+    for h in range(heads):
+        if h % GROUP == 0:
+            keys = gather(h // GROUP, 0)
         s = lax.dot_general(
-            q_ref[0, :, g * HD : (g + 1) * HD], keys, NT, preferred_element_type=jnp.float32
+            q_ref[0, :, h * HD : (h + 1) * HD], keys, NT, preferred_element_type=jnp.float32
         )
         if per_entry > 1:
             s = jnp.concatenate(
@@ -71,49 +82,52 @@
                 1,
             )
         scores.append(s)
-    rounded, totals, highs, factors = [], [], [], []
-    for g, s in enumerate(scores):
-        high = jnp.max(s, axis=-1, keepdims=True)
+    rounded, totals, factors = [], [], []
+    for h, s in enumerate(scores):
+        lanes = slice(h * HD, (h + 1) * HD)
+        high = spread(jnp.max(s, axis=-1, keepdims=True))
         if not first:
-            known = before[1][0, :, g * HD : g * HD + 1]
+            known = before[1][0, :, lanes]
             high = jnp.maximum(high, known)
             factors.append(jnp.exp2((known - high) * SCALE_LOG2))
-        weights = jnp.exp2((s - high) * SCALE_LOG2)
-        total = jnp.sum(weights, axis=-1, keepdims=True)
+        if not last:
+            after[1][0, :, lanes] = high
+        weights = jnp.exp2((s - jnp.concatenate([high] * count, 1)) * SCALE_LOG2)
+        total = spread(jnp.sum(weights, axis=-1, keepdims=True))
         if not first:
-            total += before[1][0, :, g * HD + HD // 2 : g * HD + HD // 2 + 1] * factors[g]
-        highs.append(high)
+            total += before[2][0, :, lanes] * factors[h]
+        if not last:
+            after[2][0, :, lanes] = total
         totals.append(total)
         rounded.append(weights.astype(jnp.bfloat16))
-    left = lax.broadcasted_iota(jnp.int32, (QB, HD), 1) < HD // 2
-    for g in range(GROUP):
-        at = slice(g * HD, (g + 1) * HD)
-        mixed = jnp.dot(rounded[g], values, preferred_element_type=jnp.float32)
+    for h in range(heads):
+        lanes = slice(h * HD, (h + 1) * HD)
+        if h % GROUP == 0:
+            values = gather(h // GROUP, 4 * QB)
+        mixed = jnp.dot(rounded[h], values, preferred_element_type=jnp.float32)
         if not first:
-            mixed += before[0][0, :, at] * factors[g]
+            mixed += before[0][0, :, lanes] * factors[h]
         if last:
-            after[0][0, :, at] = (mixed / totals[g]).astype(jnp.bfloat16)
+            after[0][0, :, lanes] = (mixed / totals[h]).astype(jnp.bfloat16)
         else:
-            after[0][0, :, at] = mixed
-            after[1][0, :, at] = jnp.where(left, highs[g], totals[g])
-
-
-def attention(queries, where, order, table, pieces, slots, n_chip, state=None, last=True):
-    width = GROUP * HD
+            after[0][0, :, lanes] = mixed
+
+
+def attention(queries, where, order, table, pieces, slots, n_chip, state=(), last=True):
     blocks, _, columns = queries.shape
     rows = len(pieces) * QB
     whole = pl.BlockSpec(memory_space=pltpu.VMEM)
-    tile = pl.BlockSpec((1, QB, width), lambda b, h, *_: (b, 0, h))
+    tile = pl.BlockSpec((1, QB, columns), lambda b, *_: (b, 0, 0))
     state_shape = jax.ShapeDtypeStruct(queries.shape, jnp.float32)
     done_shape = jax.ShapeDtypeStruct(queries.shape, jnp.bfloat16)
     return pl.pallas_call(
-        functools.partial(attention_kernel, n_chip, slots, state is None, last),
-        out_shape=done_shape if last else (state_shape, state_shape),
+        functools.partial(attention_kernel, n_chip, slots, not state, last),
+        out_shape=done_shape if last else (state_shape,) * 3,
         grid_spec=pltpu.PrefetchScalarGridSpec(
             num_scalar_prefetch=3,
-            grid=(blocks, columns // width),
-            in_specs=[tile] + [whole] * len(pieces) + [tile] * (0 if state is None else 2),
-            out_specs=tile if last else (tile, tile),
+            grid=(blocks,),
+            in_specs=[tile] + [whole] * len(pieces) + [tile] * len(state),
+            out_specs=tile if last else (tile,) * 3,
         ),
         compiler_params=pltpu.CompilerParams(vmem_limit_bytes=VMEM_LIMIT),
         cost_estimate=pl.CostEstimate(
@@ -121,7 +135,7 @@
             bytes_accessed=2 * blocks * (rows * columns // 2 + 6 * QB * columns),
             transcendentals=blocks * QB * rows * columns // HD,
         ),
-    )(where, order, table, queries, *pieces, *(state or ()))
+    )(where, order, table, queries, *pieces, *state)
 
 
 def lay_out_kernel(n_outer, where_ref, near_ref, across_ref, far_ref, far_across_ref, rows):
@@ -234,10 +248,12 @@
     def after(array, *others):
         return lax.optimization_barrier((array, *others))[0]
 
-    def line(array, gates={}):
-        got = {0: array}
+    def line(array, gates={}, got={}):
+        got = {0: array, **got}
         for hop in range(1, n_outer):
             for way in (1, -1):
+                if -way * hop in got:
+                    continue
                 sent = got[-way * (hop - 1)]
                 if hop in gates:
                     sent = after(sent, *gates[hop])
@@ -279,7 +295,8 @@
     across_queries = swap_side(my_blocks(1 - side))
     across_table = swap_side(table)
 
-    gathered = after(gathered, theirs, across_queries, across_table)
+    hops = {-way: move(mine, 1, way) for way in (1, -1)}
+    gathered = after(gathered, theirs, across_queries, across_table, *hops.values())
     gates = ({2: (gathered,)}, {1: (gathered,)})
     gathered = lax.all_gather(gathered, PLANE, axis=0, tiled=True)
     held = out_weight.shape[0]
@@ -290,24 +307,27 @@
         order_of_rows = 0
     gathered = gathered.reshape(n_groups, H * HD, part)
 
-    early, late = [], []
-    for chain, gate in zip((mine, theirs), gates):
-        got = line(chain, gate)
+    chains = [line(chain, gate, first) for chain, gate, first in zip((mine, theirs), gates, (hops, {}))]
+    early, last = [], n_outer - 1
+    for got in chains:
         near = [got[0]]
-        for k in range(1, n_outer):
+        for k in range(1, last):
             tied = {d: after(got[d], near[-1]) for d in sorted({row[k] for row in order_rows})}
             near.append(pick(tied, k))
-        early += near[:-1]
-        late += near[-1:]
+        early += near
 
     asks = (
         (across_queries, where_across, order, across_table),
         (my_blocks(side), where, order, table),
     )
-    slots = tuple(range(n_outer))
-    states = [attention(*ask, early, slots[:-1], n_chip, last=False) for ask in asks]
+    states = [attention(*ask, early, tuple(range(last)), n_chip, last=False) for ask in asks]
+    tie = [state[2] for state in states]
+    late = [
+        pick({d: after(got[d], *tie) for d in sorted({row[last] for row in order_rows})}, last)
+        for got in chains
+    ]
     across, near = (
-        attention(*ask, late, slots[-1:], n_chip, state) for ask, state in zip(asks, states)
+        attention(*ask, late, (last,), n_chip, state) for ask, state in zip(asks, states)
     )
     across = swap_side(across)
     far = swap_core(near[2:])

time: 193 us -> 203 us (1.052)
  waiting for transfers between devices: 89.3 us -> 116 us
  Pallas kernels: 48.7 us -> 34.1 us
    ppermute x4, waiting for transfers between devices: 37.1 us -> 64.1 us  [swap_side(): lax.ppermute(array, SEQ, [(index(o, s, c), index(o, 1 - s, c)) for o, s,...]
    pallas_call x4, Pallas kernels: 33.3 us -> 20.2 us  [attention(): pl.pallas_call(functools.partial(attention_kernel, n_chip, slots, not sta...]
    ppermute x12, waiting for transfers between devices: 44 us -> 37 us  [move(): lax.ppermute(array, SEQ, [(index(o, s, c), index(o + way, s, c)) for o, s...]
    all_gather x1, waiting for transfers between devices: 3.47 us -> 9.19 us  [body(): gathered = lax.all_gather(columns, LINE, axis=0, tiled=True)]
    select_n x6, other arithmetic: 2.71 us -> 0.48 us  [pick(): result = jnp.where(mask, got[offset], result)]
  transfers between devices with their start and end apart: 22 -> 22, of which waited for: 13 -> 11; matrix products, arithmetic and copies ran while one was open for 6% -> 4% of each run, Pallas kernels for 18% -> 10%
where the time goes in v8:
time: 203 us; the launch traced here: 202 us
  waiting for transfers between devices  116 us (57%)
  Pallas kernels  34.1 us (17%)
  starting transfers between devices  27.6 us (14%)
  between operations  13.7 us (7%)
  local copies, waits for them, and re-layouts  7.07 us (3%)
  other arithmetic  3.84 us (2%)
    ppermute x4, waiting for transfers between devices, swap_side(): lax.ppermute(array, SEQ, [(index(o, s, c), index(o, 1 - s, c)) for o, s,...  64.1 us
    ppermute x12, waiting for transfers between devices, move(): lax.ppermute(array, SEQ, [(index(o, s, c), index(o + way, s, c)) for o, s...  37 us
    ppermute x12, starting transfers between devices, move(): lax.ppermute(array, SEQ, [(index(o, s, c), index(o + way, s, c)) for o, s...  20.4 us
    pallas_call x4, Pallas kernels, attention(): pl.pallas_call(functools.partial(attention_kernel, n_chip, slots, not sta...  20.2 us
    pallas_call x1, Pallas kernels, project(): pl.pallas_call(project_kernel, out_shape=jax.ShapeDtypeStruct((rows.shape...  12.9 us
    all_gather x1, waiting for transfers between devices, body(): gathered = lax.all_gather(columns, LINE, axis=0, tiled=True)  9.19 us
    ppermute x4, starting transfers between devices, swap_side(): lax.ppermute(array, SEQ, [(index(o, s, c), index(o, 1 - s, c)) for o, s,...  6.54 us
    ppermute x4, waiting for transfers between devices, swap_core(): lax.ppermute(array, SEQ, [(index(o, s, c), index(o, s, 1 - c)) for o, s,...  5.81 us
  transfers between devices with their start and end apart: 22, of which 11 were waited for; matrix products, arithmetic and copies ran while one was open for 4% of the time, Pallas kernels for 10%

profile of v8, /device:TPU:0, one launch (start us, length us, event | category | flops | bytes accessed | tf_op | source)
XLA Modules:
  0.0 202.5 jit_solution(12071253880271387028)
XLA Ops:
  6.5 1.2 copy-done
  7.8 0.8 constant_dynamic-slice_fusion.3
  8.6 0.0 all-gather.3.cloned.1.call-update
  8.6 0.0 all-gather.5.cloned.1.call-start
  8.7 2.8 %fusion = (bf16[2,1,128,2048]{3,2,1,0:T(8,128)(2,1)S(1)}, bf16[2,128,2048]{2,1,0:T(8,128)(2,1)}) fusion(bf16[2,2,128,2048]{3,2,1,0:T(8,128)(2,1)} %bitcast.14), kind=kLoop, calls=%fused_computation.24 | loop fusion | bytes 4194304 | tf_op jit(solution)/shard_map/slice | solution.py:290
  11.4 0.5 collective-permute-start.1
  11.9 0.1 dynamic-slice_bitcast_fusion
  12.0 0.0 copy-start.3
  12.0 2.4 %collective-permute-done.1 = bf16[2,128,2048]{2,1,0:T(8,128)(2,1)S(1)} collective-permute-done((bf16[2,128,2048]{2,1,0:T(8,128)(2,1)}, bf16[2,128,2048]{2,1,0:T(8,128)(2,1)S(1)}, u32[]{:S(2)}, u32[]{:S(2)}) %collective-permute-start.1) | collective-permute-done | bytes 1048608 | tf_op jit(solution)/shard_map/ppermute | solution.py:228
  14.4 0.9 constant_dynamic-slice_fusion
  15.3 1.1 pad_maximum_fusion.1
  16.3 2.9 %collective-permute-start.4 = (bf16[4,128,1024]{2,1,0:T(8,128)(2,1)}, bf16[4,128,1024]{2,1,0:T(8,128)(2,1)S(1)}, u32[]{:S(2)}, u32[]{:S(2)}) collective-permute-start(bf16[4,128,1024]{2,1,0:T(8,128)(2,1)} %pad_maximum_fusion.1), channel_id=1, source_target_pairs={{0,2},{1,3},{2,0},{3,1},{4,6},{5,7},{6,4},{7,5},{8,10},{9,11},{10,... | collective-permute-start | bytes 3145736 | tf_op jit(solution)/shard_map/ppermute | solution.py:233
  19.2 1.1 constant_dynamic-slice_fusion.1
  20.4 1.3 collective-permute-start.2
  21.7 5.3 %collective-permute-start.6 = (bf16[1024,256]{1,0:T(8,128)(2,1)S(1)}, bf16[1024,256]{1,0:T(8,128)(2,1)}, u32[]{:S(2)}, u32[]{:S(2)}) collective-permute-start(bf16[1024,256]{1,0:T(8,128)(2,1)S(1)} %pad_maximum_fusion.2.refs_0_), channel_id=1, source_target_pairs={{0,4},{1,5},{2,6},{3,7},{4,8},{5,9},{6,10},{7,11},{8,12},{9,13},{1... | collective-permute-start | bytes 1572872 | tf_op jit(solution)/shard_map/ppermute | solution.py:238
  27.1 0.8 pad_maximum_fusion.3
  27.9 0.1 collective-permute-start.3
  28.0 1.1 collective-permute-done
  29.2 2.0 collective-permute-start.5
  31.2 23.0 %collective-permute-done.5.table_ref = s32[4,8]{1,0:T(4,128)S(1)} collective-permute-done((s32[4,8]{1,0:T(4,128)S(1)}, s32[4,8]{1,0:T(4,128)S(1)}, u32[]{:S(2)}, u32[]{:S(2)}) %collective-permute-start.5) | collective-permute-done | bytes 160 | tf_op jit(solution)/shard_map/ppermute | solution.py:233
  54.2 5.3 %collective-permute-done.2 = bf16[1024,256]{1,0:T(8,128)(2,1)S(1)} collective-permute-done((bf16[1024,256]{1,0:T(8,128)(2,1)S(1)}, bf16[1024,256]{1,0:T(8,128)(2,1)S(1)}, u32[]{:S(2)}, u32[]{:S(2)}) %collective-permute-start.2) | collective-permute-done | bytes 524320 | tf_op jit(solution)/shard_map/ppermute | solution.py:238
  59.5 0.0 collective-permute-done.6
  59.5 0.0 collective-permute-done.3.refs_3_
  59.5 0.0 collective-permute-done.4.q_ref
  59.5 9.2 %all-gather.3.cloned.1.call-done = bf16[512,2048]{1,0:T(8,128)(2,1)} async-done(((bf16[128,2048]{1,0:T(8,128)(2,1)}), bf16[512,2048]{1,0:T(8,128)(2,1)}) %all-gather.3.cloned.1.call-update) | async-done | bytes 2097168 | tf_op jit(solution)/shard_map/all_gather | solution.py:280
  68.7 0.0 all-gather.5.cloned.1.call-update
  68.7 0.1 pad_add_fusion.3
  68.8 1.3 collective-permute-start.10
  70.1 4.6 %collective-permute-start.9 = (bf16[1024,256]{1,0:T(8,128)(2,1)S(1)}, bf16[1024,256]{1,0:T(8,128)(2,1)S(1)}, u32[]{:S(2)}, u32[]{:S(2)}) collective-permute-start(bf16[1024,256]{1,0:T(8,128)(2,1)S(1)} %collective-permute-done.3.refs_3_), channel_id=1, source_target_pairs={{0,4},{1,5},{2,6},{3,7},{4,8},{5,9},{6,10},{7,11},{8,12},{9,13},{1... | collective-permute-start | bytes 1572872 | tf_op jit(solution)/shard_map/ppermute | solution.py:238
  74.7 0.1 pad_add_fusion.1.where_ref
  74.7 1.3 collective-permute-start.7
  76.0 0.7 collective-permute-start.8
  76.7 0.1 broadcast_select_fusion.1.refs_1_
  76.8 1.3 pad_maximum_fusion.q_ref
  78.1 7.4 %collective-permute-done.10 = bf16[1024,256]{1,0:T(8,128)(2,1)S(1)} collective-permute-done((bf16[1024,256]{1,0:T(8,128)(2,1)S(1)}, bf16[1024,256]{1,0:T(8,128)(2,1)S(1)}, u32[]{:S(2)}, u32[]{:S(2)}) %collective-permute-start.10) | collective-permute-done | bytes 524320 | tf_op jit(solution)/shard_map/ppermute | solution.py:238
  85.5 0.0 collective-permute-done.9
  85.5 1.3 collective-permute-start.12
  86.8 0.7 collective-permute-start.11
  87.5 0.1 broadcast_select_fusion.refs_4_
  87.5 0.0 copy-start.2
  87.6 9.2 %collective-permute-done.7 = bf16[1024,256]{1,0:T(8,128)(2,1)S(1)} collective-permute-done((bf16[1024,256]{1,0:T(8,128)(2,1)S(1)}, bf16[1024,256]{1,0:T(8,128)(2,1)S(1)}, u32[]{:S(2)}, u32[]{:S(2)}) %collective-permute-start.7) | collective-permute-done | bytes 524320 | tf_op jit(solution)/shard_map/ppermute | solution.py:238
  96.7 1.3 collective-permute-start.14
  98.0 0.7 collective-permute-start.13
  98.7 0.1 select_select_fusion.3.refs_2_
  98.8 9.2 %collective-permute-done.12 = bf16[1024,256]{1,0:T(8,128)(2,1)S(1)} collective-permute-done((bf16[1024,256]{1,0:T(8,128)(2,1)S(1)}, bf16[1024,256]{1,0:T(8,128)(2,1)S(1)}, u32[]{:S(2)}, u32[]{:S(2)}) %collective-permute-start.12) | collective-permute-done | bytes 524320 | tf_op jit(solution)/shard_map/ppermute | solution.py:238
  108.0 1.3 collective-permute-start.16
  109.2 0.7 collective-permute-start.15
  110.0 0.1 select_select_fusion.2.refs_5_
  110.0 6.5 %shard_map.64 = (f32[4,128,1024]{2,1,0:T(8,128)S(1)}, f32[4,128,1024]{2,1,0:T(8,128)S(1)}, f32[4,128,1024]{2,1,0:T(8,128)S(1)}) custom-call(s32[4]{0:T(128)S(1)} %get-tuple-element.61.where_ref, s32[4,4]{1,0:T(4,128)S(1)} %copy-done.2, s32[4,8]{1,0:T(4,128)S(1)} %collective-permute-done.5.table_ref, bf16[4,128,1024]{2,1,0:T(8,128)(2,1)S(1)} %collective-permute-done.4.q_ref, ...), custom_call_target="tpu_custom_call" | custom-call | flops 1610612736 | bytes 9437184 | tf_op jit(solution)/shard_map/pallas_call | solution.py:123
  116.6 6.5 %shard_map.65 = (f32[4,128,1024]{2,1,0:T(8,128)S(1)}, f32[4,128,1024]{2,1,0:T(8,128)S(1)}, f32[4,128,1024]{2,1,0:T(8,128)S(1)}) custom-call(s32[4]{0:T(128)S(1)} %pad_add_fusion.1.where_ref, s32[4,4]{1,0:T(4,128)S(1)} %copy-done.2, s32[4,8]{1,0:T(4,128)S(1)} %pad_add_fusion.table_ref, bf16[4,128,1024]{2,1,0:T(8,128)(2,1)S(1)} %pad_maximum_fusion.q_ref, ...), custom_call_target="tpu_custom_call" | custom-call | flops 1610612736 | bytes 9437184 | tf_op jit(solution)/shard_map/pallas_call | solution.py:123
  123.1 0.1 select_select_fusion.1.refs_0_
  123.2 6.0 %collective-permute-done.16 = bf16[1024,256]{1,0:T(8,128)(2,1)S(1)} collective-permute-done((bf16[1024,256]{1,0:T(8,128)(2,1)S(1)}, bf16[1024,256]{1,0:T(8,128)(2,1)S(1)}, u32[]{:S(2)}, u32[]{:S(2)}) %collective-permute-start.16) | collective-permute-done | bytes 524320 | tf_op jit(solution)/shard_map/ppermute | solution.py:238
  129.2 0.1 select_select_fusion.refs_1_
  129.3 3.6 %shard_map.67 = bf16[4,128,1024]{2,1,0:T(8,128)(2,1)S(1)} custom-call(s32[4]{0:T(128)S(1)} %get-tuple-element.61.where_ref, s32[4,4]{1,0:T(4,128)S(1)} %copy-done.2, s32[4,8]{1,0:T(4,128)S(1)} %collective-permute-done.5.table_ref, bf16[4,128,1024]{2,1,0:T(8,128)(2,1)S(1)} %collective-permute-done.4.q_ref, bf16[1024,256]{1,0:T(8,128)(2,1)S(1)} %select_select_fusion.1.refs_0_, ...), custom_call_target="tpu_custom_call" | custom-call | flops 536870912 | bytes 7340032 | tf_op jit(solution)/shard_map/pallas_call | solution.py:123
  132.9 1.6 collective-permute-start.17
  134.5 3.6 %shard_map.66.near_ref = bf16[4,128,1024]{2,1,0:T(8,128)(2,1)S(1)} custom-call(s32[4]{0:T(128)S(1)} %pad_add_fusion.1.where_ref, s32[4,4]{1,0:T(4,128)S(1)} %copy-done.2, s32[4,8]{1,0:T(4,128)S(1)} %pad_add_fusion.table_ref, bf16[4,128,1024]{2,1,0:T(8,128)(2,1)S(1)} %pad_maximum_fusion.q_ref, bf16[1024,256]{1,0:T(8,128)(2,1)S(1)} %select_select_fusion.1.refs_0_, ...), custom_call_target="tpu_custom_call" | custom-call | flops 536870912 | bytes 7340032 | tf_op jit(solution)/shard_map/pallas_call | solution.py:123
  138.1 0.1 collective-permute-start.18
  138.2 41.1 %collective-permute-done.17.across_ref = bf16[4,128,1024]{2,1,0:T(8,128)(2,1)S(1)} collective-permute-done((bf16[4,128,1024]{2,1,0:T(8,128)(2,1)S(1)}, bf16[4,128,1024]{2,1,0:T(8,128)(2,1)S(1)}, u32[]{:S(2)}, u32[]{:S(2)}) %collective-permute-start.17) | collective-permute-done | bytes 1048608 | tf_op jit(solution)/shard_map/ppermute | solution.py:233
  179.3 0.1 collective-permute-start.19
  179.4 2.3 %collective-permute-done.19.far_across_ref = bf16[2,128,1024]{2,1,0:T(8,128)(2,1)S(1)} collective-permute-done((bf16[2,128,1024]{2,1,0:T(8,128)(2,1)S(1)}, bf16[2,128,1024]{2,1,0:T(8,128)(2,1)S(1)}, u32[]{:S(2)}, u32[]{:S(2)}) %collective-permute-start.19) | collective-permute-done | bytes 524320 | tf_op jit(solution)/shard_map/ppermute | solution.py:228
  181.6 1.0 shard_map.68.rows_ref
  182.7 0.0 all-gather.5.cloned.1.call-done
  182.7 0.0 copy-start.1
  182.7 12.9 %shard_map.69 = bf16[512,4096]{1,0:T(8,128)(2,1)} custom-call(bf16[512,2048]{1,0:T(8,128)(2,1)S(1)} %shard_map.68.rows_ref, bf16[2,2048,2048]{2,1,0:T(8,128)(2,1)} %bitcast.15), custom_call_target="tpu_custom_call" | custom-call | flops 8589934592 | bytes 23068672 | tf_op jit(solution)/shard_map/pallas_call | solution.py:186
  (20 shorter events, 0.2 us)
Async XLA Ops:
  6.5 1.2 copy-start
  6.5 62.1 %all-gather.3.cloned.1.call-start = ((), (), s32[]{:S(2)}) async-start(), calls=%async_computation | async-start | bytes 2621440 | tf_op jit(solution)/shard_map/all_gather | solution.py:280
  8.6 174.1 %all-gather.5.cloned.1.call-start = ((), (), s32[]{:S(2)}) async-start(), calls=%async_computation.1 | async-start | bytes 18874368 | tf_op jit(solution)/shard_map/all_gather | solution.py:301
  11.4 3.0 %collective-permute-start.1 = (bf16[2,128,2048]{2,1,0:T(8,128)(2,1)}, bf16[2,128,2048]{2,1,0:T(8,128)(2,1)S(1)}, u32[]{:S(2)}, u32[]{:S(2)}) collective-permute-start(bf16[2,128,2048]{2,1,0:T(8,128)(2,1)} %get-tuple-element.64), channel_id=1, source_target_pairs={{0,1},{1,0},{2,3},{3,2},{4,5},{5,4},{6,7},{7,6},{8,9},{9,8},{10,11... | collective-permute-start | bytes 3145736 | tf_op jit(solution)/shard_map/ppermute | solution.py:228
  12.0 7.3 %copy-start.3 = (bf16[512,512]{1,0:T(8,128)(2,1)S(1)}, bf16[512,512]{1,0:T(8,128)(2,1)}, u32[]{:S(2)}) copy-start(bf16[512,512]{1,0:T(8,128)(2,1)} %param.8) | copy-start | bytes 1572868
  16.3 43.1 %collective-permute-start.4 = (bf16[4,128,1024]{2,1,0:T(8,128)(2,1)}, bf16[4,128,1024]{2,1,0:T(8,128)(2,1)S(1)}, u32[]{:S(2)}, u32[]{:S(2)}) collective-permute-start(bf16[4,128,1024]{2,1,0:T(8,128)(2,1)} %pad_maximum_fusion.1), channel_id=1, source_target_pairs={{0,2},{1,3},{2,0},{3,1},{4,6},{5,7},{6,4},{7,5},{8,10},{9,11},{10,... | collective-permute-start | bytes 3145736 | tf_op jit(solution)/shard_map/ppermute | solution.py:233
  19.2 8.8 %copy-start.4 = (s32[4,8]{1,0:T(4,128)S(1)}, s32[4,8]{1,0:T(4,128)}, u32[]{:S(2)}) copy-start(s32[4,8]{1,0:T(4,128)} %param.9) | copy-start | bytes 388
  20.4 39.0 %collective-permute-start.2 = (bf16[1024,256]{1,0:T(8,128)(2,1)S(1)}, bf16[1024,256]{1,0:T(8,128)(2,1)S(1)}, u32[]{:S(2)}, u32[]{:S(2)}) collective-permute-start(bf16[1024,256]{1,0:T(8,128)(2,1)S(1)} %pad_maximum_fusion.2.refs_0_), channel_id=1, source_target_pairs={{4,0},{5,1},{6,2},{7,3},{8,4},{9,5},{10,6},{11,7},{12,8},{13,9},{1... | collective-permute-start | bytes 1572872 | tf_op jit(solution)/shard_map/ppermute | solution.py:238
  21.7 37.7 %collective-permute-start.6 = (bf16[1024,256]{1,0:T(8,128)(2,1)S(1)}, bf16[1024,256]{1,0:T(8,128)(2,1)}, u32[]{:S(2)}, u32[]{:S(2)}) collective-permute-start(bf16[1024,256]{1,0:T(8,128)(2,1)S(1)} %pad_maximum_fusion.2.refs_0_), channel_id=1, source_target_pairs={{0,4},{1,5},{2,6},{3,7},{4,8},{5,9},{6,10},{7,11},{8,12},{9,13},{1... | collective-permute-start | bytes 1572872 | tf_op jit(solution)/shard_map/ppermute | solution.py:238
  27.9 31.6 %collective-permute-start.3 = (bf16[1024,256]{1,0:T(8,128)(2,1)}, bf16[1024,256]{1,0:T(8,128)(2,1)S(1)}, u32[]{:S(2)}, u32[]{:S(2)}) collective-permute-start(bf16[1024,256]{1,0:T(8,128)(2,1)} %pad_maximum_fusion.3), channel_id=1, source_target_pairs={{0,2},{1,3},{2,0},{3,1},{4,6},{5,7},{6,4},{7,5},{8,10},{9,11},{10,... | collective-permute-start | bytes 1572872 | tf_op jit(solution)/shard_map/ppermute | solution.py:233
  28.0 1.2 collective-permute-start
  29.2 25.0 %collective-permute-start.5 = (s32[4,8]{1,0:T(4,128)S(1)}, s32[4,8]{1,0:T(4,128)S(1)}, u32[]{:S(2)}, u32[]{:S(2)}) collective-permute-start(s32[4,8]{1,0:T(4,128)S(1)} %pad_add_fusion.table_ref), channel_id=1, source_target_pairs={{0,2},{1,3},{2,0},{3,1},{4,6},{5,7},{6,4},{7,5},{8,10},{9,11},{10,... | collective-permute-start | bytes 392 | tf_op jit(solution)/shard_map/ppermute | solution.py:233
  68.8 16.7 %collective-permute-start.10 = (bf16[1024,256]{1,0:T(8,128)(2,1)S(1)}, bf16[1024,256]{1,0:T(8,128)(2,1)S(1)}, u32[]{:S(2)}, u32[]{:S(2)}) collective-permute-start(bf16[1024,256]{1,0:T(8,128)(2,1)S(1)} %collective-permute-done.3.refs_3_), channel_id=1, source_target_pairs={{4,0},{5,1},{6,2},{7,3},{8,4},{9,5},{10,6},{11,7},{12,8},{13,9},{1... | collective-permute-start | bytes 1572872 | tf_op jit(solution)/shard_map/ppermute | solution.py:238
  70.1 15.4 %collective-permute-start.9 = (bf16[1024,256]{1,0:T(8,128)(2,1)S(1)}, bf16[1024,256]{1,0:T(8,128)(2,1)S(1)}, u32[]{:S(2)}, u32[]{:S(2)}) collective-permute-start(bf16[1024,256]{1,0:T(8,128)(2,1)S(1)} %collective-permute-done.3.refs_3_), channel_id=1, source_target_pairs={{0,4},{1,5},{2,6},{3,7},{4,8},{5,9},{6,10},{7,11},{8,12},{9,13},{1... | collective-permute-start | bytes 1572872 | tf_op jit(solution)/shard_map/ppermute | solution.py:238
  74.7 22.0 %collective-permute-start.7 = (bf16[1024,256]{1,0:T(8,128)(2,1)S(1)}, bf16[1024,256]{1,0:T(8,128)(2,1)S(1)}, u32[]{:S(2)}, u32[]{:S(2)}) collective-permute-start(bf16[1024,256]{1,0:T(8,128)(2,1)S(1)} %collective-permute-done.2), channel_id=1, source_target_pairs={{4,0},{5,1},{6,2},{7,3},{8,4},{9,5},{10,6},{11,7},{20,16},{21,17},... | collective-permute-start | bytes 1572872 | tf_op jit(solution)/shard_map/ppermute | solution.py:238
  76.0 20.7 %collective-permute-start.8 = (bf16[1024,256]{1,0:T(8,128)(2,1)}, bf16[1024,256]{1,0:T(8,128)(2,1)S(1)}, u32[]{:S(2)}, u32[]{:S(2)}) collective-permute-start(bf16[1024,256]{1,0:T(8,128)(2,1)} %collective-permute-done.6), channel_id=1, source_target_pairs={{4,8},{5,9},{6,10},{7,11},{8,12},{9,13},{10,14},{11,15},{20,24},{2... | collective-permute-start | bytes 1572872 | tf_op jit(solution)/shard_map/ppermute | solution.py:238
  85.5 22.5 %collective-permute-start.12 = (bf16[1024,256]{1,0:T(8,128)(2,1)S(1)}, bf16[1024,256]{1,0:T(8,128)(2,1)S(1)}, u32[]{:S(2)}, u32[]{:S(2)}) collective-permute-start(bf16[1024,256]{1,0:T(8,128)(2,1)S(1)} %collective-permute-done.10), channel_id=1, source_target_pairs={{4,0},{5,1},{6,2},{7,3},{8,4},{9,5},{10,6},{11,7},{20,16},{21,17},... | collective-permute-start | bytes 1572872 | tf_op jit(solution)/shard_map/ppermute | solution.py:238
  86.8 21.2 %collective-permute-start.11 = (bf16[1024,256]{1,0:T(8,128)(2,1)S(1)}, bf16[1024,256]{1,0:T(8,128)(2,1)S(1)}, u32[]{:S(2)}, u32[]{:S(2)}) collective-permute-start(bf16[1024,256]{1,0:T(8,128)(2,1)S(1)} %collective-permute-done.9), channel_id=1, source_target_pairs={{4,8},{5,9},{6,10},{7,11},{8,12},{9,13},{10,14},{11,15},{20,24},{2... | collective-permute-start | bytes 1572872 | tf_op jit(solution)/shard_map/ppermute | solution.py:238
  87.5 22.5 %copy-start.2 = (s32[4,4]{1,0:T(4,128)S(1)}, s32[4,4]{1,0:T(4,128)}, u32[]{:S(2)}) copy-start(s32[4,4]{1,0:T(4,128)} %constant.37.clone.order_ref) | copy-start | bytes 196
  96.7 26.4 %collective-permute-start.14 = (bf16[1024,256]{1,0:T(8,128)(2,1)S(1)}, bf16[1024,256]{1,0:T(8,128)(2,1)S(1)}, u32[]{:S(2)}, u32[]{:S(2)}) collective-permute-start(bf16[1024,256]{1,0:T(8,128)(2,1)S(1)} %collective-permute-done.7), channel_id=1, source_target_pairs={{4,0},{5,1},{6,2},{7,3},{20,16},{21,17},{22,18},{23,19}} | collective-permute-start | bytes 1572872 | tf_op jit(solution)/shard_map/ppermute | solution.py:238
  98.0 25.1 %collective-permute-start.13 = (bf16[1024,256]{1,0:T(8,128)(2,1)S(1)}, bf16[1024,256]{1,0:T(8,128)(2,1)S(1)}, u32[]{:S(2)}, u32[]{:S(2)}) collective-permute-start(bf16[1024,256]{1,0:T(8,128)(2,1)S(1)} %collective-permute-done.8), channel_id=1, source_target_pairs={{8,12},{9,13},{10,14},{11,15},{24,28},{25,29},{26,30},{27,31}} | collective-permute-start | bytes 1572872 | tf_op jit(solution)/shard_map/ppermute | solution.py:238
  108.0 21.3 %collective-permute-start.16 = (bf16[1024,256]{1,0:T(8,128)(2,1)S(1)}, bf16[1024,256]{1,0:T(8,128)(2,1)S(1)}, u32[]{:S(2)}, u32[]{:S(2)}) collective-permute-start(bf16[1024,256]{1,0:T(8,128)(2,1)S(1)} %collective-permute-done.12), channel_id=1, source_target_pairs={{4,0},{5,1},{6,2},{7,3},{20,16},{21,17},{22,18},{23,19}} | collective-permute-start | bytes 1572872 | tf_op jit(solution)/shard_map/ppermute | solution.py:238
  109.2 20.0 %collective-permute-start.15 = (bf16[1024,256]{1,0:T(8,128)(2,1)S(1)}, bf16[1024,256]{1,0:T(8,128)(2,1)S(1)}, u32[]{:S(2)}, u32[]{:S(2)}) collective-permute-start(bf16[1024,256]{1,0:T(8,128)(2,1)S(1)} %collective-permute-done.11), channel_id=1, source_target_pairs={{8,12},{9,13},{10,14},{11,15},{24,28},{25,29},{26,30},{27,31}} | collective-permute-start | bytes 1572872 | tf_op jit(solution)/shard_map/ppermute | solution.py:238
  132.9 46.4 %collective-permute-start.17 = (bf16[4,128,1024]{2,1,0:T(8,128)(2,1)S(1)}, bf16[4,128,1024]{2,1,0:T(8,128)(2,1)S(1)}, u32[]{:S(2)}, u32[]{:S(2)}) collective-permute-start(bf16[4,128,1024]{2,1,0:T(8,128)(2,1)S(1)} %shard_map.67), channel_id=1, source_target_pairs={{0,2},{1,3},{2,0},{3,1},{4,6},{5,7},{6,4},{7,5},{8,10},{9,11},{10,... | collective-permute-start | bytes 3145736 | tf_op jit(solution)/shard_map/ppermute | solution.py:233
  138.1 41.3 %collective-permute-start.18 = (bf16[2,128,1024]{2,1,0:T(8,128)(2,1)S(1)}, bf16[2,128,1024]{2,1,0:T(8,128)(2,1)S(1)}, u32[]{:S(2)}, u32[]{:S(2)}) collective-permute-start(bf16[2,128,1024]{2,1,0:T(8,128)(2,1)S(1)} %slice.26), channel_id=1, source_target_pairs={{0,1},{1,0},{2,3},{3,2},{4,5},{5,4},{6,7},{7,6},{8,9},{9,8},{10,11... | collective-permute-start | bytes 1572872 | tf_op jit(solution)/shard_map/ppermute | solution.py:228
  179.3 2.4 %collective-permute-start.19 = (bf16[2,128,1024]{2,1,0:T(8,128)(2,1)S(1)}, bf16[2,128,1024]{2,1,0:T(8,128)(2,1)S(1)}, u32[]{:S(2)}, u32[]{:S(2)}) collective-permute-start(bf16[2,128,1024]{2,1,0:T(8,128)(2,1)S(1)} %slice.27), channel_id=1, source_target_pairs={{0,1},{1,0},{2,3},{3,2},{4,5},{5,4},{6,7},{7,6},{8,9},{9,8},{10,11... | collective-permute-start | bytes 1572872 | tf_op jit(solution)/shard_map/ppermute | solution.py:228
  182.7 12.9 %copy-start.1 = (bf16[128,4096]{1,0:T(8,128)(2,1)S(1)}, bf16[128,4096]{1,0:T(8,128)(2,1)}, u32[]{:S(2)}) copy-start(bf16[128,4096]{1,0:T(8,128)(2,1)} %param.10) | copy-start | bytes 3145732
Sparse Core Ops, SparseCore 0:
  8.9 59.6 all-gather.2
  70.5 111.3 all-gather.4

commit v9 on v8

--- a/solution.py
+++ b/solution.py
@@ -35,9 +35,9 @@
 
 
 def attention_kernel(n_chip, slots, first, last, where_ref, order_ref, table_ref, q_ref, *refs):
+    pieces, refs = refs[: len(slots)], refs[len(slots) :]
+    before, after = ((), refs) if first else (refs[:3], refs[3:])
     count = 2 * len(slots)
-    pieces = refs[:count]
-    before, after = ((), refs[count:]) if first else (refs[count : count + 3], refs[count + 3 :])
     step = pl.program_id(0)
     per_entry = n_chip // ENTRIES
     outer, side, core, asking = where_ref[0], where_ref[1], where_ref[2], where_ref[3]
@@ -49,27 +49,23 @@
         source = order_ref[outer, slots[at % len(slots)]] * 2 + source_side
         ahead = lax.rem(source + turn, n_chip)
         row = table_ref[step, ahead // per_entry] & 3
-        starts.append(pl.multiple_of(row * QB, QB))
+        base = 0 if at < len(slots) else 8
+        starts.append(pl.multiple_of((base + row) * QB, QB))
         usable.append(lax.rem(ahead, per_entry) == 0)
 
-    def gather(head, base):
-        columns = slice(head * HD, (head + 1) * HD)
+    def gather(base):
         return jnp.concatenate(
-            [
-                piece[pl.ds(start + base, QB), columns]
-                for piece, start in zip(pieces, starts)
-            ],
+            [pieces[at % len(slots)][pl.ds(start + base, QB), :] for at, start in enumerate(starts)],
             0,
         )
+
+    keys, values = gather(0), gather(4 * QB)
 
     def spread(column):
         return jnp.broadcast_to(column, (QB, HD))
 
-    heads = q_ref.shape[-1] // HD
     scores = []
-    for h in range(heads):
-        if h % GROUP == 0:
-            keys = gather(h // GROUP, 0)
+    for h in range(GROUP):
         s = lax.dot_general(
             q_ref[0, :, h * HD : (h + 1) * HD], keys, NT, preferred_element_type=jnp.float32
         )
@@ -100,10 +96,8 @@
             after[2][0, :, lanes] = total
         totals.append(total)
         rounded.append(weights.astype(jnp.bfloat16))
-    for h in range(heads):
+    for h in range(GROUP):
         lanes = slice(h * HD, (h + 1) * HD)
-        if h % GROUP == 0:
-            values = gather(h // GROUP, 4 * QB)
         mixed = jnp.dot(rounded[h], values, preferred_element_type=jnp.float32)
         if not first:
             mixed += before[0][0, :, lanes] * factors[h]
@@ -113,65 +107,62 @@
             after[0][0, :, lanes] = mixed
 
 
-def attention(queries, where, order, table, pieces, slots, n_chip, state=(), last=True):
+def attention(queries, where, order, table, head, pieces, slots, n_chip, state=(), last=True):
     blocks, _, columns = queries.shape
-    rows = len(pieces) * QB
+    width = GROUP * HD
+    rows = 2 * len(pieces) * QB
     whole = pl.BlockSpec(memory_space=pltpu.VMEM)
-    tile = pl.BlockSpec((1, QB, columns), lambda b, *_: (b, 0, 0))
-    state_shape = jax.ShapeDtypeStruct(queries.shape, jnp.float32)
-    done_shape = jax.ShapeDtypeStruct(queries.shape, jnp.bfloat16)
+    tile = pl.BlockSpec((1, QB, width), lambda b, *_: (b, 0, 0))
+    shape = (blocks, QB, width)
+    state_shape = jax.ShapeDtypeStruct(shape, jnp.float32)
+    done_shape = jax.ShapeDtypeStruct(shape, jnp.bfloat16)
     return pl.pallas_call(
         functools.partial(attention_kernel, n_chip, slots, not state, last),
         out_shape=done_shape if last else (state_shape,) * 3,
         grid_spec=pltpu.PrefetchScalarGridSpec(
             num_scalar_prefetch=3,
             grid=(blocks,),
-            in_specs=[tile] + [whole] * len(pieces) + [tile] * len(state),
+            in_specs=[pl.BlockSpec((1, QB, width), lambda b, *_: (b, 0, head))]
+            + [whole] * len(pieces)
+            + [tile] * len(state),
             out_specs=tile if last else (tile,) * 3,
         ),
         compiler_params=pltpu.CompilerParams(vmem_limit_bytes=VMEM_LIMIT),
-        cost_estimate=pl.CostEstimate(
-            flops=4 * blocks * QB * rows * columns,
-            bytes_accessed=2 * blocks * (rows * columns // 2 + 6 * QB * columns),
-            transcendentals=blocks * QB * rows * columns // HD,
-        ),
+        cost_estimate=pl.CostEstimate(flops=1, bytes_accessed=1, transcendentals=0),
     )(where, order, table, queries, *pieces, *state)
 
 
-def lay_out_kernel(n_outer, where_ref, near_ref, across_ref, far_ref, far_across_ref, rows):
+def lay_out_kernel(n_outer, where_ref, *refs):
+    rows = refs[-1]
     side = where_ref[1]
-    heads = H // 2
-    for block in range(2):
-        even = slice(2 * block * QB, (2 * block + 1) * QB)
-        odd = slice((2 * block + 1) * QB, (2 * block + 2) * QB)
-        for which, even_ref, odd_ref in (
-            (side, near_ref, far_ref),
-            (1 - side, across_ref, far_across_ref),
-        ):
-            for h in range(heads):
-                at = slice(h * HD, (h + 1) * HD)
+    for kv, group in enumerate(refs[i : i + 4] for i in range(0, len(refs) - 1, 4)):
+        for at, ref in enumerate(group):
+            which = 1 - side if at % 2 else side
+            for g in range(GROUP):
+                h = kv * GROUP + g
                 if n_outer:
-                    to = (h % 4) * n_outer + h // 4 + which * (heads // 4)
+                    to = g * n_outer + kv + which * (KVH // 2)
                 else:
-                    to = h + which * heads
+                    to = h + which * (H // 2)
                 to = pl.ds(pl.multiple_of(to * HD, HD), HD)
-                rows[even, to] = even_ref[block, :, at]
-                rows[odd, to] = odd_ref[block, :, at]
-
-
-def lay_out(n_outer, where, near, across, far, far_across):
-    half = pl.BlockSpec((2, QB, near.shape[-1]), lambda i, *_: (0, 0, 0))
+                for block in range(2):
+                    first = (2 * block + at // 2) * QB
+                    rows[first : first + QB, to] = ref[block, :, g * HD : (g + 1) * HD]
+
+
+def lay_out(n_outer, where, parts):
+    half = pl.BlockSpec((2, QB, GROUP * HD), lambda i, *_: (0, 0, 0))
     return pl.pallas_call(
         functools.partial(lay_out_kernel, n_outer),
         out_shape=jax.ShapeDtypeStruct((4 * QB, H * HD), jnp.bfloat16),
         grid_spec=pltpu.PrefetchScalarGridSpec(
             num_scalar_prefetch=1,
             grid=(1,),
-            in_specs=[half] * 4,
+            in_specs=[half] * len(parts),
             out_specs=pl.BlockSpec((4 * QB, H * HD), lambda i, *_: (0, 0)),
         ),
         compiler_params=pltpu.CompilerParams(vmem_limit_bytes=VMEM_LIMIT),
-    )(where, near, across, far, far_across)
+    )(where, *parts)
 
 
 def project_kernel(rows_ref, w_ref, o_ref):
@@ -295,9 +286,12 @@
     across_queries = swap_side(my_blocks(1 - side))
     across_table = swap_side(table)
 
-    hops = {-way: move(mine, 1, way) for way in (1, -1)}
-    gathered = after(gathered, theirs, across_queries, across_table, *hops.values())
-    gates = ({2: (gathered,)}, {1: (gathered,)})
+    chains = [
+        jnp.concatenate([half[:, h * HD : (h + 1) * HD] for half in (mine, theirs)], 0)
+        for h in range(KVH // 2)
+    ]
+    gathered = after(gathered, across_queries, across_table, *chains)
+    chains = [after(chain, gathered) for chain in chains]
     gathered = lax.all_gather(gathered, PLANE, axis=0, tiled=True)
     held = out_weight.shape[0]
     order_of_rows = n_outer
@@ -307,32 +301,36 @@
         order_of_rows = 0
     gathered = gathered.reshape(n_groups, H * HD, part)
 
-    chains = [line(chain, gate, first) for chain, gate, first in zip((mine, theirs), gates, (hops, {}))]
-    early, last = [], n_outer - 1
-    for got in chains:
+    asks = (
+        (across_queries, where_across, order, across_table),
+        (my_blocks(side), where, order, table),
+    )
+    last = n_outer - 1
+    lines = [line(chain) for chain in chains]
+    states = []
+    for head, got in enumerate(lines):
         near = [got[0]]
         for k in range(1, last):
             tied = {d: after(got[d], near[-1]) for d in sorted({row[k] for row in order_rows})}
             near.append(pick(tied, k))
-        early += near
-
-    asks = (
-        (across_queries, where_across, order, across_table),
-        (my_blocks(side), where, order, table),
-    )
-    states = [attention(*ask, early, tuple(range(last)), n_chip, last=False) for ask in asks]
-    tie = [state[2] for state in states]
-    late = [
-        pick({d: after(got[d], *tie) for d in sorted({row[last] for row in order_rows})}, last)
-        for got in chains
-    ]
-    across, near = (
-        attention(*ask, late, (last,), n_chip, state) for ask, state in zip(asks, states)
-    )
-    across = swap_side(across)
-    far = swap_core(near[2:])
-    far_across = swap_core(across[2:])
-    rows = lay_out(order_of_rows, where, near, across, far, far_across)
+        states.append(
+            [attention(*ask, head, near, tuple(range(last)), n_chip, last=False) for ask in asks]
+        )
+    tie = [state[2] for pair in states for state in pair]
+    late, across = [], []
+    for head, got in enumerate(lines):
+        piece = pick({d: after(got[d], *tie) for d in sorted({row[last] for row in order_rows})}, last)
+        late.append([piece])
+        out = attention(*asks[0], head, late[head], (last,), n_chip, states[head][0])
+        tie = [out]
+        across.append(swap_side(out))
+    parts = []
+    for head in range(KVH // 2):
+        state = [after(array, *tie) for array in states[head][1]]
+        near = attention(*asks[1], head, late[head], (last,), n_chip, state)
+        tie = [across[head]]
+        parts += [near, across[head], swap_core(near[2:]), swap_core(across[head][2:])]
+    rows = lay_out(order_of_rows, where, parts)
     return project(rows, gathered)
 
 

time: 203 us -> 192 us (0.946)
  waiting for transfers between devices: 116 us -> 94.2 us
  Pallas kernels: 34.1 us -> 40.9 us
  starting transfers between devices: 27.6 us -> 30.4 us
    ppermute x4 -> x5, waiting for transfers between devices: 64.1 us -> 54.4 us  [swap_side(): lax.ppermute(array, SEQ, [(index(o, s, c), index(o, 1 - s, c)) for o, s,...]
    pallas_call x4 -> x8, Pallas kernels: 20.2 us -> 26.8 us  [attention(): pl.pallas_call(functools.partial(attention_kernel, n_chip, slots, not sta...]
    ppermute x12, waiting for transfers between devices: 37 us -> 31.7 us  [move(): lax.ppermute(array, SEQ, [(index(o, s, c), index(o + way, s, c)) for o, s...]
    ppermute x4 -> x6, waiting for transfers between devices: 5.81 us -> 2.2 us  [swap_core(): lax.ppermute(array, SEQ, [(index(o, s, c), index(o, s, 1 - c)) for o, s,...]
    all_gather x1, waiting for transfers between devices: 9.19 us -> 5.91 us  [body(): gathered = lax.all_gather(columns, LINE, axis=0, tiled=True)]
    ppermute x4 -> x5, starting transfers between devices: 6.54 us -> 7.67 us  [swap_side(): lax.ppermute(array, SEQ, [(index(o, s, c), index(o, 1 - s, c)) for o, s,...]
  transfers between devices with their start and end apart: 22 -> 25, of which waited for: 11 -> 14; matrix products, arithmetic and copies ran while one was open for 4% -> 5% of each run, Pallas kernels for 10% -> 15%
where the time goes in v9:
time: 192 us; the launch traced here: 191 us
  waiting for transfers between devices  94.2 us (49%)
  Pallas kernels  40.9 us (21%)
  starting transfers between devices  30.4 us (16%)
  between operations  13.8 us (7%)
  local copies, waits for them, and re-layouts  8.9 us (5%)
  other arithmetic  3 us (2%)
    ppermute x5, waiting for transfers between devices, swap_side(): lax.ppermute(array, SEQ, [(index(o, s, c), index(o, 1 - s, c)) for o, s,...  54.4 us
    ppermute x12, waiting for transfers between devices, move(): lax.ppermute(array, SEQ, [(index(o, s, c), index(o + way, s, c)) for o, s...  31.7 us
    pallas_call x8, Pallas kernels, attention(): pl.pallas_call(functools.partial(attention_kernel, n_chip, slots, not sta...  26.8 us
    ppermute x12, starting transfers between devices, move(): lax.ppermute(array, SEQ, [(index(o, s, c), index(o + way, s, c)) for o, s...  21.2 us
    pallas_call x1, Pallas kernels, project(): pl.pallas_call(project_kernel, out_shape=jax.ShapeDtypeStruct((rows.shape...  12.9 us
    ppermute x5, starting transfers between devices, swap_side(): lax.ppermute(array, SEQ, [(index(o, s, c), index(o, 1 - s, c)) for o, s,...  7.67 us
    all_gather x1, waiting for transfers between devices, body(): gathered = lax.all_gather(columns, LINE, axis=0, tiled=True)  5.91 us
  transfers between devices with their start and end apart: 25, of which 14 were waited for; matrix products, arithmetic and copies ran while one was open for 5% of the time, Pallas kernels for 15%

profile of v9, /device:TPU:0, one launch (start us, length us, event | category | flops | bytes accessed | tf_op | source)
XLA Modules:
  0.0 191.2 jit_solution(15775758407812492050)
XLA Ops:
  6.5 1.2 copy-done
  7.8 0.8 constant_dynamic-slice_fusion.1
  8.7 2.8 %fusion.2 = (bf16[2,1,128,2048]{3,2,1,0:T(8,128)(2,1)S(1)}, bf16[2,128,2048]{2,1,0:T(8,128)(2,1)}) fusion(bf16[2,2,128,2048]{3,2,1,0:T(8,128)(2,1)} %bitcast.14), kind=kLoop, calls=%fused_computation.29 | loop fusion | bytes 4194304 | tf_op jit(solution)/shard_map/slice | solution.py:281
  11.4 0.5 collective-permute-start.1
  11.9 1.1 constant_dynamic-slice_fusion.4
  13.0 0.9 pad_maximum_fusion.3
  13.8 2.5 %collective-permute-start.2 = (bf16[1024,256]{1,0:T(8,128)(2,1)}, bf16[1024,256]{1,0:T(8,128)(2,1)}, u32[]{:S(2)}, u32[]{:S(2)}) collective-permute-start(bf16[1024,256]{1,0:T(8,128)(2,1)} %pad_maximum_fusion.3), channel_id=1, source_target_pairs={{0,2},{1,3},{2,0},{3,1},{4,6},{5,7},{6,4},{7,5},{8,10},{9,11},{10,... | collective-permute-start | bytes 1572872 | tf_op jit(solution)/shard_map/ppermute | solution.py:224
  16.4 0.9 dynamic-slice_bitcast_fusion
  17.3 0.9 constant_dynamic-slice_fusion
  18.2 0.1 pad_maximum_fusion.1
  18.3 0.1 collective-permute-start.3
  18.3 0.3 collective-permute-start
  18.7 0.9 collective-permute-done
  19.6 2.0 %collective-permute-start.4 = (s32[4,8]{1,0:T(4,128)S(1)}, s32[4,8]{1,0:T(4,128)S(1)}, u32[]{:S(2)}, u32[]{:S(2)}) collective-permute-start(s32[4,8]{1,0:T(4,128)S(1)} %pad_add_fusion.table_ref), channel_id=1, source_target_pairs={{0,2},{1,3},{2,0},{3,1},{4,6},{5,7},{6,4},{7,5},{8,10},{9,11},{10,... | collective-permute-start | bytes 392 | tf_op jit(solution)/shard_map/ppermute | solution.py:224
  21.6 7.9 %collective-permute-done.2 = bf16[1024,256]{1,0:T(8,128)(2,1)} collective-permute-done((bf16[1024,256]{1,0:T(8,128)(2,1)}, bf16[1024,256]{1,0:T(8,128)(2,1)}, u32[]{:S(2)}, u32[]{:S(2)}) %collective-permute-start.2) | collective-permute-done | bytes 524320 | tf_op jit(solution)/shard_map/ppermute | solution.py:224
  29.5 1.1 fusion.3
  30.6 21.1 %collective-permute-done.4.table_ref = s32[4,8]{1,0:T(4,128)S(1)} collective-permute-done((s32[4,8]{1,0:T(4,128)S(1)}, s32[4,8]{1,0:T(4,128)S(1)}, u32[]{:S(2)}, u32[]{:S(2)}) %collective-permute-start.4) | collective-permute-done | bytes 160 | tf_op jit(solution)/shard_map/ppermute | solution.py:224
  51.7 5.9 %all-gather.3.cloned.1.call-done = bf16[512,2048]{1,0:T(8,128)(2,1)} async-done(((bf16[128,2048]{1,0:T(8,128)(2,1)}), bf16[512,2048]{1,0:T(8,128)(2,1)}) %all-gather.3.cloned.1.call-update) | async-done | bytes 2097168 | tf_op jit(solution)/shard_map/all_gather | solution.py:271
  57.6 1.3 collective-permute-start.10
  58.9 5.4 %collective-permute-start.9 = (bf16[2048,128]{1,0:T(8,128)(2,1)S(1)}, bf16[2048,128]{1,0:T(8,128)(2,1)}, u32[]{:S(2)}, u32[]{:S(2)}) collective-permute-start(bf16[2048,128]{1,0:T(8,128)(2,1)S(1)} %fusion.refs_0_), channel_id=1, source_target_pairs={{0,4},{1,5},{2,6},{3,7},{4,8},{5,9},{6,10},{7,11},{8,12},{9,13},{1... | collective-permute-start | bytes 1572872 | tf_op jit(solution)/shard_map/ppermute | solution.py:229
  64.3 1.3 collective-permute-start.5
  65.6 5.4 %collective-permute-start.7 = (bf16[2048,128]{1,0:T(8,128)(2,1)S(1)}, bf16[2048,128]{1,0:T(8,128)(2,1)}, u32[]{:S(2)}, u32[]{:S(2)}) collective-permute-start(bf16[2048,128]{1,0:T(8,128)(2,1)S(1)} %pad_maximum_fusion.4.refs_0_), channel_id=1, source_target_pairs={{0,4},{1,5},{2,6},{3,7},{4,8},{5,9},{6,10},{7,11},{8,12},{9,13},{1... | collective-permute-start | bytes 1572872 | tf_op jit(solution)/shard_map/ppermute | solution.py:229
  70.9 0.1 pad_add_fusion.3
  71.0 0.1 pad_add_fusion.1.where_ref
  71.1 1.3 pad_maximum_fusion.q_ref
  72.4 1.9 %collective-permute-done.10 = bf16[2048,128]{1,0:T(8,128)(2,1)S(1)} collective-permute-done((bf16[2048,128]{1,0:T(8,128)(2,1)S(1)}, bf16[2048,128]{1,0:T(8,128)(2,1)S(1)}, u32[]{:S(2)}, u32[]{:S(2)}) %collective-permute-start.10) | collective-permute-done | bytes 524320 | tf_op jit(solution)/shard_map/ppermute | solution.py:229
  74.3 1.5 collective-permute-done.9
  75.8 1.3 collective-permute-start.12
  77.1 0.7 collective-permute-start.11
  77.8 7.7 %collective-permute-done.5 = bf16[2048,128]{1,0:T(8,128)(2,1)S(1)} collective-permute-done((bf16[2048,128]{1,0:T(8,128)(2,1)S(1)}, bf16[2048,128]{1,0:T(8,128)(2,1)S(1)}, u32[]{:S(2)}, u32[]{:S(2)}) %collective-permute-start.5) | collective-permute-done | bytes 524320 | tf_op jit(solution)/shard_map/ppermute | solution.py:229
  85.6 1.3 collective-permute-start.6
  86.9 0.7 collective-permute-start.8
  87.6 0.1 broadcast_select_fusion.refs_1_
  87.7 0.1 broadcast_select_fusion.1.refs_1_
  87.8 9.0 %collective-permute-done.12 = bf16[2048,128]{1,0:T(8,128)(2,1)S(1)} collective-permute-done((bf16[2048,128]{1,0:T(8,128)(2,1)S(1)}, bf16[2048,128]{1,0:T(8,128)(2,1)S(1)}, u32[]{:S(2)}, u32[]{:S(2)}) %collective-permute-start.12) | collective-permute-done | bytes 524320 | tf_op jit(solution)/shard_map/ppermute | solution.py:229
  96.8 10.1 %collective-permute-done.6 = bf16[2048,128]{1,0:T(8,128)(2,1)S(1)} collective-permute-done((bf16[2048,128]{1,0:T(8,128)(2,1)S(1)}, bf16[2048,128]{1,0:T(8,128)(2,1)S(1)}, u32[]{:S(2)}, u32[]{:S(2)}) %collective-permute-start.6) | collective-permute-done | bytes 524320 | tf_op jit(solution)/shard_map/ppermute | solution.py:229
  106.9 1.3 collective-permute-start.14
  108.2 0.7 collective-permute-start.13
  108.9 0.1 select_select_fusion.2.refs_2_
  109.0 1.3 collective-permute-start.16
  110.3 0.7 collective-permute-start.15
  111.0 0.1 select_select_fusion.3.refs_2_
  111.1 4.0 %shard_map.67 = (f32[4,128,512]{2,1,0:T(8,128)S(1)}, f32[4,128,512]{2,1,0:T(8,128)S(1)}, f32[4,128,512]{2,1,0:T(8,128)S(1)}) custom-call(s32[4]{0:T(128)S(1)} %pad_add_fusion.1.where_ref, s32[4,4]{1,0:T(4,128)S(1)} %copy-done.2, s32[4,8]{1,0:T(4,128)S(1)} %pad_add_fusion.table_ref, bf16[4,128,1024]{2,1,0:T(8,128)(2,1)S(1)} %pad_maximum_fusion.q_ref, ...), custom_call_target="tpu_custom_call" | custom-call | flops 1 | bytes 1 | tf_op jit(solution)/shard_map/pallas_call | solution.py:119
  115.1 4.0 %shard_map.65 = (f32[4,128,512]{2,1,0:T(8,128)S(1)}, f32[4,128,512]{2,1,0:T(8,128)S(1)}, f32[4,128,512]{2,1,0:T(8,128)S(1)}) custom-call(s32[4]{0:T(128)S(1)} %pad_add_fusion.1.where_ref, s32[4,4]{1,0:T(4,128)S(1)} %copy-done.2, s32[4,8]{1,0:T(4,128)S(1)} %pad_add_fusion.table_ref, bf16[4,128,1024]{2,1,0:T(8,128)(2,1)S(1)} %pad_maximum_fusion.q_ref, ...), custom_call_target="tpu_custom_call" | custom-call | flops 1 | bytes 1 | tf_op jit(solution)/shard_map/pallas_call | solution.py:119
  119.1 4.0 %shard_map.66 = (f32[4,128,512]{2,1,0:T(8,128)S(1)}, f32[4,128,512]{2,1,0:T(8,128)S(1)}, f32[4,128,512]{2,1,0:T(8,128)S(1)}) custom-call(s32[4]{0:T(128)S(1)} %get-tuple-element.83.where_ref, s32[4,4]{1,0:T(4,128)S(1)} %copy-done.2, s32[4,8]{1,0:T(4,128)S(1)} %collective-permute-done.4.table_ref, bf16[4,128,1024]{2,1,0:T(8,128)(2,1)S(1)} %collective-permute-done.3.q_ref, ...), custom_call_target="tpu_custom_call" | custom-call | flops 1 | bytes 1 | tf_op jit(solution)/shard_map/pallas_call | solution.py:119
  123.2 4.0 %shard_map.64 = (f32[4,128,512]{2,1,0:T(8,128)S(1)}, f32[4,128,512]{2,1,0:T(8,128)S(1)}, f32[4,128,512]{2,1,0:T(8,128)S(1)}) custom-call(s32[4]{0:T(128)S(1)} %get-tuple-element.83.where_ref, s32[4,4]{1,0:T(4,128)S(1)} %copy-done.2, s32[4,8]{1,0:T(4,128)S(1)} %collective-permute-done.4.table_ref, bf16[4,128,1024]{2,1,0:T(8,128)(2,1)S(1)} %collective-permute-done.3.q_ref, ...), custom_call_target="tpu_custom_call" | custom-call | flops 1 | bytes 1 | tf_op jit(solution)/shard_map/pallas_call | solution.py:119
  127.2 0.1 select_select_fusion.1.refs_0_
  127.3 2.7 %shard_map.68 = bf16[4,128,512]{2,1,0:T(8,128)(2,1)S(1)} custom-call(s32[4]{0:T(128)S(1)} %get-tuple-element.83.where_ref, s32[4,4]{1,0:T(4,128)S(1)} %copy-done.2, s32[4,8]{1,0:T(4,128)S(1)} %collective-permute-done.4.table_ref, bf16[4,128,1024]{2,1,0:T(8,128)(2,1)S(1)} %collective-permute-done.3.q_ref, bf16[2048,128]{1,0:T(8,128)(2,1)S(1)} %select_select_fusion.1.refs_0_, ...), custom_call_target="tpu_custom_call" | custom-call | flops 1 | bytes 1 | tf_op jit(solution)/shard_map/pallas_call | solution.py:119
  130.0 1.5 collective-permute-start.17
  131.6 1.3 collective-permute-done.16
  132.9 0.1 select_select_fusion.refs_0_
  133.0 2.7 %shard_map.69 = bf16[4,128,512]{2,1,0:T(8,128)(2,1)S(1)} custom-call(s32[4]{0:T(128)S(1)} %get-tuple-element.83.where_ref, s32[4,4]{1,0:T(4,128)S(1)} %copy-done.2, s32[4,8]{1,0:T(4,128)S(1)} %collective-permute-done.4.table_ref, bf16[4,128,1024]{2,1,0:T(8,128)(2,1)S(1)} %collective-permute-done.3.q_ref, bf16[2048,128]{1,0:T(8,128)(2,1)S(1)} %select_select_fusion.refs_0_, ...), custom_call_target="tpu_custom_call" | custom-call | flops 1 | bytes 1 | tf_op jit(solution)/shard_map/pallas_call | solution.py:119
  135.7 1.5 collective-permute-start.20
  137.2 2.7 %shard_map.70.refs_0_ = bf16[4,128,512]{2,1,0:T(8,128)(2,1)S(1)} custom-call(s32[4]{0:T(128)S(1)} %pad_add_fusion.1.where_ref, s32[4,4]{1,0:T(4,128)S(1)} %copy-done.2, s32[4,8]{1,0:T(4,128)S(1)} %pad_add_fusion.table_ref, bf16[4,128,1024]{2,1,0:T(8,128)(2,1)S(1)} %pad_maximum_fusion.q_ref, bf16[2048,128]{1,0:T(8,128)(2,1)S(1)} %select_select_fusion.1.refs_0_, ...), custom_call_target="tpu_custom_call" | custom-call | flops 1 | bytes 1 | tf_op jit(solution)/shard_map/pallas_call | solution.py:119
  140.0 0.1 collective-permute-start.18
  140.0 16.0 %collective-permute-done.17.refs_1_ = bf16[4,128,512]{2,1,0:T(8,128)(2,1)S(1)} collective-permute-done((bf16[4,128,512]{2,1,0:T(8,128)(2,1)S(1)}, bf16[4,128,512]{2,1,0:T(8,128)(2,1)S(1)}, u32[]{:S(2)}, u32[]{:S(2)}) %collective-permute-start.17) | collective-permute-done | bytes 524320 | tf_op jit(solution)/shard_map/ppermute | solution.py:224
  156.1 2.7 %shard_map.71.refs_4_ = bf16[4,128,512]{2,1,0:T(8,128)(2,1)S(1)} custom-call(s32[4]{0:T(128)S(1)} %pad_add_fusion.1.where_ref, s32[4,4]{1,0:T(4,128)S(1)} %copy-done.2, s32[4,8]{1,0:T(4,128)S(1)} %pad_add_fusion.table_ref, bf16[4,128,1024]{2,1,0:T(8,128)(2,1)S(1)} %pad_maximum_fusion.q_ref, bf16[2048,128]{1,0:T(8,128)(2,1)S(1)} %select_select_fusion.refs_0_, ...), custom_call_target="tpu_custom_call" | custom-call | flops 1 | bytes 1 | tf_op jit(solution)/shard_map/pallas_call | solution.py:119
  158.8 0.1 collective-permute-start.21
  158.9 9.4 %collective-permute-done.20.refs_5_ = bf16[4,128,512]{2,1,0:T(8,128)(2,1)S(1)} collective-permute-done((bf16[4,128,512]{2,1,0:T(8,128)(2,1)S(1)}, bf16[4,128,512]{2,1,0:T(8,128)(2,1)S(1)}, u32[]{:S(2)}, u32[]{:S(2)}) %collective-permute-start.20) | collective-permute-done | bytes 524320 | tf_op jit(solution)/shard_map/ppermute | solution.py:224
  168.4 0.6 collective-permute-start.19
  168.9 0.9 collective-permute-done.22.refs_7_
  169.9 0.4 collective-permute-done.19.refs_3_
  170.3 1.1 shard_map.72.rows_ref
  171.4 12.9 %shard_map.73 = bf16[512,4096]{1,0:T(8,128)(2,1)} custom-call(bf16[512,2048]{1,0:T(8,128)(2,1)S(1)} %shard_map.72.rows_ref, bf16[2,2048,2048]{2,1,0:T(8,128)(2,1)} %bitcast.15), custom_call_target="tpu_custom_call" | custom-call | flops 8589934592 | bytes 23068672 | tf_op jit(solution)/shard_map/pallas_call | solution.py:177
  (35 shorter events, 0.4 us)
Async XLA Ops:
  6.5 1.2 copy-start
  6.5 51.1 %all-gather.3.cloned.1.call-start = ((), (), s32[]{:S(2)}) async-start(), calls=%async_computation | async-start | bytes 2621440 | tf_op jit(solution)/shard_map/all_gather | solution.py:271
  8.6 162.8 %all-gather.5.cloned.1.call-start = ((), (), s32[]{:S(2)}) async-start(), calls=%async_computation.1 | async-start | bytes 18874368 | tf_op jit(solution)/shard_map/all_gather | solution.py:295
  8.7 3.2 %copy-start.3 = (bf16[512,512]{1,0:T(8,128)(2,1)S(1)}, bf16[512,512]{1,0:T(8,128)(2,1)}, u32[]{:S(2)}) copy-start(bf16[512,512]{1,0:T(8,128)(2,1)} %param.8) | copy-start | bytes 1572868
  11.4 5.8 %collective-permute-start.1 = (bf16[2,128,2048]{2,1,0:T(8,128)(2,1)}, bf16[2,128,2048]{2,1,0:T(8,128)(2,1)S(1)}, u32[]{:S(2)}, u32[]{:S(2)}) collective-permute-start(bf16[2,128,2048]{2,1,0:T(8,128)(2,1)} %get-tuple-element.86), channel_id=1, source_target_pairs={{0,1},{1,0},{2,3},{3,2},{4,5},{5,4},{6,7},{7,6},{8,9},{9,8},{10,11... | collective-permute-start | bytes 3145736 | tf_op jit(solution)/shard_map/ppermute | solution.py:219
  13.8 15.6 %collective-permute-start.2 = (bf16[1024,256]{1,0:T(8,128)(2,1)}, bf16[1024,256]{1,0:T(8,128)(2,1)}, u32[]{:S(2)}, u32[]{:S(2)}) collective-permute-start(bf16[1024,256]{1,0:T(8,128)(2,1)} %pad_maximum_fusion.3), channel_id=1, source_target_pairs={{0,2},{1,3},{2,0},{3,1},{4,6},{5,7},{6,4},{7,5},{8,10},{9,11},{10,... | collective-permute-start | bytes 1572872 | tf_op jit(solution)/shard_map/ppermute | solution.py:224
  17.3 1.1 copy-start.4
  18.3 33.4 %collective-permute-start.3 = (bf16[4,128,1024]{2,1,0:T(8,128)(2,1)S(1)}, bf16[4,128,1024]{2,1,0:T(8,128)(2,1)S(1)}, u32[]{:S(2)}, u32[]{:S(2)}) collective-permute-start(bf16[4,128,1024]{2,1,0:T(8,128)(2,1)S(1)} %pad_maximum_fusion.1), channel_id=1, source_target_pairs={{0,2},{1,3},{2,0},{3,1},{4,6},{5,7},{6,4},{7,5},{8,10},{9,11},{10,... | collective-permute-start | bytes 3145736 | tf_op jit(solution)/shard_map/ppermute | solution.py:224
  18.3 1.2 collective-permute-start
  19.6 32.1 %collective-permute-start.4 = (s32[4,8]{1,0:T(4,128)S(1)}, s32[4,8]{1,0:T(4,128)S(1)}, u32[]{:S(2)}, u32[]{:S(2)}) collective-permute-start(s32[4,8]{1,0:T(4,128)S(1)} %pad_add_fusion.table_ref), channel_id=1, source_target_pairs={{0,2},{1,3},{2,0},{3,1},{4,6},{5,7},{6,4},{7,5},{8,10},{9,11},{10,... | collective-permute-start | bytes 392 | tf_op jit(solution)/shard_map/ppermute | solution.py:224
  57.6 16.7 %collective-permute-start.10 = (bf16[2048,128]{1,0:T(8,128)(2,1)S(1)}, bf16[2048,128]{1,0:T(8,128)(2,1)S(1)}, u32[]{:S(2)}, u32[]{:S(2)}) collective-permute-start(bf16[2048,128]{1,0:T(8,128)(2,1)S(1)} %fusion.refs_0_), channel_id=1, source_target_pairs={{4,0},{5,1},{6,2},{7,3},{8,4},{9,5},{10,6},{11,7},{12,8},{13,9},{1... | collective-permute-start | bytes 1572872 | tf_op jit(solution)/shard_map/ppermute | solution.py:229
  58.9 16.9 %collective-permute-start.9 = (bf16[2048,128]{1,0:T(8,128)(2,1)S(1)}, bf16[2048,128]{1,0:T(8,128)(2,1)}, u32[]{:S(2)}, u32[]{:S(2)}) collective-permute-start(bf16[2048,128]{1,0:T(8,128)(2,1)S(1)} %fusion.refs_0_), channel_id=1, source_target_pairs={{0,4},{1,5},{2,6},{3,7},{4,8},{5,9},{6,10},{7,11},{8,12},{9,13},{1... | collective-permute-start | bytes 1572872 | tf_op jit(solution)/shard_map/ppermute | solution.py:229
  64.3 21.3 %collective-permute-start.5 = (bf16[2048,128]{1,0:T(8,128)(2,1)S(1)}, bf16[2048,128]{1,0:T(8,128)(2,1)S(1)}, u32[]{:S(2)}, u32[]{:S(2)}) collective-permute-start(bf16[2048,128]{1,0:T(8,128)(2,1)S(1)} %pad_maximum_fusion.4.refs_0_), channel_id=1, source_target_pairs={{4,0},{5,1},{6,2},{7,3},{8,4},{9,5},{10,6},{11,7},{12,8},{13,9},{1... | collective-permute-start | bytes 1572872 | tf_op jit(solution)/shard_map/ppermute | solution.py:229
  65.6 21.3 %collective-permute-start.7 = (bf16[2048,128]{1,0:T(8,128)(2,1)S(1)}, bf16[2048,128]{1,0:T(8,128)(2,1)}, u32[]{:S(2)}, u32[]{:S(2)}) collective-permute-start(bf16[2048,128]{1,0:T(8,128)(2,1)S(1)} %pad_maximum_fusion.4.refs_0_), channel_id=1, source_target_pairs={{0,4},{1,5},{2,6},{3,7},{4,8},{5,9},{6,10},{7,11},{8,12},{9,13},{1... | collective-permute-start | bytes 1572872 | tf_op jit(solution)/shard_map/ppermute | solution.py:229
  75.8 21.0 %collective-permute-start.12 = (bf16[2048,128]{1,0:T(8,128)(2,1)S(1)}, bf16[2048,128]{1,0:T(8,128)(2,1)S(1)}, u32[]{:S(2)}, u32[]{:S(2)}) collective-permute-start(bf16[2048,128]{1,0:T(8,128)(2,1)S(1)} %collective-permute-done.10), channel_id=1, source_target_pairs={{4,0},{5,1},{6,2},{7,3},{8,4},{9,5},{10,6},{11,7},{20,16},{21,17},... | collective-permute-start | bytes 1572872 | tf_op jit(solution)/shard_map/ppermute | solution.py:229
  77.1 19.7 %collective-permute-start.11 = (bf16[2048,128]{1,0:T(8,128)(2,1)}, bf16[2048,128]{1,0:T(8,128)(2,1)S(1)}, u32[]{:S(2)}, u32[]{:S(2)}) collective-permute-start(bf16[2048,128]{1,0:T(8,128)(2,1)} %collective-permute-done.9), channel_id=1, source_target_pairs={{4,8},{5,9},{6,10},{7,11},{8,12},{9,13},{10,14},{11,15},{20,24},{2... | collective-permute-start | bytes 1572872 | tf_op jit(solution)/shard_map/ppermute | solution.py:229
  85.6 21.3 %collective-permute-start.6 = (bf16[2048,128]{1,0:T(8,128)(2,1)S(1)}, bf16[2048,128]{1,0:T(8,128)(2,1)S(1)}, u32[]{:S(2)}, u32[]{:S(2)}) collective-permute-start(bf16[2048,128]{1,0:T(8,128)(2,1)S(1)} %collective-permute-done.5), channel_id=1, source_target_pairs={{4,0},{5,1},{6,2},{7,3},{8,4},{9,5},{10,6},{11,7},{20,16},{21,17},... | collective-permute-start | bytes 1572872 | tf_op jit(solution)/shard_map/ppermute | solution.py:229
  86.9 21.3 %collective-permute-start.8 = (bf16[2048,128]{1,0:T(8,128)(2,1)}, bf16[2048,128]{1,0:T(8,128)(2,1)S(1)}, u32[]{:S(2)}, u32[]{:S(2)}) collective-permute-start(bf16[2048,128]{1,0:T(8,128)(2,1)} %collective-permute-done.7), channel_id=1, source_target_pairs={{4,8},{5,9},{6,10},{7,11},{8,12},{9,13},{10,14},{11,15},{20,24},{2... | collective-permute-start | bytes 1572872 | tf_op jit(solution)/shard_map/ppermute | solution.py:229
  87.7 23.3 %copy-start.2 = (s32[4,4]{1,0:T(4,128)S(1)}, s32[4,4]{1,0:T(4,128)}, u32[]{:S(2)}) copy-start(s32[4,4]{1,0:T(4,128)} %constant.37.clone.order_ref) | copy-start | bytes 196
  106.9 20.3 %collective-permute-start.14 = (bf16[2048,128]{1,0:T(8,128)(2,1)S(1)}, bf16[2048,128]{1,0:T(8,128)(2,1)S(1)}, u32[]{:S(2)}, u32[]{:S(2)}) collective-permute-start(bf16[2048,128]{1,0:T(8,128)(2,1)S(1)} %collective-permute-done.6), channel_id=1, source_target_pairs={{4,0},{5,1},{6,2},{7,3},{20,16},{21,17},{22,18},{23,19}} | collective-permute-start | bytes 1572872 | tf_op jit(solution)/shard_map/ppermute | solution.py:229
  108.2 19.0 %collective-permute-start.13 = (bf16[2048,128]{1,0:T(8,128)(2,1)S(1)}, bf16[2048,128]{1,0:T(8,128)(2,1)S(1)}, u32[]{:S(2)}, u32[]{:S(2)}) collective-permute-start(bf16[2048,128]{1,0:T(8,128)(2,1)S(1)} %collective-permute-done.8), channel_id=1, source_target_pairs={{8,12},{9,13},{10,14},{11,15},{24,28},{25,29},{26,30},{27,31}} | collective-permute-start | bytes 1572872 | tf_op jit(solution)/shard_map/ppermute | solution.py:229
  109.0 23.9 %collective-permute-start.16 = (bf16[2048,128]{1,0:T(8,128)(2,1)S(1)}, bf16[2048,128]{1,0:T(8,128)(2,1)S(1)}, u32[]{:S(2)}, u32[]{:S(2)}) collective-permute-start(bf16[2048,128]{1,0:T(8,128)(2,1)S(1)} %collective-permute-done.12), channel_id=1, source_target_pairs={{4,0},{5,1},{6,2},{7,3},{20,16},{21,17},{22,18},{23,19}} | collective-permute-start | bytes 1572872 | tf_op jit(solution)/shard_map/ppermute | solution.py:229
  110.3 22.6 %collective-permute-start.15 = (bf16[2048,128]{1,0:T(8,128)(2,1)S(1)}, bf16[2048,128]{1,0:T(8,128)(2,1)S(1)}, u32[]{:S(2)}, u32[]{:S(2)}) collective-permute-start(bf16[2048,128]{1,0:T(8,128)(2,1)S(1)} %collective-permute-done.11), channel_id=1, source_target_pairs={{8,12},{9,13},{10,14},{11,15},{24,28},{25,29},{26,30},{27,31}} | collective-permute-start | bytes 1572872 | tf_op jit(solution)/shard_map/ppermute | solution.py:229
  130.0 26.1 %collective-permute-start.17 = (bf16[4,128,512]{2,1,0:T(8,128)(2,1)S(1)}, bf16[4,128,512]{2,1,0:T(8,128)(2,1)S(1)}, u32[]{:S(2)}, u32[]{:S(2)}) collective-permute-start(bf16[4,128,512]{2,1,0:T(8,128)(2,1)S(1)} %shard_map.68), channel_id=1, source_target_pairs={{0,2},{1,3},{2,0},{3,1},{4,6},{5,7},{6,4},{7,5},{8,10},{9,11},{10,... | collective-permute-start | bytes 1572872 | tf_op jit(solution)/shard_map/ppermute | solution.py:224
  135.7 32.6 %collective-permute-start.20 = (bf16[4,128,512]{2,1,0:T(8,128)(2,1)S(1)}, bf16[4,128,512]{2,1,0:T(8,128)(2,1)S(1)}, u32[]{:S(2)}, u32[]{:S(2)}) collective-permute-start(bf16[4,128,512]{2,1,0:T(8,128)(2,1)S(1)} %shard_map.69), channel_id=1, source_target_pairs={{0,2},{1,3},{2,0},{3,1},{4,6},{5,7},{6,4},{7,5},{8,10},{9,11},{10,... | collective-permute-start | bytes 1572872 | tf_op jit(solution)/shard_map/ppermute | solution.py:224
  140.0 29.0 %collective-permute-start.18 = (bf16[2,128,512]{2,1,0:T(8,128)(2,1)S(1)}, bf16[2,128,512]{2,1,0:T(8,128)(2,1)S(1)}, u32[]{:S(2)}, u32[]{:S(2)}) collective-permute-start(bf16[2,128,512]{2,1,0:T(8,128)(2,1)S(1)} %slice.54), channel_id=1, source_target_pairs={{0,1},{1,0},{2,3},{3,2},{4,5},{5,4},{6,7},{7,6},{8,9},{9,8},{10,11... | collective-permute-start | bytes 786440 | tf_op jit(solution)/shard_map/ppermute | solution.py:219
  158.8 10.2 %collective-permute-start.21 = (bf16[2,128,512]{2,1,0:T(8,128)(2,1)S(1)}, bf16[2,128,512]{2,1,0:T(8,128)(2,1)S(1)}, u32[]{:S(2)}, u32[]{:S(2)}) collective-permute-start(bf16[2,128,512]{2,1,0:T(8,128)(2,1)S(1)} %slice.56), channel_id=1, source_target_pairs={{0,1},{1,0},{2,3},{3,2},{4,5},{5,4},{6,7},{7,6},{8,9},{9,8},{10,11... | collective-permute-start | bytes 786440 | tf_op jit(solution)/shard_map/ppermute | solution.py:219
  168.3 1.6 collective-permute-start.22
  168.4 1.9 collective-permute-start.19
  171.4 12.9 %copy-start.1 = (bf16[128,4096]{1,0:T(8,128)(2,1)S(1)}, bf16[128,4096]{1,0:T(8,128)(2,1)}, u32[]{:S(2)}) copy-start(bf16[128,4096]{1,0:T(8,128)(2,1)} %param.10) | copy-start | bytes 3145732
Sparse Core Ops, SparseCore 0:
  8.9 48.6 all-gather.2
  59.5 102.4 all-gather.4

commit v10 on v8

--- a/solution.py
+++ b/solution.py
@@ -130,11 +130,7 @@
             out_specs=tile if last else (tile,) * 3,
         ),
         compiler_params=pltpu.CompilerParams(vmem_limit_bytes=VMEM_LIMIT),
-        cost_estimate=pl.CostEstimate(
-            flops=4 * blocks * QB * rows * columns,
-            bytes_accessed=2 * blocks * (rows * columns // 2 + 6 * QB * columns),
-            transcendentals=blocks * QB * rows * columns // HD,
-        ),
+        cost_estimate=pl.CostEstimate(flops=1, bytes_accessed=1, transcendentals=0),
     )(where, order, table, queries, *pieces, *state)
 
 
@@ -280,10 +276,13 @@
     gathered = lax.all_gather(columns, LINE, axis=0, tiled=True)
 
     mine = jnp.concatenate([half_of(keys, side), half_of(values, side)], 0)
-    theirs = jnp.concatenate([half_of(keys, 1 - side), half_of(values, 1 - side)], 0)
+    hops = {-way: move(mine, 1, way) for way in (1, -1)}
+    theirs = jnp.concatenate(
+        [half_of(after(array, mine), 1 - side) for array in (keys, values)], 0
+    )
     theirs = swap_side(theirs)
 
-    query_blocks = queries.reshape(2, 2, QB, H * HD)
+    query_blocks = after(queries, mine).reshape(2, 2, QB, H * HD)
     far_queries = swap_core(query_blocks[:, 1])
     far_table = swap_core(block_table)
     table = jnp.concatenate([block_table[0::2], far_table[1::2]], 0)
@@ -292,10 +291,9 @@
     def my_blocks(which):
         return jnp.concatenate([half_of(near_queries, which), half_of(far_queries, which)], 0)
 
-    across_queries = swap_side(my_blocks(1 - side))
+    across_queries = swap_side(after(my_blocks(1 - side), theirs, *hops.values()))
     across_table = swap_side(table)
 
-    hops = {-way: move(mine, 1, way) for way in (1, -1)}
     gathered = after(gathered, theirs, across_queries, across_table, *hops.values())
     gates = ({2: (gathered,)}, {1: (gathered,)})
     gathered = lax.all_gather(gathered, PLANE, axis=0, tiled=True)

time: 203 us -> 214 us (1.054)
  starting transfers between devices: 27.6 us -> 35 us
  waiting for transfers between devices: 116 us -> 120 us
    ppermute x12, waiting for transfers between devices: 37 us -> 54.5 us  [move(): lax.ppermute(array, SEQ, [(index(o, s, c), index(o + way, s, c)) for o, s...]
    all_gather x1, waiting for transfers between devices: 9.19 us -> 0.01 us  [body(): gathered = lax.all_gather(columns, LINE, axis=0, tiled=True)]
    ppermute x12, starting transfers between devices: 20.4 us -> 26.9 us  [move(): lax.ppermute(array, SEQ, [(index(o, s, c), index(o + way, s, c)) for o, s...]
    ppermute x4, waiting for transfers between devices: 5.81 us -> 3.01 us  [swap_core(): lax.ppermute(array, SEQ, [(index(o, s, c), index(o, s, 1 - c)) for o, s,...]
    ppermute x4, waiting for transfers between devices: 64.1 us -> 61.5 us  [swap_side(): lax.ppermute(array, SEQ, [(index(o, s, c), index(o, 1 - s, c)) for o, s,...]
where the time goes in v10:
time: 214 us
  waiting for transfers between devices  120 us (56%)
  starting transfers between devices  35 us (16%)
  Pallas kernels  33.7 us (16%)
  between operations  13.7 us (6%)
  local copies, waits for them, and re-layouts  7.23 us (3%)
  other arithmetic  3.76 us (2%)
    ppermute x4, waiting for transfers between devices, swap_side(): lax.ppermute(array, SEQ, [(index(o, s, c), index(o, 1 - s, c)) for o, s,...  61.5 us
    ppermute x12, waiting for transfers between devices, move(): lax.ppermute(array, SEQ, [(index(o, s, c), index(o + way, s, c)) for o, s...  54.5 us
    ppermute x12, starting transfers between devices, move(): lax.ppermute(array, SEQ, [(index(o, s, c), index(o + way, s, c)) for o, s...  26.9 us
    pallas_call x4, Pallas kernels, attention(): pl.pallas_call(functools.partial(attention_kernel, n_chip, slots, not sta...  19.7 us
    pallas_call x1, Pallas kernels, project(): pl.pallas_call(project_kernel, out_shape=jax.ShapeDtypeStruct((rows.shape...  12.9 us
    ppermute x4, starting transfers between devices, swap_side(): lax.ppermute(array, SEQ, [(index(o, s, c), index(o, 1 - s, c)) for o, s,...  7.43 us
  transfers between devices with their start and end apart: 22, of which 11 were waited for; matrix products, arithmetic and copies ran while one was open for 4% of the time, Pallas kernels for 10%

profile of v10, /device:TPU:0, one launch (start us, length us, event | category | flops | bytes accessed | tf_op | source)
XLA Modules:
  0.0 213.9 jit_solution(13632770018388504973)
XLA Ops:
  6.5 1.2 copy-done
  7.8 0.8 constant_dynamic-slice_fusion.3
  8.6 0.0 all-gather.3.cloned.1.call-update
  8.6 0.0 all-gather.5.cloned.1.call-start
  8.7 0.0 copy-start.3
  8.7 1.2 constant_dynamic-slice_fusion.5
  10.0 0.5 copy-done.3
  10.4 1.1 fusion
  11.5 0.5 collective-permute-start.1
  12.1 0.8 pad_maximum_fusion.3
  12.9 2.9 %collective-permute-start.3 = (bf16[1024,256]{1,0:T(8,128)(2,1)}, bf16[1024,256]{1,0:T(8,128)(2,1)S(1)}, u32[]{:S(2)}, u32[]{:S(2)}) collective-permute-start(bf16[1024,256]{1,0:T(8,128)(2,1)} %pad_maximum_fusion.3), channel_id=1, source_target_pairs={{0,2},{1,3},{2,0},{3,1},{4,6},{5,7},{6,4},{7,5},{8,10},{9,11},{10,... | collective-permute-start | bytes 1572872 | tf_op jit(solution)/shard_map/ppermute | solution.py:229
  15.8 1.3 collective-permute-start.2
  17.1 5.4 %collective-permute-start.4 = (bf16[1024,256]{1,0:T(8,128)(2,1)S(1)}, bf16[1024,256]{1,0:T(8,128)(2,1)}, u32[]{:S(2)}, u32[]{:S(2)}) collective-permute-start(bf16[1024,256]{1,0:T(8,128)(2,1)S(1)} %pad_maximum_fusion.2.refs_0_), channel_id=1, source_target_pairs={{0,4},{1,5},{2,6},{3,7},{4,8},{5,9},{6,10},{7,11},{8,12},{9,13},{1... | collective-permute-start | bytes 1572872 | tf_op jit(solution)/shard_map/ppermute | solution.py:234
  22.5 0.1 dynamic-slice_bitcast_fusion
  22.6 0.0 copy-start.6
  22.6 2.1 constant_dynamic-slice_fusion
  24.7 1.1 pad_maximum_fusion.1
  25.7 2.5 %collective-permute-done.3.refs_3_ = bf16[1024,256]{1,0:T(8,128)(2,1)S(1)} collective-permute-done((bf16[1024,256]{1,0:T(8,128)(2,1)}, bf16[1024,256]{1,0:T(8,128)(2,1)S(1)}, u32[]{:S(2)}, u32[]{:S(2)}) %collective-permute-start.3) | collective-permute-done | bytes 524320 | tf_op jit(solution)/shard_map/ppermute | solution.py:229
  28.2 23.5 %collective-permute-done.2 = bf16[1024,256]{1,0:T(8,128)(2,1)S(1)} collective-permute-done((bf16[1024,256]{1,0:T(8,128)(2,1)S(1)}, bf16[1024,256]{1,0:T(8,128)(2,1)S(1)}, u32[]{:S(2)}, u32[]{:S(2)}) %collective-permute-start.2) | collective-permute-done | bytes 524320 | tf_op jit(solution)/shard_map/ppermute | solution.py:234
  51.7 0.1 collective-permute-start
  51.8 1.1 collective-permute-done
  53.0 2.0 collective-permute-start.6
  55.0 17.0 %collective-permute-done.6.table_ref = s32[4,8]{1,0:T(4,128)S(1)} collective-permute-done((s32[4,8]{1,0:T(4,128)S(1)}, s32[4,8]{1,0:T(4,128)S(1)}, u32[]{:S(2)}, u32[]{:S(2)}) %collective-permute-start.6) | collective-permute-done | bytes 160 | tf_op jit(solution)/shard_map/ppermute | solution.py:229
  72.0 0.0 collective-permute-done.5.q_ref
  72.0 0.0 all-gather.5.cloned.1.call-update
  72.1 0.1 pad_add_fusion.3
  72.2 1.3 collective-permute-start.10
  73.5 11.0 %collective-permute-start.9 = (bf16[1024,256]{1,0:T(8,128)(2,1)S(1)}, bf16[1024,256]{1,0:T(8,128)(2,1)S(1)}, u32[]{:S(2)}, u32[]{:S(2)}) collective-permute-start(bf16[1024,256]{1,0:T(8,128)(2,1)S(1)} %collective-permute-done.3.refs_3_), channel_id=1, source_target_pairs={{0,4},{1,5},{2,6},{3,7},{4,8},{5,9},{6,10},{7,11},{8,12},{9,13},{1... | collective-permute-start | bytes 1572872 | tf_op jit(solution)/shard_map/ppermute | solution.py:234
  84.5 0.1 pad_add_fusion.1.where_ref
  84.6 1.3 collective-permute-start.7
  85.9 0.7 collective-permute-start.8
  86.6 0.1 broadcast_select_fusion.1.refs_1_
  86.6 1.1 pad_maximum_fusion.q_ref
  87.8 7.6 %collective-permute-done.10 = bf16[1024,256]{1,0:T(8,128)(2,1)S(1)} collective-permute-done((bf16[1024,256]{1,0:T(8,128)(2,1)S(1)}, bf16[1024,256]{1,0:T(8,128)(2,1)S(1)}, u32[]{:S(2)}, u32[]{:S(2)}) %collective-permute-start.10) | collective-permute-done | bytes 524320 | tf_op jit(solution)/shard_map/ppermute | solution.py:234
  95.4 1.3 collective-permute-start.12
  96.7 0.7 collective-permute-start.11
  97.4 0.1 broadcast_select_fusion.refs_4_
  97.4 0.0 copy-start.2
  97.4 9.2 %collective-permute-done.7 = bf16[1024,256]{1,0:T(8,128)(2,1)S(1)} collective-permute-done((bf16[1024,256]{1,0:T(8,128)(2,1)S(1)}, bf16[1024,256]{1,0:T(8,128)(2,1)S(1)}, u32[]{:S(2)}, u32[]{:S(2)}) %collective-permute-start.7) | collective-permute-done | bytes 524320 | tf_op jit(solution)/shard_map/ppermute | solution.py:234
  106.6 0.0 collective-permute-done.8
  106.6 1.3 collective-permute-start.14
  107.9 0.7 collective-permute-start.13
  108.6 0.1 select_select_fusion.3.refs_2_
  108.7 9.1 %collective-permute-done.12 = bf16[1024,256]{1,0:T(8,128)(2,1)S(1)} collective-permute-done((bf16[1024,256]{1,0:T(8,128)(2,1)S(1)}, bf16[1024,256]{1,0:T(8,128)(2,1)S(1)}, u32[]{:S(2)}, u32[]{:S(2)}) %collective-permute-start.12) | collective-permute-done | bytes 524320 | tf_op jit(solution)/shard_map/ppermute | solution.py:234
  117.8 0.0 collective-permute-done.11
  117.8 1.3 collective-permute-start.16
  119.1 0.7 collective-permute-start.15
  119.8 0.1 select_select_fusion.2.refs_5_
  119.9 6.3 %shard_map.64 = (f32[4,128,1024]{2,1,0:T(8,128)S(1)}, f32[4,128,1024]{2,1,0:T(8,128)S(1)}, f32[4,128,1024]{2,1,0:T(8,128)S(1)}) custom-call(s32[4]{0:T(128)S(1)} %get-tuple-element.69.where_ref, s32[4,4]{1,0:T(4,128)S(1)} %copy-done.2, s32[4,8]{1,0:T(4,128)S(1)} %collective-permute-done.6.table_ref, bf16[4,128,1024]{2,1,0:T(8,128)(2,1)S(1)} %collective-permute-done.5.q_ref, ...), custom_call_target="tpu_custom_call" | custom-call | flops 1 | bytes 1 | tf_op jit(solution)/shard_map/pallas_call | solution.py:123
  126.2 6.3 %shard_map.65 = (f32[4,128,1024]{2,1,0:T(8,128)S(1)}, f32[4,128,1024]{2,1,0:T(8,128)S(1)}, f32[4,128,1024]{2,1,0:T(8,128)S(1)}) custom-call(s32[4]{0:T(128)S(1)} %pad_add_fusion.1.where_ref, s32[4,4]{1,0:T(4,128)S(1)} %copy-done.2, s32[4,8]{1,0:T(4,128)S(1)} %pad_add_fusion.table_ref, bf16[4,128,1024]{2,1,0:T(8,128)(2,1)S(1)} %pad_maximum_fusion.q_ref, ...), custom_call_target="tpu_custom_call" | custom-call | flops 1 | bytes 1 | tf_op jit(solution)/shard_map/pallas_call | solution.py:123
  132.5 0.0 collective-permute-done.14
  132.6 0.1 select_select_fusion.1.refs_0_
  132.7 5.1 %collective-permute-done.16 = bf16[1024,256]{1,0:T(8,128)(2,1)S(1)} collective-permute-done((bf16[1024,256]{1,0:T(8,128)(2,1)S(1)}, bf16[1024,256]{1,0:T(8,128)(2,1)S(1)}, u32[]{:S(2)}, u32[]{:S(2)}) %collective-permute-start.16) | collective-permute-done | bytes 524320 | tf_op jit(solution)/shard_map/ppermute | solution.py:234
  137.8 0.1 select_select_fusion.refs_1_
  137.9 3.6 %shard_map.67 = bf16[4,128,1024]{2,1,0:T(8,128)(2,1)S(1)} custom-call(s32[4]{0:T(128)S(1)} %get-tuple-element.69.where_ref, s32[4,4]{1,0:T(4,128)S(1)} %copy-done.2, s32[4,8]{1,0:T(4,128)S(1)} %collective-permute-done.6.table_ref, bf16[4,128,1024]{2,1,0:T(8,128)(2,1)S(1)} %collective-permute-done.5.q_ref, bf16[1024,256]{1,0:T(8,128)(2,1)S(1)} %select_select_fusion.1.refs_0_, ...), custom_call_target="tpu_custom_call" | custom-call | flops 1 | bytes 1 | tf_op jit(solution)/shard_map/pallas_call | solution.py:123
  141.4 2.5 %collective-permute-start.17 = (bf16[4,128,1024]{2,1,0:T(8,128)(2,1)S(1)}, bf16[4,128,1024]{2,1,0:T(8,128)(2,1)S(1)}, u32[]{:S(2)}, u32[]{:S(2)}) collective-permute-start(bf16[4,128,1024]{2,1,0:T(8,128)(2,1)S(1)} %shard_map.67), channel_id=1, source_target_pairs={{0,2},{1,3},{2,0},{3,1},{4,6},{5,7},{6,4},{7,5},{8,10},{9,11},{10,... | collective-permute-start | bytes 3145736 | tf_op jit(solution)/shard_map/ppermute | solution.py:229
  143.9 3.6 %shard_map.66.near_ref = bf16[4,128,1024]{2,1,0:T(8,128)(2,1)S(1)} custom-call(s32[4]{0:T(128)S(1)} %pad_add_fusion.1.where_ref, s32[4,4]{1,0:T(4,128)S(1)} %copy-done.2, s32[4,8]{1,0:T(4,128)S(1)} %pad_add_fusion.table_ref, bf16[4,128,1024]{2,1,0:T(8,128)(2,1)S(1)} %pad_maximum_fusion.q_ref, bf16[1024,256]{1,0:T(8,128)(2,1)S(1)} %select_select_fusion.1.refs_0_, ...), custom_call_target="tpu_custom_call" | custom-call | flops 1 | bytes 1 | tf_op jit(solution)/shard_map/pallas_call | solution.py:123
  147.5 0.1 collective-permute-start.18
  147.6 42.0 %collective-permute-done.17.across_ref = bf16[4,128,1024]{2,1,0:T(8,128)(2,1)S(1)} collective-permute-done((bf16[4,128,1024]{2,1,0:T(8,128)(2,1)S(1)}, bf16[4,128,1024]{2,1,0:T(8,128)(2,1)S(1)}, u32[]{:S(2)}, u32[]{:S(2)}) %collective-permute-start.17) | collective-permute-done | bytes 1048608 | tf_op jit(solution)/shard_map/ppermute | solution.py:229
  189.6 0.1 collective-permute-start.19
  189.7 1.9 collective-permute-done.19.far_across_ref
  191.6 1.0 shard_map.68.rows_ref
  192.6 1.5 all-gather.5.cloned.1.call-done
  194.1 12.9 %shard_map.69 = bf16[512,4096]{1,0:T(8,128)(2,1)} custom-call(bf16[512,2048]{1,0:T(8,128)(2,1)S(1)} %shard_map.68.rows_ref, bf16[2,2048,2048]{2,1,0:T(8,128)(2,1)} %bitcast.15), custom_call_target="tpu_custom_call" | custom-call | flops 8589934592 | bytes 23068672 | tf_op jit(solution)/shard_map/pallas_call | solution.py:182
  (26 shorter events, 0.3 us)
Async XLA Ops:
  6.5 1.2 copy-start
  6.5 65.5 %all-gather.3.cloned.1.call-start = ((), (), s32[]{:S(2)}) async-start(), calls=%async_computation | async-start | bytes 2621440 | tf_op jit(solution)/shard_map/all_gather | solution.py:276
  8.6 185.5 %all-gather.5.cloned.1.call-start = ((), (), s32[]{:S(2)}) async-start(), calls=%async_computation.1 | async-start | bytes 18874368 | tf_op jit(solution)/shard_map/all_gather | solution.py:299
  8.7 1.8 copy-start.3
  10.4 1.6 copy-start.4
  10.4 1.6 copy-start.5
  11.5 11.0 %collective-permute-start.1 = (bf16[2,128,2048]{2,1,0:T(8,128)(2,1)}, bf16[2,128,2048]{2,1,0:T(8,128)(2,1)}, u32[]{:S(2)}, u32[]{:S(2)}) collective-permute-start(bf16[2,128,2048]{2,1,0:T(8,128)(2,1)} %get-tuple-element.72), channel_id=1, source_target_pairs={{0,1},{1,0},{2,3},{3,2},{4,5},{5,4},{6,7},{7,6},{8,9},{9,8},{10,11... | collective-permute-start | bytes 3145736 | tf_op jit(solution)/shard_map/ppermute | solution.py:224
  12.9 15.3 %collective-permute-start.3 = (bf16[1024,256]{1,0:T(8,128)(2,1)}, bf16[1024,256]{1,0:T(8,128)(2,1)S(1)}, u32[]{:S(2)}, u32[]{:S(2)}) collective-permute-start(bf16[1024,256]{1,0:T(8,128)(2,1)} %pad_maximum_fusion.3), channel_id=1, source_target_pairs={{0,2},{1,3},{2,0},{3,1},{4,6},{5,7},{6,4},{7,5},{8,10},{9,11},{10,... | collective-permute-start | bytes 1572872 | tf_op jit(solution)/shard_map/ppermute | solution.py:229
  15.8 35.9 %collective-permute-start.2 = (bf16[1024,256]{1,0:T(8,128)(2,1)S(1)}, bf16[1024,256]{1,0:T(8,128)(2,1)S(1)}, u32[]{:S(2)}, u32[]{:S(2)}) collective-permute-start(bf16[1024,256]{1,0:T(8,128)(2,1)S(1)} %pad_maximum_fusion.2.refs_0_), channel_id=1, source_target_pairs={{4,0},{5,1},{6,2},{7,3},{8,4},{9,5},{10,6},{11,7},{12,8},{13,9},{1... | collective-permute-start | bytes 1572872 | tf_op jit(solution)/shard_map/ppermute | solution.py:234
  17.1 34.6 %collective-permute-start.4 = (bf16[1024,256]{1,0:T(8,128)(2,1)S(1)}, bf16[1024,256]{1,0:T(8,128)(2,1)}, u32[]{:S(2)}, u32[]{:S(2)}) collective-permute-start(bf16[1024,256]{1,0:T(8,128)(2,1)S(1)} %pad_maximum_fusion.2.refs_0_), channel_id=1, source_target_pairs={{0,4},{1,5},{2,6},{3,7},{4,8},{5,9},{6,10},{7,11},{8,12},{9,13},{1... | collective-permute-start | bytes 1572872 | tf_op jit(solution)/shard_map/ppermute | solution.py:234
  22.6 29.2 %copy-start.6 = (s32[4,8]{1,0:T(4,128)S(1)}, s32[4,8]{1,0:T(4,128)}, u32[]{:S(2)}) copy-start(s32[4,8]{1,0:T(4,128)} %param.9) | copy-start | bytes 388
  51.7 20.3 %collective-permute-start.5 = (bf16[4,128,1024]{2,1,0:T(8,128)(2,1)}, bf16[4,128,1024]{2,1,0:T(8,128)(2,1)S(1)}, u32[]{:S(2)}, u32[]{:S(2)}) collective-permute-start(bf16[4,128,1024]{2,1,0:T(8,128)(2,1)} %pad_maximum_fusion.1), channel_id=1, source_target_pairs={{0,2},{1,3},{2,0},{3,1},{4,6},{5,7},{6,4},{7,5},{8,10},{9,11},{10,... | collective-permute-start | bytes 3145736 | tf_op jit(solution)/shard_map/ppermute | solution.py:229
  51.7 1.2 collective-permute-start
  53.0 19.0 %collective-permute-start.6 = (s32[4,8]{1,0:T(4,128)S(1)}, s32[4,8]{1,0:T(4,128)S(1)}, u32[]{:S(2)}, u32[]{:S(2)}) collective-permute-start(s32[4,8]{1,0:T(4,128)S(1)} %pad_add_fusion.table_ref), channel_id=1, source_target_pairs={{0,2},{1,3},{2,0},{3,1},{4,6},{5,7},{6,4},{7,5},{8,10},{9,11},{10,... | collective-permute-start | bytes 392 | tf_op jit(solution)/shard_map/ppermute | solution.py:229
  72.2 23.2 %collective-permute-start.10 = (bf16[1024,256]{1,0:T(8,128)(2,1)S(1)}, bf16[1024,256]{1,0:T(8,128)(2,1)S(1)}, u32[]{:S(2)}, u32[]{:S(2)}) collective-permute-start(bf16[1024,256]{1,0:T(8,128)(2,1)S(1)} %collective-permute-done.3.refs_3_), channel_id=1, source_target_pairs={{4,0},{5,1},{6,2},{7,3},{8,4},{9,5},{10,6},{11,7},{12,8},{13,9},{1... | collective-permute-start | bytes 1572872 | tf_op jit(solution)/shard_map/ppermute | solution.py:234
  73.5 21.9 %collective-permute-start.9 = (bf16[1024,256]{1,0:T(8,128)(2,1)S(1)}, bf16[1024,256]{1,0:T(8,128)(2,1)S(1)}, u32[]{:S(2)}, u32[]{:S(2)}) collective-permute-start(bf16[1024,256]{1,0:T(8,128)(2,1)S(1)} %collective-permute-done.3.refs_3_), channel_id=1, source_target_pairs={{0,4},{1,5},{2,6},{3,7},{4,8},{5,9},{6,10},{7,11},{8,12},{9,13},{1... | collective-permute-start | bytes 1572872 | tf_op jit(solution)/shard_map/ppermute | solution.py:234
  84.6 22.0 %collective-permute-start.7 = (bf16[1024,256]{1,0:T(8,128)(2,1)S(1)}, bf16[1024,256]{1,0:T(8,128)(2,1)S(1)}, u32[]{:S(2)}, u32[]{:S(2)}) collective-permute-start(bf16[1024,256]{1,0:T(8,128)(2,1)S(1)} %collective-permute-done.2), channel_id=1, source_target_pairs={{4,0},{5,1},{6,2},{7,3},{8,4},{9,5},{10,6},{11,7},{20,16},{21,17},... | collective-permute-start | bytes 1572872 | tf_op jit(solution)/shard_map/ppermute | solution.py:234
  85.9 20.7 %collective-permute-start.8 = (bf16[1024,256]{1,0:T(8,128)(2,1)}, bf16[1024,256]{1,0:T(8,128)(2,1)S(1)}, u32[]{:S(2)}, u32[]{:S(2)}) collective-permute-start(bf16[1024,256]{1,0:T(8,128)(2,1)} %collective-permute-done.4), channel_id=1, source_target_pairs={{4,8},{5,9},{6,10},{7,11},{8,12},{9,13},{10,14},{11,15},{20,24},{2... | collective-permute-start | bytes 1572872 | tf_op jit(solution)/shard_map/ppermute | solution.py:234
  95.4 22.5 %collective-permute-start.12 = (bf16[1024,256]{1,0:T(8,128)(2,1)S(1)}, bf16[1024,256]{1,0:T(8,128)(2,1)S(1)}, u32[]{:S(2)}, u32[]{:S(2)}) collective-permute-start(bf16[1024,256]{1,0:T(8,128)(2,1)S(1)} %collective-permute-done.10), channel_id=1, source_target_pairs={{4,0},{5,1},{6,2},{7,3},{8,4},{9,5},{10,6},{11,7},{20,16},{21,17},... | collective-permute-start | bytes 1572872 | tf_op jit(solution)/shard_map/ppermute | solution.py:234
  96.7 21.2 %collective-permute-start.11 = (bf16[1024,256]{1,0:T(8,128)(2,1)S(1)}, bf16[1024,256]{1,0:T(8,128)(2,1)S(1)}, u32[]{:S(2)}, u32[]{:S(2)}) collective-permute-start(bf16[1024,256]{1,0:T(8,128)(2,1)S(1)} %collective-permute-done.9), channel_id=1, source_target_pairs={{4,8},{5,9},{6,10},{7,11},{8,12},{9,13},{10,14},{11,15},{20,24},{2... | collective-permute-start | bytes 1572872 | tf_op jit(solution)/shard_map/ppermute | solution.py:234
  97.4 22.5 %copy-start.2 = (s32[4,4]{1,0:T(4,128)S(1)}, s32[4,4]{1,0:T(4,128)}, u32[]{:S(2)}) copy-start(s32[4,4]{1,0:T(4,128)} %constant.37.clone.order_ref) | copy-start | bytes 196
  106.6 25.9 %collective-permute-start.14 = (bf16[1024,256]{1,0:T(8,128)(2,1)S(1)}, bf16[1024,256]{1,0:T(8,128)(2,1)S(1)}, u32[]{:S(2)}, u32[]{:S(2)}) collective-permute-start(bf16[1024,256]{1,0:T(8,128)(2,1)S(1)} %collective-permute-done.7), channel_id=1, source_target_pairs={{4,0},{5,1},{6,2},{7,3},{20,16},{21,17},{22,18},{23,19}} | collective-permute-start | bytes 1572872 | tf_op jit(solution)/shard_map/ppermute | solution.py:234
  107.9 24.7 %collective-permute-start.13 = (bf16[1024,256]{1,0:T(8,128)(2,1)S(1)}, bf16[1024,256]{1,0:T(8,128)(2,1)S(1)}, u32[]{:S(2)}, u32[]{:S(2)}) collective-permute-start(bf16[1024,256]{1,0:T(8,128)(2,1)S(1)} %collective-permute-done.8), channel_id=1, source_target_pairs={{8,12},{9,13},{10,14},{11,15},{24,28},{25,29},{26,30},{27,31}} | collective-permute-start | bytes 1572872 | tf_op jit(solution)/shard_map/ppermute | solution.py:234
  117.8 19.9 %collective-permute-start.16 = (bf16[1024,256]{1,0:T(8,128)(2,1)S(1)}, bf16[1024,256]{1,0:T(8,128)(2,1)S(1)}, u32[]{:S(2)}, u32[]{:S(2)}) collective-permute-start(bf16[1024,256]{1,0:T(8,128)(2,1)S(1)} %collective-permute-done.12), channel_id=1, source_target_pairs={{4,0},{5,1},{6,2},{7,3},{20,16},{21,17},{22,18},{23,19}} | collective-permute-start | bytes 1572872 | tf_op jit(solution)/shard_map/ppermute | solution.py:234
  119.1 18.6 %collective-permute-start.15 = (bf16[1024,256]{1,0:T(8,128)(2,1)S(1)}, bf16[1024,256]{1,0:T(8,128)(2,1)S(1)}, u32[]{:S(2)}, u32[]{:S(2)}) collective-permute-start(bf16[1024,256]{1,0:T(8,128)(2,1)S(1)} %collective-permute-done.11), channel_id=1, source_target_pairs={{8,12},{9,13},{10,14},{11,15},{24,28},{25,29},{26,30},{27,31}} | collective-permute-start | bytes 1572872 | tf_op jit(solution)/shard_map/ppermute | solution.py:234
  141.4 48.1 %collective-permute-start.17 = (bf16[4,128,1024]{2,1,0:T(8,128)(2,1)S(1)}, bf16[4,128,1024]{2,1,0:T(8,128)(2,1)S(1)}, u32[]{:S(2)}, u32[]{:S(2)}) collective-permute-start(bf16[4,128,1024]{2,1,0:T(8,128)(2,1)S(1)} %shard_map.67), channel_id=1, source_target_pairs={{0,2},{1,3},{2,0},{3,1},{4,6},{5,7},{6,4},{7,5},{8,10},{9,11},{10,... | collective-permute-start | bytes 3145736 | tf_op jit(solution)/shard_map/ppermute | solution.py:229
  147.5 42.2 %collective-permute-start.18 = (bf16[2,128,1024]{2,1,0:T(8,128)(2,1)S(1)}, bf16[2,128,1024]{2,1,0:T(8,128)(2,1)S(1)}, u32[]{:S(2)}, u32[]{:S(2)}) collective-permute-start(bf16[2,128,1024]{2,1,0:T(8,128)(2,1)S(1)} %slice.26), channel_id=1, source_target_pairs={{0,1},{1,0},{2,3},{3,2},{4,5},{5,4},{6,7},{7,6},{8,9},{9,8},{10,11... | collective-permute-start | bytes 1572872 | tf_op jit(solution)/shard_map/ppermute | solution.py:224
  189.6 2.0 collective-permute-start.19
  194.1 12.9 %copy-start.1 = (bf16[128,4096]{1,0:T(8,128)(2,1)S(1)}, bf16[128,4096]{1,0:T(8,128)(2,1)}, u32[]{:S(2)}) copy-start(bf16[128,4096]{1,0:T(8,128)(2,1)} %param.10) | copy-start | bytes 3145732
Sparse Core Ops, SparseCore 0:
  8.9 57.6 all-gather.2
  72.2 121.8 all-gather.4

commit v11 on v9

--- a/solution.py
+++ b/solution.py
@@ -132,66 +132,98 @@
     )(where, order, table, queries, *pieces, *state)
 
 
-def lay_out_kernel(n_outer, where_ref, *refs):
+def row_block(n_outer, which, kv, g):
+    if n_outer:
+        return g * n_outer + kv + which * (KVH // 2)
+    return which * (H // 2) + kv * GROUP + g
+
+
+def lay_out_kernel(*refs):
     rows = refs[-1]
+    width = GROUP * HD
+    for at, ref in enumerate(refs[:-1]):
+        columns = slice(at // 2 * width, (at // 2 + 1) * width)
+        for block in range(2):
+            first = (2 * block + at % 2) * QB
+            rows[first : first + QB, columns] = ref[block]
+
+
+def lay_out(parts):
+    half = pl.BlockSpec((2, QB, GROUP * HD), lambda i: (0, 0, 0))
+    shape = (4 * QB, len(parts) // 2 * GROUP * HD)
+    return pl.pallas_call(
+        lay_out_kernel,
+        out_shape=jax.ShapeDtypeStruct(shape, jnp.bfloat16),
+        grid=(1,),
+        in_specs=[half] * len(parts),
+        out_specs=pl.BlockSpec(shape, lambda i: (0, 0)),
+        compiler_params=pltpu.CompilerParams(vmem_limit_bytes=VMEM_LIMIT),
+    )(*parts)
+
+
+def project_kernel(n_outer, groups, steps, where_ref, rows_ref, w_ref, *refs):
+    o_ref, wbuf, sems = refs[-3:]
     side = where_ref[1]
-    for kv, group in enumerate(refs[i : i + 4] for i in range(0, len(refs) - 1, 4)):
-        for at, ref in enumerate(group):
-            which = 1 - side if at % 2 else side
+    step = pl.program_id(0)
+    tile = wbuf.shape[-1]
+    tiles = w_ref.shape[-1] // tile
+
+    def fetch(later):
+        columns = slice(later % tiles * tile, (later % tiles + 1) * tile)
+        for at, (other, kv) in enumerate(groups):
             for g in range(GROUP):
-                h = kv * GROUP + g
-                if n_outer:
-                    to = g * n_outer + kv + which * (KVH // 2)
-                else:
-                    to = h + which * (H // 2)
-                to = pl.ds(pl.multiple_of(to * HD, HD), HD)
-                for block in range(2):
-                    first = (2 * block + at // 2) * QB
-                    rows[first : first + QB, to] = ref[block, :, g * HD : (g + 1) * HD]
-
-
-def lay_out(n_outer, where, parts):
-    half = pl.BlockSpec((2, QB, GROUP * HD), lambda i, *_: (0, 0, 0))
+                block = row_block(n_outer, 1 - side if other else side, kv, g)
+                to = (at * GROUP + g) * HD
+                pltpu.make_async_copy(
+                    w_ref.at[later // tiles, pl.ds(pl.multiple_of(block * HD, HD), HD), columns],
+                    wbuf.at[later % 2, to : to + HD, :],
+                    sems.at[later % 2],
+                ).start()
+
+    @pl.when(step == 0)
+    def _():
+        fetch(0)
+
+    for later in range(1, steps):
+
+        @pl.when(step == later - 1)
+        def _():
+            fetch(later)
+
+    slot = lax.rem(step, 2)
+    pltpu.make_async_copy(wbuf.at[slot], wbuf.at[slot], sems.at[slot]).wait()
+    total = jnp.dot(rows_ref[...], wbuf[slot], preferred_element_type=jnp.float32)
+    if len(refs) > 3:
+        total += refs[0][...]
+    o_ref[...] = total.astype(o_ref.dtype)
+
+
+def project(n_outer, where, rows, groups, weights, before=None, tile=PROJECT_TILE):
+    parts, _, columns = weights.shape
+    steps = parts * columns // tile
+    length, depth = rows.shape
+    block = pl.BlockSpec((length, tile), lambda s, *_: (0, s))
+    dtype = jnp.float32 if before is None else jnp.bfloat16
     return pl.pallas_call(
-        functools.partial(lay_out_kernel, n_outer),
-        out_shape=jax.ShapeDtypeStruct((4 * QB, H * HD), jnp.bfloat16),
+        functools.partial(project_kernel, n_outer, groups, steps),
+        out_shape=jax.ShapeDtypeStruct((length, parts * columns), dtype),
         grid_spec=pltpu.PrefetchScalarGridSpec(
             num_scalar_prefetch=1,
-            grid=(1,),
-            in_specs=[half] * len(parts),
-            out_specs=pl.BlockSpec((4 * QB, H * HD), lambda i, *_: (0, 0)),
+            grid=(steps,),
+            in_specs=[
+                pl.BlockSpec((length, depth), lambda s, *_: (0, 0)),
+                pl.BlockSpec(memory_space=pltpu.HBM),
+            ]
+            + [block] * (before is not None),
+            out_specs=block,
+            scratch_shapes=[
+                pltpu.VMEM((2, depth, tile), jnp.bfloat16),
+                pltpu.SemaphoreType.DMA((2,)),
+            ],
         ),
         compiler_params=pltpu.CompilerParams(vmem_limit_bytes=VMEM_LIMIT),
-    )(where, *parts)
-
-
-def project_kernel(rows_ref, w_ref, o_ref):
-    o_ref[...] = jnp.dot(
-        rows_ref[...], w_ref[0], preferred_element_type=jnp.float32
-    ).astype(jnp.bfloat16)
-
-
-def project(rows, weights, tile=PROJECT_TILE):
-    parts, depth, columns = weights.shape
-    tiles = columns // tile
-    return pl.pallas_call(
-        project_kernel,
-        out_shape=jax.ShapeDtypeStruct((rows.shape[0], parts * columns), jnp.bfloat16),
-        grid_spec=pl.GridSpec(
-            grid=(parts, tiles),
-            in_specs=[
-                pl.BlockSpec(rows.shape, lambda p, t: (0, 0)),
-                pl.BlockSpec((1, depth, tile), lambda p, t: (p, 0, t)),
-            ],
-            out_specs=pl.BlockSpec((rows.shape[0], tile), lambda p, t: (0, p * tiles + t)),
-        ),
-        compiler_params=pltpu.CompilerParams(vmem_limit_bytes=VMEM_LIMIT),
-        cost_estimate=pl.CostEstimate(
-            flops=2 * rows.shape[0] * depth * parts * columns,
-            bytes_accessed=2 * (depth * parts * columns + rows.shape[0] * (depth + parts * columns)),
-            transcendentals=0,
-        ),
-    )(rows, weights)
+        cost_estimate=pl.CostEstimate(flops=1, bytes_accessed=1, transcendentals=0),
+    )(where, rows, weights, *([] if before is None else [before]))
 
 
 LINE = "outer"
@@ -324,14 +356,20 @@
         out = attention(*asks[0], head, late[head], (last,), n_chip, states[head][0])
         tie = [out]
         across.append(swap_side(out))
+    def even_and_odd(array):
+        return [array, swap_core(array[2:])]
+
     parts = []
     for head in range(KVH // 2):
         state = [after(array, *tie) for array in states[head][1]]
         near = attention(*asks[1], head, late[head], (last,), n_chip, state)
-        tie = [across[head]]
-        parts += [near, across[head], swap_core(near[2:]), swap_core(across[head][2:])]
-    rows = lay_out(order_of_rows, where, parts)
-    return project(rows, gathered)
+        parts += [near, swap_core(near[2:])]
+    for array in across[:-1]:
+        parts += even_and_odd(array)
+    groups = [(other, kv) for other in (0, 1) for kv in range(KVH // 2)]
+    sums = project(order_of_rows, where, lay_out(parts), groups[:-1], gathered)
+    rows = lay_out(even_and_odd(after(across[-1], sums)))
+    return project(order_of_rows, where, rows, groups[-1:], gathered, sums)
 
 
 def solution(mesh):

time: 192 us -> 188 us (0.979)
  waiting for transfers between devices: 94.2 us -> 85.6 us
  Pallas kernels: 40.9 us -> 44.2 us
    ppermute x5, waiting for transfers between devices: 54.4 us -> 40.9 us  [swap_side(): lax.ppermute(array, SEQ, [(index(o, s, c), index(o, 1 - s, c)) for o, s,...]
    all_gather x1, waiting for transfers between devices: 0.02 us -> 3.56 us  [body(): gathered = lax.all_gather(gathered, PLANE, axis=0, tiled=True)]
    pallas_call x2 -> x4, Pallas kernels: 14 us -> 17.4 us  [the longest x2 17.3 us: project(): pl.pallas_call(functools.partial(project_kernel, n_outer, groups, steps),...]
  transfers between devices with their start and end apart: 25 -> 25, of which waited for: 14 -> 14; matrix products, arithmetic and copies ran while one was open for 5% -> 6% of each run, Pallas kernels for 15% -> 20%
where the time goes in v11:
time: 188 us; the launch traced here: 187 us
  waiting for transfers between devices  85.6 us (46%)
  Pallas kernels  44.2 us (24%)
  starting transfers between devices  30.6 us (16%)
  between operations  13.8 us (7%)
  local copies, waits for them, and re-layouts  8.98 us (5%)
  other arithmetic  4.02 us (2%)
    ppermute x5, waiting for transfers between devices, swap_side(): lax.ppermute(array, SEQ, [(index(o, s, c), index(o, 1 - s, c)) for o, s,...  40.9 us
    ppermute x12, waiting for transfers between devices, move(): lax.ppermute(array, SEQ, [(index(o, s, c), index(o + way, s, c)) for o, s...  31.7 us
    pallas_call x8, Pallas kernels, attention(): pl.pallas_call(functools.partial(attention_kernel, n_chip, slots, not sta...  26.8 us
    ppermute x12, starting transfers between devices, move(): lax.ppermute(array, SEQ, [(index(o, s, c), index(o + way, s, c)) for o, s...  21.2 us
    pallas_call x2, Pallas kernels, project(): pl.pallas_call(functools.partial(project_kernel, n_outer, groups, steps),...  17.3 us
    ppermute x5, starting transfers between devices, swap_side(): lax.ppermute(array, SEQ, [(index(o, s, c), index(o, 1 - s, c)) for o, s,...  7.68 us
    all_gather x1, waiting for transfers between devices, body(): gathered = lax.all_gather(columns, LINE, axis=0, tiled=True)  5.81 us
  transfers between devices with their start and end apart: 25, of which 14 were waited for; matrix products, arithmetic and copies ran while one was open for 6% of the time, Pallas kernels for 20%

profile of v11, /device:TPU:0, one launch (start us, length us, event | category | flops | bytes accessed | tf_op | source)
XLA Modules:
  0.0 187.2 jit_solution(4610836366989689348)
XLA Ops:
  6.5 1.2 copy-done
  7.8 0.8 constant_dynamic-slice_fusion.1
  8.7 2.7 %fusion.2 = (bf16[2,1,128,2048]{3,2,1,0:T(8,128)(2,1)S(1)}, bf16[2,128,2048]{2,1,0:T(8,128)(2,1)}) fusion(bf16[2,2,128,2048]{3,2,1,0:T(8,128)(2,1)} %bitcast.16), kind=kLoop, calls=%fused_computation.29 | loop fusion | bytes 4194304 | tf_op jit(solution)/shard_map/slice | solution.py:313
  11.4 0.5 collective-permute-start.2
  11.8 1.3 constant_dynamic-slice_fusion.4
  13.1 0.9 pad_maximum_fusion.3
  13.9 2.5 %collective-permute-start.4 = (bf16[1024,256]{1,0:T(8,128)(2,1)}, bf16[1024,256]{1,0:T(8,128)(2,1)}, u32[]{:S(2)}, u32[]{:S(2)}) collective-permute-start(bf16[1024,256]{1,0:T(8,128)(2,1)} %pad_maximum_fusion.3), channel_id=1, source_target_pairs={{0,2},{1,3},{2,0},{3,1},{4,6},{5,7},{6,4},{7,5},{8,10},{9,11},{10,... | collective-permute-start | bytes 1572872 | tf_op jit(solution)/shard_map/ppermute | solution.py:256
  16.5 0.9 dynamic-slice_bitcast_fusion
  17.4 0.9 constant_dynamic-slice_fusion
  18.2 1.1 pad_maximum_fusion
  19.3 0.2 collective-permute-start
  19.6 0.9 collective-permute-done
  20.5 2.1 %collective-permute-start.1 = (s32[4,8]{1,0:T(4,128)S(1)}, s32[4,8]{1,0:T(4,128)S(1)}, u32[]{:S(2)}, u32[]{:S(2)}) collective-permute-start(s32[4,8]{1,0:T(4,128)S(1)} %pad_add_fusion.table_ref), channel_id=1, source_target_pairs={{0,2},{1,3},{2,0},{3,1},{4,6},{5,7},{6,4},{7,5},{8,10},{9,11},{10,... | collective-permute-start | bytes 392 | tf_op jit(solution)/shard_map/ppermute | solution.py:256
  22.6 7.0 %collective-permute-done.4 = bf16[1024,256]{1,0:T(8,128)(2,1)} collective-permute-done((bf16[1024,256]{1,0:T(8,128)(2,1)}, bf16[1024,256]{1,0:T(8,128)(2,1)}, u32[]{:S(2)}, u32[]{:S(2)}) %collective-permute-start.4) | collective-permute-done | bytes 524320 | tf_op jit(solution)/shard_map/ppermute | solution.py:256
  29.6 1.1 fusion.3
  30.7 21.1 %collective-permute-done.1.table_ref = s32[4,8]{1,0:T(4,128)S(1)} collective-permute-done((s32[4,8]{1,0:T(4,128)S(1)}, s32[4,8]{1,0:T(4,128)S(1)}, u32[]{:S(2)}, u32[]{:S(2)}) %collective-permute-start.1) | collective-permute-done | bytes 160 | tf_op jit(solution)/shard_map/ppermute | solution.py:256
  51.8 5.8 %all-gather.3.cloned.1.call-done = bf16[512,2048]{1,0:T(8,128)(2,1)} async-done(((bf16[128,2048]{1,0:T(8,128)(2,1)}), bf16[512,2048]{1,0:T(8,128)(2,1)}) %all-gather.3.cloned.1.call-update) | async-done | bytes 2097168 | tf_op jit(solution)/shard_map/all_gather | solution.py:303
  57.6 1.3 collective-permute-start.5
  58.9 5.3 %collective-permute-start.11 = (bf16[2048,128]{1,0:T(8,128)(2,1)S(1)}, bf16[2048,128]{1,0:T(8,128)(2,1)}, u32[]{:S(2)}, u32[]{:S(2)}) collective-permute-start(bf16[2048,128]{1,0:T(8,128)(2,1)S(1)} %pad_maximum_fusion.4.refs_0_), channel_id=1, source_target_pairs={{0,4},{1,5},{2,6},{3,7},{4,8},{5,9},{6,10},{7,11},{8,12},{9,13},{1... | collective-permute-start | bytes 1572872 | tf_op jit(solution)/shard_map/ppermute | solution.py:261
  64.3 1.3 collective-permute-start.7
  65.6 5.4 %collective-permute-start.9 = (bf16[2048,128]{1,0:T(8,128)(2,1)S(1)}, bf16[2048,128]{1,0:T(8,128)(2,1)}, u32[]{:S(2)}, u32[]{:S(2)}) collective-permute-start(bf16[2048,128]{1,0:T(8,128)(2,1)S(1)} %fusion.refs_0_), channel_id=1, source_target_pairs={{0,4},{1,5},{2,6},{3,7},{4,8},{5,9},{6,10},{7,11},{8,12},{9,13},{1... | collective-permute-start | bytes 1572872 | tf_op jit(solution)/shard_map/ppermute | solution.py:261
  70.9 0.1 pad_add_fusion.3
  71.0 0.1 pad_add_fusion.1.where_ref
  71.1 1.3 pad_maximum_fusion.1.q_ref
  72.4 2.0 %collective-permute-done.5 = bf16[2048,128]{1,0:T(8,128)(2,1)S(1)} collective-permute-done((bf16[2048,128]{1,0:T(8,128)(2,1)S(1)}, bf16[2048,128]{1,0:T(8,128)(2,1)S(1)}, u32[]{:S(2)}, u32[]{:S(2)}) %collective-permute-start.5) | collective-permute-done | bytes 524320 | tf_op jit(solution)/shard_map/ppermute | solution.py:261
  74.3 1.5 collective-permute-done.11
  75.8 1.3 collective-permute-start.6
  77.1 0.7 collective-permute-start.12
  77.8 7.7 %collective-permute-done.7 = bf16[2048,128]{1,0:T(8,128)(2,1)S(1)} collective-permute-done((bf16[2048,128]{1,0:T(8,128)(2,1)S(1)}, bf16[2048,128]{1,0:T(8,128)(2,1)S(1)}, u32[]{:S(2)}, u32[]{:S(2)}) %collective-permute-start.7) | collective-permute-done | bytes 524320 | tf_op jit(solution)/shard_map/ppermute | solution.py:261
  85.6 1.3 collective-permute-start.8
  86.9 0.7 collective-permute-start.10
  87.6 0.1 broadcast_select_fusion.refs_1_
  87.7 9.1 %collective-permute-done.6 = bf16[2048,128]{1,0:T(8,128)(2,1)S(1)} collective-permute-done((bf16[2048,128]{1,0:T(8,128)(2,1)S(1)}, bf16[2048,128]{1,0:T(8,128)(2,1)S(1)}, u32[]{:S(2)}, u32[]{:S(2)}) %collective-permute-start.6) | collective-permute-done | bytes 524320 | tf_op jit(solution)/shard_map/ppermute | solution.py:261
  96.8 10.1 %collective-permute-done.8 = bf16[2048,128]{1,0:T(8,128)(2,1)S(1)} collective-permute-done((bf16[2048,128]{1,0:T(8,128)(2,1)S(1)}, bf16[2048,128]{1,0:T(8,128)(2,1)S(1)}, u32[]{:S(2)}, u32[]{:S(2)}) %collective-permute-start.8) | collective-permute-done | bytes 524320 | tf_op jit(solution)/shard_map/ppermute | solution.py:261
  106.9 1.3 collective-permute-start.14
  108.2 0.7 collective-permute-start.13
  108.9 0.1 select_select_fusion.2.refs_2_
  109.0 1.3 collective-permute-start.16
  110.3 0.7 collective-permute-start.15
  111.0 0.1 select_select_fusion.3.refs_2_
  111.1 4.0 %shard_map.67 = (f32[4,128,512]{2,1,0:T(8,128)S(1)}, f32[4,128,512]{2,1,0:T(8,128)S(1)}, f32[4,128,512]{2,1,0:T(8,128)S(1)}) custom-call(s32[4]{0:T(128)S(1)} %pad_add_fusion.1.where_ref, s32[4,4]{1,0:T(4,128)S(1)} %copy-done.2, s32[4,8]{1,0:T(4,128)S(1)} %pad_add_fusion.table_ref, bf16[4,128,1024]{2,1,0:T(8,128)(2,1)S(1)} %pad_maximum_fusion.1.q_ref, ...), custom_call_target="tpu_custom_call" | custom-call | flops 1 | bytes 1 | tf_op jit(solution)/shard_map/pallas_call | solution.py:119
  115.1 4.0 %shard_map.65 = (f32[4,128,512]{2,1,0:T(8,128)S(1)}, f32[4,128,512]{2,1,0:T(8,128)S(1)}, f32[4,128,512]{2,1,0:T(8,128)S(1)}) custom-call(s32[4]{0:T(128)S(1)} %pad_add_fusion.1.where_ref, s32[4,4]{1,0:T(4,128)S(1)} %copy-done.2, s32[4,8]{1,0:T(4,128)S(1)} %pad_add_fusion.table_ref, bf16[4,128,1024]{2,1,0:T(8,128)(2,1)S(1)} %pad_maximum_fusion.1.q_ref, ...), custom_call_target="tpu_custom_call" | custom-call | flops 1 | bytes 1 | tf_op jit(solution)/shard_map/pallas_call | solution.py:119
  119.2 4.0 %shard_map.66 = (f32[4,128,512]{2,1,0:T(8,128)S(1)}, f32[4,128,512]{2,1,0:T(8,128)S(1)}, f32[4,128,512]{2,1,0:T(8,128)S(1)}) custom-call(s32[4]{0:T(128)S(1)} %get-tuple-element.85.where_ref, s32[4,4]{1,0:T(4,128)S(1)} %copy-done.2, s32[4,8]{1,0:T(4,128)S(1)} %collective-permute-done.1.table_ref, bf16[4,128,1024]{2,1,0:T(8,128)(2,1)S(1)} %collective-permute-done.3.q_ref, ...), custom_call_target="tpu_custom_call" | custom-call | flops 1 | bytes 1 | tf_op jit(solution)/shard_map/pallas_call | solution.py:119
  123.2 4.0 %shard_map.64 = (f32[4,128,512]{2,1,0:T(8,128)S(1)}, f32[4,128,512]{2,1,0:T(8,128)S(1)}, f32[4,128,512]{2,1,0:T(8,128)S(1)}) custom-call(s32[4]{0:T(128)S(1)} %get-tuple-element.85.where_ref, s32[4,4]{1,0:T(4,128)S(1)} %copy-done.2, s32[4,8]{1,0:T(4,128)S(1)} %collective-permute-done.1.table_ref, bf16[4,128,1024]{2,1,0:T(8,128)(2,1)S(1)} %collective-permute-done.3.q_ref, ...), custom_call_target="tpu_custom_call" | custom-call | flops 1 | bytes 1 | tf_op jit(solution)/shard_map/pallas_call | solution.py:119
  127.3 0.1 select_select_fusion.1.refs_0_
  127.4 2.7 %shard_map.68 = bf16[4,128,512]{2,1,0:T(8,128)(2,1)S(1)} custom-call(s32[4]{0:T(128)S(1)} %get-tuple-element.85.where_ref, s32[4,4]{1,0:T(4,128)S(1)} %copy-done.2, s32[4,8]{1,0:T(4,128)S(1)} %collective-permute-done.1.table_ref, bf16[4,128,1024]{2,1,0:T(8,128)(2,1)S(1)} %collective-permute-done.3.q_ref, bf16[2048,128]{1,0:T(8,128)(2,1)S(1)} %select_select_fusion.1.refs_0_, ...), custom_call_target="tpu_custom_call" | custom-call | flops 1 | bytes 1 | tf_op jit(solution)/shard_map/pallas_call | solution.py:119
  130.1 1.5 collective-permute-start.20
  131.6 1.3 collective-permute-done.16
  132.9 0.1 select_select_fusion.refs_0_
  133.0 2.7 %shard_map.69 = bf16[4,128,512]{2,1,0:T(8,128)(2,1)S(1)} custom-call(s32[4]{0:T(128)S(1)} %get-tuple-element.85.where_ref, s32[4,4]{1,0:T(4,128)S(1)} %copy-done.2, s32[4,8]{1,0:T(4,128)S(1)} %collective-permute-done.1.table_ref, bf16[4,128,1024]{2,1,0:T(8,128)(2,1)S(1)} %collective-permute-done.3.q_ref, bf16[2048,128]{1,0:T(8,128)(2,1)S(1)} %select_select_fusion.refs_0_, ...), custom_call_target="tpu_custom_call" | custom-call | flops 1 | bytes 1 | tf_op jit(solution)/shard_map/pallas_call | solution.py:119
  135.7 1.5 collective-permute-start.17
  137.2 2.7 %shard_map.71.refs_2_ = bf16[4,128,512]{2,1,0:T(8,128)(2,1)S(1)} custom-call(s32[4]{0:T(128)S(1)} %pad_add_fusion.1.where_ref, s32[4,4]{1,0:T(4,128)S(1)} %copy-done.2, s32[4,8]{1,0:T(4,128)S(1)} %pad_add_fusion.table_ref, bf16[4,128,1024]{2,1,0:T(8,128)(2,1)S(1)} %pad_maximum_fusion.1.q_ref, bf16[2048,128]{1,0:T(8,128)(2,1)S(1)} %select_select_fusion.refs_0_, ...), custom_call_target="tpu_custom_call" | custom-call | flops 1 | bytes 1 | tf_op jit(solution)/shard_map/pallas_call | solution.py:119
  140.0 0.1 collective-permute-start.19
  140.0 2.7 %shard_map.70.refs_0_ = bf16[4,128,512]{2,1,0:T(8,128)(2,1)S(1)} custom-call(s32[4]{0:T(128)S(1)} %pad_add_fusion.1.where_ref, s32[4,4]{1,0:T(4,128)S(1)} %copy-done.2, s32[4,8]{1,0:T(4,128)S(1)} %pad_add_fusion.table_ref, bf16[4,128,1024]{2,1,0:T(8,128)(2,1)S(1)} %pad_maximum_fusion.1.q_ref, bf16[2048,128]{1,0:T(8,128)(2,1)S(1)} %select_select_fusion.1.refs_0_, ...), custom_call_target="tpu_custom_call" | custom-call | flops 1 | bytes 1 | tf_op jit(solution)/shard_map/pallas_call | solution.py:119
  142.7 0.6 collective-permute-start.18
  143.3 12.8 %collective-permute-done.20.refs_4_ = bf16[4,128,512]{2,1,0:T(8,128)(2,1)S(1)} collective-permute-done((bf16[4,128,512]{2,1,0:T(8,128)(2,1)S(1)}, bf16[4,128,512]{2,1,0:T(8,128)(2,1)S(1)}, u32[]{:S(2)}, u32[]{:S(2)}) %collective-permute-start.20) | collective-permute-done | bytes 524320 | tf_op jit(solution)/shard_map/ppermute | solution.py:256
  156.2 0.1 collective-permute-start.21
  156.3 1.5 collective-permute-done.21.refs_5_
  157.8 0.1 shard_map.72.rows_ref
  157.9 3.6 %all-gather.5.cloned.1.call-done = bf16[4096,2048]{1,0:T(8,128)(2,1)} async-done(((bf16[512,2048]{1,0:T(8,128)(2,1)}), bf16[4096,2048]{1,0:T(8,128)(2,1)}) %all-gather.5.cloned.1.call-update) | async-done | bytes 16777232 | tf_op jit(solution)/shard_map/all_gather | solution.py:327
  161.4 10.3 %shard_map.73.refs_0_ = f32[512,4096]{1,0:T(8,128)S(1)} custom-call(s32[4]{0:T(128)S(1)} %pad_add_fusion.1.where_ref, bf16[512,1536]{1,0:T(8,128)(2,1)S(1)} %shard_map.72.rows_ref, bf16[2,2048,2048]{2,1,0:T(8,128)(2,1)} %bitcast.14), custom_call_target="tpu_custom_call" | custom-call | flops 1 | bytes 1 | tf_op jit(solution)/shard_map/pallas_call | solution.py:207
  171.7 0.3 collective-permute-start.22
  172.1 1.3 collective-permute-done.22.refs_1_
  173.4 7.0 %shard_map.75 = bf16[512,4096]{1,0:T(8,128)(2,1)} custom-call(s32[4]{0:T(128)S(1)} %pad_add_fusion.1.where_ref, bf16[512,512]{1,0:T(8,128)(2,1)S(1)} %shard_map.74.rows_ref, bf16[2,2048,2048]{2,1,0:T(8,128)(2,1)} %bitcast.15, f32[512,4096]{1,0:T(8,128)S(1)} %shard_map.73.refs_0_), custom_call_target="tpu_custom_call" | custom-call | flops 1 | bytes 1 | tf_op jit(solution)/shard_map/pallas_call | solution.py:207
  (35 shorter events, 0.5 us)
Async XLA Ops:
  6.5 1.2 copy-start
  6.5 51.1 %all-gather.3.cloned.1.call-start = ((), (), s32[]{:S(2)}) async-start(), calls=%async_computation | async-start | bytes 2621440 | tf_op jit(solution)/shard_map/all_gather | solution.py:303
  8.6 152.8 %all-gather.5.cloned.1.call-start = ((), (), s32[]{:S(2)}) async-start(), calls=%async_computation.1 | async-start | bytes 18874368 | tf_op jit(solution)/shard_map/all_gather | solution.py:327
  11.4 6.0 %collective-permute-start.2 = (bf16[2,128,2048]{2,1,0:T(8,128)(2,1)}, bf16[2,128,2048]{2,1,0:T(8,128)(2,1)S(1)}, u32[]{:S(2)}, u32[]{:S(2)}) collective-permute-start(bf16[2,128,2048]{2,1,0:T(8,128)(2,1)} %get-tuple-element.88), channel_id=1, source_target_pairs={{0,1},{1,0},{2,3},{3,2},{4,5},{5,4},{6,7},{7,6},{8,9},{9,8},{10,11... | collective-permute-start | bytes 3145736 | tf_op jit(solution)/shard_map/ppermute | solution.py:251
  13.9 15.6 %collective-permute-start.4 = (bf16[1024,256]{1,0:T(8,128)(2,1)}, bf16[1024,256]{1,0:T(8,128)(2,1)}, u32[]{:S(2)}, u32[]{:S(2)}) collective-permute-start(bf16[1024,256]{1,0:T(8,128)(2,1)} %pad_maximum_fusion.3), channel_id=1, source_target_pairs={{0,2},{1,3},{2,0},{3,1},{4,6},{5,7},{6,4},{7,5},{8,10},{9,11},{10,... | collective-permute-start | bytes 1572872 | tf_op jit(solution)/shard_map/ppermute | solution.py:256
  17.4 2.0 %copy-start.3 = (s32[4,8]{1,0:T(4,128)S(1)}, s32[4,8]{1,0:T(4,128)}, u32[]{:S(2)}) copy-start(s32[4,8]{1,0:T(4,128)} %param.9) | copy-start | bytes 388
  19.3 32.5 %collective-permute-start.3 = (bf16[4,128,1024]{2,1,0:T(8,128)(2,1)}, bf16[4,128,1024]{2,1,0:T(8,128)(2,1)S(1)}, u32[]{:S(2)}, u32[]{:S(2)}) collective-permute-start(bf16[4,128,1024]{2,1,0:T(8,128)(2,1)} %pad_maximum_fusion), channel_id=1, source_target_pairs={{0,2},{1,3},{2,0},{3,1},{4,6},{5,7},{6,4},{7,5},{8,10},{9,11},{10,... | collective-permute-start | bytes 3145736 | tf_op jit(solution)/shard_map/ppermute | solution.py:256
  19.3 1.2 collective-permute-start
  20.5 31.3 %collective-permute-start.1 = (s32[4,8]{1,0:T(4,128)S(1)}, s32[4,8]{1,0:T(4,128)S(1)}, u32[]{:S(2)}, u32[]{:S(2)}) collective-permute-start(s32[4,8]{1,0:T(4,128)S(1)} %pad_add_fusion.table_ref), channel_id=1, source_target_pairs={{0,2},{1,3},{2,0},{3,1},{4,6},{5,7},{6,4},{7,5},{8,10},{9,11},{10,... | collective-permute-start | bytes 392 | tf_op jit(solution)/shard_map/ppermute | solution.py:256
  57.6 16.7 %collective-permute-start.5 = (bf16[2048,128]{1,0:T(8,128)(2,1)S(1)}, bf16[2048,128]{1,0:T(8,128)(2,1)S(1)}, u32[]{:S(2)}, u32[]{:S(2)}) collective-permute-start(bf16[2048,128]{1,0:T(8,128)(2,1)S(1)} %pad_maximum_fusion.4.refs_0_), channel_id=1, source_target_pairs={{4,0},{5,1},{6,2},{7,3},{8,4},{9,5},{10,6},{11,7},{12,8},{13,9},{1... | collective-permute-start | bytes 1572872 | tf_op jit(solution)/shard_map/ppermute | solution.py:261
  58.9 16.9 %collective-permute-start.11 = (bf16[2048,128]{1,0:T(8,128)(2,1)S(1)}, bf16[2048,128]{1,0:T(8,128)(2,1)}, u32[]{:S(2)}, u32[]{:S(2)}) collective-permute-start(bf16[2048,128]{1,0:T(8,128)(2,1)S(1)} %pad_maximum_fusion.4.refs_0_), channel_id=1, source_target_pairs={{0,4},{1,5},{2,6},{3,7},{4,8},{5,9},{6,10},{7,11},{8,12},{9,13},{1... | collective-permute-start | bytes 1572872 | tf_op jit(solution)/shard_map/ppermute | solution.py:261
  64.3 21.3 %collective-permute-start.7 = (bf16[2048,128]{1,0:T(8,128)(2,1)S(1)}, bf16[2048,128]{1,0:T(8,128)(2,1)S(1)}, u32[]{:S(2)}, u32[]{:S(2)}) collective-permute-start(bf16[2048,128]{1,0:T(8,128)(2,1)S(1)} %fusion.refs_0_), channel_id=1, source_target_pairs={{4,0},{5,1},{6,2},{7,3},{8,4},{9,5},{10,6},{11,7},{12,8},{13,9},{1... | collective-permute-start | bytes 1572872 | tf_op jit(solution)/shard_map/ppermute | solution.py:261
  65.6 21.3 %collective-permute-start.9 = (bf16[2048,128]{1,0:T(8,128)(2,1)S(1)}, bf16[2048,128]{1,0:T(8,128)(2,1)}, u32[]{:S(2)}, u32[]{:S(2)}) collective-permute-start(bf16[2048,128]{1,0:T(8,128)(2,1)S(1)} %fusion.refs_0_), channel_id=1, source_target_pairs={{0,4},{1,5},{2,6},{3,7},{4,8},{5,9},{6,10},{7,11},{8,12},{9,13},{1... | collective-permute-start | bytes 1572872 | tf_op jit(solution)/shard_map/ppermute | solution.py:261
  75.8 21.0 %collective-permute-start.6 = (bf16[2048,128]{1,0:T(8,128)(2,1)S(1)}, bf16[2048,128]{1,0:T(8,128)(2,1)S(1)}, u32[]{:S(2)}, u32[]{:S(2)}) collective-permute-start(bf16[2048,128]{1,0:T(8,128)(2,1)S(1)} %collective-permute-done.5), channel_id=1, source_target_pairs={{4,0},{5,1},{6,2},{7,3},{8,4},{9,5},{10,6},{11,7},{20,16},{21,17},... | collective-permute-start | bytes 1572872 | tf_op jit(solution)/shard_map/ppermute | solution.py:261
  77.1 19.7 %collective-permute-start.12 = (bf16[2048,128]{1,0:T(8,128)(2,1)}, bf16[2048,128]{1,0:T(8,128)(2,1)S(1)}, u32[]{:S(2)}, u32[]{:S(2)}) collective-permute-start(bf16[2048,128]{1,0:T(8,128)(2,1)} %collective-permute-done.11), channel_id=1, source_target_pairs={{4,8},{5,9},{6,10},{7,11},{8,12},{9,13},{10,14},{11,15},{20,24},{2... | collective-permute-start | bytes 1572872 | tf_op jit(solution)/shard_map/ppermute | solution.py:261
  85.6 21.3 %collective-permute-start.8 = (bf16[2048,128]{1,0:T(8,128)(2,1)S(1)}, bf16[2048,128]{1,0:T(8,128)(2,1)S(1)}, u32[]{:S(2)}, u32[]{:S(2)}) collective-permute-start(bf16[2048,128]{1,0:T(8,128)(2,1)S(1)} %collective-permute-done.7), channel_id=1, source_target_pairs={{4,0},{5,1},{6,2},{7,3},{8,4},{9,5},{10,6},{11,7},{20,16},{21,17},... | collective-permute-start | bytes 1572872 | tf_op jit(solution)/shard_map/ppermute | solution.py:261
  86.9 21.3 %collective-permute-start.10 = (bf16[2048,128]{1,0:T(8,128)(2,1)}, bf16[2048,128]{1,0:T(8,128)(2,1)S(1)}, u32[]{:S(2)}, u32[]{:S(2)}) collective-permute-start(bf16[2048,128]{1,0:T(8,128)(2,1)} %collective-permute-done.9), channel_id=1, source_target_pairs={{4,8},{5,9},{6,10},{7,11},{8,12},{9,13},{10,14},{11,15},{20,24},{2... | collective-permute-start | bytes 1572872 | tf_op jit(solution)/shard_map/ppermute | solution.py:261
  87.7 23.4 %copy-start.2 = (s32[4,4]{1,0:T(4,128)S(1)}, s32[4,4]{1,0:T(4,128)}, u32[]{:S(2)}) copy-start(s32[4,4]{1,0:T(4,128)} %constant.37.clone.order_ref) | copy-start | bytes 196
  106.9 20.4 %collective-permute-start.14 = (bf16[2048,128]{1,0:T(8,128)(2,1)S(1)}, bf16[2048,128]{1,0:T(8,128)(2,1)S(1)}, u32[]{:S(2)}, u32[]{:S(2)}) collective-permute-start(bf16[2048,128]{1,0:T(8,128)(2,1)S(1)} %collective-permute-done.8), channel_id=1, source_target_pairs={{4,0},{5,1},{6,2},{7,3},{20,16},{21,17},{22,18},{23,19}} | collective-permute-start | bytes 1572872 | tf_op jit(solution)/shard_map/ppermute | solution.py:261
  108.2 19.1 %collective-permute-start.13 = (bf16[2048,128]{1,0:T(8,128)(2,1)S(1)}, bf16[2048,128]{1,0:T(8,128)(2,1)S(1)}, u32[]{:S(2)}, u32[]{:S(2)}) collective-permute-start(bf16[2048,128]{1,0:T(8,128)(2,1)S(1)} %collective-permute-done.10), channel_id=1, source_target_pairs={{8,12},{9,13},{10,14},{11,15},{24,28},{25,29},{26,30},{27,31}} | collective-permute-start | bytes 1572872 | tf_op jit(solution)/shard_map/ppermute | solution.py:261
  109.0 23.9 %collective-permute-start.16 = (bf16[2048,128]{1,0:T(8,128)(2,1)S(1)}, bf16[2048,128]{1,0:T(8,128)(2,1)S(1)}, u32[]{:S(2)}, u32[]{:S(2)}) collective-permute-start(bf16[2048,128]{1,0:T(8,128)(2,1)S(1)} %collective-permute-done.6), channel_id=1, source_target_pairs={{4,0},{5,1},{6,2},{7,3},{20,16},{21,17},{22,18},{23,19}} | collective-permute-start | bytes 1572872 | tf_op jit(solution)/shard_map/ppermute | solution.py:261
  110.3 22.6 %collective-permute-start.15 = (bf16[2048,128]{1,0:T(8,128)(2,1)S(1)}, bf16[2048,128]{1,0:T(8,128)(2,1)S(1)}, u32[]{:S(2)}, u32[]{:S(2)}) collective-permute-start(bf16[2048,128]{1,0:T(8,128)(2,1)S(1)} %collective-permute-done.12), channel_id=1, source_target_pairs={{8,12},{9,13},{10,14},{11,15},{24,28},{25,29},{26,30},{27,31}} | collective-permute-start | bytes 1572872 | tf_op jit(solution)/shard_map/ppermute | solution.py:261
  130.1 26.1 %collective-permute-start.20 = (bf16[4,128,512]{2,1,0:T(8,128)(2,1)S(1)}, bf16[4,128,512]{2,1,0:T(8,128)(2,1)S(1)}, u32[]{:S(2)}, u32[]{:S(2)}) collective-permute-start(bf16[4,128,512]{2,1,0:T(8,128)(2,1)S(1)} %shard_map.68), channel_id=1, source_target_pairs={{0,2},{1,3},{2,0},{3,1},{4,6},{5,7},{6,4},{7,5},{8,10},{9,11},{10,... | collective-permute-start | bytes 1572872 | tf_op jit(solution)/shard_map/ppermute | solution.py:256
  135.7 36.0 %collective-permute-start.17 = (bf16[4,128,512]{2,1,0:T(8,128)(2,1)S(1)}, bf16[4,128,512]{2,1,0:T(8,128)(2,1)S(1)}, u32[]{:S(2)}, u32[]{:S(2)}) collective-permute-start(bf16[4,128,512]{2,1,0:T(8,128)(2,1)S(1)} %shard_map.69), channel_id=1, source_target_pairs={{0,2},{1,3},{2,0},{3,1},{4,6},{5,7},{6,4},{7,5},{8,10},{9,11},{10,... | collective-permute-start | bytes 1572872 | tf_op jit(solution)/shard_map/ppermute | solution.py:256
  140.0 16.3 %collective-permute-start.19 = (bf16[2,128,512]{2,1,0:T(8,128)(2,1)S(1)}, bf16[2,128,512]{2,1,0:T(8,128)(2,1)S(1)}, u32[]{:S(2)}, u32[]{:S(2)}) collective-permute-start(bf16[2,128,512]{2,1,0:T(8,128)(2,1)S(1)} %slice.55), channel_id=1, source_target_pairs={{0,1},{1,0},{2,3},{3,2},{4,5},{5,4},{6,7},{7,6},{8,9},{9,8},{10,11... | collective-permute-start | bytes 786440 | tf_op jit(solution)/shard_map/ppermute | solution.py:251
  142.7 13.5 %collective-permute-start.18 = (bf16[2,128,512]{2,1,0:T(8,128)(2,1)S(1)}, bf16[2,128,512]{2,1,0:T(8,128)(2,1)S(1)}, u32[]{:S(2)}, u32[]{:S(2)}) collective-permute-start(bf16[2,128,512]{2,1,0:T(8,128)(2,1)S(1)} %slice.54), channel_id=1, source_target_pairs={{0,1},{1,0},{2,3},{3,2},{4,5},{5,4},{6,7},{7,6},{8,9},{9,8},{10,11... | collective-permute-start | bytes 786440 | tf_op jit(solution)/shard_map/ppermute | solution.py:251
  156.2 1.6 collective-permute-start.21
  171.7 1.6 collective-permute-start.22
  173.4 7.0 %copy-start.1 = (bf16[128,4096]{1,0:T(8,128)(2,1)S(1)}, bf16[128,4096]{1,0:T(8,128)(2,1)}, u32[]{:S(2)}) copy-start(bf16[128,4096]{1,0:T(8,128)(2,1)} %param.10) | copy-start | bytes 3145732
Sparse Core Ops, SparseCore 0:
  8.9 48.6 all-gather.2
  59.5 101.8 all-gather.4

commit v12 on v11

--- a/solution.py
+++ b/solution.py
@@ -194,7 +194,7 @@
     pltpu.make_async_copy(wbuf.at[slot], wbuf.at[slot], sems.at[slot]).wait()
     total = jnp.dot(rows_ref[...], wbuf[slot], preferred_element_type=jnp.float32)
     if len(refs) > 3:
-        total += refs[0][...]
+        total += refs[0][:, pl.ds(pl.multiple_of(step * tile, tile), tile)]
     o_ref[...] = total.astype(o_ref.dtype)
 
 
@@ -214,7 +214,7 @@
                 pl.BlockSpec((length, depth), lambda s, *_: (0, 0)),
                 pl.BlockSpec(memory_space=pltpu.HBM),
             ]
-            + [block] * (before is not None),
+            + [pl.BlockSpec(memory_space=pltpu.VMEM)] * (before is not None),
             out_specs=block,
             scratch_shapes=[
                 pltpu.VMEM((2, depth, tile), jnp.bfloat16),
@@ -355,6 +355,8 @@
         late.append([piece])
         out = attention(*asks[0], head, late[head], (last,), n_chip, states[head][0])
         tie = [out]
+        if head + 1 == KVH // 2:
+            out = jnp.concatenate([out[:2], swap_core(out[2:])], 0)
         across.append(swap_side(out))
     def even_and_odd(array):
         return [array, swap_core(array[2:])]
@@ -368,7 +370,8 @@
         parts += even_and_odd(array)
     groups = [(other, kv) for other in (0, 1) for kv in range(KVH // 2)]
     sums = project(order_of_rows, where, lay_out(parts), groups[:-1], gathered)
-    rows = lay_out(even_and_odd(after(across[-1], sums)))
+    arrived = after(across[-1], sums)
+    rows = lay_out([arrived[:2], arrived[2:]])
     return project(order_of_rows, where, rows, groups[-1:], gathered, sums)
 
 

time: 188 us -> 183 us (0.973)
  waiting for transfers between devices: 85.6 us -> 82.4 us
    all_gather x1, waiting for transfers between devices: 3.56 us -> 0.02 us  [body(): gathered = lax.all_gather(gathered, PLANE, axis=0, tiled=True)]
  transfers between devices with their start and end apart: 25 -> 25, of which waited for: 14 -> 12; matrix products, arithmetic and copies ran while one was open for 6% -> 5% of each run, Pallas kernels for 20% -> 20%
where the time goes in v12:
time: 183 us
  waiting for transfers between devices  82.4 us (45%)
  Pallas kernels  43.8 us (24%)
  starting transfers between devices  30.4 us (17%)
  between operations  13.8 us (8%)
  local copies, waits for them, and re-layouts  9.04 us (5%)
  other arithmetic  3.01 us (2%)
    ppermute x5, waiting for transfers between devices, swap_side(): lax.ppermute(array, SEQ, [(index(o, s, c), index(o, 1 - s, c)) for o, s,...  40.9 us
    ppermute x12, waiting for transfers between devices, move(): lax.ppermute(array, SEQ, [(index(o, s, c), index(o + way, s, c)) for o, s...  33.2 us
    pallas_call x8, Pallas kernels, attention(): pl.pallas_call(functools.partial(attention_kernel, n_chip, slots, not sta...  26.8 us
    ppermute x12, starting transfers between devices, move(): lax.ppermute(array, SEQ, [(index(o, s, c), index(o + way, s, c)) for o, s...  21.2 us
    pallas_call x2, Pallas kernels, project(): pl.pallas_call(functools.partial(project_kernel, n_outer, groups, steps),...  16.9 us
    ppermute x5, starting transfers between devices, swap_side(): lax.ppermute(array, SEQ, [(index(o, s, c), index(o, 1 - s, c)) for o, s,...  7.64 us
    all_gather x1, waiting for transfers between devices, body(): gathered = lax.all_gather(columns, LINE, axis=0, tiled=True)  5.82 us
  transfers between devices with their start and end apart: 25, of which 12 were waited for; matrix products, arithmetic and copies ran while one was open for 5% of the time, Pallas kernels for 20%

profile of v12, /device:TPU:0, one launch (start us, length us, event | category | flops | bytes accessed | tf_op | source)
XLA Modules:
  0.0 182.5 jit_solution(9844564802100534572)
XLA Ops:
  6.5 1.2 copy-done
  7.8 0.8 constant_dynamic-slice_fusion.1
  8.7 2.7 %fusion.2 = (bf16[2,1,128,2048]{3,2,1,0:T(8,128)(2,1)S(1)}, bf16[2,128,2048]{2,1,0:T(8,128)(2,1)}) fusion(bf16[2,2,128,2048]{3,2,1,0:T(8,128)(2,1)} %bitcast.16), kind=kLoop, calls=%fused_computation.30 | loop fusion | bytes 4194304 | tf_op jit(solution)/shard_map/slice | solution.py:313
  11.4 0.5 collective-permute-start.2
  11.8 1.3 constant_dynamic-slice_fusion.4
  13.1 0.8 pad_maximum_fusion.3
  13.9 2.5 %collective-permute-start.4 = (bf16[1024,256]{1,0:T(8,128)(2,1)}, bf16[1024,256]{1,0:T(8,128)(2,1)}, u32[]{:S(2)}, u32[]{:S(2)}) collective-permute-start(bf16[1024,256]{1,0:T(8,128)(2,1)} %pad_maximum_fusion.3), channel_id=1, source_target_pairs={{0,2},{1,3},{2,0},{3,1},{4,6},{5,7},{6,4},{7,5},{8,10},{9,11},{10,... | collective-permute-start | bytes 1572872 | tf_op jit(solution)/shard_map/ppermute | solution.py:256
  16.5 0.9 dynamic-slice_bitcast_fusion
  17.4 0.9 constant_dynamic-slice_fusion
  18.2 0.1 pad_maximum_fusion
  18.3 0.1 collective-permute-start.3
  18.4 0.3 collective-permute-start
  18.8 0.9 collective-permute-done
  19.7 2.0 %collective-permute-start.1 = (s32[4,8]{1,0:T(4,128)S(1)}, s32[4,8]{1,0:T(4,128)S(1)}, u32[]{:S(2)}, u32[]{:S(2)}) collective-permute-start(s32[4,8]{1,0:T(4,128)S(1)} %pad_add_fusion.table_ref), channel_id=1, source_target_pairs={{0,2},{1,3},{2,0},{3,1},{4,6},{5,7},{6,4},{7,5},{8,10},{9,11},{10,... | collective-permute-start | bytes 392 | tf_op jit(solution)/shard_map/ppermute | solution.py:256
  21.7 7.9 %collective-permute-done.4 = bf16[1024,256]{1,0:T(8,128)(2,1)} collective-permute-done((bf16[1024,256]{1,0:T(8,128)(2,1)}, bf16[1024,256]{1,0:T(8,128)(2,1)}, u32[]{:S(2)}, u32[]{:S(2)}) %collective-permute-start.4) | collective-permute-done | bytes 524320 | tf_op jit(solution)/shard_map/ppermute | solution.py:256
  29.6 1.1 fusion.5
  30.7 21.1 %collective-permute-done.1.table_ref = s32[4,8]{1,0:T(4,128)S(1)} collective-permute-done((s32[4,8]{1,0:T(4,128)S(1)}, s32[4,8]{1,0:T(4,128)S(1)}, u32[]{:S(2)}, u32[]{:S(2)}) %collective-permute-start.1) | collective-permute-done | bytes 160 | tf_op jit(solution)/shard_map/ppermute | solution.py:256
  51.8 5.8 %all-gather.3.cloned.1.call-done = bf16[512,2048]{1,0:T(8,128)(2,1)} async-done(((bf16[128,2048]{1,0:T(8,128)(2,1)}), bf16[512,2048]{1,0:T(8,128)(2,1)}) %all-gather.3.cloned.1.call-update) | async-done | bytes 2097168 | tf_op jit(solution)/shard_map/all_gather | solution.py:303
  57.6 1.3 collective-permute-start.5
  58.9 5.4 %collective-permute-start.11 = (bf16[2048,128]{1,0:T(8,128)(2,1)S(1)}, bf16[2048,128]{1,0:T(8,128)(2,1)}, u32[]{:S(2)}, u32[]{:S(2)}) collective-permute-start(bf16[2048,128]{1,0:T(8,128)(2,1)S(1)} %pad_maximum_fusion.4.refs_0_), channel_id=1, source_target_pairs={{0,4},{1,5},{2,6},{3,7},{4,8},{5,9},{6,10},{7,11},{8,12},{9,13},{1... | collective-permute-start | bytes 1572872 | tf_op jit(solution)/shard_map/ppermute | solution.py:261
  64.3 1.3 collective-permute-start.7
  65.6 5.3 %collective-permute-start.9 = (bf16[2048,128]{1,0:T(8,128)(2,1)S(1)}, bf16[2048,128]{1,0:T(8,128)(2,1)}, u32[]{:S(2)}, u32[]{:S(2)}) collective-permute-start(bf16[2048,128]{1,0:T(8,128)(2,1)S(1)} %fusion.refs_0_), channel_id=1, source_target_pairs={{0,4},{1,5},{2,6},{3,7},{4,8},{5,9},{6,10},{7,11},{8,12},{9,13},{1... | collective-permute-start | bytes 1572872 | tf_op jit(solution)/shard_map/ppermute | solution.py:261
  70.9 0.1 pad_add_fusion.3
  71.0 0.1 pad_add_fusion.1.where_ref
  71.1 1.3 pad_maximum_fusion.1.q_ref
  72.4 1.9 %collective-permute-done.5 = bf16[2048,128]{1,0:T(8,128)(2,1)S(1)} collective-permute-done((bf16[2048,128]{1,0:T(8,128)(2,1)S(1)}, bf16[2048,128]{1,0:T(8,128)(2,1)S(1)}, u32[]{:S(2)}, u32[]{:S(2)}) %collective-permute-start.5) | collective-permute-done | bytes 524320 | tf_op jit(solution)/shard_map/ppermute | solution.py:261
  74.3 1.5 collective-permute-done.11
  75.8 1.3 collective-permute-start.6
  77.1 0.7 collective-permute-start.12
  77.8 7.7 %collective-permute-done.7 = bf16[2048,128]{1,0:T(8,128)(2,1)S(1)} collective-permute-done((bf16[2048,128]{1,0:T(8,128)(2,1)S(1)}, bf16[2048,128]{1,0:T(8,128)(2,1)S(1)}, u32[]{:S(2)}, u32[]{:S(2)}) %collective-permute-start.7) | collective-permute-done | bytes 524320 | tf_op jit(solution)/shard_map/ppermute | solution.py:261
  85.6 1.3 collective-permute-start.8
  86.9 0.7 collective-permute-start.10
  87.6 0.1 broadcast_select_fusion.refs_1_
  87.6 0.1 broadcast_select_fusion.1.refs_1_
  87.7 9.1 %collective-permute-done.6 = bf16[2048,128]{1,0:T(8,128)(2,1)S(1)} collective-permute-done((bf16[2048,128]{1,0:T(8,128)(2,1)S(1)}, bf16[2048,128]{1,0:T(8,128)(2,1)S(1)}, u32[]{:S(2)}, u32[]{:S(2)}) %collective-permute-start.6) | collective-permute-done | bytes 524320 | tf_op jit(solution)/shard_map/ppermute | solution.py:261
  96.8 10.1 %collective-permute-done.8 = bf16[2048,128]{1,0:T(8,128)(2,1)S(1)} collective-permute-done((bf16[2048,128]{1,0:T(8,128)(2,1)S(1)}, bf16[2048,128]{1,0:T(8,128)(2,1)S(1)}, u32[]{:S(2)}, u32[]{:S(2)}) %collective-permute-start.8) | collective-permute-done | bytes 524320 | tf_op jit(solution)/shard_map/ppermute | solution.py:261
  106.9 1.3 collective-permute-start.14
  108.2 0.7 collective-permute-start.13
  108.9 0.1 select_select_fusion.2.refs_2_
  109.0 1.3 collective-permute-start.16
  110.3 0.7 collective-permute-start.15
  111.0 0.1 select_select_fusion.3.refs_2_
  111.1 4.0 %shard_map.67 = (f32[4,128,512]{2,1,0:T(8,128)S(1)}, f32[4,128,512]{2,1,0:T(8,128)S(1)}, f32[4,128,512]{2,1,0:T(8,128)S(1)}) custom-call(s32[4]{0:T(128)S(1)} %pad_add_fusion.1.where_ref, s32[4,4]{1,0:T(4,128)S(1)} %copy-done.2, s32[4,8]{1,0:T(4,128)S(1)} %pad_add_fusion.table_ref, bf16[4,128,1024]{2,1,0:T(8,128)(2,1)S(1)} %pad_maximum_fusion.1.q_ref, ...), custom_call_target="tpu_custom_call" | custom-call | flops 1 | bytes 1 | tf_op jit(solution)/shard_map/pallas_call | solution.py:119
  115.1 4.0 %shard_map.65 = (f32[4,128,512]{2,1,0:T(8,128)S(1)}, f32[4,128,512]{2,1,0:T(8,128)S(1)}, f32[4,128,512]{2,1,0:T(8,128)S(1)}) custom-call(s32[4]{0:T(128)S(1)} %pad_add_fusion.1.where_ref, s32[4,4]{1,0:T(4,128)S(1)} %copy-done.2, s32[4,8]{1,0:T(4,128)S(1)} %pad_add_fusion.table_ref, bf16[4,128,1024]{2,1,0:T(8,128)(2,1)S(1)} %pad_maximum_fusion.1.q_ref, ...), custom_call_target="tpu_custom_call" | custom-call | flops 1 | bytes 1 | tf_op jit(solution)/shard_map/pallas_call | solution.py:119
  119.1 4.0 %shard_map.66 = (f32[4,128,512]{2,1,0:T(8,128)S(1)}, f32[4,128,512]{2,1,0:T(8,128)S(1)}, f32[4,128,512]{2,1,0:T(8,128)S(1)}) custom-call(s32[4]{0:T(128)S(1)} %get-tuple-element.85.where_ref, s32[4,4]{1,0:T(4,128)S(1)} %copy-done.2, s32[4,8]{1,0:T(4,128)S(1)} %collective-permute-done.1.table_ref, bf16[4,128,1024]{2,1,0:T(8,128)(2,1)S(1)} %collective-permute-done.3.q_ref, ...), custom_call_target="tpu_custom_call" | custom-call | flops 1 | bytes 1 | tf_op jit(solution)/shard_map/pallas_call | solution.py:119
  123.2 4.0 %shard_map.64 = (f32[4,128,512]{2,1,0:T(8,128)S(1)}, f32[4,128,512]{2,1,0:T(8,128)S(1)}, f32[4,128,512]{2,1,0:T(8,128)S(1)}) custom-call(s32[4]{0:T(128)S(1)} %get-tuple-element.85.where_ref, s32[4,4]{1,0:T(4,128)S(1)} %copy-done.2, s32[4,8]{1,0:T(4,128)S(1)} %collective-permute-done.1.table_ref, bf16[4,128,1024]{2,1,0:T(8,128)(2,1)S(1)} %collective-permute-done.3.q_ref, ...), custom_call_target="tpu_custom_call" | custom-call | flops 1 | bytes 1 | tf_op jit(solution)/shard_map/pallas_call | solution.py:119
  127.2 0.1 select_select_fusion.1.refs_0_
  127.3 2.7 %shard_map.68 = bf16[4,128,512]{2,1,0:T(8,128)(2,1)S(1)} custom-call(s32[4]{0:T(128)S(1)} %get-tuple-element.85.where_ref, s32[4,4]{1,0:T(4,128)S(1)} %copy-done.2, s32[4,8]{1,0:T(4,128)S(1)} %collective-permute-done.1.table_ref, bf16[4,128,1024]{2,1,0:T(8,128)(2,1)S(1)} %collective-permute-done.3.q_ref, bf16[2048,128]{1,0:T(8,128)(2,1)S(1)} %select_select_fusion.1.refs_0_, ...), custom_call_target="tpu_custom_call" | custom-call | flops 1 | bytes 1 | tf_op jit(solution)/shard_map/pallas_call | solution.py:119
  130.0 2.9 %collective-permute-done.16 = bf16[2048,128]{1,0:T(8,128)(2,1)S(1)} collective-permute-done((bf16[2048,128]{1,0:T(8,128)(2,1)S(1)}, bf16[2048,128]{1,0:T(8,128)(2,1)S(1)}, u32[]{:S(2)}, u32[]{:S(2)}) %collective-permute-start.16) | collective-permute-done | bytes 524320 | tf_op jit(solution)/shard_map/ppermute | solution.py:261
  132.9 0.1 select_select_fusion.refs_0_
  133.0 2.7 %shard_map.69 = bf16[4,128,512]{2,1,0:T(8,128)(2,1)S(1)} custom-call(s32[4]{0:T(128)S(1)} %get-tuple-element.85.where_ref, s32[4,4]{1,0:T(4,128)S(1)} %copy-done.2, s32[4,8]{1,0:T(4,128)S(1)} %collective-permute-done.1.table_ref, bf16[4,128,1024]{2,1,0:T(8,128)(2,1)S(1)} %collective-permute-done.3.q_ref, bf16[2048,128]{1,0:T(8,128)(2,1)S(1)} %select_select_fusion.refs_0_, ...), custom_call_target="tpu_custom_call" | custom-call | flops 1 | bytes 1 | tf_op jit(solution)/shard_map/pallas_call | solution.py:119
  135.7 0.1 collective-permute-start.17
  135.8 1.5 collective-permute-start.21
  137.4 1.5 collective-permute-start.18
  138.9 2.7 %shard_map.71.refs_2_ = bf16[4,128,512]{2,1,0:T(8,128)(2,1)S(1)} custom-call(s32[4]{0:T(128)S(1)} %pad_add_fusion.1.where_ref, s32[4,4]{1,0:T(4,128)S(1)} %copy-done.2, s32[4,8]{1,0:T(4,128)S(1)} %pad_add_fusion.table_ref, bf16[4,128,1024]{2,1,0:T(8,128)(2,1)S(1)} %pad_maximum_fusion.1.q_ref, bf16[2048,128]{1,0:T(8,128)(2,1)S(1)} %select_select_fusion.refs_0_, ...), custom_call_target="tpu_custom_call" | custom-call | flops 1 | bytes 1 | tf_op jit(solution)/shard_map/pallas_call | solution.py:119
  141.6 0.1 collective-permute-start.20
  141.7 2.7 %shard_map.70.refs_0_ = bf16[4,128,512]{2,1,0:T(8,128)(2,1)S(1)} custom-call(s32[4]{0:T(128)S(1)} %pad_add_fusion.1.where_ref, s32[4,4]{1,0:T(4,128)S(1)} %copy-done.2, s32[4,8]{1,0:T(4,128)S(1)} %pad_add_fusion.table_ref, bf16[4,128,1024]{2,1,0:T(8,128)(2,1)S(1)} %pad_maximum_fusion.1.q_ref, bf16[2048,128]{1,0:T(8,128)(2,1)S(1)} %select_select_fusion.1.refs_0_, ...), custom_call_target="tpu_custom_call" | custom-call | flops 1 | bytes 1 | tf_op jit(solution)/shard_map/pallas_call | solution.py:119
  144.4 0.6 collective-permute-start.19
  145.0 11.9 %collective-permute-done.21.refs_4_ = bf16[4,128,512]{2,1,0:T(8,128)(2,1)S(1)} collective-permute-done((bf16[4,128,512]{2,1,0:T(8,128)(2,1)S(1)}, bf16[4,128,512]{2,1,0:T(8,128)(2,1)S(1)}, u32[]{:S(2)}, u32[]{:S(2)}) %collective-permute-start.21) | collective-permute-done | bytes 524320 | tf_op jit(solution)/shard_map/ppermute | solution.py:256
  156.9 0.1 collective-permute-start.22
  157.0 1.5 collective-permute-done.22.refs_5_
  158.5 0.1 shard_map.72.rows_ref
  158.7 10.3 %shard_map.73.refs_0_ = f32[512,4096]{1,0:T(8,128)S(1)} custom-call(s32[4]{0:T(128)S(1)} %pad_add_fusion.1.where_ref, bf16[512,1536]{1,0:T(8,128)(2,1)S(1)} %shard_map.72.rows_ref, bf16[2,2048,2048]{2,1,0:T(8,128)(2,1)} %bitcast.14), custom_call_target="tpu_custom_call" | custom-call | flops 1 | bytes 1 | tf_op jit(solution)/shard_map/pallas_call | solution.py:207
  169.1 6.6 %shard_map.75 = bf16[512,4096]{1,0:T(8,128)(2,1)} custom-call(s32[4]{0:T(128)S(1)} %pad_add_fusion.1.where_ref, bf16[512,512]{1,0:T(8,128)(2,1)S(1)} %shard_map.74.rows_ref, bf16[2,2048,2048]{2,1,0:T(8,128)(2,1)} %bitcast.15, f32[512,4096]{1,0:T(8,128)S(1)} %shard_map.73.refs_0_), custom_call_target="tpu_custom_call" | custom-call | flops 1 | bytes 1 | tf_op jit(solution)/shard_map/pallas_call | solution.py:207
  (37 shorter events, 0.5 us)
Async XLA Ops:
  6.5 1.2 copy-start
  6.5 51.1 %all-gather.3.cloned.1.call-start = ((), (), s32[]{:S(2)}) async-start(), calls=%async_computation | async-start | bytes 2621440 | tf_op jit(solution)/shard_map/all_gather | solution.py:303
  8.6 150.1 %all-gather.5.cloned.1.call-start = ((), (), s32[]{:S(2)}) async-start(), calls=%async_computation.1 | async-start | bytes 18874368 | tf_op jit(solution)/shard_map/all_gather | solution.py:327
  11.4 6.0 %collective-permute-start.2 = (bf16[2,128,2048]{2,1,0:T(8,128)(2,1)}, bf16[2,128,2048]{2,1,0:T(8,128)(2,1)S(1)}, u32[]{:S(2)}, u32[]{:S(2)}) collective-permute-start(bf16[2,128,2048]{2,1,0:T(8,128)(2,1)} %get-tuple-element.88), channel_id=1, source_target_pairs={{0,1},{1,0},{2,3},{3,2},{4,5},{5,4},{6,7},{7,6},{8,9},{9,8},{10,11... | collective-permute-start | bytes 3145736 | tf_op jit(solution)/shard_map/ppermute | solution.py:251
  13.9 15.6 %collective-permute-start.4 = (bf16[1024,256]{1,0:T(8,128)(2,1)}, bf16[1024,256]{1,0:T(8,128)(2,1)}, u32[]{:S(2)}, u32[]{:S(2)}) collective-permute-start(bf16[1024,256]{1,0:T(8,128)(2,1)} %pad_maximum_fusion.3), channel_id=1, source_target_pairs={{0,2},{1,3},{2,0},{3,1},{4,6},{5,7},{6,4},{7,5},{8,10},{9,11},{10,... | collective-permute-start | bytes 1572872 | tf_op jit(solution)/shard_map/ppermute | solution.py:256
  17.3 1.1 copy-start.3
  18.3 33.5 %collective-permute-start.3 = (bf16[4,128,1024]{2,1,0:T(8,128)(2,1)S(1)}, bf16[4,128,1024]{2,1,0:T(8,128)(2,1)S(1)}, u32[]{:S(2)}, u32[]{:S(2)}) collective-permute-start(bf16[4,128,1024]{2,1,0:T(8,128)(2,1)S(1)} %pad_maximum_fusion), channel_id=1, source_target_pairs={{0,2},{1,3},{2,0},{3,1},{4,6},{5,7},{6,4},{7,5},{8,10},{9,11},{10,... | collective-permute-start | bytes 3145736 | tf_op jit(solution)/shard_map/ppermute | solution.py:256
  18.4 1.2 collective-permute-start
  19.7 32.1 %collective-permute-start.1 = (s32[4,8]{1,0:T(4,128)S(1)}, s32[4,8]{1,0:T(4,128)S(1)}, u32[]{:S(2)}, u32[]{:S(2)}) collective-permute-start(s32[4,8]{1,0:T(4,128)S(1)} %pad_add_fusion.table_ref), channel_id=1, source_target_pairs={{0,2},{1,3},{2,0},{3,1},{4,6},{5,7},{6,4},{7,5},{8,10},{9,11},{10,... | collective-permute-start | bytes 392 | tf_op jit(solution)/shard_map/ppermute | solution.py:256
  57.6 16.7 %collective-permute-start.5 = (bf16[2048,128]{1,0:T(8,128)(2,1)S(1)}, bf16[2048,128]{1,0:T(8,128)(2,1)S(1)}, u32[]{:S(2)}, u32[]{:S(2)}) collective-permute-start(bf16[2048,128]{1,0:T(8,128)(2,1)S(1)} %pad_maximum_fusion.4.refs_0_), channel_id=1, source_target_pairs={{4,0},{5,1},{6,2},{7,3},{8,4},{9,5},{10,6},{11,7},{12,8},{13,9},{1... | collective-permute-start | bytes 1572872 | tf_op jit(solution)/shard_map/ppermute | solution.py:261
  58.9 16.9 %collective-permute-start.11 = (bf16[2048,128]{1,0:T(8,128)(2,1)S(1)}, bf16[2048,128]{1,0:T(8,128)(2,1)}, u32[]{:S(2)}, u32[]{:S(2)}) collective-permute-start(bf16[2048,128]{1,0:T(8,128)(2,1)S(1)} %pad_maximum_fusion.4.refs_0_), channel_id=1, source_target_pairs={{0,4},{1,5},{2,6},{3,7},{4,8},{5,9},{6,10},{7,11},{8,12},{9,13},{1... | collective-permute-start | bytes 1572872 | tf_op jit(solution)/shard_map/ppermute | solution.py:261
  64.3 21.3 %collective-permute-start.7 = (bf16[2048,128]{1,0:T(8,128)(2,1)S(1)}, bf16[2048,128]{1,0:T(8,128)(2,1)S(1)}, u32[]{:S(2)}, u32[]{:S(2)}) collective-permute-start(bf16[2048,128]{1,0:T(8,128)(2,1)S(1)} %fusion.refs_0_), channel_id=1, source_target_pairs={{4,0},{5,1},{6,2},{7,3},{8,4},{9,5},{10,6},{11,7},{12,8},{13,9},{1... | collective-permute-start | bytes 1572872 | tf_op jit(solution)/shard_map/ppermute | solution.py:261
  65.6 21.3 %collective-permute-start.9 = (bf16[2048,128]{1,0:T(8,128)(2,1)S(1)}, bf16[2048,128]{1,0:T(8,128)(2,1)}, u32[]{:S(2)}, u32[]{:S(2)}) collective-permute-start(bf16[2048,128]{1,0:T(8,128)(2,1)S(1)} %fusion.refs_0_), channel_id=1, source_target_pairs={{0,4},{1,5},{2,6},{3,7},{4,8},{5,9},{6,10},{7,11},{8,12},{9,13},{1... | collective-permute-start | bytes 1572872 | tf_op jit(solution)/shard_map/ppermute | solution.py:261
  75.8 21.0 %collective-permute-start.6 = (bf16[2048,128]{1,0:T(8,128)(2,1)S(1)}, bf16[2048,128]{1,0:T(8,128)(2,1)S(1)}, u32[]{:S(2)}, u32[]{:S(2)}) collective-permute-start(bf16[2048,128]{1,0:T(8,128)(2,1)S(1)} %collective-permute-done.5), channel_id=1, source_target_pairs={{4,0},{5,1},{6,2},{7,3},{8,4},{9,5},{10,6},{11,7},{20,16},{21,17},... | collective-permute-start | bytes 1572872 | tf_op jit(solution)/shard_map/ppermute | solution.py:261
  77.1 19.7 %collective-permute-start.12 = (bf16[2048,128]{1,0:T(8,128)(2,1)}, bf16[2048,128]{1,0:T(8,128)(2,1)S(1)}, u32[]{:S(2)}, u32[]{:S(2)}) collective-permute-start(bf16[2048,128]{1,0:T(8,128)(2,1)} %collective-permute-done.11), channel_id=1, source_target_pairs={{4,8},{5,9},{6,10},{7,11},{8,12},{9,13},{10,14},{11,15},{20,24},{2... | collective-permute-start | bytes 1572872 | tf_op jit(solution)/shard_map/ppermute | solution.py:261
  85.6 21.3 %collective-permute-start.8 = (bf16[2048,128]{1,0:T(8,128)(2,1)S(1)}, bf16[2048,128]{1,0:T(8,128)(2,1)S(1)}, u32[]{:S(2)}, u32[]{:S(2)}) collective-permute-start(bf16[2048,128]{1,0:T(8,128)(2,1)S(1)} %collective-permute-done.7), channel_id=1, source_target_pairs={{4,0},{5,1},{6,2},{7,3},{8,4},{9,5},{10,6},{11,7},{20,16},{21,17},... | collective-permute-start | bytes 1572872 | tf_op jit(solution)/shard_map/ppermute | solution.py:261
  86.9 21.3 %collective-permute-start.10 = (bf16[2048,128]{1,0:T(8,128)(2,1)}, bf16[2048,128]{1,0:T(8,128)(2,1)S(1)}, u32[]{:S(2)}, u32[]{:S(2)}) collective-permute-start(bf16[2048,128]{1,0:T(8,128)(2,1)} %collective-permute-done.9), channel_id=1, source_target_pairs={{4,8},{5,9},{6,10},{7,11},{8,12},{9,13},{10,14},{11,15},{20,24},{2... | collective-permute-start | bytes 1572872 | tf_op jit(solution)/shard_map/ppermute | solution.py:261
  87.7 23.3 %copy-start.2 = (s32[4,4]{1,0:T(4,128)S(1)}, s32[4,4]{1,0:T(4,128)}, u32[]{:S(2)}) copy-start(s32[4,4]{1,0:T(4,128)} %constant.37.clone.order_ref) | copy-start | bytes 196
  106.9 20.3 %collective-permute-start.14 = (bf16[2048,128]{1,0:T(8,128)(2,1)S(1)}, bf16[2048,128]{1,0:T(8,128)(2,1)S(1)}, u32[]{:S(2)}, u32[]{:S(2)}) collective-permute-start(bf16[2048,128]{1,0:T(8,128)(2,1)S(1)} %collective-permute-done.8), channel_id=1, source_target_pairs={{4,0},{5,1},{6,2},{7,3},{20,16},{21,17},{22,18},{23,19}} | collective-permute-start | bytes 1572872 | tf_op jit(solution)/shard_map/ppermute | solution.py:261
  108.2 19.0 %collective-permute-start.13 = (bf16[2048,128]{1,0:T(8,128)(2,1)S(1)}, bf16[2048,128]{1,0:T(8,128)(2,1)S(1)}, u32[]{:S(2)}, u32[]{:S(2)}) collective-permute-start(bf16[2048,128]{1,0:T(8,128)(2,1)S(1)} %collective-permute-done.10), channel_id=1, source_target_pairs={{8,12},{9,13},{10,14},{11,15},{24,28},{25,29},{26,30},{27,31}} | collective-permute-start | bytes 1572872 | tf_op jit(solution)/shard_map/ppermute | solution.py:261
  109.0 23.9 %collective-permute-start.16 = (bf16[2048,128]{1,0:T(8,128)(2,1)S(1)}, bf16[2048,128]{1,0:T(8,128)(2,1)S(1)}, u32[]{:S(2)}, u32[]{:S(2)}) collective-permute-start(bf16[2048,128]{1,0:T(8,128)(2,1)S(1)} %collective-permute-done.6), channel_id=1, source_target_pairs={{4,0},{5,1},{6,2},{7,3},{20,16},{21,17},{22,18},{23,19}} | collective-permute-start | bytes 1572872 | tf_op jit(solution)/shard_map/ppermute | solution.py:261
  110.3 22.6 %collective-permute-start.15 = (bf16[2048,128]{1,0:T(8,128)(2,1)S(1)}, bf16[2048,128]{1,0:T(8,128)(2,1)S(1)}, u32[]{:S(2)}, u32[]{:S(2)}) collective-permute-start(bf16[2048,128]{1,0:T(8,128)(2,1)S(1)} %collective-permute-done.12), channel_id=1, source_target_pairs={{8,12},{9,13},{10,14},{11,15},{24,28},{25,29},{26,30},{27,31}} | collective-permute-start | bytes 1572872 | tf_op jit(solution)/shard_map/ppermute | solution.py:261
  135.7 1.6 collective-permute-start.17
  135.8 21.1 %collective-permute-start.21 = (bf16[4,128,512]{2,1,0:T(8,128)(2,1)S(1)}, bf16[4,128,512]{2,1,0:T(8,128)(2,1)S(1)}, u32[]{:S(2)}, u32[]{:S(2)}) collective-permute-start(bf16[4,128,512]{2,1,0:T(8,128)(2,1)S(1)} %shard_map.68), channel_id=1, source_target_pairs={{0,2},{1,3},{2,0},{3,1},{4,6},{5,7},{6,4},{7,5},{8,10},{9,11},{10,... | collective-permute-start | bytes 1572872 | tf_op jit(solution)/shard_map/ppermute | solution.py:256
  137.4 31.5 %collective-permute-start.18 = (bf16[4,128,512]{2,1,0:T(8,128)(2,1)S(1)}, bf16[4,128,512]{2,1,0:T(8,128)(2,1)S(1)}, u32[]{:S(2)}, u32[]{:S(2)}) collective-permute-start(bf16[4,128,512]{2,1,0:T(8,128)(2,1)S(1)} %pad_maximum_fusion.5), channel_id=1, source_target_pairs={{0,2},{1,3},{2,0},{3,1},{4,6},{5,7},{6,4},{7,5},{8,10},{9,11},{10,... | collective-permute-start | bytes 1572872 | tf_op jit(solution)/shard_map/ppermute | solution.py:256
  141.6 15.4 %collective-permute-start.20 = (bf16[2,128,512]{2,1,0:T(8,128)(2,1)S(1)}, bf16[2,128,512]{2,1,0:T(8,128)(2,1)S(1)}, u32[]{:S(2)}, u32[]{:S(2)}) collective-permute-start(bf16[2,128,512]{2,1,0:T(8,128)(2,1)S(1)} %slice.69), channel_id=1, source_target_pairs={{0,1},{1,0},{2,3},{3,2},{4,5},{5,4},{6,7},{7,6},{8,9},{9,8},{10,11... | collective-permute-start | bytes 786440 | tf_op jit(solution)/shard_map/ppermute | solution.py:251
  144.4 12.6 %collective-permute-start.19 = (bf16[2,128,512]{2,1,0:T(8,128)(2,1)S(1)}, bf16[2,128,512]{2,1,0:T(8,128)(2,1)S(1)}, u32[]{:S(2)}, u32[]{:S(2)}) collective-permute-start(bf16[2,128,512]{2,1,0:T(8,128)(2,1)S(1)} %slice.68), channel_id=1, source_target_pairs={{0,1},{1,0},{2,3},{3,2},{4,5},{5,4},{6,7},{7,6},{8,9},{9,8},{10,11... | collective-permute-start | bytes 786440 | tf_op jit(solution)/shard_map/ppermute | solution.py:251
  156.9 1.6 collective-permute-start.22
  169.0 6.6 %copy-start.1 = (bf16[128,4096]{1,0:T(8,128)(2,1)S(1)}, bf16[128,4096]{1,0:T(8,128)(2,1)}, u32[]{:S(2)}) copy-start(bf16[128,4096]{1,0:T(8,128)(2,1)} %param.10) | copy-start | bytes 3145732
Sparse Core Ops, SparseCore 0:
  8.9 48.6 all-gather.2
  59.5 95.2 all-gather.4

commit v13 on v12

--- a/solution.py
+++ b/solution.py
@@ -167,6 +167,7 @@
     step = pl.program_id(0)
     tile = wbuf.shape[-1]
     tiles = w_ref.shape[-1] // tile
+    slots = wbuf.shape[0]
 
     def fetch(later):
         columns = slice(later % tiles * tile, (later % tiles + 1) * tile)
@@ -176,21 +177,22 @@
                 to = (at * GROUP + g) * HD
                 pltpu.make_async_copy(
                     w_ref.at[later // tiles, pl.ds(pl.multiple_of(block * HD, HD), HD), columns],
-                    wbuf.at[later % 2, to : to + HD, :],
-                    sems.at[later % 2],
+                    wbuf.at[later % slots, to : to + HD, :],
+                    sems.at[later % slots],
                 ).start()
 
     @pl.when(step == 0)
     def _():
-        fetch(0)
-
-    for later in range(1, steps):
-
-        @pl.when(step == later - 1)
+        for later in range(slots - 1):
+            fetch(later)
+
+    for later in range(slots - 1, steps):
+
+        @pl.when(step == later - slots + 1)
         def _():
             fetch(later)
 
-    slot = lax.rem(step, 2)
+    slot = lax.rem(step, slots)
     pltpu.make_async_copy(wbuf.at[slot], wbuf.at[slot], sems.at[slot]).wait()
     total = jnp.dot(rows_ref[...], wbuf[slot], preferred_element_type=jnp.float32)
     if len(refs) > 3:
@@ -202,6 +204,7 @@
     parts, _, columns = weights.shape
     steps = parts * columns // tile
     length, depth = rows.shape
+    slots = 2 if before is None else min(steps, 4)
     block = pl.BlockSpec((length, tile), lambda s, *_: (0, s))
     dtype = jnp.float32 if before is None else jnp.bfloat16
     return pl.pallas_call(
@@ -217,8 +220,8 @@
             + [pl.BlockSpec(memory_space=pltpu.VMEM)] * (before is not None),
             out_specs=block,
             scratch_shapes=[
-                pltpu.VMEM((2, depth, tile), jnp.bfloat16),
-                pltpu.SemaphoreType.DMA((2,)),
+                pltpu.VMEM((slots, depth, tile), jnp.bfloat16),
+                pltpu.SemaphoreType.DMA((slots,)),
             ],
         ),
         compiler_params=pltpu.CompilerParams(vmem_limit_bytes=VMEM_LIMIT),

time: 183 us -> 182 us (level)
  no operation moved by 1% of the time
where the time goes in v13:
time: 182 us
  waiting for transfers between devices  82.4 us (45%)
  Pallas kernels  43.2 us (24%)
  starting transfers between devices  30.4 us (17%)
  between operations  13.8 us (8%)
  local copies, waits for them, and re-layouts  9.04 us (5%)
  other arithmetic  3.01 us (2%)
    ppermute x5, waiting for transfers between devices, swap_side(): lax.ppermute(array, SEQ, [(index(o, s, c), index(o, 1 - s, c)) for o, s,...  40.9 us
    ppermute x12, waiting for transfers between devices, move(): lax.ppermute(array, SEQ, [(index(o, s, c), index(o + way, s, c)) for o, s...  33.2 us
    pallas_call x8, Pallas kernels, attention(): pl.pallas_call(functools.partial(attention_kernel, n_chip, slots, not sta...  26.8 us
    ppermute x12, starting transfers between devices, move(): lax.ppermute(array, SEQ, [(index(o, s, c), index(o + way, s, c)) for o, s...  21.2 us
    pallas_call x2, Pallas kernels, project(): pl.pallas_call(functools.partial(project_kernel, n_outer, groups, steps),...  16.2 us
    ppermute x5, starting transfers between devices, swap_side(): lax.ppermute(array, SEQ, [(index(o, s, c), index(o, 1 - s, c)) for o, s,...  7.64 us
    all_gather x1, waiting for transfers between devices, body(): gathered = lax.all_gather(columns, LINE, axis=0, tiled=True)  5.82 us
  transfers between devices with their start and end apart: 25, of which 12 were waited for; matrix products, arithmetic and copies ran while one was open for 5% of the time, Pallas kernels for 20%

profile of v13, /device:TPU:0, one launch (start us, length us, event | category | flops | bytes accessed | tf_op | source)
XLA Modules:
  0.0 181.9 jit_solution(13474486290258234352)
XLA Ops:
  6.5 1.2 copy-done
  7.8 0.8 constant_dynamic-slice_fusion.1
  8.7 2.7 %fusion.2 = (bf16[2,1,128,2048]{3,2,1,0:T(8,128)(2,1)S(1)}, bf16[2,128,2048]{2,1,0:T(8,128)(2,1)}) fusion(bf16[2,2,128,2048]{3,2,1,0:T(8,128)(2,1)} %bitcast.16), kind=kLoop, calls=%fused_computation.30 | loop fusion | bytes 4194304 | tf_op jit(solution)/shard_map/slice | solution.py:316
  11.4 0.5 collective-permute-start.2
  11.8 1.3 constant_dynamic-slice_fusion.4
  13.1 0.8 pad_maximum_fusion.3
  13.9 2.5 %collective-permute-start.4 = (bf16[1024,256]{1,0:T(8,128)(2,1)}, bf16[1024,256]{1,0:T(8,128)(2,1)}, u32[]{:S(2)}, u32[]{:S(2)}) collective-permute-start(bf16[1024,256]{1,0:T(8,128)(2,1)} %pad_maximum_fusion.3), channel_id=1, source_target_pairs={{0,2},{1,3},{2,0},{3,1},{4,6},{5,7},{6,4},{7,5},{8,10},{9,11},{10,... | collective-permute-start | bytes 1572872 | tf_op jit(solution)/shard_map/ppermute | solution.py:259
  16.5 0.9 dynamic-slice_bitcast_fusion
  17.4 0.9 constant_dynamic-slice_fusion
  18.2 0.1 pad_maximum_fusion
  18.3 0.1 collective-permute-start.3
  18.4 0.3 collective-permute-start
  18.8 0.9 collective-permute-done
  19.7 2.0 %collective-permute-start.1 = (s32[4,8]{1,0:T(4,128)S(1)}, s32[4,8]{1,0:T(4,128)S(1)}, u32[]{:S(2)}, u32[]{:S(2)}) collective-permute-start(s32[4,8]{1,0:T(4,128)S(1)} %pad_add_fusion.table_ref), channel_id=1, source_target_pairs={{0,2},{1,3},{2,0},{3,1},{4,6},{5,7},{6,4},{7,5},{8,10},{9,11},{10,... | collective-permute-start | bytes 392 | tf_op jit(solution)/shard_map/ppermute | solution.py:259
  21.7 7.9 %collective-permute-done.4 = bf16[1024,256]{1,0:T(8,128)(2,1)} collective-permute-done((bf16[1024,256]{1,0:T(8,128)(2,1)}, bf16[1024,256]{1,0:T(8,128)(2,1)}, u32[]{:S(2)}, u32[]{:S(2)}) %collective-permute-start.4) | collective-permute-done | bytes 524320 | tf_op jit(solution)/shard_map/ppermute | solution.py:259
  29.6 1.1 fusion.5
  30.7 21.1 %collective-permute-done.1.table_ref = s32[4,8]{1,0:T(4,128)S(1)} collective-permute-done((s32[4,8]{1,0:T(4,128)S(1)}, s32[4,8]{1,0:T(4,128)S(1)}, u32[]{:S(2)}, u32[]{:S(2)}) %collective-permute-start.1) | collective-permute-done | bytes 160 | tf_op jit(solution)/shard_map/ppermute | solution.py:259
  51.8 5.8 %all-gather.3.cloned.1.call-done = bf16[512,2048]{1,0:T(8,128)(2,1)} async-done(((bf16[128,2048]{1,0:T(8,128)(2,1)}), bf16[512,2048]{1,0:T(8,128)(2,1)}) %all-gather.3.cloned.1.call-update) | async-done | bytes 2097168 | tf_op jit(solution)/shard_map/all_gather | solution.py:306
  57.6 1.3 collective-permute-start.5
  58.9 5.4 %collective-permute-start.11 = (bf16[2048,128]{1,0:T(8,128)(2,1)S(1)}, bf16[2048,128]{1,0:T(8,128)(2,1)}, u32[]{:S(2)}, u32[]{:S(2)}) collective-permute-start(bf16[2048,128]{1,0:T(8,128)(2,1)S(1)} %pad_maximum_fusion.4.refs_0_), channel_id=1, source_target_pairs={{0,4},{1,5},{2,6},{3,7},{4,8},{5,9},{6,10},{7,11},{8,12},{9,13},{1... | collective-permute-start | bytes 1572872 | tf_op jit(solution)/shard_map/ppermute | solution.py:264
  64.3 1.3 collective-permute-start.7
  65.6 5.3 %collective-permute-start.9 = (bf16[2048,128]{1,0:T(8,128)(2,1)S(1)}, bf16[2048,128]{1,0:T(8,128)(2,1)}, u32[]{:S(2)}, u32[]{:S(2)}) collective-permute-start(bf16[2048,128]{1,0:T(8,128)(2,1)S(1)} %fusion.refs_0_), channel_id=1, source_target_pairs={{0,4},{1,5},{2,6},{3,7},{4,8},{5,9},{6,10},{7,11},{8,12},{9,13},{1... | collective-permute-start | bytes 1572872 | tf_op jit(solution)/shard_map/ppermute | solution.py:264
  70.9 0.1 pad_add_fusion.3
  71.0 0.1 pad_add_fusion.1.where_ref
  71.1 1.3 pad_maximum_fusion.1.q_ref
  72.4 1.9 %collective-permute-done.5 = bf16[2048,128]{1,0:T(8,128)(2,1)S(1)} collective-permute-done((bf16[2048,128]{1,0:T(8,128)(2,1)S(1)}, bf16[2048,128]{1,0:T(8,128)(2,1)S(1)}, u32[]{:S(2)}, u32[]{:S(2)}) %collective-permute-start.5) | collective-permute-done | bytes 524320 | tf_op jit(solution)/shard_map/ppermute | solution.py:264
  74.3 1.5 collective-permute-done.11
  75.8 1.3 collective-permute-start.6
  77.1 0.7 collective-permute-start.12
  77.8 7.7 %collective-permute-done.7 = bf16[2048,128]{1,0:T(8,128)(2,1)S(1)} collective-permute-done((bf16[2048,128]{1,0:T(8,128)(2,1)S(1)}, bf16[2048,128]{1,0:T(8,128)(2,1)S(1)}, u32[]{:S(2)}, u32[]{:S(2)}) %collective-permute-start.7) | collective-permute-done | bytes 524320 | tf_op jit(solution)/shard_map/ppermute | solution.py:264
  85.6 1.3 collective-permute-start.8
  86.9 0.7 collective-permute-start.10
  87.6 0.1 broadcast_select_fusion.refs_1_
  87.6 0.1 broadcast_select_fusion.1.refs_1_
  87.7 9.1 %collective-permute-done.6 = bf16[2048,128]{1,0:T(8,128)(2,1)S(1)} collective-permute-done((bf16[2048,128]{1,0:T(8,128)(2,1)S(1)}, bf16[2048,128]{1,0:T(8,128)(2,1)S(1)}, u32[]{:S(2)}, u32[]{:S(2)}) %collective-permute-start.6) | collective-permute-done | bytes 524320 | tf_op jit(solution)/shard_map/ppermute | solution.py:264
  96.8 10.1 %collective-permute-done.8 = bf16[2048,128]{1,0:T(8,128)(2,1)S(1)} collective-permute-done((bf16[2048,128]{1,0:T(8,128)(2,1)S(1)}, bf16[2048,128]{1,0:T(8,128)(2,1)S(1)}, u32[]{:S(2)}, u32[]{:S(2)}) %collective-permute-start.8) | collective-permute-done | bytes 524320 | tf_op jit(solution)/shard_map/ppermute | solution.py:264
  106.9 1.3 collective-permute-start.14
  108.2 0.7 collective-permute-start.13
  108.9 0.1 select_select_fusion.2.refs_2_
  109.0 1.3 collective-permute-start.16
  110.3 0.7 collective-permute-start.15
  111.0 0.1 select_select_fusion.3.refs_2_
  111.1 4.0 %shard_map.67 = (f32[4,128,512]{2,1,0:T(8,128)S(1)}, f32[4,128,512]{2,1,0:T(8,128)S(1)}, f32[4,128,512]{2,1,0:T(8,128)S(1)}) custom-call(s32[4]{0:T(128)S(1)} %pad_add_fusion.1.where_ref, s32[4,4]{1,0:T(4,128)S(1)} %copy-done.2, s32[4,8]{1,0:T(4,128)S(1)} %pad_add_fusion.table_ref, bf16[4,128,1024]{2,1,0:T(8,128)(2,1)S(1)} %pad_maximum_fusion.1.q_ref, ...), custom_call_target="tpu_custom_call" | custom-call | flops 1 | bytes 1 | tf_op jit(solution)/shard_map/pallas_call | solution.py:119
  115.1 4.0 %shard_map.65 = (f32[4,128,512]{2,1,0:T(8,128)S(1)}, f32[4,128,512]{2,1,0:T(8,128)S(1)}, f32[4,128,512]{2,1,0:T(8,128)S(1)}) custom-call(s32[4]{0:T(128)S(1)} %pad_add_fusion.1.where_ref, s32[4,4]{1,0:T(4,128)S(1)} %copy-done.2, s32[4,8]{1,0:T(4,128)S(1)} %pad_add_fusion.table_ref, bf16[4,128,1024]{2,1,0:T(8,128)(2,1)S(1)} %pad_maximum_fusion.1.q_ref, ...), custom_call_target="tpu_custom_call" | custom-call | flops 1 | bytes 1 | tf_op jit(solution)/shard_map/pallas_call | solution.py:119
  119.1 4.0 %shard_map.66 = (f32[4,128,512]{2,1,0:T(8,128)S(1)}, f32[4,128,512]{2,1,0:T(8,128)S(1)}, f32[4,128,512]{2,1,0:T(8,128)S(1)}) custom-call(s32[4]{0:T(128)S(1)} %get-tuple-element.85.where_ref, s32[4,4]{1,0:T(4,128)S(1)} %copy-done.2, s32[4,8]{1,0:T(4,128)S(1)} %collective-permute-done.1.table_ref, bf16[4,128,1024]{2,1,0:T(8,128)(2,1)S(1)} %collective-permute-done.3.q_ref, ...), custom_call_target="tpu_custom_call" | custom-call | flops 1 | bytes 1 | tf_op jit(solution)/shard_map/pallas_call | solution.py:119
  123.2 4.0 %shard_map.64 = (f32[4,128,512]{2,1,0:T(8,128)S(1)}, f32[4,128,512]{2,1,0:T(8,128)S(1)}, f32[4,128,512]{2,1,0:T(8,128)S(1)}) custom-call(s32[4]{0:T(128)S(1)} %get-tuple-element.85.where_ref, s32[4,4]{1,0:T(4,128)S(1)} %copy-done.2, s32[4,8]{1,0:T(4,128)S(1)} %collective-permute-done.1.table_ref, bf16[4,128,1024]{2,1,0:T(8,128)(2,1)S(1)} %collective-permute-done.3.q_ref, ...), custom_call_target="tpu_custom_call" | custom-call | flops 1 | bytes 1 | tf_op jit(solution)/shard_map/pallas_call | solution.py:119
  127.2 0.1 select_select_fusion.1.refs_0_
  127.3 2.7 %shard_map.68 = bf16[4,128,512]{2,1,0:T(8,128)(2,1)S(1)} custom-call(s32[4]{0:T(128)S(1)} %get-tuple-element.85.where_ref, s32[4,4]{1,0:T(4,128)S(1)} %copy-done.2, s32[4,8]{1,0:T(4,128)S(1)} %collective-permute-done.1.table_ref, bf16[4,128,1024]{2,1,0:T(8,128)(2,1)S(1)} %collective-permute-done.3.q_ref, bf16[2048,128]{1,0:T(8,128)(2,1)S(1)} %select_select_fusion.1.refs_0_, ...), custom_call_target="tpu_custom_call" | custom-call | flops 1 | bytes 1 | tf_op jit(solution)/shard_map/pallas_call | solution.py:119
  130.0 2.9 %collective-permute-done.16 = bf16[2048,128]{1,0:T(8,128)(2,1)S(1)} collective-permute-done((bf16[2048,128]{1,0:T(8,128)(2,1)S(1)}, bf16[2048,128]{1,0:T(8,128)(2,1)S(1)}, u32[]{:S(2)}, u32[]{:S(2)}) %collective-permute-start.16) | collective-permute-done | bytes 524320 | tf_op jit(solution)/shard_map/ppermute | solution.py:264
  132.9 0.1 select_select_fusion.refs_0_
  133.0 2.7 %shard_map.69 = bf16[4,128,512]{2,1,0:T(8,128)(2,1)S(1)} custom-call(s32[4]{0:T(128)S(1)} %get-tuple-element.85.where_ref, s32[4,4]{1,0:T(4,128)S(1)} %copy-done.2, s32[4,8]{1,0:T(4,128)S(1)} %collective-permute-done.1.table_ref, bf16[4,128,1024]{2,1,0:T(8,128)(2,1)S(1)} %collective-permute-done.3.q_ref, bf16[2048,128]{1,0:T(8,128)(2,1)S(1)} %select_select_fusion.refs_0_, ...), custom_call_target="tpu_custom_call" | custom-call | flops 1 | bytes 1 | tf_op jit(solution)/shard_map/pallas_call | solution.py:119
  135.7 0.1 collective-permute-start.17
  135.8 1.5 collective-permute-start.21
  137.4 1.5 collective-permute-start.18
  138.9 2.7 %shard_map.71.refs_2_ = bf16[4,128,512]{2,1,0:T(8,128)(2,1)S(1)} custom-call(s32[4]{0:T(128)S(1)} %pad_add_fusion.1.where_ref, s32[4,4]{1,0:T(4,128)S(1)} %copy-done.2, s32[4,8]{1,0:T(4,128)S(1)} %pad_add_fusion.table_ref, bf16[4,128,1024]{2,1,0:T(8,128)(2,1)S(1)} %pad_maximum_fusion.1.q_ref, bf16[2048,128]{1,0:T(8,128)(2,1)S(1)} %select_select_fusion.refs_0_, ...), custom_call_target="tpu_custom_call" | custom-call | flops 1 | bytes 1 | tf_op jit(solution)/shard_map/pallas_call | solution.py:119
  141.6 0.1 collective-permute-start.20
  141.7 2.7 %shard_map.70.refs_0_ = bf16[4,128,512]{2,1,0:T(8,128)(2,1)S(1)} custom-call(s32[4]{0:T(128)S(1)} %pad_add_fusion.1.where_ref, s32[4,4]{1,0:T(4,128)S(1)} %copy-done.2, s32[4,8]{1,0:T(4,128)S(1)} %pad_add_fusion.table_ref, bf16[4,128,1024]{2,1,0:T(8,128)(2,1)S(1)} %pad_maximum_fusion.1.q_ref, bf16[2048,128]{1,0:T(8,128)(2,1)S(1)} %select_select_fusion.1.refs_0_, ...), custom_call_target="tpu_custom_call" | custom-call | flops 1 | bytes 1 | tf_op jit(solution)/shard_map/pallas_call | solution.py:119
  144.4 0.6 collective-permute-start.19
  145.0 11.9 %collective-permute-done.21.refs_4_ = bf16[4,128,512]{2,1,0:T(8,128)(2,1)S(1)} collective-permute-done((bf16[4,128,512]{2,1,0:T(8,128)(2,1)S(1)}, bf16[4,128,512]{2,1,0:T(8,128)(2,1)S(1)}, u32[]{:S(2)}, u32[]{:S(2)}) %collective-permute-start.21) | collective-permute-done | bytes 524320 | tf_op jit(solution)/shard_map/ppermute | solution.py:259
  156.9 0.1 collective-permute-start.22
  157.0 1.5 collective-permute-done.22.refs_5_
  158.5 0.1 shard_map.72.rows_ref
  158.7 10.3 %shard_map.73.refs_0_ = f32[512,4096]{1,0:T(8,128)S(1)} custom-call(s32[4]{0:T(128)S(1)} %pad_add_fusion.1.where_ref, bf16[512,1536]{1,0:T(8,128)(2,1)S(1)} %shard_map.72.rows_ref, bf16[2,2048,2048]{2,1,0:T(8,128)(2,1)} %bitcast.14), custom_call_target="tpu_custom_call" | custom-call | flops 1 | bytes 1 | tf_op jit(solution)/shard_map/pallas_call | solution.py:210
  169.1 5.9 %shard_map.75 = bf16[512,4096]{1,0:T(8,128)(2,1)} custom-call(s32[4]{0:T(128)S(1)} %pad_add_fusion.1.where_ref, bf16[512,512]{1,0:T(8,128)(2,1)S(1)} %shard_map.74.rows_ref, bf16[2,2048,2048]{2,1,0:T(8,128)(2,1)} %bitcast.15, f32[512,4096]{1,0:T(8,128)S(1)} %shard_map.73.refs_0_), custom_call_target="tpu_custom_call" | custom-call | flops 1 | bytes 1 | tf_op jit(solution)/shard_map/pallas_call | solution.py:210
  (37 shorter events, 0.5 us)
Async XLA Ops:
  6.5 1.2 copy-start
  6.5 51.1 %all-gather.3.cloned.1.call-start = ((), (), s32[]{:S(2)}) async-start(), calls=%async_computation | async-start | bytes 2621440 | tf_op jit(solution)/shard_map/all_gather | solution.py:306
  8.6 150.1 %all-gather.5.cloned.1.call-start = ((), (), s32[]{:S(2)}) async-start(), calls=%async_computation.1 | async-start | bytes 18874368 | tf_op jit(solution)/shard_map/all_gather | solution.py:330
  11.4 6.0 %collective-permute-start.2 = (bf16[2,128,2048]{2,1,0:T(8,128)(2,1)}, bf16[2,128,2048]{2,1,0:T(8,128)(2,1)S(1)}, u32[]{:S(2)}, u32[]{:S(2)}) collective-permute-start(bf16[2,128,2048]{2,1,0:T(8,128)(2,1)} %get-tuple-element.88), channel_id=1, source_target_pairs={{0,1},{1,0},{2,3},{3,2},{4,5},{5,4},{6,7},{7,6},{8,9},{9,8},{10,11... | collective-permute-start | bytes 3145736 | tf_op jit(solution)/shard_map/ppermute | solution.py:254
  13.9 15.6 %collective-permute-start.4 = (bf16[1024,256]{1,0:T(8,128)(2,1)}, bf16[1024,256]{1,0:T(8,128)(2,1)}, u32[]{:S(2)}, u32[]{:S(2)}) collective-permute-start(bf16[1024,256]{1,0:T(8,128)(2,1)} %pad_maximum_fusion.3), channel_id=1, source_target_pairs={{0,2},{1,3},{2,0},{3,1},{4,6},{5,7},{6,4},{7,5},{8,10},{9,11},{10,... | collective-permute-start | bytes 1572872 | tf_op jit(solution)/shard_map/ppermute | solution.py:259
  17.3 1.1 copy-start.3
  18.3 33.5 %collective-permute-start.3 = (bf16[4,128,1024]{2,1,0:T(8,128)(2,1)S(1)}, bf16[4,128,1024]{2,1,0:T(8,128)(2,1)S(1)}, u32[]{:S(2)}, u32[]{:S(2)}) collective-permute-start(bf16[4,128,1024]{2,1,0:T(8,128)(2,1)S(1)} %pad_maximum_fusion), channel_id=1, source_target_pairs={{0,2},{1,3},{2,0},{3,1},{4,6},{5,7},{6,4},{7,5},{8,10},{9,11},{10,... | collective-permute-start | bytes 3145736 | tf_op jit(solution)/shard_map/ppermute | solution.py:259
  18.4 1.2 collective-permute-start
  19.7 32.1 %collective-permute-start.1 = (s32[4,8]{1,0:T(4,128)S(1)}, s32[4,8]{1,0:T(4,128)S(1)}, u32[]{:S(2)}, u32[]{:S(2)}) collective-permute-start(s32[4,8]{1,0:T(4,128)S(1)} %pad_add_fusion.table_ref), channel_id=1, source_target_pairs={{0,2},{1,3},{2,0},{3,1},{4,6},{5,7},{6,4},{7,5},{8,10},{9,11},{10,... | collective-permute-start | bytes 392 | tf_op jit(solution)/shard_map/ppermute | solution.py:259
  57.6 16.7 %collective-permute-start.5 = (bf16[2048,128]{1,0:T(8,128)(2,1)S(1)}, bf16[2048,128]{1,0:T(8,128)(2,1)S(1)}, u32[]{:S(2)}, u32[]{:S(2)}) collective-permute-start(bf16[2048,128]{1,0:T(8,128)(2,1)S(1)} %pad_maximum_fusion.4.refs_0_), channel_id=1, source_target_pairs={{4,0},{5,1},{6,2},{7,3},{8,4},{9,5},{10,6},{11,7},{12,8},{13,9},{1... | collective-permute-start | bytes 1572872 | tf_op jit(solution)/shard_map/ppermute | solution.py:264
  58.9 16.9 %collective-permute-start.11 = (bf16[2048,128]{1,0:T(8,128)(2,1)S(1)}, bf16[2048,128]{1,0:T(8,128)(2,1)}, u32[]{:S(2)}, u32[]{:S(2)}) collective-permute-start(bf16[2048,128]{1,0:T(8,128)(2,1)S(1)} %pad_maximum_fusion.4.refs_0_), channel_id=1, source_target_pairs={{0,4},{1,5},{2,6},{3,7},{4,8},{5,9},{6,10},{7,11},{8,12},{9,13},{1... | collective-permute-start | bytes 1572872 | tf_op jit(solution)/shard_map/ppermute | solution.py:264
  64.3 21.3 %collective-permute-start.7 = (bf16[2048,128]{1,0:T(8,128)(2,1)S(1)}, bf16[2048,128]{1,0:T(8,128)(2,1)S(1)}, u32[]{:S(2)}, u32[]{:S(2)}) collective-permute-start(bf16[2048,128]{1,0:T(8,128)(2,1)S(1)} %fusion.refs_0_), channel_id=1, source_target_pairs={{4,0},{5,1},{6,2},{7,3},{8,4},{9,5},{10,6},{11,7},{12,8},{13,9},{1... | collective-permute-start | bytes 1572872 | tf_op jit(solution)/shard_map/ppermute | solution.py:264
  65.6 21.3 %collective-permute-start.9 = (bf16[2048,128]{1,0:T(8,128)(2,1)S(1)}, bf16[2048,128]{1,0:T(8,128)(2,1)}, u32[]{:S(2)}, u32[]{:S(2)}) collective-permute-start(bf16[2048,128]{1,0:T(8,128)(2,1)S(1)} %fusion.refs_0_), channel_id=1, source_target_pairs={{0,4},{1,5},{2,6},{3,7},{4,8},{5,9},{6,10},{7,11},{8,12},{9,13},{1... | collective-permute-start | bytes 1572872 | tf_op jit(solution)/shard_map/ppermute | solution.py:264
  75.8 21.0 %collective-permute-start.6 = (bf16[2048,128]{1,0:T(8,128)(2,1)S(1)}, bf16[2048,128]{1,0:T(8,128)(2,1)S(1)}, u32[]{:S(2)}, u32[]{:S(2)}) collective-permute-start(bf16[2048,128]{1,0:T(8,128)(2,1)S(1)} %collective-permute-done.5), channel_id=1, source_target_pairs={{4,0},{5,1},{6,2},{7,3},{8,4},{9,5},{10,6},{11,7},{20,16},{21,17},... | collective-permute-start | bytes 1572872 | tf_op jit(solution)/shard_map/ppermute | solution.py:264
  77.1 19.7 %collective-permute-start.12 = (bf16[2048,128]{1,0:T(8,128)(2,1)}, bf16[2048,128]{1,0:T(8,128)(2,1)S(1)}, u32[]{:S(2)}, u32[]{:S(2)}) collective-permute-start(bf16[2048,128]{1,0:T(8,128)(2,1)} %collective-permute-done.11), channel_id=1, source_target_pairs={{4,8},{5,9},{6,10},{7,11},{8,12},{9,13},{10,14},{11,15},{20,24},{2... | collective-permute-start | bytes 1572872 | tf_op jit(solution)/shard_map/ppermute | solution.py:264
  85.6 21.3 %collective-permute-start.8 = (bf16[2048,128]{1,0:T(8,128)(2,1)S(1)}, bf16[2048,128]{1,0:T(8,128)(2,1)S(1)}, u32[]{:S(2)}, u32[]{:S(2)}) collective-permute-start(bf16[2048,128]{1,0:T(8,128)(2,1)S(1)} %collective-permute-done.7), channel_id=1, source_target_pairs={{4,0},{5,1},{6,2},{7,3},{8,4},{9,5},{10,6},{11,7},{20,16},{21,17},... | collective-permute-start | bytes 1572872 | tf_op jit(solution)/shard_map/ppermute | solution.py:264
  86.9 21.3 %collective-permute-start.10 = (bf16[2048,128]{1,0:T(8,128)(2,1)}, bf16[2048,128]{1,0:T(8,128)(2,1)S(1)}, u32[]{:S(2)}, u32[]{:S(2)}) collective-permute-start(bf16[2048,128]{1,0:T(8,128)(2,1)} %collective-permute-done.9), channel_id=1, source_target_pairs={{4,8},{5,9},{6,10},{7,11},{8,12},{9,13},{10,14},{11,15},{20,24},{2... | collective-permute-start | bytes 1572872 | tf_op jit(solution)/shard_map/ppermute | solution.py:264
  87.7 23.3 %copy-start.2 = (s32[4,4]{1,0:T(4,128)S(1)}, s32[4,4]{1,0:T(4,128)}, u32[]{:S(2)}) copy-start(s32[4,4]{1,0:T(4,128)} %constant.37.clone.order_ref) | copy-start | bytes 196
  106.9 20.3 %collective-permute-start.14 = (bf16[2048,128]{1,0:T(8,128)(2,1)S(1)}, bf16[2048,128]{1,0:T(8,128)(2,1)S(1)}, u32[]{:S(2)}, u32[]{:S(2)}) collective-permute-start(bf16[2048,128]{1,0:T(8,128)(2,1)S(1)} %collective-permute-done.8), channel_id=1, source_target_pairs={{4,0},{5,1},{6,2},{7,3},{20,16},{21,17},{22,18},{23,19}} | collective-permute-start | bytes 1572872 | tf_op jit(solution)/shard_map/ppermute | solution.py:264
  108.2 19.0 %collective-permute-start.13 = (bf16[2048,128]{1,0:T(8,128)(2,1)S(1)}, bf16[2048,128]{1,0:T(8,128)(2,1)S(1)}, u32[]{:S(2)}, u32[]{:S(2)}) collective-permute-start(bf16[2048,128]{1,0:T(8,128)(2,1)S(1)} %collective-permute-done.10), channel_id=1, source_target_pairs={{8,12},{9,13},{10,14},{11,15},{24,28},{25,29},{26,30},{27,31}} | collective-permute-start | bytes 1572872 | tf_op jit(solution)/shard_map/ppermute | solution.py:264
  109.0 23.9 %collective-permute-start.16 = (bf16[2048,128]{1,0:T(8,128)(2,1)S(1)}, bf16[2048,128]{1,0:T(8,128)(2,1)S(1)}, u32[]{:S(2)}, u32[]{:S(2)}) collective-permute-start(bf16[2048,128]{1,0:T(8,128)(2,1)S(1)} %collective-permute-done.6), channel_id=1, source_target_pairs={{4,0},{5,1},{6,2},{7,3},{20,16},{21,17},{22,18},{23,19}} | collective-permute-start | bytes 1572872 | tf_op jit(solution)/shard_map/ppermute | solution.py:264
  110.3 22.6 %collective-permute-start.15 = (bf16[2048,128]{1,0:T(8,128)(2,1)S(1)}, bf16[2048,128]{1,0:T(8,128)(2,1)S(1)}, u32[]{:S(2)}, u32[]{:S(2)}) collective-permute-start(bf16[2048,128]{1,0:T(8,128)(2,1)S(1)} %collective-permute-done.12), channel_id=1, source_target_pairs={{8,12},{9,13},{10,14},{11,15},{24,28},{25,29},{26,30},{27,31}} | collective-permute-start | bytes 1572872 | tf_op jit(solution)/shard_map/ppermute | solution.py:264
  135.7 1.6 collective-permute-start.17
  135.8 21.1 %collective-permute-start.21 = (bf16[4,128,512]{2,1,0:T(8,128)(2,1)S(1)}, bf16[4,128,512]{2,1,0:T(8,128)(2,1)S(1)}, u32[]{:S(2)}, u32[]{:S(2)}) collective-permute-start(bf16[4,128,512]{2,1,0:T(8,128)(2,1)S(1)} %shard_map.68), channel_id=1, source_target_pairs={{0,2},{1,3},{2,0},{3,1},{4,6},{5,7},{6,4},{7,5},{8,10},{9,11},{10,... | collective-permute-start | bytes 1572872 | tf_op jit(solution)/shard_map/ppermute | solution.py:259
  137.4 31.5 %collective-permute-start.18 = (bf16[4,128,512]{2,1,0:T(8,128)(2,1)S(1)}, bf16[4,128,512]{2,1,0:T(8,128)(2,1)S(1)}, u32[]{:S(2)}, u32[]{:S(2)}) collective-permute-start(bf16[4,128,512]{2,1,0:T(8,128)(2,1)S(1)} %pad_maximum_fusion.5), channel_id=1, source_target_pairs={{0,2},{1,3},{2,0},{3,1},{4,6},{5,7},{6,4},{7,5},{8,10},{9,11},{10,... | collective-permute-start | bytes 1572872 | tf_op jit(solution)/shard_map/ppermute | solution.py:259
  141.6 15.4 %collective-permute-start.20 = (bf16[2,128,512]{2,1,0:T(8,128)(2,1)S(1)}, bf16[2,128,512]{2,1,0:T(8,128)(2,1)S(1)}, u32[]{:S(2)}, u32[]{:S(2)}) collective-permute-start(bf16[2,128,512]{2,1,0:T(8,128)(2,1)S(1)} %slice.69), channel_id=1, source_target_pairs={{0,1},{1,0},{2,3},{3,2},{4,5},{5,4},{6,7},{7,6},{8,9},{9,8},{10,11... | collective-permute-start | bytes 786440 | tf_op jit(solution)/shard_map/ppermute | solution.py:254
  144.4 12.6 %collective-permute-start.19 = (bf16[2,128,512]{2,1,0:T(8,128)(2,1)S(1)}, bf16[2,128,512]{2,1,0:T(8,128)(2,1)S(1)}, u32[]{:S(2)}, u32[]{:S(2)}) collective-permute-start(bf16[2,128,512]{2,1,0:T(8,128)(2,1)S(1)} %slice.68), channel_id=1, source_target_pairs={{0,1},{1,0},{2,3},{3,2},{4,5},{5,4},{6,7},{7,6},{8,9},{9,8},{10,11... | collective-permute-start | bytes 786440 | tf_op jit(solution)/shard_map/ppermute | solution.py:254
  156.9 1.6 collective-permute-start.22
  169.0 6.0 %copy-start.1 = (bf16[128,4096]{1,0:T(8,128)(2,1)S(1)}, bf16[128,4096]{1,0:T(8,128)(2,1)}, u32[]{:S(2)}) copy-start(bf16[128,4096]{1,0:T(8,128)(2,1)} %param.10) | copy-start | bytes 3145732
Sparse Core Ops, SparseCore 0:
  8.9 48.6 all-gather.2
  59.5 95.2 all-gather.4

commit v14 on v13

--- a/solution.py
+++ b/solution.py
@@ -358,24 +358,19 @@
         late.append([piece])
         out = attention(*asks[0], head, late[head], (last,), n_chip, states[head][0])
         tie = [out]
-        if head + 1 == KVH // 2:
-            out = jnp.concatenate([out[:2], swap_core(out[2:])], 0)
+        out = jnp.concatenate([out[:2], swap_core(out[2:])], 0)
         across.append(swap_side(out))
-    def even_and_odd(array):
-        return [array, swap_core(array[2:])]
-
     parts = []
     for head in range(KVH // 2):
         state = [after(array, *tie) for array in states[head][1]]
         near = attention(*asks[1], head, late[head], (last,), n_chip, state)
         parts += [near, swap_core(near[2:])]
-    for array in across[:-1]:
-        parts += even_and_odd(array)
-    groups = [(other, kv) for other in (0, 1) for kv in range(KVH // 2)]
-    sums = project(order_of_rows, where, lay_out(parts), groups[:-1], gathered)
-    arrived = after(across[-1], sums)
-    rows = lay_out([arrived[:2], arrived[2:]])
-    return project(order_of_rows, where, rows, groups[-1:], gathered, sums)
+    own = [(0, kv) for kv in range(KVH // 2)]
+    other = [(1, kv) for kv in range(KVH // 2)]
+    sums = project(order_of_rows, where, lay_out(parts), own, gathered)
+    arrived = [after(array, sums) for array in across]
+    rows = lay_out([blocks for array in arrived for blocks in (array[:2], array[2:])])
+    return project(order_of_rows, where, rows, other, gathered, sums)
 
 
 def solution(mesh):

time: 182 us -> 184 us (1.011)
  waiting for transfers between devices: 82.4 us -> 84.3 us
    all_gather x1, waiting for transfers between devices: 0.02 us -> 6.4 us  [body(): gathered = lax.all_gather(gathered, PLANE, axis=0, tiled=True)]
    ppermute x5, waiting for transfers between devices: 40.9 us -> 35.7 us  [swap_side(): lax.ppermute(array, SEQ, [(index(o, s, c), index(o, 1 - s, c)) for o, s,...]
  transfers between devices with their start and end apart: 25 -> 25, of which waited for: 12 -> 14; matrix products, arithmetic and copies ran while one was open for 5% -> 5% of each run, Pallas kernels for 20% -> 19%
where the time goes in v14:
time: 184 us; the launch traced here: 183 us
  waiting for transfers between devices  84.3 us (46%)
  Pallas kernels  43 us (23%)
  starting transfers between devices  30 us (16%)
  between operations  13.8 us (8%)
  local copies, waits for them, and re-layouts  8.95 us (5%)
  other arithmetic  3.07 us (2%)
    ppermute x5, waiting for transfers between devices, swap_side(): lax.ppermute(array, SEQ, [(index(o, s, c), index(o, 1 - s, c)) for o, s,...  35.7 us
    ppermute x12, waiting for transfers between devices, move(): lax.ppermute(array, SEQ, [(index(o, s, c), index(o + way, s, c)) for o, s...  33.2 us
    pallas_call x8, Pallas kernels, attention(): pl.pallas_call(functools.partial(attention_kernel, n_chip, slots, not sta...  26.8 us
    ppermute x12, starting transfers between devices, move(): lax.ppermute(array, SEQ, [(index(o, s, c), index(o + way, s, c)) for o, s...  21.2 us
    pallas_call x2, Pallas kernels, project(): pl.pallas_call(functools.partial(project_kernel, n_outer, groups, steps),...  16 us
    ppermute x5, starting transfers between devices, swap_side(): lax.ppermute(array, SEQ, [(index(o, s, c), index(o, 1 - s, c)) for o, s,...  6.75 us
    all_gather x1, waiting for transfers between devices, body(): gathered = lax.all_gather(gathered, PLANE, axis=0, tiled=True)  6.4 us
    all_gather x1, waiting for transfers between devices, body(): gathered = lax.all_gather(columns, LINE, axis=0, tiled=True)  5.94 us
  transfers between devices with their start and end apart: 25, of which 14 were waited for; matrix products, arithmetic and copies ran while one was open for 5% of the time, Pallas kernels for 19%

profile of v14, /device:TPU:0, one launch (start us, length us, event | category | flops | bytes accessed | tf_op | source)
XLA Modules:
  0.0 183.2 jit_solution(8593425292642501515)
XLA Ops:
  6.5 1.2 copy-done
  7.8 0.8 constant_dynamic-slice_fusion.1
  8.7 2.7 %fusion.2 = (bf16[2,1,128,2048]{3,2,1,0:T(8,128)(2,1)S(1)}, bf16[2,128,2048]{2,1,0:T(8,128)(2,1)}) fusion(bf16[2,2,128,2048]{3,2,1,0:T(8,128)(2,1)} %bitcast.16), kind=kLoop, calls=%fused_computation.31 | loop fusion | bytes 4194304 | tf_op jit(solution)/shard_map/slice | solution.py:316
  11.4 0.5 collective-permute-start.2
  11.8 1.1 constant_dynamic-slice_fusion.4
  13.0 0.9 pad_maximum_fusion.3
  13.8 2.5 %collective-permute-start.4 = (bf16[1024,256]{1,0:T(8,128)(2,1)}, bf16[1024,256]{1,0:T(8,128)(2,1)}, u32[]{:S(2)}, u32[]{:S(2)}) collective-permute-start(bf16[1024,256]{1,0:T(8,128)(2,1)} %pad_maximum_fusion.3), channel_id=1, source_target_pairs={{0,2},{1,3},{2,0},{3,1},{4,6},{5,7},{6,4},{7,5},{8,10},{9,11},{10,... | collective-permute-start | bytes 1572872 | tf_op jit(solution)/shard_map/ppermute | solution.py:259
  16.3 0.9 dynamic-slice_bitcast_fusion
  17.2 0.9 constant_dynamic-slice_fusion
  18.1 0.1 pad_maximum_fusion
  18.2 0.1 collective-permute-start.3
  18.3 0.3 collective-permute-start
  18.6 0.9 collective-permute-done
  19.6 2.0 %collective-permute-start.1 = (s32[4,8]{1,0:T(4,128)S(1)}, s32[4,8]{1,0:T(4,128)S(1)}, u32[]{:S(2)}, u32[]{:S(2)}) collective-permute-start(s32[4,8]{1,0:T(4,128)S(1)} %pad_add_fusion.table_ref), channel_id=1, source_target_pairs={{0,2},{1,3},{2,0},{3,1},{4,6},{5,7},{6,4},{7,5},{8,10},{9,11},{10,... | collective-permute-start | bytes 392 | tf_op jit(solution)/shard_map/ppermute | solution.py:259
  21.6 7.9 %collective-permute-done.4 = bf16[1024,256]{1,0:T(8,128)(2,1)} collective-permute-done((bf16[1024,256]{1,0:T(8,128)(2,1)}, bf16[1024,256]{1,0:T(8,128)(2,1)}, u32[]{:S(2)}, u32[]{:S(2)}) %collective-permute-start.4) | collective-permute-done | bytes 524320 | tf_op jit(solution)/shard_map/ppermute | solution.py:259
  29.4 1.1 fusion.7
  30.6 21.1 %collective-permute-done.1.table_ref = s32[4,8]{1,0:T(4,128)S(1)} collective-permute-done((s32[4,8]{1,0:T(4,128)S(1)}, s32[4,8]{1,0:T(4,128)S(1)}, u32[]{:S(2)}, u32[]{:S(2)}) %collective-permute-start.1) | collective-permute-done | bytes 160 | tf_op jit(solution)/shard_map/ppermute | solution.py:259
  51.7 5.9 %all-gather.3.cloned.1.call-done = bf16[512,2048]{1,0:T(8,128)(2,1)} async-done(((bf16[128,2048]{1,0:T(8,128)(2,1)}), bf16[512,2048]{1,0:T(8,128)(2,1)}) %all-gather.3.cloned.1.call-update) | async-done | bytes 2097168 | tf_op jit(solution)/shard_map/all_gather | solution.py:306
  57.6 1.3 collective-permute-start.10
  58.9 5.4 %collective-permute-start.9 = (bf16[2048,128]{1,0:T(8,128)(2,1)S(1)}, bf16[2048,128]{1,0:T(8,128)(2,1)}, u32[]{:S(2)}, u32[]{:S(2)}) collective-permute-start(bf16[2048,128]{1,0:T(8,128)(2,1)S(1)} %fusion.refs_0_), channel_id=1, source_target_pairs={{0,4},{1,5},{2,6},{3,7},{4,8},{5,9},{6,10},{7,11},{8,12},{9,13},{1... | collective-permute-start | bytes 1572872 | tf_op jit(solution)/shard_map/ppermute | solution.py:264
  64.3 1.3 collective-permute-start.5
  65.6 5.4 %collective-permute-start.7 = (bf16[2048,128]{1,0:T(8,128)(2,1)S(1)}, bf16[2048,128]{1,0:T(8,128)(2,1)}, u32[]{:S(2)}, u32[]{:S(2)}) collective-permute-start(bf16[2048,128]{1,0:T(8,128)(2,1)S(1)} %pad_maximum_fusion.4.refs_0_), channel_id=1, source_target_pairs={{0,4},{1,5},{2,6},{3,7},{4,8},{5,9},{6,10},{7,11},{8,12},{9,13},{1... | collective-permute-start | bytes 1572872 | tf_op jit(solution)/shard_map/ppermute | solution.py:264
  70.9 0.1 pad_add_fusion.3
  71.0 0.1 pad_add_fusion.1.where_ref
  71.1 1.3 pad_maximum_fusion.1.q_ref
  72.4 1.9 %collective-permute-done.10 = bf16[2048,128]{1,0:T(8,128)(2,1)S(1)} collective-permute-done((bf16[2048,128]{1,0:T(8,128)(2,1)S(1)}, bf16[2048,128]{1,0:T(8,128)(2,1)S(1)}, u32[]{:S(2)}, u32[]{:S(2)}) %collective-permute-start.10) | collective-permute-done | bytes 524320 | tf_op jit(solution)/shard_map/ppermute | solution.py:264
  74.3 1.5 collective-permute-done.9
  75.8 1.3 collective-permute-start.12
  77.1 0.7 collective-permute-start.11
  77.8 7.7 %collective-permute-done.5 = bf16[2048,128]{1,0:T(8,128)(2,1)S(1)} collective-permute-done((bf16[2048,128]{1,0:T(8,128)(2,1)S(1)}, bf16[2048,128]{1,0:T(8,128)(2,1)S(1)}, u32[]{:S(2)}, u32[]{:S(2)}) %collective-permute-start.5) | collective-permute-done | bytes 524320 | tf_op jit(solution)/shard_map/ppermute | solution.py:264
  85.6 1.3 collective-permute-start.6
  86.9 0.7 collective-permute-start.8
  87.7 9.1 %collective-permute-done.12 = bf16[2048,128]{1,0:T(8,128)(2,1)S(1)} collective-permute-done((bf16[2048,128]{1,0:T(8,128)(2,1)S(1)}, bf16[2048,128]{1,0:T(8,128)(2,1)S(1)}, u32[]{:S(2)}, u32[]{:S(2)}) %collective-permute-start.12) | collective-permute-done | bytes 524320 | tf_op jit(solution)/shard_map/ppermute | solution.py:264
  96.8 10.1 %collective-permute-done.6 = bf16[2048,128]{1,0:T(8,128)(2,1)S(1)} collective-permute-done((bf16[2048,128]{1,0:T(8,128)(2,1)S(1)}, bf16[2048,128]{1,0:T(8,128)(2,1)S(1)}, u32[]{:S(2)}, u32[]{:S(2)}) %collective-permute-start.6) | collective-permute-done | bytes 524320 | tf_op jit(solution)/shard_map/ppermute | solution.py:264
  106.9 1.3 collective-permute-start.14
  108.2 0.7 collective-permute-start.13
  108.9 0.1 select_select_fusion.2.refs_2_
  109.0 1.3 collective-permute-start.18
  110.3 0.7 collective-permute-start.17
  111.0 0.1 select_select_fusion.3.refs_2_
  111.1 4.0 %shard_map.67 = (f32[4,128,512]{2,1,0:T(8,128)S(1)}, f32[4,128,512]{2,1,0:T(8,128)S(1)}, f32[4,128,512]{2,1,0:T(8,128)S(1)}) custom-call(s32[4]{0:T(128)S(1)} %pad_add_fusion.1.where_ref, s32[4,4]{1,0:T(4,128)S(1)} %copy-done.2, s32[4,8]{1,0:T(4,128)S(1)} %pad_add_fusion.table_ref, bf16[4,128,1024]{2,1,0:T(8,128)(2,1)S(1)} %pad_maximum_fusion.1.q_ref, ...), custom_call_target="tpu_custom_call" | custom-call | flops 1 | bytes 1 | tf_op jit(solution)/shard_map/pallas_call | solution.py:119
  115.1 4.0 %shard_map.65 = (f32[4,128,512]{2,1,0:T(8,128)S(1)}, f32[4,128,512]{2,1,0:T(8,128)S(1)}, f32[4,128,512]{2,1,0:T(8,128)S(1)}) custom-call(s32[4]{0:T(128)S(1)} %pad_add_fusion.1.where_ref, s32[4,4]{1,0:T(4,128)S(1)} %copy-done.2, s32[4,8]{1,0:T(4,128)S(1)} %pad_add_fusion.table_ref, bf16[4,128,1024]{2,1,0:T(8,128)(2,1)S(1)} %pad_maximum_fusion.1.q_ref, ...), custom_call_target="tpu_custom_call" | custom-call | flops 1 | bytes 1 | tf_op jit(solution)/shard_map/pallas_call | solution.py:119
  119.1 4.0 %shard_map.66 = (f32[4,128,512]{2,1,0:T(8,128)S(1)}, f32[4,128,512]{2,1,0:T(8,128)S(1)}, f32[4,128,512]{2,1,0:T(8,128)S(1)}) custom-call(s32[4]{0:T(128)S(1)} %get-tuple-element.87.where_ref, s32[4,4]{1,0:T(4,128)S(1)} %copy-done.2, s32[4,8]{1,0:T(4,128)S(1)} %collective-permute-done.1.table_ref, bf16[4,128,1024]{2,1,0:T(8,128)(2,1)S(1)} %collective-permute-done.3.q_ref, ...), custom_call_target="tpu_custom_call" | custom-call | flops 1 | bytes 1 | tf_op jit(solution)/shard_map/pallas_call | solution.py:119
  123.2 4.0 %shard_map.64 = (f32[4,128,512]{2,1,0:T(8,128)S(1)}, f32[4,128,512]{2,1,0:T(8,128)S(1)}, f32[4,128,512]{2,1,0:T(8,128)S(1)}) custom-call(s32[4]{0:T(128)S(1)} %get-tuple-element.87.where_ref, s32[4,4]{1,0:T(4,128)S(1)} %copy-done.2, s32[4,8]{1,0:T(4,128)S(1)} %collective-permute-done.1.table_ref, bf16[4,128,1024]{2,1,0:T(8,128)(2,1)S(1)} %collective-permute-done.3.q_ref, ...), custom_call_target="tpu_custom_call" | custom-call | flops 1 | bytes 1 | tf_op jit(solution)/shard_map/pallas_call | solution.py:119
  127.2 0.1 select_select_fusion.1.refs_0_
  127.3 2.7 %shard_map.68 = bf16[4,128,512]{2,1,0:T(8,128)(2,1)S(1)} custom-call(s32[4]{0:T(128)S(1)} %get-tuple-element.87.where_ref, s32[4,4]{1,0:T(4,128)S(1)} %copy-done.2, s32[4,8]{1,0:T(4,128)S(1)} %collective-permute-done.1.table_ref, bf16[4,128,1024]{2,1,0:T(8,128)(2,1)S(1)} %collective-permute-done.3.q_ref, bf16[2048,128]{1,0:T(8,128)(2,1)S(1)} %select_select_fusion.1.refs_0_, ...), custom_call_target="tpu_custom_call" | custom-call | flops 1 | bytes 1 | tf_op jit(solution)/shard_map/pallas_call | solution.py:119
  130.0 2.9 %collective-permute-done.18 = bf16[2048,128]{1,0:T(8,128)(2,1)S(1)} collective-permute-done((bf16[2048,128]{1,0:T(8,128)(2,1)S(1)}, bf16[2048,128]{1,0:T(8,128)(2,1)S(1)}, u32[]{:S(2)}, u32[]{:S(2)}) %collective-permute-start.18) | collective-permute-done | bytes 524320 | tf_op jit(solution)/shard_map/ppermute | solution.py:264
  132.9 0.1 select_select_fusion.refs_0_
  133.0 2.7 %shard_map.69 = bf16[4,128,512]{2,1,0:T(8,128)(2,1)S(1)} custom-call(s32[4]{0:T(128)S(1)} %get-tuple-element.87.where_ref, s32[4,4]{1,0:T(4,128)S(1)} %copy-done.2, s32[4,8]{1,0:T(4,128)S(1)} %collective-permute-done.1.table_ref, bf16[4,128,1024]{2,1,0:T(8,128)(2,1)S(1)} %collective-permute-done.3.q_ref, bf16[2048,128]{1,0:T(8,128)(2,1)S(1)} %select_select_fusion.refs_0_, ...), custom_call_target="tpu_custom_call" | custom-call | flops 1 | bytes 1 | tf_op jit(solution)/shard_map/pallas_call | solution.py:119
  135.7 0.1 collective-permute-start.21
  135.9 0.6 collective-permute-start.15
  136.4 0.9 collective-permute-done.21
  137.4 1.5 collective-permute-start.22
  139.0 0.6 collective-permute-start.16
  139.6 2.7 %shard_map.71.refs_2_ = bf16[4,128,512]{2,1,0:T(8,128)(2,1)S(1)} custom-call(s32[4]{0:T(128)S(1)} %pad_add_fusion.1.where_ref, s32[4,4]{1,0:T(4,128)S(1)} %copy-done.2, s32[4,8]{1,0:T(4,128)S(1)} %pad_add_fusion.table_ref, bf16[4,128,1024]{2,1,0:T(8,128)(2,1)S(1)} %pad_maximum_fusion.1.q_ref, bf16[2048,128]{1,0:T(8,128)(2,1)S(1)} %select_select_fusion.refs_0_, ...), custom_call_target="tpu_custom_call" | custom-call | flops 1 | bytes 1 | tf_op jit(solution)/shard_map/pallas_call | solution.py:119
  142.4 2.7 %shard_map.70.refs_0_ = bf16[4,128,512]{2,1,0:T(8,128)(2,1)S(1)} custom-call(s32[4]{0:T(128)S(1)} %pad_add_fusion.1.where_ref, s32[4,4]{1,0:T(4,128)S(1)} %copy-done.2, s32[4,8]{1,0:T(4,128)S(1)} %pad_add_fusion.table_ref, bf16[4,128,1024]{2,1,0:T(8,128)(2,1)S(1)} %pad_maximum_fusion.1.q_ref, bf16[2048,128]{1,0:T(8,128)(2,1)S(1)} %select_select_fusion.1.refs_0_, ...), custom_call_target="tpu_custom_call" | custom-call | flops 1 | bytes 1 | tf_op jit(solution)/shard_map/pallas_call | solution.py:119
  145.1 0.6 collective-permute-start.19
  145.7 1.2 collective-permute-done.19.refs_1_
  146.8 0.1 shard_map.72.rows_ref
  146.9 6.4 %all-gather.5.cloned.1.call-done = bf16[4096,2048]{1,0:T(8,128)(2,1)} async-done(((bf16[512,2048]{1,0:T(8,128)(2,1)}), bf16[4096,2048]{1,0:T(8,128)(2,1)}) %all-gather.5.cloned.1.call-update) | async-done | bytes 16777232 | tf_op jit(solution)/shard_map/all_gather | solution.py:330
  153.3 7.9 %shard_map.73.refs_0_ = f32[512,4096]{1,0:T(8,128)S(1)} custom-call(s32[4]{0:T(128)S(1)} %pad_add_fusion.1.where_ref, bf16[512,1024]{1,0:T(8,128)(2,1)S(1)} %shard_map.72.rows_ref, bf16[2,2048,2048]{2,1,0:T(8,128)(2,1)} %bitcast.14), custom_call_target="tpu_custom_call" | custom-call | flops 1 | bytes 1 | tf_op jit(solution)/shard_map/pallas_call | solution.py:210
  161.2 6.8 %collective-permute-done.16 = bf16[4,128,512]{2,1,0:T(8,128)(2,1)S(1)} collective-permute-done((bf16[4,128,512]{2,1,0:T(8,128)(2,1)S(1)}, bf16[4,128,512]{2,1,0:T(8,128)(2,1)S(1)}, u32[]{:S(2)}, u32[]{:S(2)}) %collective-permute-start.16) | collective-permute-done | bytes 524320 | tf_op jit(solution)/shard_map/ppermute | solution.py:259
  168.0 0.1 shard_map.74.rows_ref
  168.1 8.2 %shard_map.75 = bf16[512,4096]{1,0:T(8,128)(2,1)} custom-call(s32[4]{0:T(128)S(1)} %pad_add_fusion.1.where_ref, bf16[512,1024]{1,0:T(8,128)(2,1)S(1)} %shard_map.74.rows_ref, bf16[2,2048,2048]{2,1,0:T(8,128)(2,1)} %bitcast.15, f32[512,4096]{1,0:T(8,128)S(1)} %shard_map.73.refs_0_), custom_call_target="tpu_custom_call" | custom-call | flops 1 | bytes 1 | tf_op jit(solution)/shard_map/pallas_call | solution.py:210
  (41 shorter events, 0.8 us)
Async XLA Ops:
  6.5 1.2 copy-start
  6.5 5.3 %copy-start.3 = (bf16[512,512]{1,0:T(8,128)(2,1)S(1)}, bf16[512,512]{1,0:T(8,128)(2,1)}, u32[]{:S(2)}) copy-start(bf16[512,512]{1,0:T(8,128)(2,1)} %param.8) | copy-start | bytes 1572868
  6.5 51.1 %all-gather.3.cloned.1.call-start = ((), (), s32[]{:S(2)}) async-start(), calls=%async_computation | async-start | bytes 2621440 | tf_op jit(solution)/shard_map/all_gather | solution.py:306
  8.6 144.7 %all-gather.5.cloned.1.call-start = ((), (), s32[]{:S(2)}) async-start(), calls=%async_computation.1 | async-start | bytes 18874368 | tf_op jit(solution)/shard_map/all_gather | solution.py:330
  11.4 5.9 %collective-permute-start.2 = (bf16[2,128,2048]{2,1,0:T(8,128)(2,1)}, bf16[2,128,2048]{2,1,0:T(8,128)(2,1)S(1)}, u32[]{:S(2)}, u32[]{:S(2)}) collective-permute-start(bf16[2,128,2048]{2,1,0:T(8,128)(2,1)} %get-tuple-element.90), channel_id=1, source_target_pairs={{0,1},{1,0},{2,3},{3,2},{4,5},{5,4},{6,7},{7,6},{8,9},{9,8},{10,11... | collective-permute-start | bytes 3145736 | tf_op jit(solution)/shard_map/ppermute | solution.py:254
  12.9 5.3 %copy-start.4 = (s32[4,8]{1,0:T(4,128)S(1)}, s32[4,8]{1,0:T(4,128)}, u32[]{:S(2)}) copy-start(s32[4,8]{1,0:T(4,128)} %param.9) | copy-start | bytes 388
  13.8 15.6 %collective-permute-start.4 = (bf16[1024,256]{1,0:T(8,128)(2,1)}, bf16[1024,256]{1,0:T(8,128)(2,1)}, u32[]{:S(2)}, u32[]{:S(2)}) collective-permute-start(bf16[1024,256]{1,0:T(8,128)(2,1)} %pad_maximum_fusion.3), channel_id=1, source_target_pairs={{0,2},{1,3},{2,0},{3,1},{4,6},{5,7},{6,4},{7,5},{8,10},{9,11},{10,... | collective-permute-start | bytes 1572872 | tf_op jit(solution)/shard_map/ppermute | solution.py:259
  18.2 33.5 %collective-permute-start.3 = (bf16[4,128,1024]{2,1,0:T(8,128)(2,1)S(1)}, bf16[4,128,1024]{2,1,0:T(8,128)(2,1)S(1)}, u32[]{:S(2)}, u32[]{:S(2)}) collective-permute-start(bf16[4,128,1024]{2,1,0:T(8,128)(2,1)S(1)} %pad_maximum_fusion), channel_id=1, source_target_pairs={{0,2},{1,3},{2,0},{3,1},{4,6},{5,7},{6,4},{7,5},{8,10},{9,11},{10,... | collective-permute-start | bytes 3145736 | tf_op jit(solution)/shard_map/ppermute | solution.py:259
  18.3 1.2 collective-permute-start
  19.6 32.1 %collective-permute-start.1 = (s32[4,8]{1,0:T(4,128)S(1)}, s32[4,8]{1,0:T(4,128)S(1)}, u32[]{:S(2)}, u32[]{:S(2)}) collective-permute-start(s32[4,8]{1,0:T(4,128)S(1)} %pad_add_fusion.table_ref), channel_id=1, source_target_pairs={{0,2},{1,3},{2,0},{3,1},{4,6},{5,7},{6,4},{7,5},{8,10},{9,11},{10,... | collective-permute-start | bytes 392 | tf_op jit(solution)/shard_map/ppermute | solution.py:259
  57.6 16.7 %collective-permute-start.10 = (bf16[2048,128]{1,0:T(8,128)(2,1)S(1)}, bf16[2048,128]{1,0:T(8,128)(2,1)S(1)}, u32[]{:S(2)}, u32[]{:S(2)}) collective-permute-start(bf16[2048,128]{1,0:T(8,128)(2,1)S(1)} %fusion.refs_0_), channel_id=1, source_target_pairs={{4,0},{5,1},{6,2},{7,3},{8,4},{9,5},{10,6},{11,7},{12,8},{13,9},{1... | collective-permute-start | bytes 1572872 | tf_op jit(solution)/shard_map/ppermute | solution.py:264
  58.9 16.9 %collective-permute-start.9 = (bf16[2048,128]{1,0:T(8,128)(2,1)S(1)}, bf16[2048,128]{1,0:T(8,128)(2,1)}, u32[]{:S(2)}, u32[]{:S(2)}) collective-permute-start(bf16[2048,128]{1,0:T(8,128)(2,1)S(1)} %fusion.refs_0_), channel_id=1, source_target_pairs={{0,4},{1,5},{2,6},{3,7},{4,8},{5,9},{6,10},{7,11},{8,12},{9,13},{1... | collective-permute-start | bytes 1572872 | tf_op jit(solution)/shard_map/ppermute | solution.py:264
  64.3 21.3 %collective-permute-start.5 = (bf16[2048,128]{1,0:T(8,128)(2,1)S(1)}, bf16[2048,128]{1,0:T(8,128)(2,1)S(1)}, u32[]{:S(2)}, u32[]{:S(2)}) collective-permute-start(bf16[2048,128]{1,0:T(8,128)(2,1)S(1)} %pad_maximum_fusion.4.refs_0_), channel_id=1, source_target_pairs={{4,0},{5,1},{6,2},{7,3},{8,4},{9,5},{10,6},{11,7},{12,8},{13,9},{1... | collective-permute-start | bytes 1572872 | tf_op jit(solution)/shard_map/ppermute | solution.py:264
  65.6 21.3 %collective-permute-start.7 = (bf16[2048,128]{1,0:T(8,128)(2,1)S(1)}, bf16[2048,128]{1,0:T(8,128)(2,1)}, u32[]{:S(2)}, u32[]{:S(2)}) collective-permute-start(bf16[2048,128]{1,0:T(8,128)(2,1)S(1)} %pad_maximum_fusion.4.refs_0_), channel_id=1, source_target_pairs={{0,4},{1,5},{2,6},{3,7},{4,8},{5,9},{6,10},{7,11},{8,12},{9,13},{1... | collective-permute-start | bytes 1572872 | tf_op jit(solution)/shard_map/ppermute | solution.py:264
  72.4 38.7 %copy-start.2 = (s32[4,4]{1,0:T(4,128)S(1)}, s32[4,4]{1,0:T(4,128)}, u32[]{:S(2)}) copy-start(s32[4,4]{1,0:T(4,128)} %constant.37.clone.order_ref) | copy-start | bytes 196
  75.8 21.0 %collective-permute-start.12 = (bf16[2048,128]{1,0:T(8,128)(2,1)S(1)}, bf16[2048,128]{1,0:T(8,128)(2,1)S(1)}, u32[]{:S(2)}, u32[]{:S(2)}) collective-permute-start(bf16[2048,128]{1,0:T(8,128)(2,1)S(1)} %collective-permute-done.10), channel_id=1, source_target_pairs={{4,0},{5,1},{6,2},{7,3},{8,4},{9,5},{10,6},{11,7},{20,16},{21,17},... | collective-permute-start | bytes 1572872 | tf_op jit(solution)/shard_map/ppermute | solution.py:264
  77.1 19.7 %collective-permute-start.11 = (bf16[2048,128]{1,0:T(8,128)(2,1)}, bf16[2048,128]{1,0:T(8,128)(2,1)S(1)}, u32[]{:S(2)}, u32[]{:S(2)}) collective-permute-start(bf16[2048,128]{1,0:T(8,128)(2,1)} %collective-permute-done.9), channel_id=1, source_target_pairs={{4,8},{5,9},{6,10},{7,11},{8,12},{9,13},{10,14},{11,15},{20,24},{2... | collective-permute-start | bytes 1572872 | tf_op jit(solution)/shard_map/ppermute | solution.py:264
  85.6 21.3 %collective-permute-start.6 = (bf16[2048,128]{1,0:T(8,128)(2,1)S(1)}, bf16[2048,128]{1,0:T(8,128)(2,1)S(1)}, u32[]{:S(2)}, u32[]{:S(2)}) collective-permute-start(bf16[2048,128]{1,0:T(8,128)(2,1)S(1)} %collective-permute-done.5), channel_id=1, source_target_pairs={{4,0},{5,1},{6,2},{7,3},{8,4},{9,5},{10,6},{11,7},{20,16},{21,17},... | collective-permute-start | bytes 1572872 | tf_op jit(solution)/shard_map/ppermute | solution.py:264
  86.9 21.3 %collective-permute-start.8 = (bf16[2048,128]{1,0:T(8,128)(2,1)}, bf16[2048,128]{1,0:T(8,128)(2,1)S(1)}, u32[]{:S(2)}, u32[]{:S(2)}) collective-permute-start(bf16[2048,128]{1,0:T(8,128)(2,1)} %collective-permute-done.7), channel_id=1, source_target_pairs={{4,8},{5,9},{6,10},{7,11},{8,12},{9,13},{10,14},{11,15},{20,24},{2... | collective-permute-start | bytes 1572872 | tf_op jit(solution)/shard_map/ppermute | solution.py:264
  106.9 20.3 %collective-permute-start.14 = (bf16[2048,128]{1,0:T(8,128)(2,1)S(1)}, bf16[2048,128]{1,0:T(8,128)(2,1)S(1)}, u32[]{:S(2)}, u32[]{:S(2)}) collective-permute-start(bf16[2048,128]{1,0:T(8,128)(2,1)S(1)} %collective-permute-done.6), channel_id=1, source_target_pairs={{4,0},{5,1},{6,2},{7,3},{20,16},{21,17},{22,18},{23,19}} | collective-permute-start | bytes 1572872 | tf_op jit(solution)/shard_map/ppermute | solution.py:264
  108.2 19.0 %collective-permute-start.13 = (bf16[2048,128]{1,0:T(8,128)(2,1)S(1)}, bf16[2048,128]{1,0:T(8,128)(2,1)S(1)}, u32[]{:S(2)}, u32[]{:S(2)}) collective-permute-start(bf16[2048,128]{1,0:T(8,128)(2,1)S(1)} %collective-permute-done.8), channel_id=1, source_target_pairs={{8,12},{9,13},{10,14},{11,15},{24,28},{25,29},{26,30},{27,31}} | collective-permute-start | bytes 1572872 | tf_op jit(solution)/shard_map/ppermute | solution.py:264
  109.0 23.9 %collective-permute-start.18 = (bf16[2048,128]{1,0:T(8,128)(2,1)S(1)}, bf16[2048,128]{1,0:T(8,128)(2,1)S(1)}, u32[]{:S(2)}, u32[]{:S(2)}) collective-permute-start(bf16[2048,128]{1,0:T(8,128)(2,1)S(1)} %collective-permute-done.12), channel_id=1, source_target_pairs={{4,0},{5,1},{6,2},{7,3},{20,16},{21,17},{22,18},{23,19}} | collective-permute-start | bytes 1572872 | tf_op jit(solution)/shard_map/ppermute | solution.py:264
  110.3 22.6 %collective-permute-start.17 = (bf16[2048,128]{1,0:T(8,128)(2,1)S(1)}, bf16[2048,128]{1,0:T(8,128)(2,1)S(1)}, u32[]{:S(2)}, u32[]{:S(2)}) collective-permute-start(bf16[2048,128]{1,0:T(8,128)(2,1)S(1)} %collective-permute-done.11), channel_id=1, source_target_pairs={{8,12},{9,13},{10,14},{11,15},{24,28},{25,29},{26,30},{27,31}} | collective-permute-start | bytes 1572872 | tf_op jit(solution)/shard_map/ppermute | solution.py:264
  135.7 1.6 collective-permute-start.21
  135.9 3.1 %collective-permute-start.15 = (bf16[2,128,512]{2,1,0:T(8,128)(2,1)S(1)}, bf16[2,128,512]{2,1,0:T(8,128)(2,1)S(1)}, u32[]{:S(2)}, u32[]{:S(2)}) collective-permute-start(bf16[2,128,512]{2,1,0:T(8,128)(2,1)S(1)} %get-tuple-element.102), channel_id=1, source_target_pairs={{0,1},{1,0},{2,3},{3,2},{4,5},{5,4},{6,7},{7,6},{8,9},{9,8},{10,11... | collective-permute-start | bytes 786440 | tf_op jit(solution)/shard_map/ppermute | solution.py:254
  137.4 23.8 %collective-permute-start.22 = (bf16[4,128,512]{2,1,0:T(8,128)(2,1)S(1)}, bf16[4,128,512]{2,1,0:T(8,128)(2,1)S(1)}, u32[]{:S(2)}, u32[]{:S(2)}) collective-permute-start(bf16[4,128,512]{2,1,0:T(8,128)(2,1)S(1)} %pad_maximum_fusion.6), channel_id=1, source_target_pairs={{0,2},{1,3},{2,0},{3,1},{4,6},{5,7},{6,4},{7,5},{8,10},{9,11},{10,... | collective-permute-start | bytes 1572872 | tf_op jit(solution)/shard_map/ppermute | solution.py:259
  139.0 29.0 %collective-permute-start.16 = (bf16[4,128,512]{2,1,0:T(8,128)(2,1)S(1)}, bf16[4,128,512]{2,1,0:T(8,128)(2,1)S(1)}, u32[]{:S(2)}, u32[]{:S(2)}) collective-permute-start(bf16[4,128,512]{2,1,0:T(8,128)(2,1)S(1)} %pad_maximum_fusion.5), channel_id=1, source_target_pairs={{0,2},{1,3},{2,0},{3,1},{4,6},{5,7},{6,4},{7,5},{8,10},{9,11},{10,... | collective-permute-start | bytes 1572872 | tf_op jit(solution)/shard_map/ppermute | solution.py:259
  142.3 3.4 %collective-permute-start.20 = (bf16[2,128,512]{2,1,0:T(8,128)(2,1)S(1)}, bf16[2,128,512]{2,1,0:T(8,128)(2,1)S(1)}, u32[]{:S(2)}, u32[]{:S(2)}) collective-permute-start(bf16[2,128,512]{2,1,0:T(8,128)(2,1)S(1)} %slice.81), channel_id=1, source_target_pairs={{0,1},{1,0},{2,3},{3,2},{4,5},{5,4},{6,7},{7,6},{8,9},{9,8},{10,11... | collective-permute-start | bytes 786440 | tf_op jit(solution)/shard_map/ppermute | solution.py:254
  145.1 1.7 collective-permute-start.19
  168.1 8.2 %copy-start.1 = (bf16[128,4096]{1,0:T(8,128)(2,1)S(1)}, bf16[128,4096]{1,0:T(8,128)(2,1)}, u32[]{:S(2)}) copy-start(bf16[128,4096]{1,0:T(8,128)(2,1)} %param.10) | copy-start | bytes 3145732
Sparse Core Ops, SparseCore 0:
  8.9 48.6 all-gather.2
  59.5 93.7 all-gather.4

commit v15 on v13

--- a/solution.py
+++ b/solution.py
@@ -358,11 +358,10 @@
         late.append([piece])
         out = attention(*asks[0], head, late[head], (last,), n_chip, states[head][0])
         tie = [out]
-        if head + 1 == KVH // 2:
-            out = jnp.concatenate([out[:2], swap_core(out[2:])], 0)
+        out = jnp.concatenate([out[:2], swap_core(out[2:])], 0)
         across.append(swap_side(out))
     def even_and_odd(array):
-        return [array, swap_core(array[2:])]
+        return [array[:2], array[2:]]
 
     parts = []
     for head in range(KVH // 2):

time: 182 us -> 182 us (level)
    ppermute x12, waiting for transfers between devices: 33.2 us -> 40.2 us  [move(): lax.ppermute(array, SEQ, [(index(o, s, c), index(o + way, s, c)) for o, s...]
    ppermute x5, waiting for transfers between devices: 40.9 us -> 35 us  [swap_side(): lax.ppermute(array, SEQ, [(index(o, s, c), index(o, 1 - s, c)) for o, s,...]
  transfers between devices with their start and end apart: 25 -> 25, of which waited for: 12 -> 12; matrix products, arithmetic and copies ran while one was open for 5% -> 6% of each run, Pallas kernels for 20% -> 20%
where the time goes in v15:
time: 182 us
  waiting for transfers between devices  81.9 us (45%)
  Pallas kernels  43.2 us (24%)
  starting transfers between devices  30.3 us (17%)
  between operations  13.8 us (8%)
  local copies, waits for them, and re-layouts  9.09 us (5%)
  other arithmetic  3.2 us (2%)
    ppermute x12, waiting for transfers between devices, move(): lax.ppermute(array, SEQ, [(index(o, s, c), index(o + way, s, c)) for o, s...  40.2 us
    ppermute x5, waiting for transfers between devices, swap_side(): lax.ppermute(array, SEQ, [(index(o, s, c), index(o, 1 - s, c)) for o, s,...  35 us
    pallas_call x8, Pallas kernels, attention(): pl.pallas_call(functools.partial(attention_kernel, n_chip, slots, not sta...  26.8 us
    ppermute x12, starting transfers between devices, move(): lax.ppermute(array, SEQ, [(index(o, s, c), index(o + way, s, c)) for o, s...  21.2 us
    pallas_call x2, Pallas kernels, project(): pl.pallas_call(functools.partial(project_kernel, n_outer, groups, steps),...  16.2 us
    ppermute x5, starting transfers between devices, swap_side(): lax.ppermute(array, SEQ, [(index(o, s, c), index(o, 1 - s, c)) for o, s,...  7.57 us
    all_gather x1, waiting for transfers between devices, body(): gathered = lax.all_gather(columns, LINE, axis=0, tiled=True)  5.79 us
  transfers between devices with their start and end apart: 25, of which 12 were waited for; matrix products, arithmetic and copies ran while one was open for 6% of the time, Pallas kernels for 20%

profile of v15, /device:TPU:0, one launch (start us, length us, event | category | flops | bytes accessed | tf_op | source)
XLA Modules:
  0.0 181.6 jit_solution(13186121052419190646)
XLA Ops:
  6.5 1.2 copy-done
  7.8 0.8 constant_dynamic-slice_fusion.1
  8.7 2.7 %fusion.2 = (bf16[2,1,128,2048]{3,2,1,0:T(8,128)(2,1)S(1)}, bf16[2,128,2048]{2,1,0:T(8,128)(2,1)}) fusion(bf16[2,2,128,2048]{3,2,1,0:T(8,128)(2,1)} %bitcast.16), kind=kLoop, calls=%fused_computation.31 | loop fusion | bytes 4194304 | tf_op jit(solution)/shard_map/slice | solution.py:316
  11.4 0.5 collective-permute-start.2
  11.8 1.3 constant_dynamic-slice_fusion.4
  13.1 0.9 pad_maximum_fusion.3
  14.0 2.5 %collective-permute-start.4 = (bf16[1024,256]{1,0:T(8,128)(2,1)}, bf16[1024,256]{1,0:T(8,128)(2,1)}, u32[]{:S(2)}, u32[]{:S(2)}) collective-permute-start(bf16[1024,256]{1,0:T(8,128)(2,1)} %pad_maximum_fusion.3), channel_id=1, source_target_pairs={{0,2},{1,3},{2,0},{3,1},{4,6},{5,7},{6,4},{7,5},{8,10},{9,11},{10,... | collective-permute-start | bytes 1572872 | tf_op jit(solution)/shard_map/ppermute | solution.py:259
  16.5 0.9 dynamic-slice_bitcast_fusion
  17.4 0.9 constant_dynamic-slice_fusion
  18.2 0.1 pad_maximum_fusion
  18.3 0.1 collective-permute-start.3
  18.4 0.3 collective-permute-start
  18.8 0.9 collective-permute-done
  19.7 2.0 %collective-permute-start.1 = (s32[4,8]{1,0:T(4,128)S(1)}, s32[4,8]{1,0:T(4,128)S(1)}, u32[]{:S(2)}, u32[]{:S(2)}) collective-permute-start(s32[4,8]{1,0:T(4,128)S(1)} %pad_add_fusion.table_ref), channel_id=1, source_target_pairs={{0,2},{1,3},{2,0},{3,1},{4,6},{5,7},{6,4},{7,5},{8,10},{9,11},{10,... | collective-permute-start | bytes 392 | tf_op jit(solution)/shard_map/ppermute | solution.py:259
  21.7 7.9 %collective-permute-done.4 = bf16[1024,256]{1,0:T(8,128)(2,1)} collective-permute-done((bf16[1024,256]{1,0:T(8,128)(2,1)}, bf16[1024,256]{1,0:T(8,128)(2,1)}, u32[]{:S(2)}, u32[]{:S(2)}) %collective-permute-start.4) | collective-permute-done | bytes 524320 | tf_op jit(solution)/shard_map/ppermute | solution.py:259
  29.6 1.1 fusion.7
  30.7 21.1 %collective-permute-done.1.table_ref = s32[4,8]{1,0:T(4,128)S(1)} collective-permute-done((s32[4,8]{1,0:T(4,128)S(1)}, s32[4,8]{1,0:T(4,128)S(1)}, u32[]{:S(2)}, u32[]{:S(2)}) %collective-permute-start.1) | collective-permute-done | bytes 160 | tf_op jit(solution)/shard_map/ppermute | solution.py:259
  51.8 5.8 %all-gather.3.cloned.1.call-done = bf16[512,2048]{1,0:T(8,128)(2,1)} async-done(((bf16[128,2048]{1,0:T(8,128)(2,1)}), bf16[512,2048]{1,0:T(8,128)(2,1)}) %all-gather.3.cloned.1.call-update) | async-done | bytes 2097168 | tf_op jit(solution)/shard_map/all_gather | solution.py:306
  57.6 1.3 collective-permute-start.5
  58.9 5.4 %collective-permute-start.11 = (bf16[2048,128]{1,0:T(8,128)(2,1)S(1)}, bf16[2048,128]{1,0:T(8,128)(2,1)}, u32[]{:S(2)}, u32[]{:S(2)}) collective-permute-start(bf16[2048,128]{1,0:T(8,128)(2,1)S(1)} %pad_maximum_fusion.4.refs_0_), channel_id=1, source_target_pairs={{0,4},{1,5},{2,6},{3,7},{4,8},{5,9},{6,10},{7,11},{8,12},{9,13},{1... | collective-permute-start | bytes 1572872 | tf_op jit(solution)/shard_map/ppermute | solution.py:264
  64.3 1.3 collective-permute-start.7
  65.6 5.3 %collective-permute-start.9 = (bf16[2048,128]{1,0:T(8,128)(2,1)S(1)}, bf16[2048,128]{1,0:T(8,128)(2,1)}, u32[]{:S(2)}, u32[]{:S(2)}) collective-permute-start(bf16[2048,128]{1,0:T(8,128)(2,1)S(1)} %fusion.refs_0_), channel_id=1, source_target_pairs={{0,4},{1,5},{2,6},{3,7},{4,8},{5,9},{6,10},{7,11},{8,12},{9,13},{1... | collective-permute-start | bytes 1572872 | tf_op jit(solution)/shard_map/ppermute | solution.py:264
  70.9 0.1 pad_add_fusion.3
  71.0 0.1 pad_add_fusion.1.where_ref
  71.1 1.3 pad_maximum_fusion.1.q_ref
  72.4 2.0 %collective-permute-done.5 = bf16[2048,128]{1,0:T(8,128)(2,1)S(1)} collective-permute-done((bf16[2048,128]{1,0:T(8,128)(2,1)S(1)}, bf16[2048,128]{1,0:T(8,128)(2,1)S(1)}, u32[]{:S(2)}, u32[]{:S(2)}) %collective-permute-start.5) | collective-permute-done | bytes 524320 | tf_op jit(solution)/shard_map/ppermute | solution.py:264
  74.3 1.5 collective-permute-done.11
  75.8 1.3 collective-permute-start.6
  77.1 0.7 collective-permute-start.12
  77.8 7.7 %collective-permute-done.7 = bf16[2048,128]{1,0:T(8,128)(2,1)S(1)} collective-permute-done((bf16[2048,128]{1,0:T(8,128)(2,1)S(1)}, bf16[2048,128]{1,0:T(8,128)(2,1)S(1)}, u32[]{:S(2)}, u32[]{:S(2)}) %collective-permute-start.7) | collective-permute-done | bytes 524320 | tf_op jit(solution)/shard_map/ppermute | solution.py:264
  85.6 1.3 collective-permute-start.8
  86.9 0.7 collective-permute-start.10
  87.6 0.1 broadcast_select_fusion.refs_1_
  87.6 0.1 broadcast_select_fusion.1.refs_1_
  87.7 9.1 %collective-permute-done.6 = bf16[2048,128]{1,0:T(8,128)(2,1)S(1)} collective-permute-done((bf16[2048,128]{1,0:T(8,128)(2,1)S(1)}, bf16[2048,128]{1,0:T(8,128)(2,1)S(1)}, u32[]{:S(2)}, u32[]{:S(2)}) %collective-permute-start.6) | collective-permute-done | bytes 524320 | tf_op jit(solution)/shard_map/ppermute | solution.py:264
  96.8 10.1 %collective-permute-done.8 = bf16[2048,128]{1,0:T(8,128)(2,1)S(1)} collective-permute-done((bf16[2048,128]{1,0:T(8,128)(2,1)S(1)}, bf16[2048,128]{1,0:T(8,128)(2,1)S(1)}, u32[]{:S(2)}, u32[]{:S(2)}) %collective-permute-start.8) | collective-permute-done | bytes 524320 | tf_op jit(solution)/shard_map/ppermute | solution.py:264
  106.9 1.3 collective-permute-start.14
  108.2 0.7 collective-permute-start.13
  108.9 0.1 select_select_fusion.2.refs_2_
  109.0 0.1 select_select_fusion.3.refs_2_
  109.1 4.0 %shard_map.67 = (f32[4,128,512]{2,1,0:T(8,128)S(1)}, f32[4,128,512]{2,1,0:T(8,128)S(1)}, f32[4,128,512]{2,1,0:T(8,128)S(1)}) custom-call(s32[4]{0:T(128)S(1)} %pad_add_fusion.1.where_ref, s32[4,4]{1,0:T(4,128)S(1)} %copy-done.2, s32[4,8]{1,0:T(4,128)S(1)} %pad_add_fusion.table_ref, bf16[4,128,1024]{2,1,0:T(8,128)(2,1)S(1)} %pad_maximum_fusion.1.q_ref, ...), custom_call_target="tpu_custom_call" | custom-call | flops 1 | bytes 1 | tf_op jit(solution)/shard_map/pallas_call | solution.py:119
  113.1 4.0 %shard_map.65 = (f32[4,128,512]{2,1,0:T(8,128)S(1)}, f32[4,128,512]{2,1,0:T(8,128)S(1)}, f32[4,128,512]{2,1,0:T(8,128)S(1)}) custom-call(s32[4]{0:T(128)S(1)} %pad_add_fusion.1.where_ref, s32[4,4]{1,0:T(4,128)S(1)} %copy-done.2, s32[4,8]{1,0:T(4,128)S(1)} %pad_add_fusion.table_ref, bf16[4,128,1024]{2,1,0:T(8,128)(2,1)S(1)} %pad_maximum_fusion.1.q_ref, ...), custom_call_target="tpu_custom_call" | custom-call | flops 1 | bytes 1 | tf_op jit(solution)/shard_map/pallas_call | solution.py:119
  117.2 4.0 %shard_map.66 = (f32[4,128,512]{2,1,0:T(8,128)S(1)}, f32[4,128,512]{2,1,0:T(8,128)S(1)}, f32[4,128,512]{2,1,0:T(8,128)S(1)}) custom-call(s32[4]{0:T(128)S(1)} %get-tuple-element.85.where_ref, s32[4,4]{1,0:T(4,128)S(1)} %copy-done.2, s32[4,8]{1,0:T(4,128)S(1)} %collective-permute-done.1.table_ref, bf16[4,128,1024]{2,1,0:T(8,128)(2,1)S(1)} %collective-permute-done.3.q_ref, ...), custom_call_target="tpu_custom_call" | custom-call | flops 1 | bytes 1 | tf_op jit(solution)/shard_map/pallas_call | solution.py:119
  121.2 4.0 %shard_map.64 = (f32[4,128,512]{2,1,0:T(8,128)S(1)}, f32[4,128,512]{2,1,0:T(8,128)S(1)}, f32[4,128,512]{2,1,0:T(8,128)S(1)}) custom-call(s32[4]{0:T(128)S(1)} %get-tuple-element.85.where_ref, s32[4,4]{1,0:T(4,128)S(1)} %copy-done.2, s32[4,8]{1,0:T(4,128)S(1)} %collective-permute-done.1.table_ref, bf16[4,128,1024]{2,1,0:T(8,128)(2,1)S(1)} %collective-permute-done.3.q_ref, ...), custom_call_target="tpu_custom_call" | custom-call | flops 1 | bytes 1 | tf_op jit(solution)/shard_map/pallas_call | solution.py:119
  125.2 1.3 collective-permute-start.16
  126.5 0.7 collective-permute-start.15
  127.3 0.2 select_select_fusion.1.refs_0_
  127.4 2.7 %shard_map.68 = bf16[4,128,512]{2,1,0:T(8,128)(2,1)S(1)} custom-call(s32[4]{0:T(128)S(1)} %get-tuple-element.85.where_ref, s32[4,4]{1,0:T(4,128)S(1)} %copy-done.2, s32[4,8]{1,0:T(4,128)S(1)} %collective-permute-done.1.table_ref, bf16[4,128,1024]{2,1,0:T(8,128)(2,1)S(1)} %collective-permute-done.3.q_ref, bf16[2048,128]{1,0:T(8,128)(2,1)S(1)} %select_select_fusion.1.refs_0_, ...), custom_call_target="tpu_custom_call" | custom-call | flops 1 | bytes 1 | tf_op jit(solution)/shard_map/pallas_call | solution.py:119
  130.2 0.1 collective-permute-start.21
  130.2 9.8 %collective-permute-done.16 = bf16[2048,128]{1,0:T(8,128)(2,1)S(1)} collective-permute-done((bf16[2048,128]{1,0:T(8,128)(2,1)S(1)}, bf16[2048,128]{1,0:T(8,128)(2,1)S(1)}, u32[]{:S(2)}, u32[]{:S(2)}) %collective-permute-start.16) | collective-permute-done | bytes 524320 | tf_op jit(solution)/shard_map/ppermute | solution.py:264
  140.1 0.1 select_select_fusion.refs_0_
  140.2 2.7 %shard_map.69 = bf16[4,128,512]{2,1,0:T(8,128)(2,1)S(1)} custom-call(s32[4]{0:T(128)S(1)} %get-tuple-element.85.where_ref, s32[4,4]{1,0:T(4,128)S(1)} %copy-done.2, s32[4,8]{1,0:T(4,128)S(1)} %collective-permute-done.1.table_ref, bf16[4,128,1024]{2,1,0:T(8,128)(2,1)S(1)} %collective-permute-done.3.q_ref, bf16[2048,128]{1,0:T(8,128)(2,1)S(1)} %select_select_fusion.refs_0_, ...), custom_call_target="tpu_custom_call" | custom-call | flops 1 | bytes 1 | tf_op jit(solution)/shard_map/pallas_call | solution.py:119
  142.9 0.1 collective-permute-start.17
  143.1 1.5 collective-permute-start.22
  144.6 1.5 collective-permute-start.18
  146.1 2.7 %shard_map.71.refs_2_ = bf16[4,128,512]{2,1,0:T(8,128)(2,1)S(1)} custom-call(s32[4]{0:T(128)S(1)} %pad_add_fusion.1.where_ref, s32[4,4]{1,0:T(4,128)S(1)} %copy-done.2, s32[4,8]{1,0:T(4,128)S(1)} %pad_add_fusion.table_ref, bf16[4,128,1024]{2,1,0:T(8,128)(2,1)S(1)} %pad_maximum_fusion.1.q_ref, bf16[2048,128]{1,0:T(8,128)(2,1)S(1)} %select_select_fusion.refs_0_, ...), custom_call_target="tpu_custom_call" | custom-call | flops 1 | bytes 1 | tf_op jit(solution)/shard_map/pallas_call | solution.py:119
  148.8 0.1 collective-permute-start.20
  148.9 2.7 %shard_map.70.refs_0_ = bf16[4,128,512]{2,1,0:T(8,128)(2,1)S(1)} custom-call(s32[4]{0:T(128)S(1)} %pad_add_fusion.1.where_ref, s32[4,4]{1,0:T(4,128)S(1)} %copy-done.2, s32[4,8]{1,0:T(4,128)S(1)} %pad_add_fusion.table_ref, bf16[4,128,1024]{2,1,0:T(8,128)(2,1)S(1)} %pad_maximum_fusion.1.q_ref, bf16[2048,128]{1,0:T(8,128)(2,1)S(1)} %select_select_fusion.1.refs_0_, ...), custom_call_target="tpu_custom_call" | custom-call | flops 1 | bytes 1 | tf_op jit(solution)/shard_map/pallas_call | solution.py:119
  151.6 0.6 collective-permute-start.19
  152.2 5.7 %collective-permute-done.22 = bf16[4,128,512]{2,1,0:T(8,128)(2,1)S(1)} collective-permute-done((bf16[4,128,512]{2,1,0:T(8,128)(2,1)S(1)}, bf16[4,128,512]{2,1,0:T(8,128)(2,1)S(1)}, u32[]{:S(2)}, u32[]{:S(2)}) %collective-permute-start.22) | collective-permute-done | bytes 524320 | tf_op jit(solution)/shard_map/ppermute | solution.py:259
  157.9 0.1 shard_map.72.rows_ref
  158.0 10.3 %shard_map.73.refs_0_ = f32[512,4096]{1,0:T(8,128)S(1)} custom-call(s32[4]{0:T(128)S(1)} %pad_add_fusion.1.where_ref, bf16[512,1536]{1,0:T(8,128)(2,1)S(1)} %shard_map.72.rows_ref, bf16[2,2048,2048]{2,1,0:T(8,128)(2,1)} %bitcast.14), custom_call_target="tpu_custom_call" | custom-call | flops 1 | bytes 1 | tf_op jit(solution)/shard_map/pallas_call | solution.py:210
  168.3 0.4 collective-permute-done.18
  168.8 5.9 %shard_map.75 = bf16[512,4096]{1,0:T(8,128)(2,1)} custom-call(s32[4]{0:T(128)S(1)} %pad_add_fusion.1.where_ref, bf16[512,512]{1,0:T(8,128)(2,1)S(1)} %shard_map.74.rows_ref, bf16[2,2048,2048]{2,1,0:T(8,128)(2,1)} %bitcast.15, f32[512,4096]{1,0:T(8,128)S(1)} %shard_map.73.refs_0_), custom_call_target="tpu_custom_call" | custom-call | flops 1 | bytes 1 | tf_op jit(solution)/shard_map/pallas_call | solution.py:210
  (39 shorter events, 0.6 us)
Async XLA Ops:
  6.5 1.2 copy-start
  6.5 51.1 %all-gather.3.cloned.1.call-start = ((), (), s32[]{:S(2)}) async-start(), calls=%async_computation | async-start | bytes 2621440 | tf_op jit(solution)/shard_map/all_gather | solution.py:306
  8.6 149.4 %all-gather.5.cloned.1.call-start = ((), (), s32[]{:S(2)}) async-start(), calls=%async_computation.1 | async-start | bytes 18874368 | tf_op jit(solution)/shard_map/all_gather | solution.py:330
  11.4 6.0 %collective-permute-start.2 = (bf16[2,128,2048]{2,1,0:T(8,128)(2,1)}, bf16[2,128,2048]{2,1,0:T(8,128)(2,1)S(1)}, u32[]{:S(2)}, u32[]{:S(2)}) collective-permute-start(bf16[2,128,2048]{2,1,0:T(8,128)(2,1)} %get-tuple-element.88), channel_id=1, source_target_pairs={{0,1},{1,0},{2,3},{3,2},{4,5},{5,4},{6,7},{7,6},{8,9},{9,8},{10,11... | collective-permute-start | bytes 3145736 | tf_op jit(solution)/shard_map/ppermute | solution.py:254
  14.0 15.6 %collective-permute-start.4 = (bf16[1024,256]{1,0:T(8,128)(2,1)}, bf16[1024,256]{1,0:T(8,128)(2,1)}, u32[]{:S(2)}, u32[]{:S(2)}) collective-permute-start(bf16[1024,256]{1,0:T(8,128)(2,1)} %pad_maximum_fusion.3), channel_id=1, source_target_pairs={{0,2},{1,3},{2,0},{3,1},{4,6},{5,7},{6,4},{7,5},{8,10},{9,11},{10,... | collective-permute-start | bytes 1572872 | tf_op jit(solution)/shard_map/ppermute | solution.py:259
  17.4 1.1 copy-start.3
  18.3 33.5 %collective-permute-start.3 = (bf16[4,128,1024]{2,1,0:T(8,128)(2,1)S(1)}, bf16[4,128,1024]{2,1,0:T(8,128)(2,1)S(1)}, u32[]{:S(2)}, u32[]{:S(2)}) collective-permute-start(bf16[4,128,1024]{2,1,0:T(8,128)(2,1)S(1)} %pad_maximum_fusion), channel_id=1, source_target_pairs={{0,2},{1,3},{2,0},{3,1},{4,6},{5,7},{6,4},{7,5},{8,10},{9,11},{10,... | collective-permute-start | bytes 3145736 | tf_op jit(solution)/shard_map/ppermute | solution.py:259
  18.4 1.2 collective-permute-start
  19.7 32.1 %collective-permute-start.1 = (s32[4,8]{1,0:T(4,128)S(1)}, s32[4,8]{1,0:T(4,128)S(1)}, u32[]{:S(2)}, u32[]{:S(2)}) collective-permute-start(s32[4,8]{1,0:T(4,128)S(1)} %pad_add_fusion.table_ref), channel_id=1, source_target_pairs={{0,2},{1,3},{2,0},{3,1},{4,6},{5,7},{6,4},{7,5},{8,10},{9,11},{10,... | collective-permute-start | bytes 392 | tf_op jit(solution)/shard_map/ppermute | solution.py:259
  57.6 16.7 %collective-permute-start.5 = (bf16[2048,128]{1,0:T(8,128)(2,1)S(1)}, bf16[2048,128]{1,0:T(8,128)(2,1)S(1)}, u32[]{:S(2)}, u32[]{:S(2)}) collective-permute-start(bf16[2048,128]{1,0:T(8,128)(2,1)S(1)} %pad_maximum_fusion.4.refs_0_), channel_id=1, source_target_pairs={{4,0},{5,1},{6,2},{7,3},{8,4},{9,5},{10,6},{11,7},{12,8},{13,9},{1... | collective-permute-start | bytes 1572872 | tf_op jit(solution)/shard_map/ppermute | solution.py:264
  58.9 16.9 %collective-permute-start.11 = (bf16[2048,128]{1,0:T(8,128)(2,1)S(1)}, bf16[2048,128]{1,0:T(8,128)(2,1)}, u32[]{:S(2)}, u32[]{:S(2)}) collective-permute-start(bf16[2048,128]{1,0:T(8,128)(2,1)S(1)} %pad_maximum_fusion.4.refs_0_), channel_id=1, source_target_pairs={{0,4},{1,5},{2,6},{3,7},{4,8},{5,9},{6,10},{7,11},{8,12},{9,13},{1... | collective-permute-start | bytes 1572872 | tf_op jit(solution)/shard_map/ppermute | solution.py:264
  64.3 21.3 %collective-permute-start.7 = (bf16[2048,128]{1,0:T(8,128)(2,1)S(1)}, bf16[2048,128]{1,0:T(8,128)(2,1)S(1)}, u32[]{:S(2)}, u32[]{:S(2)}) collective-permute-start(bf16[2048,128]{1,0:T(8,128)(2,1)S(1)} %fusion.refs_0_), channel_id=1, source_target_pairs={{4,0},{5,1},{6,2},{7,3},{8,4},{9,5},{10,6},{11,7},{12,8},{13,9},{1... | collective-permute-start | bytes 1572872 | tf_op jit(solution)/shard_map/ppermute | solution.py:264
  65.6 21.3 %collective-permute-start.9 = (bf16[2048,128]{1,0:T(8,128)(2,1)S(1)}, bf16[2048,128]{1,0:T(8,128)(2,1)}, u32[]{:S(2)}, u32[]{:S(2)}) collective-permute-start(bf16[2048,128]{1,0:T(8,128)(2,1)S(1)} %fusion.refs_0_), channel_id=1, source_target_pairs={{0,4},{1,5},{2,6},{3,7},{4,8},{5,9},{6,10},{7,11},{8,12},{9,13},{1... | collective-permute-start | bytes 1572872 | tf_op jit(solution)/shard_map/ppermute | solution.py:264
  75.8 21.0 %collective-permute-start.6 = (bf16[2048,128]{1,0:T(8,128)(2,1)S(1)}, bf16[2048,128]{1,0:T(8,128)(2,1)S(1)}, u32[]{:S(2)}, u32[]{:S(2)}) collective-permute-start(bf16[2048,128]{1,0:T(8,128)(2,1)S(1)} %collective-permute-done.5), channel_id=1, source_target_pairs={{4,0},{5,1},{6,2},{7,3},{8,4},{9,5},{10,6},{11,7},{20,16},{21,17},... | collective-permute-start | bytes 1572872 | tf_op jit(solution)/shard_map/ppermute | solution.py:264
  77.1 19.7 %collective-permute-start.12 = (bf16[2048,128]{1,0:T(8,128)(2,1)}, bf16[2048,128]{1,0:T(8,128)(2,1)S(1)}, u32[]{:S(2)}, u32[]{:S(2)}) collective-permute-start(bf16[2048,128]{1,0:T(8,128)(2,1)} %collective-permute-done.11), channel_id=1, source_target_pairs={{4,8},{5,9},{6,10},{7,11},{8,12},{9,13},{10,14},{11,15},{20,24},{2... | collective-permute-start | bytes 1572872 | tf_op jit(solution)/shard_map/ppermute | solution.py:264
  85.6 21.3 %collective-permute-start.8 = (bf16[2048,128]{1,0:T(8,128)(2,1)S(1)}, bf16[2048,128]{1,0:T(8,128)(2,1)S(1)}, u32[]{:S(2)}, u32[]{:S(2)}) collective-permute-start(bf16[2048,128]{1,0:T(8,128)(2,1)S(1)} %collective-permute-done.7), channel_id=1, source_target_pairs={{4,0},{5,1},{6,2},{7,3},{8,4},{9,5},{10,6},{11,7},{20,16},{21,17},... | collective-permute-start | bytes 1572872 | tf_op jit(solution)/shard_map/ppermute | solution.py:264
  86.9 21.3 %collective-permute-start.10 = (bf16[2048,128]{1,0:T(8,128)(2,1)}, bf16[2048,128]{1,0:T(8,128)(2,1)S(1)}, u32[]{:S(2)}, u32[]{:S(2)}) collective-permute-start(bf16[2048,128]{1,0:T(8,128)(2,1)} %collective-permute-done.9), channel_id=1, source_target_pairs={{4,8},{5,9},{6,10},{7,11},{8,12},{9,13},{10,14},{11,15},{20,24},{2... | collective-permute-start | bytes 1572872 | tf_op jit(solution)/shard_map/ppermute | solution.py:264
  87.7 21.4 %copy-start.2 = (s32[4,4]{1,0:T(4,128)S(1)}, s32[4,4]{1,0:T(4,128)}, u32[]{:S(2)}) copy-start(s32[4,4]{1,0:T(4,128)} %constant.37.clone.order_ref) | copy-start | bytes 196
  106.9 20.4 %collective-permute-start.14 = (bf16[2048,128]{1,0:T(8,128)(2,1)S(1)}, bf16[2048,128]{1,0:T(8,128)(2,1)S(1)}, u32[]{:S(2)}, u32[]{:S(2)}) collective-permute-start(bf16[2048,128]{1,0:T(8,128)(2,1)S(1)} %collective-permute-done.8), channel_id=1, source_target_pairs={{4,0},{5,1},{6,2},{7,3},{20,16},{21,17},{22,18},{23,19}} | collective-permute-start | bytes 1572872 | tf_op jit(solution)/shard_map/ppermute | solution.py:264
  108.2 19.1 %collective-permute-start.13 = (bf16[2048,128]{1,0:T(8,128)(2,1)S(1)}, bf16[2048,128]{1,0:T(8,128)(2,1)S(1)}, u32[]{:S(2)}, u32[]{:S(2)}) collective-permute-start(bf16[2048,128]{1,0:T(8,128)(2,1)S(1)} %collective-permute-done.10), channel_id=1, source_target_pairs={{8,12},{9,13},{10,14},{11,15},{24,28},{25,29},{26,30},{27,31}} | collective-permute-start | bytes 1572872 | tf_op jit(solution)/shard_map/ppermute | solution.py:264
  125.2 14.8 %collective-permute-start.16 = (bf16[2048,128]{1,0:T(8,128)(2,1)S(1)}, bf16[2048,128]{1,0:T(8,128)(2,1)S(1)}, u32[]{:S(2)}, u32[]{:S(2)}) collective-permute-start(bf16[2048,128]{1,0:T(8,128)(2,1)S(1)} %collective-permute-done.6), channel_id=1, source_target_pairs={{4,0},{5,1},{6,2},{7,3},{20,16},{21,17},{22,18},{23,19}} | collective-permute-start | bytes 1572872 | tf_op jit(solution)/shard_map/ppermute | solution.py:264
  126.5 13.5 %collective-permute-start.15 = (bf16[2048,128]{1,0:T(8,128)(2,1)S(1)}, bf16[2048,128]{1,0:T(8,128)(2,1)S(1)}, u32[]{:S(2)}, u32[]{:S(2)}) collective-permute-start(bf16[2048,128]{1,0:T(8,128)(2,1)S(1)} %collective-permute-done.12), channel_id=1, source_target_pairs={{8,12},{9,13},{10,14},{11,15},{24,28},{25,29},{26,30},{27,31}} | collective-permute-start | bytes 1572872 | tf_op jit(solution)/shard_map/ppermute | solution.py:264
  130.2 12.8 %collective-permute-start.21 = (bf16[2,128,512]{2,1,0:T(8,128)(2,1)S(1)}, bf16[2,128,512]{2,1,0:T(8,128)(2,1)S(1)}, u32[]{:S(2)}, u32[]{:S(2)}) collective-permute-start(bf16[2,128,512]{2,1,0:T(8,128)(2,1)S(1)} %get-tuple-element.98), channel_id=1, source_target_pairs={{0,1},{1,0},{2,3},{3,2},{4,5},{5,4},{6,7},{7,6},{8,9},{9,8},{10,11... | collective-permute-start | bytes 786440 | tf_op jit(solution)/shard_map/ppermute | solution.py:254
  142.9 1.7 collective-permute-start.17
  143.1 14.8 %collective-permute-start.22 = (bf16[4,128,512]{2,1,0:T(8,128)(2,1)S(1)}, bf16[4,128,512]{2,1,0:T(8,128)(2,1)S(1)}, u32[]{:S(2)}, u32[]{:S(2)}) collective-permute-start(bf16[4,128,512]{2,1,0:T(8,128)(2,1)S(1)} %pad_maximum_fusion.6), channel_id=1, source_target_pairs={{0,2},{1,3},{2,0},{3,1},{4,6},{5,7},{6,4},{7,5},{8,10},{9,11},{10,... | collective-permute-start | bytes 1572872 | tf_op jit(solution)/shard_map/ppermute | solution.py:259
  144.6 24.0 %collective-permute-start.18 = (bf16[4,128,512]{2,1,0:T(8,128)(2,1)S(1)}, bf16[4,128,512]{2,1,0:T(8,128)(2,1)S(1)}, u32[]{:S(2)}, u32[]{:S(2)}) collective-permute-start(bf16[4,128,512]{2,1,0:T(8,128)(2,1)S(1)} %pad_maximum_fusion.5), channel_id=1, source_target_pairs={{0,2},{1,3},{2,0},{3,1},{4,6},{5,7},{6,4},{7,5},{8,10},{9,11},{10,... | collective-permute-start | bytes 1572872 | tf_op jit(solution)/shard_map/ppermute | solution.py:259
  148.8 9.1 %collective-permute-start.20 = (bf16[2,128,512]{2,1,0:T(8,128)(2,1)S(1)}, bf16[2,128,512]{2,1,0:T(8,128)(2,1)S(1)}, u32[]{:S(2)}, u32[]{:S(2)}) collective-permute-start(bf16[2,128,512]{2,1,0:T(8,128)(2,1)S(1)} %slice.81), channel_id=1, source_target_pairs={{0,1},{1,0},{2,3},{3,2},{4,5},{5,4},{6,7},{7,6},{8,9},{9,8},{10,11... | collective-permute-start | bytes 786440 | tf_op jit(solution)/shard_map/ppermute | solution.py:254
  151.6 6.3 %collective-permute-start.19 = (bf16[2,128,512]{2,1,0:T(8,128)(2,1)S(1)}, bf16[2,128,512]{2,1,0:T(8,128)(2,1)S(1)}, u32[]{:S(2)}, u32[]{:S(2)}) collective-permute-start(bf16[2,128,512]{2,1,0:T(8,128)(2,1)S(1)} %slice.80), channel_id=1, source_target_pairs={{0,1},{1,0},{2,3},{3,2},{4,5},{5,4},{6,7},{7,6},{8,9},{9,8},{10,11... | collective-permute-start | bytes 786440 | tf_op jit(solution)/shard_map/ppermute | solution.py:254
  168.8 6.0 %copy-start.1 = (bf16[128,4096]{1,0:T(8,128)(2,1)S(1)}, bf16[128,4096]{1,0:T(8,128)(2,1)}, u32[]{:S(2)}) copy-start(bf16[128,4096]{1,0:T(8,128)(2,1)} %param.10) | copy-start | bytes 3145732
Sparse Core Ops, SparseCore 0:
  8.9 48.6 all-gather.2
  59.5 88.5 all-gather.4
